TPU v7x, 32 devices: a whole 2x2x4 slice. The times are simulated.
32 devices in a mesh: rep: 2 (over x), grp: 8 (over z, y), mem: 2 (over core).
Axes of the slice: x: 2, y: 2, z: 4, core: 2. Of those that a mesh axis runs over, the one named last changes fastest.
Arguments:
- layer_input: bfloat16 [4096, 2048], P(('rep', 'grp', 'mem')), parts along dimension 0, may hold values from -6 to 6
- output_grad: bfloat16 [4096, 2048], P(('rep', 'grp', 'mem')), parts along dimension 0, may hold values from -24 to 24
- expert_ids: int32 [4096, 8], P(('rep', 'grp', 'mem')), parts along dimension 0, may hold values from 0 to 15, all different within a row; in each aligned block of 128 rows (0 to 127, 128 to 255, ...) at most 72 rows name the same one
- route_ints: int32 [4096, 8], P(('rep', 'grp', 'mem')), parts along dimension 0, may hold values from 1 to 255
- w_gate: bfloat16 [16, 2048, 384], P(('grp', 'mem')), may hold values from -0.125 to 0.125
- w_up: bfloat16 [16, 2048, 384], P(('grp', 'mem')), may hold values from -0.125 to 0.125
- w_down: bfloat16 [16, 384, 2048], P(('grp', 'mem')), may hold values from -0.3125 to 0.3125
Outputs:
- input_grad: bfloat16 [4096, 2048], P(('rep', 'grp', 'mem')), parts along dimension 0
- grad_gate: bfloat16 [32, 2048, 384], P(('rep', 'grp', 'mem')), parts along dimension 0
- grad_up: bfloat16 [32, 2048, 384], P(('rep', 'grp', 'mem')), parts along dimension 0
- grad_down: bfloat16 [32, 384, 2048], P(('rep', 'grp', 'mem')), parts along dimension 0
There are 2 independent parts, one for each index of `rep`. A program takes and returns all parts, laid end to end along the dimension named above; an argument that names none is the same for every part. Nothing has to cross between parts.
Inputs may be any that keep to these rules, and one draw needn't show every extreme that they name: `expert_ids`: each row names 8 different experts. The 128 rows of one device name any one expert at most 72 times, and in every draw some device names some expert exactly 72 times.
All inputs are finite; a program needn't handle non-finite values.
Results may differ from a plain program's by a relative error of at most 0.0064.
Values may be sent and summed in bfloat16 or wider, within the bound.
No kernel may reach another device: no remote copies, remote signals or barrier semaphores. Data moves between devices by JAX's collectives and lax.ppermute only.
A program may use at most 128 MiB of HBM per device.

v0:
```python
import jax
import jax.numpy as jnp
from jax import lax
from jax.sharding import PartitionSpec as P


def local(layer_input, output_grad, expert_ids, route_ints, w_gate, w_up, w_down):
    devices = lax.axis_size("grp") * lax.axis_size("mem")
    tok_rows = layer_input.shape[0]
    model_width = layer_input.shape[1]
    top_count = expert_ids.shape[1]
    pair_count = tok_rows * top_count
    capacity = max(2, 9 * tok_rows * top_count // (8 * devices))
    slot_count = devices * capacity
    quotas = route_ints.astype(jnp.float32)
    route_ratio = quotas / jnp.sum(quotas, axis=1, keepdims=True)
    scaled = (route_ratio[:, :, None] * output_grad.astype(jnp.float32)[:, None, :]).astype(
        jnp.bfloat16
    )
    scaled = scaled.reshape(pair_count, model_width)
    flat_ids = expert_ids.reshape(pair_count)
    pair_order = jnp.arange(pair_count, dtype=jnp.int32)
    earlier = (flat_ids[None, :] == flat_ids[:, None]) & (pair_order[None, :] < pair_order[:, None])
    slot_rank = jnp.sum(earlier.astype(jnp.int32), axis=1)
    slot_key = flat_ids * capacity + slot_rank
    slot_match = slot_key[None, :] == jnp.arange(slot_count, dtype=jnp.int32)[:, None]
    filled = jnp.any(slot_match, axis=1)
    source_pair = jnp.sum(jnp.where(slot_match, pair_order[None, :], 0), axis=1)
    send_x = jnp.where(
        filled[:, None], layer_input[source_pair // top_count], jnp.zeros((), jnp.bfloat16)
    )
    send_grad = jnp.where(filled[:, None], scaled[source_pair], jnp.zeros((), jnp.bfloat16))
    recv_x, recv_grad = (
        lax.all_to_all(
            send_x.reshape(devices, capacity, model_width),
            ("grp", "mem"),
            split_axis=0,
            concat_axis=0,
            tiled=True,
        ),
        lax.all_to_all(
            send_grad.reshape(devices, capacity, model_width),
            ("grp", "mem"),
            split_axis=0,
            concat_axis=0,
            tiled=True,
        ),
    )
    rows_x = recv_x.reshape(slot_count, model_width)
    rows_grad = recv_grad.reshape(slot_count, model_width)
    gate_w = w_gate[0]
    up_w = w_up[0]
    down_w = w_down[0]
    gate_pre = jnp.dot(rows_x, gate_w, preferred_element_type=jnp.float32)
    up_pre = jnp.dot(rows_x, up_w, preferred_element_type=jnp.float32)
    sigmoid_gate = jax.nn.sigmoid(gate_pre)
    activity = gate_pre * sigmoid_gate
    hidden = (activity * up_pre).astype(jnp.bfloat16)
    hidden_grad = jnp.dot(rows_grad, down_w.T, preferred_element_type=jnp.float32)
    up_grad = (hidden_grad * activity).astype(jnp.bfloat16)
    gate_grad = (
        hidden_grad * up_pre * sigmoid_gate * (1.0 + gate_pre * (1.0 - sigmoid_gate))
    ).astype(jnp.bfloat16)
    row_grad = (
        jnp.dot(gate_grad, gate_w.T, preferred_element_type=jnp.float32)
        + jnp.dot(up_grad, up_w.T, preferred_element_type=jnp.float32)
    ).astype(jnp.bfloat16)
    returned = lax.all_to_all(
        row_grad.reshape(devices, capacity, model_width),
        ("grp", "mem"),
        split_axis=0,
        concat_axis=0,
        tiled=True,
    )
    down_wgrad = jnp.dot(hidden.T, rows_grad, preferred_element_type=jnp.float32).astype(
        jnp.bfloat16
    )
    gate_wgrad = jnp.dot(rows_x.T, gate_grad, preferred_element_type=jnp.float32).astype(
        jnp.bfloat16
    )
    up_wgrad = jnp.dot(rows_x.T, up_grad, preferred_element_type=jnp.float32).astype(jnp.bfloat16)
    back_rows = returned.reshape(slot_count, model_width)
    pair_rows = back_rows[slot_key].reshape(tok_rows, top_count, model_width)
    input_grad = jnp.sum(pair_rows.astype(jnp.float32), axis=1).astype(jnp.bfloat16)
    return (input_grad, gate_wgrad[None], up_wgrad[None], down_wgrad[None])


def solution(mesh):
    return jax.shard_map(
        local,
        mesh=mesh,
        in_specs=(
            P(("rep", "grp", "mem"), None),
            P(("rep", "grp", "mem"), None),
            P(("rep", "grp", "mem"), None),
            P(("rep", "grp", "mem"), None),
            P(("grp", "mem"), None, None),
            P(("grp", "mem"), None, None),
            P(("grp", "mem"), None, None),
        ),
        out_specs=(
            P(("rep", "grp", "mem"), None),
            P(("rep", "grp", "mem"), None, None),
            P(("rep", "grp", "mem"), None, None),
            P(("rep", "grp", "mem"), None, None),
        ),
        check_vma=False,
    )
```

profile of v0, /device:TPU:15, one launch (start us, length us, event | category | flops | bytes accessed | tf_op | source)
XLA Modules:
  0.0 393.0 jit_solution(4096251935754755626)
XLA Ops:
  0.6 0.9 copy.14
  1.6 0.1 reshape.153
  1.6 0.5 convert_reduce_fusion
  2.2 0.6 fusion.2
  2.8 0.6 select_reduce_fusion
  3.3 0.7 convert_reduce_fusion.1
  4.1 0.7 convert_divide_fusion
  4.7 0.1 copy.15
  4.8 0.1 mul.65
  4.9 0.1 broadcast_in_dim.52
  5.1 1.1 convert_element_type.38
  6.3 2.5 fusion
  8.7 13.4 %gather_fusion = bf16[1152,2048]{1,0:T(8,128)(2,1)} fusion(bf16[1024,2048]{1,0:T(8,128)(2,1)} %fusion, s32[2048]{0:T(1024)S(1)} %get-tuple-element.11), kind=kCustom, calls=%fused_computation | custom fusion | bytes 9441792 | tf_op jit(solution)/shard_map/gather | solution.py:32
  22.2 5.9 %gather_fusion.1 = bf16[1152,2048]{1,0:T(8,128)(2,1)} fusion(bf16[128,2048]{1,0:T(8,128)(2,1)S(1)} %copy-done.1, s32[2048]{0:T(1024)S(1)} %get-tuple-element.10), kind=kCustom, calls=%fused_computation.1 | custom fusion | bytes 9441792 | tf_op jit(solution)/shard_map/gather | solution.py:30
  28.1 5.6 %broadcast_select_fusion.1 = (bf16[16,72,2048]{2,1,0:T(8,128)(2,1)}, bf16[16,72,2048]{2,1,0:T(8,128)(2,1)S(1)}) fusion(bf16[16,72,2048]{2,1,0:T(8,128)(2,1)} %bitcast.45, pred[16,72]{1,0:T(8,128)(4,1)S(1)} %broadcast_in_dim.52, bf16[16,72,2048]{2,1,0:T(8,128)(2,1)} %bitcast.46), kind=kLoop, calls=%fused_computation.11 | loop fusion | flops 4718592 | bytes 18875520 | tf_op jit(solution)/shard_map/jit(_where)/select_n | solution.py:32
  33.7 109.9 %all_to_all.15 = bf16[16,72,2048]{2,1,0:T(8,128)(2,1)} all-to-all(bf16[16,72,2048]{2,1,0:T(8,128)(2,1)S(1)} %get-tuple-element.9), channel_id=1, replica_groups=mesh['rep'=2,'grp'=8,'mem'=2] {'grp','mem'}, dimensions={0} | all-to-all | bytes 9437184 | tf_op jit(solution)/shard_map/all_to_all | solution.py:34
  143.5 5.4 %all-to-all-start = ((bf16[16,72,2048]{2,1,0:T(8,128)(2,1)}), bf16[16,72,2048]{2,1,0:T(8,128)(2,1)}, u32[]{:S(2)}, u32[]{:S(2)}) async-start(bf16[16,72,2048]{2,1,0:T(8,128)(2,1)} %get-tuple-element.8), calls=%async_computation | async-start | bytes 9437184 | tf_op jit(solution)/shard_map/all_to_all | solution.py:41
  149.0 6.3 %fusion.10 = f32[1152,384]{1,0:T(8,128)} fusion(bf16[1152,2048]{1,0:T(8,128)(2,1)} %bitcast.48, bf16[1,2048,384]{2,1,0:T(8,128)(2,1)S(1)} %copy-done), kind=kOutput, calls=%fused_computation.29 | convolution fusion | flops 1811939328 | bytes 8060928 | tf_op jit(solution)/shard_map/dot_general | solution.py:54
  155.3 3.9 fusion.13
  159.2 93.4 %all-to-all-done = bf16[16,72,2048]{2,1,0:T(8,128)(2,1)} async-done(((bf16[16,72,2048]{2,1,0:T(8,128)(2,1)}), bf16[16,72,2048]{2,1,0:T(8,128)(2,1)}, u32[]{:S(2)}, u32[]{:S(2)}) %all-to-all-start) | async-done | bytes 4718624 | tf_op jit(solution)/shard_map/all_to_all | solution.py:41
  252.6 7.1 %multiply_convert_fusion.1 = (bf16[1152,384]{1,0:T(8,128)(2,1)S(1)}, bf16[1152,384]{1,0:T(8,128)(2,1)S(1)}) fusion(f32[1152,384]{1,0:T(8,128)} %fusion.10, f32[1152,384]{1,0:T(8,128)} %fusion.13, bf16[1152,2048]{1,0:T(8,128)(2,1)} %bitcast.2, bf16[1,384,2048]{2,1,0:T(8,128)(2,1)} %param.13), kind=kOutput, calls=%fused_computation.23 | convolution fusion | flops 1817690112 | bytes 11599872 | tf_op jit(solution)/shard_map/dot_general | solution.py:59
  259.7 2.6 fusion.8
  262.4 4.3 %fusion.1 = bf16[1152,2048]{1,0:T(8,128)(2,1)} fusion(f32[1152,2048]{1,0:T(8,128)S(1)} %fusion.8, bf16[1152,384]{1,0:T(8,128)(2,1)S(1)} %get-tuple-element.6, bf16[1,2048,384]{2,1,0:T(8,128)(2,1)S(1)} %copy-done.3), kind=kOutput, calls=%fused_computation.6 | convolution fusion | flops 1816657920 | bytes 16613376 | tf_op jit(solution)/shard_map/dot_general | solution.py:66
  266.7 4.9 %all-to-all-start.2 = ((bf16[16,72,2048]{2,1,0:T(8,128)(2,1)}), bf16[16,72,2048]{2,1,0:T(8,128)(2,1)}, u32[]{:S(2)}, u32[]{:S(2)}) async-start(bf16[16,72,2048]{2,1,0:T(8,128)(2,1)} %bitcast.47), calls=%async_computation.2 | async-start | bytes 9437184 | tf_op jit(solution)/shard_map/all_to_all | solution.py:68
  271.7 0.1 copy.16
  271.8 0.1 mul.78
  271.9 6.7 %fusion.5 = bf16[1,2048,384]{2,1,0:T(8,128)(2,1)} fusion(bf16[1152,2048]{1,0:T(8,128)(2,1)} %bitcast.49, bf16[1152,384]{1,0:T(8,128)(2,1)} %copy-done.4), kind=kOutput, calls=%fused_computation.20 | convolution fusion | flops 1812725760 | bytes 7176192 | tf_op jit(solution)/shard_map/dot_general | solution.py:81
  278.6 3.9 fusion.4
  282.6 5.9 %fusion.6 = bf16[1,384,2048]{2,1,0:T(8,128)(2,1)} fusion(bf16[1152,2048]{1,0:T(8,128)(2,1)} %bitcast.2, f32[1152,384]{1,0:T(8,128)S(1)} %copy-done.7, f32[1152,384]{1,0:T(8,128)S(1)} %copy-done.6), kind=kOutput, calls=%fused_computation.21 | convolution fusion | flops 1815379968 | bytes 9830400 | tf_op jit(solution)/shard_map/dot_general | solution.py:75
  288.4 86.9 %all-to-all-done.2 = bf16[16,72,2048]{2,1,0:T(8,128)(2,1)} async-done(((bf16[16,72,2048]{2,1,0:T(8,128)(2,1)}), bf16[16,72,2048]{2,1,0:T(8,128)(2,1)}, u32[]{:S(2)}, u32[]{:S(2)}) %all-to-all-start.2) | async-done | bytes 4718624 | tf_op jit(solution)/shard_map/all_to_all | solution.py:68
  375.4 11.8 %gather_fusion.2 = bf16[1024,2048]{1,0:T(8,128)(2,1)} fusion(bf16[1152,2048]{1,0:T(8,128)(2,1)} %bitcast.9, s32[1024]{0:T(1024)S(1)} %broadcast_clamp_fusion), kind=kCustom, calls=%fused_computation.2 | custom fusion | bytes 8392704 | tf_op jit(solution)/shard_map/gather | solution.py:83
  387.1 5.9 %bitcast_reduce_fusion = bf16[128,2048]{1,0:T(8,128)(2,1)} fusion(bf16[1024,2048]{1,0:T(8,128)(2,1)} %gather_fusion.2), kind=kLoop, calls=%fused_computation.12 | loop fusion | flops 1835008 | bytes 4718592 | tf_op jit(solution)/shard_map/reduce_sum | solution.py:84
  (32 shorter events, 0.1 us)
Async XLA Ops:
  0.6 148.3 %copy-start = (bf16[1,2048,384]{2,1,0:T(8,128)(2,1)S(1)}, bf16[1,2048,384]{2,1,0:T(8,128)(2,1)}, u32[]{:S(2)}) copy-start(bf16[1,2048,384]{2,1,0:T(8,128)(2,1)} %param.11) | copy-start | bytes 4718596
  8.7 13.5 %copy-start.1 = (bf16[128,2048]{1,0:T(8,128)(2,1)S(1)}, bf16[128,2048]{1,0:T(8,128)(2,1)}, u32[]{:S(2)}) copy-start(bf16[128,2048]{1,0:T(8,128)(2,1)} %param.7) | copy-start | bytes 1572868
  143.5 11.7 %slice-start = ((s8[4718592]{0:T(1024)(128)(4,1)}), s8[524288]{0:T(1024)(128)(4,1)S(1)}, s32[]{:S(2)}) async-start(s8[4718592]{0:T(1024)(128)(4,1)} %bitcast.50), calls=%async_computation.3 | async-start | bytes 1048576
  143.5 109.1 %all-to-all-start = ((bf16[16,72,2048]{2,1,0:T(8,128)(2,1)}), bf16[16,72,2048]{2,1,0:T(8,128)(2,1)}, u32[]{:S(2)}, u32[]{:S(2)}) async-start(bf16[16,72,2048]{2,1,0:T(8,128)(2,1)} %get-tuple-element.8), calls=%async_computation | async-start | bytes 9437184 | tf_op jit(solution)/shard_map/all_to_all | solution.py:41
  148.9 6.4 %slice-start.1 = ((s8[4718592]{0:T(1024)(128)(4,1)}), s8[4194304]{0:T(1024)(128)(4,1)S(1)}, s32[]{:S(2)}) async-start(s8[4718592]{0:T(1024)(128)(4,1)} %bitcast.50), calls=%async_computation.4 | async-start | bytes 8388608
  148.9 6.3 %copy-start.2 = (bf16[1,2048,384]{2,1,0:T(8,128)(2,1)S(1)}, bf16[1,2048,384]{2,1,0:T(8,128)(2,1)}, u32[]{:S(2)}) copy-start(bf16[1,2048,384]{2,1,0:T(8,128)(2,1)} %param.12) | copy-start | bytes 4718596
  259.7 2.7 copy-start.4
  259.7 2.7 copy-start.3
  266.7 4.9 %copy-start.5 = (s32[128,8]{0,1:T(8,128)S(1)}, s32[128,8]{0,1:T(8,128)}, u32[]{:S(2)}) copy-start(s32[128,8]{0,1:T(8,128)} %param.9) | copy-start | bytes 12292
  266.7 11.9 %slice-start.2 = ((s8[4718592]{0:T(1024)(128)(4,1)}), s8[524288]{0:T(1024)(128)(4,1)S(1)}, s32[]{:S(2)}) async-start(s8[4718592]{0:T(1024)(128)(4,1)} %bitcast.53), calls=%async_computation.5 | async-start | bytes 1048576
  266.7 108.6 %all-to-all-start.2 = ((bf16[16,72,2048]{2,1,0:T(8,128)(2,1)}), bf16[16,72,2048]{2,1,0:T(8,128)(2,1)}, u32[]{:S(2)}, u32[]{:S(2)}) async-start(bf16[16,72,2048]{2,1,0:T(8,128)(2,1)} %bitcast.47), calls=%async_computation.2 | async-start | bytes 9437184 | tf_op jit(solution)/shard_map/all_to_all | solution.py:68
  271.9 6.7 %slice-start.3 = ((s8[4718592]{0:T(1024)(128)(4,1)}), s8[4194304]{0:T(1024)(128)(4,1)S(1)}, s32[]{:S(2)}) async-start(s8[4718592]{0:T(1024)(128)(4,1)} %bitcast.53), calls=%async_computation.6 | async-start | bytes 8388608
  278.6 3.9 %copy-start.6 = (f32[1152,384]{1,0:T(8,128)S(1)}, f32[1152,384]{1,0:T(8,128)}, u32[]{:S(2)}) copy-start(f32[1152,384]{1,0:T(8,128)} %fusion.10) | copy-start | bytes 5308420
  278.6 3.9 %copy-start.7 = (f32[1152,384]{1,0:T(8,128)S(1)}, f32[1152,384]{1,0:T(8,128)}, u32[]{:S(2)}) copy-start(f32[1152,384]{1,0:T(8,128)} %fusion.13) | copy-start | bytes 5308420
where the time goes:
time: 394 us; the launch traced here: 393 us
  waiting for transfers between devices  180 us (46%)
  blocking collectives  110 us (28%)
  matrix products  40.7 us (10%)
  local copies, waits for them, and re-layouts  32.6 us (8%)
  other arithmetic  18.3 us (5%)
  starting transfers between devices  10.3 us (3%)
    all_to_all x1, blocking collectives, local(): lax.all_to_all(send_x.reshape(devices, capacity, model_width), ('grp', 'm...  110 us
    all_to_all x1, waiting for transfers between devices, local(): lax.all_to_all(send_grad.reshape(devices, capacity, model_width), ('grp',...  93.4 us
    all_to_all x1, waiting for transfers between devices, local(): lax.all_to_all(row_grad.reshape(devices, capacity, model_width), ('grp',...  86.9 us
    gather x1, local copies, waits for them, and re-layouts, local(): scaled[source_pair]  13.4 us
    gather x1, local copies, waits for them, and re-layouts, local(): pair_rows = back_rows[slot_key].reshape(tok_rows, top_count, model_width)  11.8 us
  transfers between devices with their start and end apart: 2, of which 2 were waited for; matrix products, arithmetic and copies ran while one was open for 7% of the time, Pallas kernels for 0%

commit v1 on v0

--- a/solution.py
+++ b/solution.py
@@ -4,7 +4,7 @@
 from jax.sharding import PartitionSpec as P
 
 
-def local(layer_input, output_grad, expert_ids, route_ints, w_gate, w_up, w_down):
+def exchange_plan(layer_input, output_grad, expert_ids, route_ints, w_gate, w_up, w_down):
     devices = lax.axis_size("grp") * lax.axis_size("mem")
     tok_rows = layer_input.shape[0]
     model_width = layer_input.shape[1]
@@ -85,6 +85,184 @@
     return (input_grad, gate_wgrad[None], up_wgrad[None], down_wgrad[None])
 
 
+TN = (((0,), (0,)), ((), ()))
+NT = (((1,), (1,)), ((), ()))
+
+
+def ring_order(count):
+    return list(range(0, count, 2)) + list(reversed(range(1, count, 2)))
+
+
+def mm(a, b, dims=(((1,), (0,)), ((), ()))):
+    return lax.dot_general(a, b, dims, preferred_element_type=jnp.float32)
+
+
+def ring_plan(layer_input, output_grad, expert_ids, route_ints, w_gate, w_up, w_down):
+    groups = lax.axis_size("grp")
+    members = lax.axis_size("mem")
+    tok_rows, _ = layer_input.shape
+    width = w_gate.shape[2]
+    span = members * width
+    order = ring_order(groups)
+    full_steps = (groups - 1) // 2
+    has_far = groups % 2 == 0 and groups > 1
+
+    def at_distance(k):
+        return [(order[i], order[(i + k) % groups]) for i in range(groups)]
+
+    def shift(array, k):
+        return lax.ppermute(array, "grp", at_distance(k))
+
+    def member_shift(array, step):
+        return lax.ppermute(array, "mem", [(m, (m + step) % members) for m in range(members)])
+
+    from_left, from_right = [], []
+    rx, rg, lx, lg = layer_input, output_grad, layer_input, output_grad
+    for _ in range(1, full_steps + 1):
+        rg, lg = shift(rg, 1), shift(lg, -1)
+        rx, lx = shift(rx, 1), shift(lx, -1)
+        from_left.append((rx, rg))
+        from_right.append((lx, lg))
+    far = (shift(rx, 1), shift(lg, -1)) if has_far else None
+
+    quotas = route_ints.astype(jnp.float32)
+    route_ratio = quotas / jnp.sum(quotas, axis=1, keepdims=True)
+    group_at = jnp.array(
+        [[order[(order.index(g) + k) % groups] for k in range(groups)] for g in range(groups)],
+        jnp.int32,
+    )
+    mine = jnp.arange(groups, dtype=jnp.int32)[:, None] == lax.axis_index("grp")
+    chip = jnp.sum(jnp.where(mine, group_at, 0), axis=0)
+    core = (lax.axis_index("mem") + jnp.arange(members, dtype=jnp.int32)) % members
+    expert = chip[:, None] * members + core[None, :]
+    chosen = expert_ids[None, None, :, :] == expert[:, :, None, None]
+    outgoing = jnp.sum(jnp.where(chosen, route_ratio[None, None], 0.0), axis=3)
+    distances = [0]
+    for k in range(1, full_steps + 1):
+        distances += [-k, k]
+    if has_far:
+        distances.append(groups // 2)
+    ratios = []
+    for d in distances:
+        ratios.append(outgoing[0] if d == 0 else shift(outgoing[(-d) % groups], -d))
+    ratios = jnp.concatenate(ratios, axis=1).T
+
+    gates, ups, downs = [w_gate[0]], [w_up[0]], [w_down[0]]
+    for k in range(1, members):
+        gates.append(member_shift(w_gate[0], members - k))
+        ups.append(member_shift(w_up[0], members - k))
+        downs.append(member_shift(w_down[0], members - k))
+    gate_w = jnp.concatenate(gates, axis=1)
+    up_w = jnp.concatenate(ups, axis=1)
+    down_w = jnp.concatenate(downs, axis=0)
+    column = jnp.arange(span, dtype=jnp.int32)[None, :] // width
+
+    def piece(x, og, ratio):
+        r = ratio[:, 0:1]
+        for m in range(1, members):
+            r = jnp.where(column == m, ratio[:, m : m + 1], r)
+        gate, up = mm(x, gate_w), mm(x, up_w)
+        s = jax.nn.sigmoid(gate)
+        act = gate * s
+        hidden = (act * up * r).astype(jnp.bfloat16)
+        hg = r * mm(og, down_w, NT)
+        ug = (hg * act).astype(jnp.bfloat16)
+        gg = (hg * up * s * (1.0 + gate * (1.0 - s))).astype(jnp.bfloat16)
+        part = mm(gg, gate_w, NT) + mm(ug, up_w, NT)
+        return part, gg, ug, hidden
+
+    kept = []
+    own_part, *rest = piece(layer_input, output_grad, ratios[:tok_rows])
+    kept.append((layer_input, output_grad, *rest))
+    part_left, part_right = [], []
+    at = tok_rows
+    for k in range(1, full_steps + 1):
+        x = jnp.concatenate([from_left[k - 1][0], from_right[k - 1][0]], axis=0)
+        og = jnp.concatenate([from_left[k - 1][1], from_right[k - 1][1]], axis=0)
+        part, *rest = piece(x, og, ratios[at : at + 2 * tok_rows])
+        at += 2 * tok_rows
+        part = part.astype(jnp.bfloat16)
+        part_left.append(part[:tok_rows])
+        part_right.append(part[tok_rows:])
+        kept.append((x, og, *rest))
+    half = tok_rows // 2
+    far_part = None
+    if has_far:
+        part, *rest = piece(far[0], far[1], ratios[at:])
+        far_part = part.astype(jnp.bfloat16)
+        kept.append((far[0], far[1], *rest))
+
+    low, high = slice(0, half), slice(half, tok_rows)
+
+    def join(moved, part):
+        return (moved.astype(jnp.float32) + part.astype(jnp.float32)).astype(jnp.bfloat16)
+
+    def send(pair):
+        return shift(pair[0], -1), shift(pair[1], 1)
+
+    def parts_at(k, rows):
+        return part_left[k - 1][rows[0]], part_right[k - 1][rows[1]]
+
+    long_rows, short_rows = (low, high), (high, low)
+    long_way = short_way = None
+    if full_steps:
+        short_way = send(parts_at(full_steps, short_rows))
+    if has_far:
+        long_way = send((far_part[low], far_part[high]))
+    before = None
+
+    def gated(parts):
+        return parts if before is None else lax.optimization_barrier((parts, before))[0]
+
+    for k in reversed(range(1, full_steps + 1)):
+        if k > 1:
+            sums = tuple(map(join, short_way, gated(parts_at(k - 1, short_rows))))
+            short_way, before = send(sums), sums
+        sums = parts_at(k, long_rows)
+        if long_way is not None:
+            sums = tuple(map(join, long_way, gated(sums)))
+            before = sums
+        long_way = send(sums)
+    back_low = [long_way and long_way[0], short_way and short_way[1]]
+    back_high = [long_way and long_way[1], short_way and short_way[0]]
+
+    def closing(rows, returned):
+        total = own_part[rows]
+        for piece_back in returned:
+            if piece_back is not None:
+                total = total + piece_back.astype(jnp.float32)
+        return total.astype(jnp.bfloat16)
+
+    input_grad = jnp.concatenate([closing(low, back_low), closing(high, back_high)], axis=0)
+
+    x_all, og_all, gg_all, ug_all, hidden_all = (
+        jnp.concatenate([k[i] for k in kept], axis=0) for i in range(5)
+    )
+
+    def member_sum(product):
+        total = None
+        for k in reversed(range(members)):
+            columns = slice(k * width, (k + 1) * width)
+            block = product(columns)
+            if k:
+                block = member_shift(block.astype(jnp.bfloat16), k).astype(jnp.float32)
+            total = block if total is None else total + block
+        return total.astype(jnp.bfloat16)[None]
+
+    gate_g = member_sum(lambda c: mm(x_all, gg_all[:, c], TN))
+    up_g = member_sum(lambda c: mm(x_all, ug_all[:, c], TN))
+    down_g = member_sum(lambda c: mm(hidden_all[:, c], og_all, TN))
+    return (input_grad, gate_g, up_g, down_g)
+
+
+def local(layer_input, output_grad, expert_ids, route_ints, w_gate, w_up, w_down):
+    devices = lax.axis_size("grp") * lax.axis_size("mem")
+    tok_rows, top_count = expert_ids.shape
+    capacity = max(2, 9 * tok_rows * top_count // (8 * devices))
+    plan = ring_plan if tok_rows <= 2 * capacity else exchange_plan
+    return plan(layer_input, output_grad, expert_ids, route_ints, w_gate, w_up, w_down)
+
+
 def solution(mesh):
     return jax.shard_map(
         local,

time: 394 us -> 213 us (0.54)
  the two profiles are of different devices: /device:TPU:15 before, /device:TPU:0 now
where the time goes in v1:
time: 213 us; the launch traced here: 210 us
  waiting for transfers between devices  98.6 us (46%)
  matrix products  52.8 us (25%)
  starting transfers between devices  47.6 us (22%)
  other arithmetic  4.73 us (2%)
  local copies, waits for them, and re-layouts  4.43 us (2%)
    ppermute x35, waiting for transfers between devices, shift(): return lax.ppermute(array, 'grp', at_distance(k))  98.6 us
    dot_general x31, matrix products, mm(): return lax.dot_general(a, b, dims, preferred_element_type=jnp.float32)  52.8 us
    ppermute x35, starting transfers between devices, shift(): return lax.ppermute(array, 'grp', at_distance(k))  46.9 us
  transfers between devices with their start and end apart: 41, of which 19 were waited for; matrix products, arithmetic and copies ran while one was open for 28% of the time, Pallas kernels for 0%

profile of v1, /device:TPU:0, one launch (start us, length us, event | category | flops | bytes accessed | tf_op | source)
XLA Modules:
  0.0 209.7 jit_solution(12220627591335906113)
XLA Ops:
  0.6 3.0 %collective-permute-start.10 = (bf16[128,2048]{1,0:T(8,128)(2,1)}, bf16[128,2048]{1,0:T(8,128)(2,1)S(1)}, u32[]{:S(2)}, u32[]{:S(2)}) collective-permute-start(bf16[128,2048]{1,0:T(8,128)(2,1)} %param.9), channel_id=1, source_target_pairs={{0,2},{4,0},{8,4},{12,8},{14,12},{10,14},{6,10},{2,6},{1,3},{5,1},... | collective-permute-start | bytes 1572872 | tf_op jit(solution)/shard_map/ppermute | solution.py:114
  3.8 2.0 collective-permute-start.14
  8.9 2.0 collective-permute-start
  13.2 15.3 %collective-permute-done = f32[2,128]{1,0:T(2,128)S(1)} collective-permute-done((f32[2,128]{1,0:T(2,128)S(1)}, f32[2,128]{1,0:T(2,128)S(1)}, u32[]{:S(2)}, u32[]{:S(2)}) %collective-permute-start) | collective-permute-done | bytes 1056 | tf_op jit(solution)/shard_map/ppermute | solution.py:114
  30.2 2.0 collective-permute-done.1
  33.7 2.9 %collective-permute-done.2 = f32[2,128]{1,0:T(2,128)S(1)} collective-permute-done((f32[2,128]{1,0:T(2,128)S(1)}, f32[2,128]{1,0:T(2,128)S(1)}, u32[]{:S(2)}, u32[]{:S(2)}) %collective-permute-start.2) | collective-permute-done | bytes 1056 | tf_op jit(solution)/shard_map/ppermute | solution.py:114
  36.6 2.6 %collective-permute-start.3 = (f32[2,128]{1,0:T(2,128)S(1)}, f32[2,128]{1,0:T(2,128)S(1)}, u32[]{:S(2)}, u32[]{:S(2)}) collective-permute-start(f32[2,128]{1,0:T(2,128)S(1)} %get-tuple-element.96), channel_id=1, source_target_pairs={{0,6},{4,2},{8,0},{12,4},{14,8},{10,12},{6,14},{2,10},{1,7},{5,3},... | collective-permute-start | bytes 3080 | tf_op jit(solution)/shard_map/ppermute | solution.py:114
  39.2 1.9 collective-permute-done.3
  41.1 2.5 %collective-permute-start.4 = (f32[2,128]{1,0:T(2,128)S(1)}, f32[2,128]{1,0:T(2,128)S(1)}, u32[]{:S(2)}, u32[]{:S(2)}) collective-permute-start(f32[2,128]{1,0:T(2,128)S(1)} %get-tuple-element.95), channel_id=1, source_target_pairs={{0,12},{4,14},{8,10},{12,6},{14,2},{10,0},{6,4},{2,8},{1,13},{5,15... | collective-permute-start | bytes 3080 | tf_op jit(solution)/shard_map/ppermute | solution.py:114
  43.6 2.8 %collective-permute-done.4 = f32[2,128]{1,0:T(2,128)S(1)} collective-permute-done((f32[2,128]{1,0:T(2,128)S(1)}, f32[2,128]{1,0:T(2,128)S(1)}, u32[]{:S(2)}, u32[]{:S(2)}) %collective-permute-start.4) | collective-permute-done | bytes 1056 | tf_op jit(solution)/shard_map/ppermute | solution.py:114
  46.5 1.8 collective-permute-start.5
  48.3 3.6 %collective-permute-done.5 = f32[2,128]{1,0:T(2,128)S(1)} collective-permute-done((f32[2,128]{1,0:T(2,128)S(1)}, f32[2,128]{1,0:T(2,128)S(1)}, u32[]{:S(2)}, u32[]{:S(2)}) %collective-permute-start.5) | collective-permute-done | bytes 1056 | tf_op jit(solution)/shard_map/ppermute | solution.py:114
  51.8 3.5 %collective-permute-start.6 = (f32[2,128]{1,0:T(2,128)S(1)}, f32[2,128]{1,0:T(2,128)S(1)}, u32[]{:S(2)}, u32[]{:S(2)}) collective-permute-start(f32[2,128]{1,0:T(2,128)S(1)} %get-tuple-element.93), channel_id=1, source_target_pairs={{0,14},{4,10},{8,6},{12,2},{14,0},{10,4},{6,8},{2,12},{1,15},{5,11... | collective-permute-start | bytes 3080 | tf_op jit(solution)/shard_map/ppermute | solution.py:114
  55.4 2.7 %collective-permute-done.6 = f32[2,128]{1,0:T(2,128)S(1)} collective-permute-done((f32[2,128]{1,0:T(2,128)S(1)}, f32[2,128]{1,0:T(2,128)S(1)}, u32[]{:S(2)}, u32[]{:S(2)}) %collective-permute-start.6) | collective-permute-done | bytes 1056 | tf_op jit(solution)/shard_map/ppermute | solution.py:114
  58.2 2.0 collective-permute-start.23
  62.6 10.4 %collective-permute-done.15 = bf16[128,2048]{1,0:T(8,128)(2,1)S(1)} collective-permute-done((bf16[128,2048]{1,0:T(8,128)(2,1)S(1)}, bf16[128,2048]{1,0:T(8,128)(2,1)S(1)}, u32[]{:S(2)}, u32[]{:S(2)}) %collective-permute-start.15) | collective-permute-done | bytes 524320 | tf_op jit(solution)/shard_map/ppermute | solution.py:114
  73.0 10.8 %collective-permute-done.20 = bf16[128,2048]{1,0:T(8,128)(2,1)S(1)} collective-permute-done((bf16[128,2048]{1,0:T(8,128)(2,1)S(1)}, bf16[128,2048]{1,0:T(8,128)(2,1)S(1)}, u32[]{:S(2)}, u32[]{:S(2)}) %collective-permute-start.20) | collective-permute-done | bytes 524320 | tf_op jit(solution)/shard_map/ppermute | solution.py:114
  86.5 12.1 %collective-permute-done.21 = bf16[128,2048]{1,0:T(8,128)(2,1)S(1)} collective-permute-done((bf16[128,2048]{1,0:T(8,128)(2,1)S(1)}, bf16[128,2048]{1,0:T(8,128)(2,1)S(1)}, u32[]{:S(2)}, u32[]{:S(2)}) %collective-permute-start.21) | collective-permute-done | bytes 524320 | tf_op jit(solution)/shard_map/ppermute | solution.py:114
  100.2 8.3 %collective-permute-done.16 = bf16[128,2048]{1,0:T(8,128)(2,1)S(1)} collective-permute-done((bf16[128,2048]{1,0:T(8,128)(2,1)S(1)}, bf16[128,2048]{1,0:T(8,128)(2,1)S(1)}, u32[]{:S(2)}, u32[]{:S(2)}) %collective-permute-start.16) | collective-permute-done | bytes 524320 | tf_op jit(solution)/shard_map/ppermute | solution.py:114
  110.3 1.9 collective-permute-start.17
  128.3 10.7 %fusion.58 = f32[256,2048]{1,0:T(8,128)S(1)} fusion(bf16[256,768]{1,0:T(8,128)(2,1)S(1)} %get-tuple-element.42, bf16[2048,384]{1,0:T(8,128)(2,1)S(1)} %collective-permute-done.8, bf16[2048,384]{1,0:T(8,128)(2,1)S(1)} %bitcast.108), kind=kOutput, calls=%fused_computation.180 | convolution fusion | flops 811597824 | bytes 5636096 | tf_op jit(solution)/shard_map/dot_general | solution.py:97
  140.2 1.6 collective-permute-start.26
  157.5 2.4 %convolution_convert_fusion.2 = bf16[2048,384]{1,0:T(8,128)(2,1)S(1)} fusion(bf16[1024,2048]{1,0:T(8,128)(2,1)S(1)} %constant_dynamic-update-slice_fusion.14, bf16[1024,768]{1,0:T(8,128)(2,1)S(1)} %get-tuple-element.30), kind=kOutput, calls=%fused_computation.8 | convolution fusion | flops 1611399168 | bytes 6553600 | tf_op jit(solution)/shard_map/dot_general | solution.py:97
  160.0 2.4 %convolution_convert_fusion.1 = bf16[2048,384]{1,0:T(8,128)(2,1)S(1)} fusion(bf16[1024,2048]{1,0:T(8,128)(2,1)S(1)} %constant_dynamic-update-slice_fusion.14, bf16[1024,768]{1,0:T(8,128)(2,1)S(1)} %get-tuple-element.64), kind=kOutput, calls=%fused_computation.7 | convolution fusion | flops 1611399168 | bytes 6553600 | tf_op jit(solution)/shard_map/dot_general | solution.py:97
  166.3 5.1 %collective-permute-done.27 = bf16[64,2048]{1,0:T(8,128)(2,1)S(1)} collective-permute-done((bf16[64,2048]{1,0:T(8,128)(2,1)S(1)}, bf16[64,2048]{1,0:T(8,128)(2,1)S(1)}, u32[]{:S(2)}, u32[]{:S(2)}) %collective-permute-start.27) | collective-permute-done | bytes 262176 | tf_op jit(solution)/shard_map/ppermute | solution.py:114
  175.0 9.4 %collective-permute-done.31 = bf16[64,2048]{1,0:T(8,128)(2,1)S(1)} collective-permute-done((bf16[64,2048]{1,0:T(8,128)(2,1)S(1)}, bf16[64,2048]{1,0:T(8,128)(2,1)S(1)}, u32[]{:S(2)}, u32[]{:S(2)}) %collective-permute-start.31) | collective-permute-done | bytes 262176 | tf_op jit(solution)/shard_map/ppermute | solution.py:114
  185.3 5.6 %collective-permute-done.35 = bf16[64,2048]{1,0:T(8,128)(2,1)S(1)} collective-permute-done((bf16[64,2048]{1,0:T(8,128)(2,1)S(1)}, bf16[64,2048]{1,0:T(8,128)(2,1)S(1)}, u32[]{:S(2)}, u32[]{:S(2)}) %collective-permute-start.35) | collective-permute-done | bytes 262176 | tf_op jit(solution)/shard_map/ppermute | solution.py:114
  193.2 1.8 convolution_convert_fusion
  195.2 2.1 %collective-permute-done.33 = bf16[64,2048]{1,0:T(8,128)(2,1)S(1)} collective-permute-done((bf16[64,2048]{1,0:T(8,128)(2,1)S(1)}, bf16[64,2048]{1,0:T(8,128)(2,1)S(1)}, u32[]{:S(2)}, u32[]{:S(2)}) %collective-permute-start.33) | collective-permute-done | bytes 262176 | tf_op jit(solution)/shard_map/ppermute | solution.py:114
  199.3 3.5 %fusion.3 = bf16[1,2048,384]{2,1,0:T(8,128)(2,1)} fusion(bf16[1024,2048]{1,0:T(8,128)(2,1)S(1)} %constant_dynamic-update-slice_fusion.14, bf16[2048,384]{1,0:T(8,128)(2,1)S(1)} %collective-permute-done.38, bf16[1024,768]{1,0:T(8,128)(2,1)S(1)} %get-tuple-element.30), kind=kOutput, calls=%fused_computation.15 | convolution fusion | flops 1612972032 | bytes 8126464 | tf_op jit(solution)/shard_map/dot_general | solution.py:97
  202.9 3.5 %fusion.4 = bf16[1,2048,384]{2,1,0:T(8,128)(2,1)} fusion(bf16[1024,2048]{1,0:T(8,128)(2,1)S(1)} %constant_dynamic-update-slice_fusion.14, bf16[2048,384]{1,0:T(8,128)(2,1)S(1)} %collective-permute-done.39, bf16[1024,768]{1,0:T(8,128)(2,1)S(1)} %get-tuple-element.64), kind=kOutput, calls=%fused_computation.16 | convolution fusion | flops 1612972032 | bytes 8126464 | tf_op jit(solution)/shard_map/dot_general | solution.py:97
  206.4 3.0 %fusion.5 = bf16[1,384,2048]{2,1,0:T(8,128)(2,1)} fusion(bf16[1024,2048]{1,0:T(8,128)(2,1)S(1)} %constant_dynamic-update-slice_fusion.32, bf16[384,2048]{1,0:T(8,128)(2,1)S(1)} %collective-permute-done.40, bf16[1024,768]{1,0:T(8,128)(2,1)S(1)} %get-tuple-element.63), kind=kOutput, calls=%fused_computation.17 | convolution fusion | flops 1612972032 | bytes 8126464 | tf_op jit(solution)/shard_map/dot_general | solution.py:97
  (142 shorter events, 62.8 us)
Async XLA Ops:
  0.6 59.6 %collective-permute-start.10 = (bf16[128,2048]{1,0:T(8,128)(2,1)}, bf16[128,2048]{1,0:T(8,128)(2,1)S(1)}, u32[]{:S(2)}, u32[]{:S(2)}) collective-permute-start(bf16[128,2048]{1,0:T(8,128)(2,1)} %param.9), channel_id=1, source_target_pairs={{0,2},{4,0},{8,4},{12,8},{14,12},{10,14},{6,10},{2,6},{1,3},{5,1},... | collective-permute-start | bytes 1572872 | tf_op jit(solution)/shard_map/ppermute | solution.py:114
  3.7 58.2 %collective-permute-start.19 = (bf16[128,2048]{1,0:T(8,128)(2,1)}, bf16[128,2048]{1,0:T(8,128)(2,1)S(1)}, u32[]{:S(2)}, u32[]{:S(2)}) collective-permute-start(bf16[128,2048]{1,0:T(8,128)(2,1)} %param.9), channel_id=1, source_target_pairs={{0,4},{4,8},{8,12},{12,14},{14,10},{10,6},{6,2},{2,0},{1,5},{5,9},... | collective-permute-start | bytes 1572872 | tf_op jit(solution)/shard_map/ppermute | solution.py:114
  3.8 54.3 %collective-permute-start.14 = (bf16[128,2048]{1,0:T(8,128)(2,1)}, bf16[128,2048]{1,0:T(8,128)(2,1)S(1)}, u32[]{:S(2)}, u32[]{:S(2)}) collective-permute-start(bf16[128,2048]{1,0:T(8,128)(2,1)} %param.8), channel_id=1, source_target_pairs={{0,4},{4,8},{8,12},{12,14},{14,10},{10,6},{6,2},{2,0},{1,5},{5,9},... | collective-permute-start | bytes 1572872 | tf_op jit(solution)/shard_map/ppermute | solution.py:114
  5.8 52.5 %collective-permute-start.22 = (bf16[128,2048]{1,0:T(8,128)(2,1)}, bf16[128,2048]{1,0:T(8,128)(2,1)S(1)}, u32[]{:S(2)}, u32[]{:S(2)}) collective-permute-start(bf16[128,2048]{1,0:T(8,128)(2,1)} %param.8), channel_id=1, source_target_pairs={{0,2},{4,0},{8,4},{12,8},{14,12},{10,14},{6,10},{2,6},{1,3},{5,1},... | collective-permute-start | bytes 1572872 | tf_op jit(solution)/shard_map/ppermute | solution.py:114
  8.9 19.7 %collective-permute-start = (f32[2,128]{1,0:T(2,128)S(1)}, f32[2,128]{1,0:T(2,128)S(1)}, u32[]{:S(2)}, u32[]{:S(2)}) collective-permute-start(f32[2,128]{1,0:T(2,128)S(1)} %get-tuple-element.99), channel_id=1, source_target_pairs={{0,4},{4,8},{8,12},{12,14},{14,10},{10,6},{6,2},{2,0},{1,5},{5,9},... | collective-permute-start | bytes 3080 | tf_op jit(solution)/shard_map/ppermute | solution.py:114
  58.1 54.9 %collective-permute-start.7 = (bf16[384,2048]{1,0:T(8,128)(2,1)}, bf16[384,2048]{1,0:T(8,128)(2,1)S(1)}, u32[]{:S(2)}, u32[]{:S(2)}) collective-permute-start(bf16[384,2048]{1,0:T(8,128)(2,1)} %bitcast.96), channel_id=1, source_target_pairs={{0,1},{1,0},{2,3},{3,2},{4,5},{5,4},{6,7},{7,6},{8,9},{9,8},{10,11... | collective-permute-start | bytes 4718600 | tf_op jit(solution)/shard_map/ppermute | solution.py:117
  58.1 14.8 %collective-permute-start.15 = (bf16[128,2048]{1,0:T(8,128)(2,1)S(1)}, bf16[128,2048]{1,0:T(8,128)(2,1)S(1)}, u32[]{:S(2)}, u32[]{:S(2)}) collective-permute-start(bf16[128,2048]{1,0:T(8,128)(2,1)S(1)} %collective-permute-done.14), channel_id=1, source_target_pairs={{0,4},{4,8},{8,12},{12,14},{14,10},{10,6},{6,2},{2,0},{1,5},{5,9},... | collective-permute-start | bytes 1572872 | tf_op jit(solution)/shard_map/ppermute | solution.py:114
  58.2 26.0 %collective-permute-start.23 = (bf16[128,2048]{1,0:T(8,128)(2,1)S(1)}, bf16[128,2048]{1,0:T(8,128)(2,1)S(1)}, u32[]{:S(2)}, u32[]{:S(2)}) collective-permute-start(bf16[128,2048]{1,0:T(8,128)(2,1)S(1)} %collective-permute-done.22), channel_id=1, source_target_pairs={{0,2},{4,0},{8,4},{12,8},{14,12},{10,14},{6,10},{2,6},{1,3},{5,1},... | collective-permute-start | bytes 1572872 | tf_op jit(solution)/shard_map/ppermute | solution.py:114
  60.2 25.0 %collective-permute-start.11 = (bf16[128,2048]{1,0:T(8,128)(2,1)S(1)}, bf16[128,2048]{1,0:T(8,128)(2,1)S(1)}, u32[]{:S(2)}, u32[]{:S(2)}) collective-permute-start(bf16[128,2048]{1,0:T(8,128)(2,1)S(1)} %collective-permute-done.10), channel_id=1, source_target_pairs={{0,2},{4,0},{8,4},{12,8},{14,12},{10,14},{6,10},{2,6},{1,3},{5,1},... | collective-permute-start | bytes 1572872 | tf_op jit(solution)/shard_map/ppermute | solution.py:114
  61.9 21.9 %collective-permute-start.20 = (bf16[128,2048]{1,0:T(8,128)(2,1)S(1)}, bf16[128,2048]{1,0:T(8,128)(2,1)S(1)}, u32[]{:S(2)}, u32[]{:S(2)}) collective-permute-start(bf16[128,2048]{1,0:T(8,128)(2,1)S(1)} %collective-permute-done.19), channel_id=1, source_target_pairs={{0,4},{4,8},{8,12},{12,14},{14,10},{10,6},{6,2},{2,0},{1,5},{5,9},... | collective-permute-start | bytes 1572872 | tf_op jit(solution)/shard_map/ppermute | solution.py:114
  73.0 39.3 %collective-permute-start.8 = (bf16[2048,384]{1,0:T(8,128)(2,1)S(1)}, bf16[2048,384]{1,0:T(8,128)(2,1)S(1)}, u32[]{:S(2)}, u32[]{:S(2)}) collective-permute-start(bf16[2048,384]{1,0:T(8,128)(2,1)S(1)} %bitcast.102), channel_id=1, source_target_pairs={{0,1},{1,0},{2,3},{3,2},{4,5},{5,4},{6,7},{7,6},{8,9},{9,8},{10,11... | collective-permute-start | bytes 4718600 | tf_op jit(solution)/shard_map/ppermute | solution.py:117
  83.8 14.8 %collective-permute-start.21 = (bf16[128,2048]{1,0:T(8,128)(2,1)S(1)}, bf16[128,2048]{1,0:T(8,128)(2,1)S(1)}, u32[]{:S(2)}, u32[]{:S(2)}) collective-permute-start(bf16[128,2048]{1,0:T(8,128)(2,1)S(1)} %collective-permute-done.20), channel_id=1, source_target_pairs={{0,4},{4,8},{8,12},{12,14},{14,10},{10,6},{6,2},{2,0},{1,5},{5,9},... | collective-permute-start | bytes 1572872 | tf_op jit(solution)/shard_map/ppermute | solution.py:114
  84.2 24.2 %collective-permute-start.16 = (bf16[128,2048]{1,0:T(8,128)(2,1)S(1)}, bf16[128,2048]{1,0:T(8,128)(2,1)S(1)}, u32[]{:S(2)}, u32[]{:S(2)}) collective-permute-start(bf16[128,2048]{1,0:T(8,128)(2,1)S(1)} %collective-permute-done.15), channel_id=1, source_target_pairs={{0,4},{4,8},{8,12},{12,14},{14,10},{10,6},{6,2},{2,0},{1,5},{5,9},... | collective-permute-start | bytes 1572872 | tf_op jit(solution)/shard_map/ppermute | solution.py:114
  85.2 23.3 %collective-permute-start.12 = (bf16[128,2048]{1,0:T(8,128)(2,1)S(1)}, bf16[128,2048]{1,0:T(8,128)(2,1)S(1)}, u32[]{:S(2)}, u32[]{:S(2)}) collective-permute-start(bf16[128,2048]{1,0:T(8,128)(2,1)S(1)} %collective-permute-done.11), channel_id=1, source_target_pairs={{0,2},{4,0},{8,4},{12,8},{14,12},{10,14},{6,10},{2,6},{1,3},{5,1},... | collective-permute-start | bytes 1572872 | tf_op jit(solution)/shard_map/ppermute | solution.py:114
  98.6 11.7 %collective-permute-start.24 = (bf16[128,2048]{1,0:T(8,128)(2,1)S(1)}, bf16[128,2048]{1,0:T(8,128)(2,1)S(1)}, u32[]{:S(2)}, u32[]{:S(2)}) collective-permute-start(bf16[128,2048]{1,0:T(8,128)(2,1)S(1)} %collective-permute-done.23), channel_id=1, source_target_pairs={{0,2},{4,0},{8,4},{12,8},{14,12},{10,14},{6,10},{2,6},{1,3},{5,1},... | collective-permute-start | bytes 1572872 | tf_op jit(solution)/shard_map/ppermute | solution.py:114
  108.5 8.6 %collective-permute-start.9 = (bf16[2048,384]{1,0:T(8,128)(2,1)S(1)}, bf16[2048,384]{1,0:T(8,128)(2,1)S(1)}, u32[]{:S(2)}, u32[]{:S(2)}) collective-permute-start(bf16[2048,384]{1,0:T(8,128)(2,1)S(1)} %bitcast.113), channel_id=1, source_target_pairs={{0,1},{1,0},{2,3},{3,2},{4,5},{5,4},{6,7},{7,6},{8,9},{9,8},{10,11... | collective-permute-start | bytes 4718600 | tf_op jit(solution)/shard_map/ppermute | solution.py:117
  108.5 42.6 %collective-permute-start.13 = (bf16[128,2048]{1,0:T(8,128)(2,1)S(1)}, bf16[128,2048]{1,0:T(8,128)(2,1)S(1)}, u32[]{:S(2)}, u32[]{:S(2)}) collective-permute-start(bf16[128,2048]{1,0:T(8,128)(2,1)S(1)} %collective-permute-done.12), channel_id=1, source_target_pairs={{0,2},{4,0},{8,4},{12,8},{14,12},{10,14},{6,10},{2,6},{1,3},{5,1},... | collective-permute-start | bytes 1572872 | tf_op jit(solution)/shard_map/ppermute | solution.py:114
  110.3 40.1 %collective-permute-start.17 = (bf16[128,2048]{1,0:T(8,128)(2,1)S(1)}, bf16[128,2048]{1,0:T(8,128)(2,1)S(1)}, u32[]{:S(2)}, u32[]{:S(2)}) collective-permute-start(bf16[128,2048]{1,0:T(8,128)(2,1)S(1)} %collective-permute-done.16), channel_id=1, source_target_pairs={{0,4},{4,8},{8,12},{12,14},{14,10},{10,6},{6,2},{2,0},{1,5},{5,9},... | collective-permute-start | bytes 1572872 | tf_op jit(solution)/shard_map/ppermute | solution.py:114
  140.2 7.2 %collective-permute-start.26 = (bf16[64,2048]{1,0:T(8,128)(2,1)S(1)}, bf16[64,2048]{1,0:T(8,128)(2,1)S(1)}, u32[]{:S(2)}, u32[]{:S(2)}) collective-permute-start(bf16[64,2048]{1,0:T(8,128)(2,1)S(1)} %get-tuple-element.59), channel_id=1, source_target_pairs={{0,4},{4,8},{8,12},{12,14},{14,10},{10,6},{6,2},{2,0},{1,5},{5,9},... | collective-permute-start | bytes 786440 | tf_op jit(solution)/shard_map/ppermute | solution.py:114
  148.3 16.0 %collective-permute-start.30 = (bf16[64,2048]{1,0:T(8,128)(2,1)S(1)}, bf16[64,2048]{1,0:T(8,128)(2,1)S(1)}, u32[]{:S(2)}, u32[]{:S(2)}) collective-permute-start(bf16[64,2048]{1,0:T(8,128)(2,1)S(1)} %get-tuple-element.57), channel_id=1, source_target_pairs={{0,4},{4,8},{8,12},{12,14},{14,10},{10,6},{6,2},{2,0},{1,5},{5,9},... | collective-permute-start | bytes 786440 | tf_op jit(solution)/shard_map/ppermute | solution.py:114
  149.2 16.2 %collective-permute-start.28 = (bf16[64,2048]{1,0:T(8,128)(2,1)S(1)}, bf16[64,2048]{1,0:T(8,128)(2,1)S(1)}, u32[]{:S(2)}, u32[]{:S(2)}) collective-permute-start(bf16[64,2048]{1,0:T(8,128)(2,1)S(1)} %get-tuple-element.58), channel_id=1, source_target_pairs={{0,2},{4,0},{8,4},{12,8},{14,12},{10,14},{6,10},{2,6},{1,3},{5,1},... | collective-permute-start | bytes 786440 | tf_op jit(solution)/shard_map/ppermute | solution.py:114
  155.4 7.0 %collective-permute-start.18 = (bf16[64,2048]{1,0:T(8,128)(2,1)S(1)}, bf16[64,2048]{1,0:T(8,128)(2,1)S(1)}, u32[]{:S(2)}, u32[]{:S(2)}) collective-permute-start(bf16[64,2048]{1,0:T(8,128)(2,1)S(1)} %get-tuple-element.82), channel_id=1, source_target_pairs={{0,2},{4,0},{8,4},{12,8},{14,12},{10,14},{6,10},{2,6},{1,3},{5,1},... | collective-permute-start | bytes 786440 | tf_op jit(solution)/shard_map/ppermute | solution.py:114
  156.4 6.7 %collective-permute-start.29 = (bf16[64,2048]{1,0:T(8,128)(2,1)S(1)}, bf16[64,2048]{1,0:T(8,128)(2,1)S(1)}, u32[]{:S(2)}, u32[]{:S(2)}) collective-permute-start(bf16[64,2048]{1,0:T(8,128)(2,1)S(1)} %get-tuple-element.81), channel_id=1, source_target_pairs={{0,4},{4,8},{8,12},{12,14},{14,10},{10,6},{6,2},{2,0},{1,5},{5,9},... | collective-permute-start | bytes 786440 | tf_op jit(solution)/shard_map/ppermute | solution.py:114
  159.9 39.4 %collective-permute-start.38 = (bf16[2048,384]{1,0:T(8,128)(2,1)S(1)}, bf16[2048,384]{1,0:T(8,128)(2,1)S(1)}, u32[]{:S(2)}, u32[]{:S(2)}) collective-permute-start(bf16[2048,384]{1,0:T(8,128)(2,1)S(1)} %convolution_convert_fusion.2), channel_id=1, source_target_pairs={{0,1},{1,0},{2,3},{3,2},{4,5},{5,4},{6,7},{7,6},{8,9},{9,8},{10,11... | collective-permute-start | bytes 4718600 | tf_op jit(solution)/shard_map/ppermute | solution.py:117
  162.5 40.4 %collective-permute-start.39 = (bf16[2048,384]{1,0:T(8,128)(2,1)S(1)}, bf16[2048,384]{1,0:T(8,128)(2,1)S(1)}, u32[]{:S(2)}, u32[]{:S(2)}) collective-permute-start(bf16[2048,384]{1,0:T(8,128)(2,1)S(1)} %convolution_convert_fusion.1), channel_id=1, source_target_pairs={{0,1},{1,0},{2,3},{3,2},{4,5},{5,4},{6,7},{7,6},{8,9},{9,8},{10,11... | collective-permute-start | bytes 4718600 | tf_op jit(solution)/shard_map/ppermute | solution.py:117
  163.1 8.3 %collective-permute-start.27 = (bf16[64,2048]{1,0:T(8,128)(2,1)S(1)}, bf16[64,2048]{1,0:T(8,128)(2,1)S(1)}, u32[]{:S(2)}, u32[]{:S(2)}) collective-permute-start(bf16[64,2048]{1,0:T(8,128)(2,1)S(1)} %add_convert_fusion.10), channel_id=1, source_target_pairs={{0,2},{4,0},{8,4},{12,8},{14,12},{10,14},{6,10},{2,6},{1,3},{5,1},... | collective-permute-start | bytes 786440 | tf_op jit(solution)/shard_map/ppermute | solution.py:114
  164.4 9.2 %collective-permute-start.32 = (bf16[64,2048]{1,0:T(8,128)(2,1)S(1)}, bf16[64,2048]{1,0:T(8,128)(2,1)S(1)}, u32[]{:S(2)}, u32[]{:S(2)}) collective-permute-start(bf16[64,2048]{1,0:T(8,128)(2,1)S(1)} %add_convert_fusion.9), channel_id=1, source_target_pairs={{0,4},{4,8},{8,12},{12,14},{14,10},{10,6},{6,2},{2,0},{1,5},{5,9},... | collective-permute-start | bytes 786440 | tf_op jit(solution)/shard_map/ppermute | solution.py:114
  165.4 26.3 %collective-permute-start.34 = (bf16[64,2048]{1,0:T(8,128)(2,1)S(1)}, bf16[64,2048]{1,0:T(8,128)(2,1)S(1)}, u32[]{:S(2)}, u32[]{:S(2)}) collective-permute-start(bf16[64,2048]{1,0:T(8,128)(2,1)S(1)} %add_convert_fusion.7), channel_id=1, source_target_pairs={{0,4},{4,8},{8,12},{12,14},{14,10},{10,6},{6,2},{2,0},{1,5},{5,9},... | collective-permute-start | bytes 786440 | tf_op jit(solution)/shard_map/ppermute | solution.py:114
  171.4 23.7 %collective-permute-start.37 = (bf16[64,2048]{1,0:T(8,128)(2,1)S(1)}, bf16[64,2048]{1,0:T(8,128)(2,1)S(1)}, u32[]{:S(2)}, u32[]{:S(2)}) collective-permute-start(bf16[64,2048]{1,0:T(8,128)(2,1)S(1)} %add_convert_fusion.8), channel_id=1, source_target_pairs={{0,2},{4,0},{8,4},{12,8},{14,12},{10,14},{6,10},{2,6},{1,3},{5,1},... | collective-permute-start | bytes 786440 | tf_op jit(solution)/shard_map/ppermute | solution.py:114
  173.6 10.8 %collective-permute-start.31 = (bf16[64,2048]{1,0:T(8,128)(2,1)S(1)}, bf16[64,2048]{1,0:T(8,128)(2,1)S(1)}, u32[]{:S(2)}, u32[]{:S(2)}) collective-permute-start(bf16[64,2048]{1,0:T(8,128)(2,1)S(1)} %add_convert_fusion.6), channel_id=1, source_target_pairs={{0,2},{4,0},{8,4},{12,8},{14,12},{10,14},{6,10},{2,6},{1,3},{5,1},... | collective-permute-start | bytes 786440 | tf_op jit(solution)/shard_map/ppermute | solution.py:114
  191.7 6.6 %collective-permute-start.36 = (bf16[64,2048]{1,0:T(8,128)(2,1)S(1)}, bf16[64,2048]{1,0:T(8,128)(2,1)S(1)}, u32[]{:S(2)}, u32[]{:S(2)}) collective-permute-start(bf16[64,2048]{1,0:T(8,128)(2,1)S(1)} %add_convert_fusion.3), channel_id=1, source_target_pairs={{0,4},{4,8},{8,12},{12,14},{14,10},{10,6},{6,2},{2,0},{1,5},{5,9},... | collective-permute-start | bytes 786440 | tf_op jit(solution)/shard_map/ppermute | solution.py:114
  195.1 11.4 %collective-permute-start.40 = (bf16[384,2048]{1,0:T(8,128)(2,1)S(1)}, bf16[384,2048]{1,0:T(8,128)(2,1)S(1)}, u32[]{:S(2)}, u32[]{:S(2)}) collective-permute-start(bf16[384,2048]{1,0:T(8,128)(2,1)S(1)} %convolution_convert_fusion), channel_id=1, source_target_pairs={{0,1},{1,0},{2,3},{3,2},{4,5},{5,4},{6,7},{7,6},{8,9},{9,8},{10,11... | collective-permute-start | bytes 4718600 | tf_op jit(solution)/shard_map/ppermute | solution.py:117
  (14 other events, 162.8 us)

commit v2 on v1

--- a/solution.py
+++ b/solution.py
@@ -119,11 +119,11 @@
     from_left, from_right = [], []
     rx, rg, lx, lg = layer_input, output_grad, layer_input, output_grad
     for _ in range(1, full_steps + 1):
-        rg, lg = shift(rg, 1), shift(lg, -1)
-        rx, lx = shift(rx, 1), shift(lx, -1)
+        rg, lx = shift(rg, 1), shift(lx, -1)
+        rx, lg = shift(rx, 1), shift(lg, -1)
         from_left.append((rx, rg))
         from_right.append((lx, lg))
-    far = (shift(rx, 1), shift(lg, -1)) if has_far else None
+    far = (shift(lx, -1), shift(rg, 1)) if has_far else None
 
     quotas = route_ints.astype(jnp.float32)
     route_ratio = quotas / jnp.sum(quotas, axis=1, keepdims=True)
@@ -137,23 +137,19 @@
     expert = chip[:, None] * members + core[None, :]
     chosen = expert_ids[None, None, :, :] == expert[:, :, None, None]
     outgoing = jnp.sum(jnp.where(chosen, route_ratio[None, None], 0.0), axis=3)
-    distances = [0]
-    for k in range(1, full_steps + 1):
-        distances += [-k, k]
-    if has_far:
-        distances.append(groups // 2)
-    ratios = []
-    for d in distances:
-        ratios.append(outgoing[0] if d == 0 else shift(outgoing[(-d) % groups], -d))
-    ratios = jnp.concatenate(ratios, axis=1).T
+
+    def ratio_from(distance):
+        if distance == 0:
+            return outgoing[0]
+        return shift(outgoing[-distance % groups], -distance)
 
     gates, ups, downs = [w_gate[0]], [w_up[0]], [w_down[0]]
     for k in range(1, members):
         gates.append(member_shift(w_gate[0], members - k))
         ups.append(member_shift(w_up[0], members - k))
         downs.append(member_shift(w_down[0], members - k))
-    gate_w = jnp.concatenate(gates, axis=1)
-    up_w = jnp.concatenate(ups, axis=1)
+    in_w = jnp.concatenate(gates + ups, axis=1)
+    gate_w, up_w = in_w[:, :span], in_w[:, span:]
     down_w = jnp.concatenate(downs, axis=0)
     column = jnp.arange(span, dtype=jnp.int32)[None, :] // width
 
@@ -161,7 +157,8 @@
         r = ratio[:, 0:1]
         for m in range(1, members):
             r = jnp.where(column == m, ratio[:, m : m + 1], r)
-        gate, up = mm(x, gate_w), mm(x, up_w)
+        pre = mm(x, in_w)
+        gate, up = pre[:, :span], pre[:, span:]
         s = jax.nn.sigmoid(gate)
         act = gate * s
         hidden = (act * up * r).astype(jnp.bfloat16)
@@ -172,15 +169,14 @@
         return part, gg, ug, hidden
 
     kept = []
-    own_part, *rest = piece(layer_input, output_grad, ratios[:tok_rows])
+    own_part, *rest = piece(layer_input, output_grad, ratio_from(0).T)
     kept.append((layer_input, output_grad, *rest))
     part_left, part_right = [], []
-    at = tok_rows
     for k in range(1, full_steps + 1):
         x = jnp.concatenate([from_left[k - 1][0], from_right[k - 1][0]], axis=0)
         og = jnp.concatenate([from_left[k - 1][1], from_right[k - 1][1]], axis=0)
-        part, *rest = piece(x, og, ratios[at : at + 2 * tok_rows])
-        at += 2 * tok_rows
+        ratio = [ratio_from(-k), ratio_from(k)]
+        part, *rest = piece(x, og, jnp.concatenate(ratio, axis=1).T)
         part = part.astype(jnp.bfloat16)
         part_left.append(part[:tok_rows])
         part_right.append(part[tok_rows:])
@@ -188,7 +184,7 @@
     half = tok_rows // 2
     far_part = None
     if has_far:
-        part, *rest = piece(far[0], far[1], ratios[at:])
+        part, *rest = piece(far[0], far[1], ratio_from(groups // 2).T)
         far_part = part.astype(jnp.bfloat16)
         kept.append((far[0], far[1], *rest))
 

time: 213 us -> 192 us (0.901); the launches traced: 210 us -> 191 us
  matrix products: 52.8 us -> 43.4 us
  waiting for transfers between devices: 98.6 us -> 92.5 us
    dot_general x31 -> x26, matrix products: 52.8 us -> 43.4 us  [mm(): return lax.dot_general(a, b, dims, preferred_element_type=jnp.float32)]
    ppermute x35, waiting for transfers between devices: 98.6 us -> 92.5 us  [shift(): return lax.ppermute(array, 'grp', at_distance(k))]
  transfers between devices with their start and end apart: 41 -> 41, of which waited for: 19 -> 21; matrix products, arithmetic and copies ran while one was open for 28% -> 25% of each run, Pallas kernels for 0% -> 0%
where the time goes in v2:
time: 192 us; the launch traced here: 191 us
  waiting for transfers between devices  92.5 us (48%)
  starting transfers between devices  46.1 us (24%)
  matrix products  43.4 us (23%)
  other arithmetic  4.76 us (2%)
  local copies, waits for them, and re-layouts  3.18 us (2%)
    ppermute x35, waiting for transfers between devices, shift(): return lax.ppermute(array, 'grp', at_distance(k))  92.5 us
    ppermute x35, starting transfers between devices, shift(): return lax.ppermute(array, 'grp', at_distance(k))  45.1 us
    dot_general x26, matrix products, mm(): return lax.dot_general(a, b, dims, preferred_element_type=jnp.float32)  43.4 us
  transfers between devices with their start and end apart: 41, of which 21 were waited for; matrix products, arithmetic and copies ran while one was open for 25% of the time, Pallas kernels for 0%

profile of v2, /device:TPU:0, one launch (start us, length us, event | category | flops | bytes accessed | tf_op | source)
XLA Modules:
  0.0 191.3 jit_solution(16582126368391246051)
XLA Ops:
  0.6 3.1 %collective-permute-start.18 = (bf16[128,2048]{1,0:T(8,128)(2,1)}, bf16[128,2048]{1,0:T(8,128)(2,1)S(1)}, u32[]{:S(2)}, u32[]{:S(2)}) collective-permute-start(bf16[128,2048]{1,0:T(8,128)(2,1)} %param.8), channel_id=1, source_target_pairs={{0,4},{4,8},{8,12},{12,14},{14,10},{10,6},{6,2},{2,0},{1,5},{5,9},... | collective-permute-start | bytes 1572872 | tf_op jit(solution)/shard_map/ppermute | solution.py:114
  6.8 2.1 %collective-permute-start.27 = (f32[2,128]{1,0:T(2,128)S(1)}, f32[2,128]{1,0:T(2,128)S(1)}, u32[]{:S(2)}, u32[]{:S(2)}) collective-permute-start(f32[2,128]{1,0:T(2,128)S(1)} %get-tuple-element.73), channel_id=1, source_target_pairs={{0,4},{4,8},{8,12},{12,14},{14,10},{10,6},{6,2},{2,0},{1,5},{5,9},... | collective-permute-start | bytes 3080 | tf_op jit(solution)/shard_map/ppermute | solution.py:114
  8.9 2.0 %collective-permute-start.15 = (bf16[128,2048]{1,0:T(8,128)(2,1)}, bf16[128,2048]{1,0:T(8,128)(2,1)S(1)}, u32[]{:S(2)}, u32[]{:S(2)}) collective-permute-start(bf16[128,2048]{1,0:T(8,128)(2,1)} %param.9), channel_id=1, source_target_pairs={{0,2},{4,0},{8,4},{12,8},{14,12},{10,14},{6,10},{2,6},{1,3},{5,1},... | collective-permute-start | bytes 1572872 | tf_op jit(solution)/shard_map/ppermute | solution.py:114
  13.1 2.8 %collective-permute-done.27 = f32[2,128]{1,0:T(2,128)S(1)} collective-permute-done((f32[2,128]{1,0:T(2,128)S(1)}, f32[2,128]{1,0:T(2,128)S(1)}, u32[]{:S(2)}, u32[]{:S(2)}) %collective-permute-start.27) | collective-permute-done | bytes 1056 | tf_op jit(solution)/shard_map/ppermute | solution.py:114
  15.9 2.8 %collective-permute-start.22 = (f32[2,128]{1,0:T(2,128)S(1)}, f32[2,128]{1,0:T(2,128)S(1)}, u32[]{:S(2)}, u32[]{:S(2)}) collective-permute-start(f32[2,128]{1,0:T(2,128)S(1)} %get-tuple-element.75), channel_id=1, source_target_pairs={{0,8},{4,12},{8,14},{12,10},{14,6},{10,2},{6,0},{2,4},{1,9},{5,13}... | collective-permute-start | bytes 3080 | tf_op jit(solution)/shard_map/ppermute | solution.py:114
  20.4 9.9 %collective-permute-start.13 = (f32[2,128]{1,0:T(2,128)S(1)}, f32[2,128]{1,0:T(2,128)S(1)}, u32[]{:S(2)}, u32[]{:S(2)}) collective-permute-start(f32[2,128]{1,0:T(2,128)S(1)} %get-tuple-element.77), channel_id=1, source_target_pairs={{0,12},{4,14},{8,10},{12,6},{14,2},{10,0},{6,4},{2,8},{1,13},{5,15... | collective-permute-start | bytes 3080 | tf_op jit(solution)/shard_map/ppermute | solution.py:114
  30.3 1.8 collective-permute-start.14
  33.7 2.0 %collective-permute-done.14 = f32[2,128]{1,0:T(2,128)S(1)} collective-permute-done((f32[2,128]{1,0:T(2,128)S(1)}, f32[2,128]{1,0:T(2,128)S(1)}, u32[]{:S(2)}, u32[]{:S(2)}) %collective-permute-start.14) | collective-permute-done | bytes 1056 | tf_op jit(solution)/shard_map/ppermute | solution.py:114
  37.3 9.1 %collective-permute-done.3 = f32[2,128]{1,0:T(2,128)S(1)} collective-permute-done((f32[2,128]{1,0:T(2,128)S(1)}, f32[2,128]{1,0:T(2,128)S(1)}, u32[]{:S(2)}, u32[]{:S(2)}) %collective-permute-start.3) | collective-permute-done | bytes 1056 | tf_op jit(solution)/shard_map/ppermute | solution.py:114
  47.1 2.1 %collective-permute-start.9 = (bf16[128,2048]{1,0:T(8,128)(2,1)S(1)}, bf16[128,2048]{1,0:T(8,128)(2,1)S(1)}, u32[]{:S(2)}, u32[]{:S(2)}) collective-permute-start(bf16[128,2048]{1,0:T(8,128)(2,1)S(1)} %collective-permute-done.8), channel_id=1, source_target_pairs={{0,2},{4,0},{8,4},{12,8},{14,12},{10,14},{6,10},{2,6},{1,3},{5,1},... | collective-permute-start | bytes 1572872 | tf_op jit(solution)/shard_map/ppermute | solution.py:114
  49.4 12.5 %collective-permute-done.19 = bf16[128,2048]{1,0:T(8,128)(2,1)S(1)} collective-permute-done((bf16[128,2048]{1,0:T(8,128)(2,1)S(1)}, bf16[128,2048]{1,0:T(8,128)(2,1)S(1)}, u32[]{:S(2)}, u32[]{:S(2)}) %collective-permute-start.19) | collective-permute-done | bytes 524320 | tf_op jit(solution)/shard_map/ppermute | solution.py:114
  61.9 2.1 %collective-permute-start.20 = (bf16[128,2048]{1,0:T(8,128)(2,1)S(1)}, bf16[128,2048]{1,0:T(8,128)(2,1)S(1)}, u32[]{:S(2)}, u32[]{:S(2)}) collective-permute-start(bf16[128,2048]{1,0:T(8,128)(2,1)S(1)} %collective-permute-done.19), channel_id=1, source_target_pairs={{0,4},{4,8},{8,12},{12,14},{14,10},{10,6},{6,2},{2,0},{1,5},{5,9},... | collective-permute-start | bytes 1572872 | tf_op jit(solution)/shard_map/ppermute | solution.py:114
  64.1 9.0 %collective-permute-done.5 = bf16[128,2048]{1,0:T(8,128)(2,1)S(1)} collective-permute-done((bf16[128,2048]{1,0:T(8,128)(2,1)S(1)}, bf16[128,2048]{1,0:T(8,128)(2,1)S(1)}, u32[]{:S(2)}, u32[]{:S(2)}) %collective-permute-start.5) | collective-permute-done | bytes 524320 | tf_op jit(solution)/shard_map/ppermute | solution.py:114
  75.3 9.1 %collective-permute-done.20 = bf16[128,2048]{1,0:T(8,128)(2,1)S(1)} collective-permute-done((bf16[128,2048]{1,0:T(8,128)(2,1)S(1)}, bf16[128,2048]{1,0:T(8,128)(2,1)S(1)}, u32[]{:S(2)}, u32[]{:S(2)}) %collective-permute-start.20) | collective-permute-done | bytes 524320 | tf_op jit(solution)/shard_map/ppermute | solution.py:114
  85.3 9.4 %collective-permute-done.6 = bf16[128,2048]{1,0:T(8,128)(2,1)S(1)} collective-permute-done((bf16[128,2048]{1,0:T(8,128)(2,1)S(1)}, bf16[128,2048]{1,0:T(8,128)(2,1)S(1)}, u32[]{:S(2)}, u32[]{:S(2)}) %collective-permute-start.6) | collective-permute-done | bytes 524320 | tf_op jit(solution)/shard_map/ppermute | solution.py:114
  94.7 1.8 collective-permute-done.17
  97.1 3.0 %fusion.26 = f32[256,1536]{1,0:T(8,128)} fusion(bf16[128,2048]{1,0:T(8,128)(2,1)S(1)} %collective-permute-done.8, bf16[128,2048]{1,0:T(8,128)(2,1)S(1)} %collective-permute-done.18, bf16[2048,384]{1,0:T(8,128)(2,1)S(1)} %collective-permute-done.2, bf16[2048,384]{1,0:T(8,128)(2,1)S(1)} %bitcast.94, bf16[2048,384]{1,0:T(8,128)(2,1)S(1)} %collective-permute-done.1, ...), kind=kOutput, calls=%fused_computation.51 | convolution fusion | flops 1637875712 | bytes 8912896 | tf_op jit(solution)/shard_map/dot_general | solution.py:97
  100.1 1.8 fusion.19
  101.9 1.8 fusion.12
  126.1 1.9 convolution_convert_fusion
  130.7 2.4 %convolution_convert_fusion.1 = bf16[2048,384]{1,0:T(8,128)(2,1)S(1)} fusion(bf16[1024,2048]{1,0:T(8,128)(2,1)S(1)} %constant_dynamic-update-slice_fusion, bf16[1024,768]{1,0:T(8,128)(2,1)S(1)} %get-tuple-element.49), kind=kOutput, calls=%fused_computation.8 | convolution fusion | flops 1611399168 | bytes 6553600 | tf_op jit(solution)/shard_map/dot_general | solution.py:97
  133.5 5.6 %collective-permute-done.29 = bf16[64,2048]{1,0:T(8,128)(2,1)S(1)} collective-permute-done((bf16[64,2048]{1,0:T(8,128)(2,1)S(1)}, bf16[64,2048]{1,0:T(8,128)(2,1)S(1)}, u32[]{:S(2)}, u32[]{:S(2)}) %collective-permute-start.29) | collective-permute-done | bytes 262176 | tf_op jit(solution)/shard_map/ppermute | solution.py:114
  140.7 6.3 %collective-permute-done.12 = bf16[64,2048]{1,0:T(8,128)(2,1)S(1)} collective-permute-done((bf16[64,2048]{1,0:T(8,128)(2,1)S(1)}, bf16[64,2048]{1,0:T(8,128)(2,1)S(1)}, u32[]{:S(2)}, u32[]{:S(2)}) %collective-permute-start.12) | collective-permute-done | bytes 262176 | tf_op jit(solution)/shard_map/ppermute | solution.py:114
  150.8 3.2 %collective-permute-done.32 = bf16[64,2048]{1,0:T(8,128)(2,1)S(1)} collective-permute-done((bf16[64,2048]{1,0:T(8,128)(2,1)S(1)}, bf16[64,2048]{1,0:T(8,128)(2,1)S(1)}, u32[]{:S(2)}, u32[]{:S(2)}) %collective-permute-start.32) | collective-permute-done | bytes 262176 | tf_op jit(solution)/shard_map/ppermute | solution.py:114
  154.4 2.2 %collective-permute-done.25 = bf16[64,2048]{1,0:T(8,128)(2,1)S(1)} collective-permute-done((bf16[64,2048]{1,0:T(8,128)(2,1)S(1)}, bf16[64,2048]{1,0:T(8,128)(2,1)S(1)}, u32[]{:S(2)}, u32[]{:S(2)}) %collective-permute-start.25) | collective-permute-done | bytes 262176 | tf_op jit(solution)/shard_map/ppermute | solution.py:114
  157.6 8.2 %collective-permute-done.35 = bf16[64,2048]{1,0:T(8,128)(2,1)S(1)} collective-permute-done((bf16[64,2048]{1,0:T(8,128)(2,1)S(1)}, bf16[64,2048]{1,0:T(8,128)(2,1)S(1)}, u32[]{:S(2)}, u32[]{:S(2)}) %collective-permute-start.35) | collective-permute-done | bytes 262176 | tf_op jit(solution)/shard_map/ppermute | solution.py:114
  167.3 6.0 %collective-permute-done.31 = bf16[64,2048]{1,0:T(8,128)(2,1)S(1)} collective-permute-done((bf16[64,2048]{1,0:T(8,128)(2,1)S(1)}, bf16[64,2048]{1,0:T(8,128)(2,1)S(1)}, u32[]{:S(2)}, u32[]{:S(2)}) %collective-permute-start.31) | collective-permute-done | bytes 262176 | tf_op jit(solution)/shard_map/ppermute | solution.py:114
  173.5 2.0 %collective-permute-start.33 = (bf16[64,2048]{1,0:T(8,128)(2,1)S(1)}, bf16[64,2048]{1,0:T(8,128)(2,1)S(1)}, u32[]{:S(2)}, u32[]{:S(2)}) collective-permute-start(bf16[64,2048]{1,0:T(8,128)(2,1)S(1)} %add_convert_fusion.4), channel_id=1, source_target_pairs={{0,2},{4,0},{8,4},{12,8},{14,12},{10,14},{6,10},{2,6},{1,3},{5,1},... | collective-permute-start | bytes 786440 | tf_op jit(solution)/shard_map/ppermute | solution.py:114
  175.4 2.4 %convolution_convert_fusion.2 = bf16[2048,384]{1,0:T(8,128)(2,1)S(1)} fusion(bf16[1024,2048]{1,0:T(8,128)(2,1)S(1)} %constant_dynamic-update-slice_fusion, bf16[1024,768]{1,0:T(8,128)(2,1)S(1)} %get-tuple-element.30), kind=kOutput, calls=%fused_computation.9 | convolution fusion | flops 1611399168 | bytes 6553600 | tf_op jit(solution)/shard_map/dot_general | solution.py:97
  180.9 3.1 %fusion.5 = bf16[1,384,2048]{2,1,0:T(8,128)(2,1)} fusion(bf16[1024,2048]{1,0:T(8,128)(2,1)S(1)} %constant_dynamic-update-slice_fusion.18, bf16[384,2048]{1,0:T(8,128)(2,1)S(1)} %collective-permute-done.40, bf16[1024,768]{1,0:T(8,128)(2,1)S(1)} %get-tuple-element.67), kind=kOutput, calls=%fused_computation.18 | convolution fusion | flops 1612972032 | bytes 8126464 | tf_op jit(solution)/shard_map/dot_general | solution.py:97
  184.0 3.6 %fusion.4 = bf16[1,2048,384]{2,1,0:T(8,128)(2,1)} fusion(bf16[1024,2048]{1,0:T(8,128)(2,1)S(1)} %constant_dynamic-update-slice_fusion, bf16[2048,384]{1,0:T(8,128)(2,1)S(1)} %collective-permute-done.39, bf16[1024,768]{1,0:T(8,128)(2,1)S(1)} %get-tuple-element.49), kind=kOutput, calls=%fused_computation.17 | convolution fusion | flops 1612972032 | bytes 8126464 | tf_op jit(solution)/shard_map/dot_general | solution.py:97
  187.6 3.6 %fusion.3 = bf16[1,2048,384]{2,1,0:T(8,128)(2,1)} fusion(bf16[1024,2048]{1,0:T(8,128)(2,1)S(1)} %constant_dynamic-update-slice_fusion, bf16[2048,384]{1,0:T(8,128)(2,1)S(1)} %collective-permute-done.38, bf16[1024,768]{1,0:T(8,128)(2,1)S(1)} %get-tuple-element.30), kind=kOutput, calls=%fused_computation.16 | convolution fusion | flops 1612972032 | bytes 8126464 | tf_op jit(solution)/shard_map/dot_general | solution.py:97
  (137 shorter events, 51.5 us)
Async XLA Ops:
  0.6 45.8 %collective-permute-start.18 = (bf16[128,2048]{1,0:T(8,128)(2,1)}, bf16[128,2048]{1,0:T(8,128)(2,1)S(1)}, u32[]{:S(2)}, u32[]{:S(2)}) collective-permute-start(bf16[128,2048]{1,0:T(8,128)(2,1)} %param.8), channel_id=1, source_target_pairs={{0,4},{4,8},{8,12},{12,14},{14,10},{10,6},{6,2},{2,0},{1,5},{5,9},... | collective-permute-start | bytes 1572872 | tf_op jit(solution)/shard_map/ppermute | solution.py:114
  3.7 43.3 %collective-permute-start.8 = (bf16[128,2048]{1,0:T(8,128)(2,1)}, bf16[128,2048]{1,0:T(8,128)(2,1)S(1)}, u32[]{:S(2)}, u32[]{:S(2)}) collective-permute-start(bf16[128,2048]{1,0:T(8,128)(2,1)} %param.8), channel_id=1, source_target_pairs={{0,2},{4,0},{8,4},{12,8},{14,12},{10,14},{6,10},{2,6},{1,3},{5,1},... | collective-permute-start | bytes 1572872 | tf_op jit(solution)/shard_map/ppermute | solution.py:114
  6.8 9.1 %collective-permute-start.27 = (f32[2,128]{1,0:T(2,128)S(1)}, f32[2,128]{1,0:T(2,128)S(1)}, u32[]{:S(2)}, u32[]{:S(2)}) collective-permute-start(f32[2,128]{1,0:T(2,128)S(1)} %get-tuple-element.73), channel_id=1, source_target_pairs={{0,4},{4,8},{8,12},{12,14},{14,10},{10,6},{6,2},{2,0},{1,5},{5,9},... | collective-permute-start | bytes 3080 | tf_op jit(solution)/shard_map/ppermute | solution.py:114
  8.9 9.9 %collective-permute-start.28 = (f32[2,128]{1,0:T(2,128)S(1)}, f32[2,128]{1,0:T(2,128)S(1)}, u32[]{:S(2)}, u32[]{:S(2)}) collective-permute-start(f32[2,128]{1,0:T(2,128)S(1)} %get-tuple-element.72), channel_id=1, source_target_pairs={{0,2},{4,0},{8,4},{12,8},{14,12},{10,14},{6,10},{2,6},{1,3},{5,1},... | collective-permute-start | bytes 3080 | tf_op jit(solution)/shard_map/ppermute | solution.py:114
  8.9 40.4 %collective-permute-start.15 = (bf16[128,2048]{1,0:T(8,128)(2,1)}, bf16[128,2048]{1,0:T(8,128)(2,1)S(1)}, u32[]{:S(2)}, u32[]{:S(2)}) collective-permute-start(bf16[128,2048]{1,0:T(8,128)(2,1)} %param.9), channel_id=1, source_target_pairs={{0,2},{4,0},{8,4},{12,8},{14,12},{10,14},{6,10},{2,6},{1,3},{5,1},... | collective-permute-start | bytes 1572872 | tf_op jit(solution)/shard_map/ppermute | solution.py:114
  18.8 11.5 %collective-permute-start.23 = (f32[2,128]{1,0:T(2,128)S(1)}, f32[2,128]{1,0:T(2,128)S(1)}, u32[]{:S(2)}, u32[]{:S(2)}) collective-permute-start(f32[2,128]{1,0:T(2,128)S(1)} %get-tuple-element.74), channel_id=1, source_target_pairs={{0,6},{4,2},{8,0},{12,4},{14,8},{10,12},{6,14},{2,10},{1,7},{5,3},... | collective-permute-start | bytes 3080 | tf_op jit(solution)/shard_map/ppermute | solution.py:114
  20.4 13.3 %collective-permute-start.13 = (f32[2,128]{1,0:T(2,128)S(1)}, f32[2,128]{1,0:T(2,128)S(1)}, u32[]{:S(2)}, u32[]{:S(2)}) collective-permute-start(f32[2,128]{1,0:T(2,128)S(1)} %get-tuple-element.77), channel_id=1, source_target_pairs={{0,12},{4,14},{8,10},{12,6},{14,2},{10,0},{6,4},{2,8},{1,13},{5,15... | collective-permute-start | bytes 3080 | tf_op jit(solution)/shard_map/ppermute | solution.py:114
  33.7 13.4 %collective-permute-start.4 = (bf16[128,2048]{1,0:T(8,128)(2,1)}, bf16[128,2048]{1,0:T(8,128)(2,1)S(1)}, u32[]{:S(2)}, u32[]{:S(2)}) collective-permute-start(bf16[128,2048]{1,0:T(8,128)(2,1)} %param.9), channel_id=1, source_target_pairs={{0,4},{4,8},{8,12},{12,14},{14,10},{10,6},{6,2},{2,0},{1,5},{5,9},... | collective-permute-start | bytes 1572872 | tf_op jit(solution)/shard_map/ppermute | solution.py:114
  35.7 10.8 %collective-permute-start.3 = (f32[2,128]{1,0:T(2,128)S(1)}, f32[2,128]{1,0:T(2,128)S(1)}, u32[]{:S(2)}, u32[]{:S(2)}) collective-permute-start(f32[2,128]{1,0:T(2,128)S(1)} %get-tuple-element.71), channel_id=1, source_target_pairs={{0,14},{4,10},{8,6},{12,2},{14,0},{10,4},{6,8},{2,12},{1,15},{5,11... | collective-permute-start | bytes 3080 | tf_op jit(solution)/shard_map/ppermute | solution.py:114
  46.4 50.6 %collective-permute-start.1 = (bf16[2048,384]{1,0:T(8,128)(2,1)}, bf16[2048,384]{1,0:T(8,128)(2,1)S(1)}, u32[]{:S(2)}, u32[]{:S(2)}) collective-permute-start(bf16[2048,384]{1,0:T(8,128)(2,1)} %bitcast.104), channel_id=1, source_target_pairs={{0,1},{1,0},{2,3},{3,2},{4,5},{5,4},{6,7},{7,6},{8,9},{9,8},{10,11... | collective-permute-start | bytes 4718600 | tf_op jit(solution)/shard_map/ppermute | solution.py:117
  46.5 50.6 %collective-permute-start.2 = (bf16[2048,384]{1,0:T(8,128)(2,1)}, bf16[2048,384]{1,0:T(8,128)(2,1)S(1)}, u32[]{:S(2)}, u32[]{:S(2)}) collective-permute-start(bf16[2048,384]{1,0:T(8,128)(2,1)} %bitcast.93), channel_id=1, source_target_pairs={{0,1},{1,0},{2,3},{3,2},{4,5},{5,4},{6,7},{7,6},{8,9},{9,8},{10,11... | collective-permute-start | bytes 4718600 | tf_op jit(solution)/shard_map/ppermute | solution.py:117
  47.0 14.9 %collective-permute-start.19 = (bf16[128,2048]{1,0:T(8,128)(2,1)S(1)}, bf16[128,2048]{1,0:T(8,128)(2,1)S(1)}, u32[]{:S(2)}, u32[]{:S(2)}) collective-permute-start(bf16[128,2048]{1,0:T(8,128)(2,1)S(1)} %collective-permute-done.18), channel_id=1, source_target_pairs={{0,4},{4,8},{8,12},{12,14},{14,10},{10,6},{6,2},{2,0},{1,5},{5,9},... | collective-permute-start | bytes 1572872 | tf_op jit(solution)/shard_map/ppermute | solution.py:114
  47.1 14.8 %collective-permute-start.9 = (bf16[128,2048]{1,0:T(8,128)(2,1)S(1)}, bf16[128,2048]{1,0:T(8,128)(2,1)S(1)}, u32[]{:S(2)}, u32[]{:S(2)}) collective-permute-start(bf16[128,2048]{1,0:T(8,128)(2,1)S(1)} %collective-permute-done.8), channel_id=1, source_target_pairs={{0,2},{4,0},{8,4},{12,8},{14,12},{10,14},{6,10},{2,6},{1,3},{5,1},... | collective-permute-start | bytes 1572872 | tf_op jit(solution)/shard_map/ppermute | solution.py:114
  49.3 23.8 %collective-permute-start.5 = (bf16[128,2048]{1,0:T(8,128)(2,1)S(1)}, bf16[128,2048]{1,0:T(8,128)(2,1)S(1)}, u32[]{:S(2)}, u32[]{:S(2)}) collective-permute-start(bf16[128,2048]{1,0:T(8,128)(2,1)S(1)} %collective-permute-done.4), channel_id=1, source_target_pairs={{0,4},{4,8},{8,12},{12,14},{14,10},{10,6},{6,2},{2,0},{1,5},{5,9},... | collective-permute-start | bytes 1572872 | tf_op jit(solution)/shard_map/ppermute | solution.py:114
  61.9 12.1 %collective-permute-start.16 = (bf16[128,2048]{1,0:T(8,128)(2,1)S(1)}, bf16[128,2048]{1,0:T(8,128)(2,1)S(1)}, u32[]{:S(2)}, u32[]{:S(2)}) collective-permute-start(bf16[128,2048]{1,0:T(8,128)(2,1)S(1)} %collective-permute-done.15), channel_id=1, source_target_pairs={{0,2},{4,0},{8,4},{12,8},{14,12},{10,14},{6,10},{2,6},{1,3},{5,1},... | collective-permute-start | bytes 1572872 | tf_op jit(solution)/shard_map/ppermute | solution.py:114
  61.9 22.4 %collective-permute-start.20 = (bf16[128,2048]{1,0:T(8,128)(2,1)S(1)}, bf16[128,2048]{1,0:T(8,128)(2,1)S(1)}, u32[]{:S(2)}, u32[]{:S(2)}) collective-permute-start(bf16[128,2048]{1,0:T(8,128)(2,1)S(1)} %collective-permute-done.19), channel_id=1, source_target_pairs={{0,4},{4,8},{8,12},{12,14},{14,10},{10,6},{6,2},{2,0},{1,5},{5,9},... | collective-permute-start | bytes 1572872 | tf_op jit(solution)/shard_map/ppermute | solution.py:114
  73.1 12.1 %collective-permute-start.10 = (bf16[128,2048]{1,0:T(8,128)(2,1)S(1)}, bf16[128,2048]{1,0:T(8,128)(2,1)S(1)}, u32[]{:S(2)}, u32[]{:S(2)}) collective-permute-start(bf16[128,2048]{1,0:T(8,128)(2,1)S(1)} %collective-permute-done.9), channel_id=1, source_target_pairs={{0,2},{4,0},{8,4},{12,8},{14,12},{10,14},{6,10},{2,6},{1,3},{5,1},... | collective-permute-start | bytes 1572872 | tf_op jit(solution)/shard_map/ppermute | solution.py:114
  74.0 20.7 %collective-permute-start.6 = (bf16[128,2048]{1,0:T(8,128)(2,1)S(1)}, bf16[128,2048]{1,0:T(8,128)(2,1)S(1)}, u32[]{:S(2)}, u32[]{:S(2)}) collective-permute-start(bf16[128,2048]{1,0:T(8,128)(2,1)S(1)} %collective-permute-done.5), channel_id=1, source_target_pairs={{0,4},{4,8},{8,12},{12,14},{14,10},{10,6},{6,2},{2,0},{1,5},{5,9},... | collective-permute-start | bytes 1572872 | tf_op jit(solution)/shard_map/ppermute | solution.py:114
  84.3 12.1 %collective-permute-start.17 = (bf16[128,2048]{1,0:T(8,128)(2,1)S(1)}, bf16[128,2048]{1,0:T(8,128)(2,1)S(1)}, u32[]{:S(2)}, u32[]{:S(2)}) collective-permute-start(bf16[128,2048]{1,0:T(8,128)(2,1)S(1)} %collective-permute-done.16), channel_id=1, source_target_pairs={{0,2},{4,0},{8,4},{12,8},{14,12},{10,14},{6,10},{2,6},{1,3},{5,1},... | collective-permute-start | bytes 1572872 | tf_op jit(solution)/shard_map/ppermute | solution.py:114
  85.2 19.5 %collective-permute-start = (bf16[384,2048]{1,0:T(8,128)(2,1)S(1)}, bf16[384,2048]{1,0:T(8,128)(2,1)S(1)}, u32[]{:S(2)}, u32[]{:S(2)}) collective-permute-start(bf16[384,2048]{1,0:T(8,128)(2,1)S(1)} %bitcast.87), channel_id=1, source_target_pairs={{0,1},{1,0},{2,3},{3,2},{4,5},{5,4},{6,7},{7,6},{8,9},{9,8},{10,11... | collective-permute-start | bytes 4718600 | tf_op jit(solution)/shard_map/ppermute | solution.py:117
  94.7 29.0 %collective-permute-start.11 = (bf16[128,2048]{1,0:T(8,128)(2,1)S(1)}, bf16[128,2048]{1,0:T(8,128)(2,1)S(1)}, u32[]{:S(2)}, u32[]{:S(2)}) collective-permute-start(bf16[128,2048]{1,0:T(8,128)(2,1)S(1)} %collective-permute-done.10), channel_id=1, source_target_pairs={{0,2},{4,0},{8,4},{12,8},{14,12},{10,14},{6,10},{2,6},{1,3},{5,1},... | collective-permute-start | bytes 1572872 | tf_op jit(solution)/shard_map/ppermute | solution.py:114
  96.5 28.2 %collective-permute-start.7 = (bf16[128,2048]{1,0:T(8,128)(2,1)S(1)}, bf16[128,2048]{1,0:T(8,128)(2,1)S(1)}, u32[]{:S(2)}, u32[]{:S(2)}) collective-permute-start(bf16[128,2048]{1,0:T(8,128)(2,1)S(1)} %collective-permute-done.6), channel_id=1, source_target_pairs={{0,4},{4,8},{8,12},{12,14},{14,10},{10,6},{6,2},{2,0},{1,5},{5,9},... | collective-permute-start | bytes 1572872 | tf_op jit(solution)/shard_map/ppermute | solution.py:114
  112.5 8.9 %collective-permute-start.21 = (bf16[64,2048]{1,0:T(8,128)(2,1)S(1)}, bf16[64,2048]{1,0:T(8,128)(2,1)S(1)}, u32[]{:S(2)}, u32[]{:S(2)}) collective-permute-start(bf16[64,2048]{1,0:T(8,128)(2,1)S(1)} %get-tuple-element.64), channel_id=1, source_target_pairs={{0,2},{4,0},{8,4},{12,8},{14,12},{10,14},{6,10},{2,6},{1,3},{5,1},... | collective-permute-start | bytes 786440 | tf_op jit(solution)/shard_map/ppermute | solution.py:114
  121.6 25.8 %collective-permute-start.26 = (bf16[64,2048]{1,0:T(8,128)(2,1)S(1)}, bf16[64,2048]{1,0:T(8,128)(2,1)S(1)}, u32[]{:S(2)}, u32[]{:S(2)}) collective-permute-start(bf16[64,2048]{1,0:T(8,128)(2,1)S(1)} %get-tuple-element.62), channel_id=1, source_target_pairs={{0,2},{4,0},{8,4},{12,8},{14,12},{10,14},{6,10},{2,6},{1,3},{5,1},... | collective-permute-start | bytes 786440 | tf_op jit(solution)/shard_map/ppermute | solution.py:114
  123.1 26.1 %collective-permute-start.30 = (bf16[64,2048]{1,0:T(8,128)(2,1)S(1)}, bf16[64,2048]{1,0:T(8,128)(2,1)S(1)}, u32[]{:S(2)}, u32[]{:S(2)}) collective-permute-start(bf16[64,2048]{1,0:T(8,128)(2,1)S(1)} %get-tuple-element.61), channel_id=1, source_target_pairs={{0,4},{4,8},{8,12},{12,14},{14,10},{10,6},{6,2},{2,0},{1,5},{5,9},... | collective-permute-start | bytes 786440 | tf_op jit(solution)/shard_map/ppermute | solution.py:114
  127.9 53.0 %collective-permute-start.40 = (bf16[384,2048]{1,0:T(8,128)(2,1)S(1)}, bf16[384,2048]{1,0:T(8,128)(2,1)S(1)}, u32[]{:S(2)}, u32[]{:S(2)}) collective-permute-start(bf16[384,2048]{1,0:T(8,128)(2,1)S(1)} %convolution_convert_fusion), channel_id=1, source_target_pairs={{0,1},{1,0},{2,3},{3,2},{4,5},{5,4},{6,7},{7,6},{8,9},{9,8},{10,11... | collective-permute-start | bytes 4718600 | tf_op jit(solution)/shard_map/ppermute | solution.py:117
  133.2 50.8 %collective-permute-start.39 = (bf16[2048,384]{1,0:T(8,128)(2,1)S(1)}, bf16[2048,384]{1,0:T(8,128)(2,1)S(1)}, u32[]{:S(2)}, u32[]{:S(2)}) collective-permute-start(bf16[2048,384]{1,0:T(8,128)(2,1)S(1)} %convolution_convert_fusion.1), channel_id=1, source_target_pairs={{0,1},{1,0},{2,3},{3,2},{4,5},{5,4},{6,7},{7,6},{8,9},{9,8},{10,11... | collective-permute-start | bytes 4718600 | tf_op jit(solution)/shard_map/ppermute | solution.py:117
  147.4 9.2 %collective-permute-start.25 = (bf16[64,2048]{1,0:T(8,128)(2,1)S(1)}, bf16[64,2048]{1,0:T(8,128)(2,1)S(1)}, u32[]{:S(2)}, u32[]{:S(2)}) collective-permute-start(bf16[64,2048]{1,0:T(8,128)(2,1)S(1)} %add_convert_fusion.10), channel_id=1, source_target_pairs={{0,2},{4,0},{8,4},{12,8},{14,12},{10,14},{6,10},{2,6},{1,3},{5,1},... | collective-permute-start | bytes 786440 | tf_op jit(solution)/shard_map/ppermute | solution.py:114
  149.2 24.2 %collective-permute-start.37 = (bf16[64,2048]{1,0:T(8,128)(2,1)S(1)}, bf16[64,2048]{1,0:T(8,128)(2,1)S(1)}, u32[]{:S(2)}, u32[]{:S(2)}) collective-permute-start(bf16[64,2048]{1,0:T(8,128)(2,1)S(1)} %add_convert_fusion.8), channel_id=1, source_target_pairs={{0,2},{4,0},{8,4},{12,8},{14,12},{10,14},{6,10},{2,6},{1,3},{5,1},... | collective-permute-start | bytes 786440 | tf_op jit(solution)/shard_map/ppermute | solution.py:114
  154.0 23.9 %collective-permute-start.34 = (bf16[64,2048]{1,0:T(8,128)(2,1)S(1)}, bf16[64,2048]{1,0:T(8,128)(2,1)S(1)}, u32[]{:S(2)}, u32[]{:S(2)}) collective-permute-start(bf16[64,2048]{1,0:T(8,128)(2,1)S(1)} %add_convert_fusion.7), channel_id=1, source_target_pairs={{0,4},{4,8},{8,12},{12,14},{14,10},{10,6},{6,2},{2,0},{1,5},{5,9},... | collective-permute-start | bytes 786440 | tf_op jit(solution)/shard_map/ppermute | solution.py:114
  156.6 9.1 %collective-permute-start.35 = (bf16[64,2048]{1,0:T(8,128)(2,1)S(1)}, bf16[64,2048]{1,0:T(8,128)(2,1)S(1)}, u32[]{:S(2)}, u32[]{:S(2)}) collective-permute-start(bf16[64,2048]{1,0:T(8,128)(2,1)S(1)} %add_convert_fusion.5), channel_id=1, source_target_pairs={{0,4},{4,8},{8,12},{12,14},{14,10},{10,6},{6,2},{2,0},{1,5},{5,9},... | collective-permute-start | bytes 786440 | tf_op jit(solution)/shard_map/ppermute | solution.py:114
  177.9 9.7 %collective-permute-start.38 = (bf16[2048,384]{1,0:T(8,128)(2,1)S(1)}, bf16[2048,384]{1,0:T(8,128)(2,1)S(1)}, u32[]{:S(2)}, u32[]{:S(2)}) collective-permute-start(bf16[2048,384]{1,0:T(8,128)(2,1)S(1)} %convolution_convert_fusion.2), channel_id=1, source_target_pairs={{0,1},{1,0},{2,3},{3,2},{4,5},{5,4},{6,7},{7,6},{8,9},{9,8},{10,11... | collective-permute-start | bytes 4718600 | tf_op jit(solution)/shard_map/ppermute | solution.py:117
  (15 other events, 167.6 us)

commit v3 on v2

--- a/solution.py
+++ b/solution.py
@@ -139,8 +139,6 @@
     outgoing = jnp.sum(jnp.where(chosen, route_ratio[None, None], 0.0), axis=3)
 
     def ratio_from(distance):
-        if distance == 0:
-            return outgoing[0]
         return shift(outgoing[-distance % groups], -distance)
 
     gates, ups, downs = [w_gate[0]], [w_up[0]], [w_down[0]]
@@ -148,8 +146,8 @@
         gates.append(member_shift(w_gate[0], members - k))
         ups.append(member_shift(w_up[0], members - k))
         downs.append(member_shift(w_down[0], members - k))
-    in_w = jnp.concatenate(gates + ups, axis=1)
-    gate_w, up_w = in_w[:, :span], in_w[:, span:]
+    gate_w = jnp.concatenate(gates, axis=1)
+    up_w = jnp.concatenate(ups, axis=1)
     down_w = jnp.concatenate(downs, axis=0)
     column = jnp.arange(span, dtype=jnp.int32)[None, :] // width
 
@@ -157,8 +155,7 @@
         r = ratio[:, 0:1]
         for m in range(1, members):
             r = jnp.where(column == m, ratio[:, m : m + 1], r)
-        pre = mm(x, in_w)
-        gate, up = pre[:, :span], pre[:, span:]
+        gate, up = mm(x, gate_w), mm(x, up_w)
         s = jax.nn.sigmoid(gate)
         act = gate * s
         hidden = (act * up * r).astype(jnp.bfloat16)
@@ -168,25 +165,30 @@
         part = mm(gg, gate_w, NT) + mm(ug, up_w, NT)
         return part, gg, ug, hidden
 
-    kept = []
-    own_part, *rest = piece(layer_input, output_grad, ratio_from(0).T)
-    kept.append((layer_input, output_grad, *rest))
-    part_left, part_right = [], []
+    kept, part_left, part_right = [], [], []
+
+    def step_piece(steps, ratios):
+        x = jnp.concatenate([x for x, _ in steps], axis=0)
+        og = jnp.concatenate([og for _, og in steps], axis=0)
+        ratio = jnp.concatenate(ratios, axis=1).T
+        if kept:
+            ratio = lax.optimization_barrier((ratio, kept[-1][2]))[0]
+        part, *rest = piece(x, og, ratio)
+        kept.append((x, og, *rest))
+        part = part.astype(jnp.bfloat16)
+        return part[:tok_rows], part[tok_rows:]
+
     for k in range(1, full_steps + 1):
-        x = jnp.concatenate([from_left[k - 1][0], from_right[k - 1][0]], axis=0)
-        og = jnp.concatenate([from_left[k - 1][1], from_right[k - 1][1]], axis=0)
         ratio = [ratio_from(-k), ratio_from(k)]
-        part, *rest = piece(x, og, jnp.concatenate(ratio, axis=1).T)
-        part = part.astype(jnp.bfloat16)
-        part_left.append(part[:tok_rows])
-        part_right.append(part[tok_rows:])
-        kept.append((x, og, *rest))
+        parts = step_piece((from_left[k - 1], from_right[k - 1]), ratio)
+        part_left.append(parts[0])
+        part_right.append(parts[1])
     half = tok_rows // 2
-    far_part = None
+    steps, ratio = [(layer_input, output_grad)], [outgoing[0]]
     if has_far:
-        part, *rest = piece(far[0], far[1], ratio_from(groups // 2).T)
-        far_part = part.astype(jnp.bfloat16)
-        kept.append((far[0], far[1], *rest))
+        steps.append(far)
+        ratio.append(ratio_from(groups // 2))
+    own_part, far_part = step_piece(steps, ratio)
 
     low, high = slice(0, half), slice(half, tok_rows)
 
@@ -223,7 +225,7 @@
     back_high = [long_way and long_way[1], short_way and short_way[0]]
 
     def closing(rows, returned):
-        total = own_part[rows]
+        total = own_part[rows].astype(jnp.float32)
         for piece_back in returned:
             if piece_back is not None:
                 total = total + piece_back.astype(jnp.float32)

time: 192 us -> 205 us (1.068); the launches traced: 191 us -> 202 us
  waiting for transfers between devices: 92.5 us -> 105 us
  matrix products: 43.4 us -> 38.5 us
  starting transfers between devices: 46.1 us -> 49.8 us
    ppermute x35, waiting for transfers between devices: 92.5 us -> 105 us  [shift(): return lax.ppermute(array, 'grp', at_distance(k))]
    dot_general x26, matrix products: 43.4 us -> 38.5 us  [mm(): return lax.dot_general(a, b, dims, preferred_element_type=jnp.float32)]
    ppermute x35, starting transfers between devices: 45.1 us -> 49.3 us  [shift(): return lax.ppermute(array, 'grp', at_distance(k))]
  transfers between devices with their start and end apart: 41 -> 41, of which waited for: 21 -> 21; matrix products, arithmetic and copies ran while one was open for 25% -> 21% of each run, Pallas kernels for 0% -> 0%
where the time goes in v3:
time: 205 us; the launch traced here: 202 us
  waiting for transfers between devices  105 us (51%)
  starting transfers between devices  49.8 us (24%)
  matrix products  38.5 us (19%)
  other arithmetic  5.1 us (2%)
    ppermute x35, waiting for transfers between devices, shift(): return lax.ppermute(array, 'grp', at_distance(k))  105 us
    ppermute x35, starting transfers between devices, shift(): return lax.ppermute(array, 'grp', at_distance(k))  49.3 us
    dot_general x26, matrix products, mm(): return lax.dot_general(a, b, dims, preferred_element_type=jnp.float32)  38.5 us
  transfers between devices with their start and end apart: 41, of which 21 were waited for; matrix products, arithmetic and copies ran while one was open for 21% of the time, Pallas kernels for 0%

profile of v3, /device:TPU:0, one launch (start us, length us, event | category | flops | bytes accessed | tf_op | source)
XLA Modules:
  0.0 202.1 jit_solution(888922664927894072)
XLA Ops:
  0.6 3.1 %collective-permute-start.7 = (bf16[128,2048]{1,0:T(8,128)(2,1)}, bf16[128,2048]{1,0:T(8,128)(2,1)S(1)}, u32[]{:S(2)}, u32[]{:S(2)}) collective-permute-start(bf16[128,2048]{1,0:T(8,128)(2,1)} %param.9), channel_id=1, source_target_pairs={{0,4},{4,8},{8,12},{12,14},{14,10},{10,6},{6,2},{2,0},{1,5},{5,9},... | collective-permute-start | bytes 1572872 | tf_op jit(solution)/shard_map/ppermute | solution.py:114
  6.8 2.1 %collective-permute-start.5 = (f32[2,128]{1,0:T(2,128)S(1)}, f32[2,128]{1,0:T(2,128)S(1)}, u32[]{:S(2)}, u32[]{:S(2)}) collective-permute-start(f32[2,128]{1,0:T(2,128)S(1)} %get-tuple-element.72), channel_id=1, source_target_pairs={{0,4},{4,8},{8,12},{12,14},{14,10},{10,6},{6,2},{2,0},{1,5},{5,9},... | collective-permute-start | bytes 3080 | tf_op jit(solution)/shard_map/ppermute | solution.py:114
  8.9 2.0 collective-permute-start.10
  10.9 5.8 %collective-permute-done.5 = f32[2,128]{1,0:T(2,128)S(1)} collective-permute-done((f32[2,128]{1,0:T(2,128)S(1)}, f32[2,128]{1,0:T(2,128)S(1)}, u32[]{:S(2)}, u32[]{:S(2)}) %collective-permute-start.5) | collective-permute-done | bytes 1056 | tf_op jit(solution)/shard_map/ppermute | solution.py:114
  16.7 3.1 %collective-permute-start.3 = (f32[2,128]{1,0:T(2,128)S(1)}, f32[2,128]{1,0:T(2,128)S(1)}, u32[]{:S(2)}, u32[]{:S(2)}) collective-permute-start(f32[2,128]{1,0:T(2,128)S(1)} %get-tuple-element.74), channel_id=1, source_target_pairs={{0,8},{4,12},{8,14},{12,10},{14,6},{10,2},{6,0},{2,4},{1,9},{5,13}... | collective-permute-start | bytes 3080 | tf_op jit(solution)/shard_map/ppermute | solution.py:114
  19.9 8.4 %collective-permute-done.3 = f32[2,128]{1,0:T(2,128)S(1)} collective-permute-done((f32[2,128]{1,0:T(2,128)S(1)}, f32[2,128]{1,0:T(2,128)S(1)}, u32[]{:S(2)}, u32[]{:S(2)}) %collective-permute-start.3) | collective-permute-done | bytes 1056 | tf_op jit(solution)/shard_map/ppermute | solution.py:114
  28.3 2.5 %collective-permute-start.1 = (f32[2,128]{1,0:T(2,128)S(1)}, f32[2,128]{1,0:T(2,128)S(1)}, u32[]{:S(2)}, u32[]{:S(2)}) collective-permute-start(f32[2,128]{1,0:T(2,128)S(1)} %get-tuple-element.76), channel_id=1, source_target_pairs={{0,12},{4,14},{8,10},{12,6},{14,2},{10,0},{6,4},{2,8},{1,13},{5,15... | collective-permute-start | bytes 3080 | tf_op jit(solution)/shard_map/ppermute | solution.py:114
  36.2 2.3 %collective-permute-start = (f32[2,128]{1,0:T(2,128)S(1)}, f32[2,128]{1,0:T(2,128)S(1)}, u32[]{:S(2)}, u32[]{:S(2)}) collective-permute-start(f32[2,128]{1,0:T(2,128)S(1)} %get-tuple-element.77), channel_id=1, source_target_pairs={{0,14},{4,10},{8,6},{12,2},{14,0},{10,4},{6,8},{2,12},{1,15},{5,11... | collective-permute-start | bytes 3080 | tf_op jit(solution)/shard_map/ppermute | solution.py:114
  38.5 4.0 %collective-permute-done = f32[2,128]{1,0:T(2,128)S(1)} collective-permute-done((f32[2,128]{1,0:T(2,128)S(1)}, f32[2,128]{1,0:T(2,128)S(1)}, u32[]{:S(2)}, u32[]{:S(2)}) %collective-permute-start) | collective-permute-done | bytes 1056 | tf_op jit(solution)/shard_map/ppermute | solution.py:114
  42.6 5.6 %collective-permute-start.14 = (bf16[128,2048]{1,0:T(8,128)(2,1)S(1)}, bf16[128,2048]{1,0:T(8,128)(2,1)S(1)}, u32[]{:S(2)}, u32[]{:S(2)}) collective-permute-start(bf16[128,2048]{1,0:T(8,128)(2,1)S(1)} %collective-permute-done.7), channel_id=1, source_target_pairs={{0,4},{4,8},{8,12},{12,14},{14,10},{10,6},{6,2},{2,0},{1,5},{5,9},... | collective-permute-start | bytes 1572872 | tf_op jit(solution)/shard_map/ppermute | solution.py:114
  50.2 10.3 %collective-permute-done.16 = bf16[128,2048]{1,0:T(8,128)(2,1)S(1)} collective-permute-done((bf16[128,2048]{1,0:T(8,128)(2,1)S(1)}, bf16[128,2048]{1,0:T(8,128)(2,1)S(1)}, u32[]{:S(2)}, u32[]{:S(2)}) %collective-permute-start.16) | collective-permute-done | bytes 524320 | tf_op jit(solution)/shard_map/ppermute | solution.py:114
  60.7 3.2 %collective-permute-done.17 = bf16[128,2048]{1,0:T(8,128)(2,1)S(1)} collective-permute-done((bf16[128,2048]{1,0:T(8,128)(2,1)S(1)}, bf16[128,2048]{1,0:T(8,128)(2,1)S(1)}, u32[]{:S(2)}, u32[]{:S(2)}) %collective-permute-start.17) | collective-permute-done | bytes 524320 | tf_op jit(solution)/shard_map/ppermute | solution.py:114
  63.9 2.0 collective-permute-start.20
  65.9 5.9 %collective-permute-done.14 = bf16[128,2048]{1,0:T(8,128)(2,1)S(1)} collective-permute-done((bf16[128,2048]{1,0:T(8,128)(2,1)S(1)}, bf16[128,2048]{1,0:T(8,128)(2,1)S(1)}, u32[]{:S(2)}, u32[]{:S(2)}) %collective-permute-start.14) | collective-permute-done | bytes 524320 | tf_op jit(solution)/shard_map/ppermute | solution.py:114
  71.8 2.5 %collective-permute-done.15 = bf16[128,2048]{1,0:T(8,128)(2,1)S(1)} collective-permute-done((bf16[128,2048]{1,0:T(8,128)(2,1)S(1)}, bf16[128,2048]{1,0:T(8,128)(2,1)S(1)}, u32[]{:S(2)}, u32[]{:S(2)}) %collective-permute-start.15) | collective-permute-done | bytes 524320 | tf_op jit(solution)/shard_map/ppermute | solution.py:114
  74.5 19.5 %collective-permute-done.18 = bf16[128,2048]{1,0:T(8,128)(2,1)S(1)} collective-permute-done((bf16[128,2048]{1,0:T(8,128)(2,1)S(1)}, bf16[128,2048]{1,0:T(8,128)(2,1)S(1)}, u32[]{:S(2)}, u32[]{:S(2)}) %collective-permute-start.18) | collective-permute-done | bytes 524320 | tf_op jit(solution)/shard_map/ppermute | solution.py:114
  96.3 11.4 %collective-permute-done.21 = bf16[128,2048]{1,0:T(8,128)(2,1)S(1)} collective-permute-done((bf16[128,2048]{1,0:T(8,128)(2,1)S(1)}, bf16[128,2048]{1,0:T(8,128)(2,1)S(1)}, u32[]{:S(2)}, u32[]{:S(2)}) %collective-permute-start.21) | collective-permute-done | bytes 524320 | tf_op jit(solution)/shard_map/ppermute | solution.py:114
  107.7 1.9 collective-permute-start.23
  123.2 1.9 collective-permute-start.26
  135.9 1.8 convolution_convert_fusion
  141.6 2.4 %convolution_convert_fusion.1 = bf16[2048,384]{1,0:T(8,128)(2,1)S(1)} fusion(bf16[1024,2048]{1,0:T(8,128)(2,1)S(1)} %get-tuple-element.54, bf16[1024,768]{1,0:T(8,128)(2,1)S(1)} %pad_maximum_fusion.4), kind=kOutput, calls=%fused_computation.7 | convolution fusion | flops 1611399168 | bytes 6553600 | tf_op jit(solution)/shard_map/dot_general | solution.py:97
  144.4 4.5 %collective-permute-done.29 = bf16[64,2048]{1,0:T(8,128)(2,1)S(1)} collective-permute-done((bf16[64,2048]{1,0:T(8,128)(2,1)S(1)}, bf16[64,2048]{1,0:T(8,128)(2,1)S(1)}, u32[]{:S(2)}, u32[]{:S(2)}) %collective-permute-start.29) | collective-permute-done | bytes 262176 | tf_op jit(solution)/shard_map/ppermute | solution.py:114
  148.8 1.9 collective-permute-start.24
  150.8 6.2 %collective-permute-done.24 = bf16[64,2048]{1,0:T(8,128)(2,1)S(1)} collective-permute-done((bf16[64,2048]{1,0:T(8,128)(2,1)S(1)}, bf16[64,2048]{1,0:T(8,128)(2,1)S(1)}, u32[]{:S(2)}, u32[]{:S(2)}) %collective-permute-start.24) | collective-permute-done | bytes 262176 | tf_op jit(solution)/shard_map/ppermute | solution.py:114
  160.9 3.0 %collective-permute-done.32 = bf16[64,2048]{1,0:T(8,128)(2,1)S(1)} collective-permute-done((bf16[64,2048]{1,0:T(8,128)(2,1)S(1)}, bf16[64,2048]{1,0:T(8,128)(2,1)S(1)}, u32[]{:S(2)}, u32[]{:S(2)}) %collective-permute-start.32) | collective-permute-done | bytes 262176 | tf_op jit(solution)/shard_map/ppermute | solution.py:114
  165.4 2.3 %collective-permute-done.27 = bf16[64,2048]{1,0:T(8,128)(2,1)S(1)} collective-permute-done((bf16[64,2048]{1,0:T(8,128)(2,1)S(1)}, bf16[64,2048]{1,0:T(8,128)(2,1)S(1)}, u32[]{:S(2)}, u32[]{:S(2)}) %collective-permute-start.27) | collective-permute-done | bytes 262176 | tf_op jit(solution)/shard_map/ppermute | solution.py:114
  168.6 7.1 %collective-permute-done.35 = bf16[64,2048]{1,0:T(8,128)(2,1)S(1)} collective-permute-done((bf16[64,2048]{1,0:T(8,128)(2,1)S(1)}, bf16[64,2048]{1,0:T(8,128)(2,1)S(1)}, u32[]{:S(2)}, u32[]{:S(2)}) %collective-permute-start.35) | collective-permute-done | bytes 262176 | tf_op jit(solution)/shard_map/ppermute | solution.py:114
  177.4 5.1 %collective-permute-done.31 = bf16[64,2048]{1,0:T(8,128)(2,1)S(1)} collective-permute-done((bf16[64,2048]{1,0:T(8,128)(2,1)S(1)}, bf16[64,2048]{1,0:T(8,128)(2,1)S(1)}, u32[]{:S(2)}, u32[]{:S(2)}) %collective-permute-start.31) | collective-permute-done | bytes 262176 | tf_op jit(solution)/shard_map/ppermute | solution.py:114
  185.1 2.4 %convolution_convert_fusion.2 = bf16[2048,384]{1,0:T(8,128)(2,1)S(1)} fusion(bf16[1024,2048]{1,0:T(8,128)(2,1)S(1)} %get-tuple-element.54, bf16[1024,768]{1,0:T(8,128)(2,1)S(1)} %pad_maximum_fusion.3), kind=kOutput, calls=%fused_computation.8 | convolution fusion | flops 1611399168 | bytes 6553600 | tf_op jit(solution)/shard_map/dot_general | solution.py:97
  191.8 3.0 %fusion.6 = bf16[1,384,2048]{2,1,0:T(8,128)(2,1)} fusion(bf16[1024,2048]{1,0:T(8,128)(2,1)S(1)} %constant_dynamic-update-slice_fusion.16, bf16[384,2048]{1,0:T(8,128)(2,1)S(1)} %collective-permute-done.40, bf16[1024,768]{1,0:T(8,128)(2,1)S(1)} %pad_maximum_fusion.5), kind=kOutput, calls=%fused_computation.19 | convolution fusion | flops 1612972032 | bytes 8126464 | tf_op jit(solution)/shard_map/dot_general | solution.py:97
  194.8 3.5 %fusion.5 = bf16[1,2048,384]{2,1,0:T(8,128)(2,1)} fusion(bf16[1024,2048]{1,0:T(8,128)(2,1)S(1)} %get-tuple-element.54, bf16[2048,384]{1,0:T(8,128)(2,1)S(1)} %collective-permute-done.39, bf16[1024,768]{1,0:T(8,128)(2,1)S(1)} %pad_maximum_fusion.4), kind=kOutput, calls=%fused_computation.18 | convolution fusion | flops 1612972032 | bytes 8126464 | tf_op jit(solution)/shard_map/dot_general | solution.py:97
  198.3 3.5 %fusion.4 = bf16[1,2048,384]{2,1,0:T(8,128)(2,1)} fusion(bf16[1024,2048]{1,0:T(8,128)(2,1)S(1)} %get-tuple-element.54, bf16[2048,384]{1,0:T(8,128)(2,1)S(1)} %collective-permute-done.38, bf16[1024,768]{1,0:T(8,128)(2,1)S(1)} %pad_maximum_fusion.3), kind=kOutput, calls=%fused_computation.17 | convolution fusion | flops 1612972032 | bytes 8126464 | tf_op jit(solution)/shard_map/dot_general | solution.py:97
  (138 shorter events, 56.6 us)
Async XLA Ops:
  0.6 41.9 %collective-permute-start.7 = (bf16[128,2048]{1,0:T(8,128)(2,1)}, bf16[128,2048]{1,0:T(8,128)(2,1)S(1)}, u32[]{:S(2)}, u32[]{:S(2)}) collective-permute-start(bf16[128,2048]{1,0:T(8,128)(2,1)} %param.9), channel_id=1, source_target_pairs={{0,4},{4,8},{8,12},{12,14},{14,10},{10,6},{6,2},{2,0},{1,5},{5,9},... | collective-permute-start | bytes 1572872 | tf_op jit(solution)/shard_map/ppermute | solution.py:114
  3.7 44.7 %collective-permute-start.8 = (bf16[128,2048]{1,0:T(8,128)(2,1)}, bf16[128,2048]{1,0:T(8,128)(2,1)S(1)}, u32[]{:S(2)}, u32[]{:S(2)}) collective-permute-start(bf16[128,2048]{1,0:T(8,128)(2,1)} %param.9), channel_id=1, source_target_pairs={{0,2},{4,0},{8,4},{12,8},{14,12},{10,14},{6,10},{2,6},{1,3},{5,1},... | collective-permute-start | bytes 1572872 | tf_op jit(solution)/shard_map/ppermute | solution.py:114
  6.8 9.9 %collective-permute-start.5 = (f32[2,128]{1,0:T(2,128)S(1)}, f32[2,128]{1,0:T(2,128)S(1)}, u32[]{:S(2)}, u32[]{:S(2)}) collective-permute-start(f32[2,128]{1,0:T(2,128)S(1)} %get-tuple-element.72), channel_id=1, source_target_pairs={{0,4},{4,8},{8,12},{12,14},{14,10},{10,6},{6,2},{2,0},{1,5},{5,9},... | collective-permute-start | bytes 3080 | tf_op jit(solution)/shard_map/ppermute | solution.py:114
  8.9 10.9 %collective-permute-start.6 = (f32[2,128]{1,0:T(2,128)S(1)}, f32[2,128]{1,0:T(2,128)S(1)}, u32[]{:S(2)}, u32[]{:S(2)}) collective-permute-start(f32[2,128]{1,0:T(2,128)S(1)} %get-tuple-element.71), channel_id=1, source_target_pairs={{0,2},{4,0},{8,4},{12,8},{14,12},{10,14},{6,10},{2,6},{1,3},{5,1},... | collective-permute-start | bytes 3080 | tf_op jit(solution)/shard_map/ppermute | solution.py:114
  8.9 33.6 %collective-permute-start.10 = (bf16[128,2048]{1,0:T(8,128)(2,1)}, bf16[128,2048]{1,0:T(8,128)(2,1)S(1)}, u32[]{:S(2)}, u32[]{:S(2)}) collective-permute-start(bf16[128,2048]{1,0:T(8,128)(2,1)} %param.8), channel_id=1, source_target_pairs={{0,4},{4,8},{8,12},{12,14},{14,10},{10,6},{6,2},{2,0},{1,5},{5,9},... | collective-permute-start | bytes 1572872 | tf_op jit(solution)/shard_map/ppermute | solution.py:114
  16.7 11.5 %collective-permute-start.3 = (f32[2,128]{1,0:T(2,128)S(1)}, f32[2,128]{1,0:T(2,128)S(1)}, u32[]{:S(2)}, u32[]{:S(2)}) collective-permute-start(f32[2,128]{1,0:T(2,128)S(1)} %get-tuple-element.74), channel_id=1, source_target_pairs={{0,8},{4,12},{8,14},{12,10},{14,6},{10,2},{6,0},{2,4},{1,9},{5,13}... | collective-permute-start | bytes 3080 | tf_op jit(solution)/shard_map/ppermute | solution.py:114
  19.8 11.0 %collective-permute-start.4 = (f32[2,128]{1,0:T(2,128)S(1)}, f32[2,128]{1,0:T(2,128)S(1)}, u32[]{:S(2)}, u32[]{:S(2)}) collective-permute-start(f32[2,128]{1,0:T(2,128)S(1)} %get-tuple-element.73), channel_id=1, source_target_pairs={{0,6},{4,2},{8,0},{12,4},{14,8},{10,12},{6,14},{2,10},{1,7},{5,3},... | collective-permute-start | bytes 3080 | tf_op jit(solution)/shard_map/ppermute | solution.py:114
  33.7 14.7 %collective-permute-start.11 = (bf16[128,2048]{1,0:T(8,128)(2,1)}, bf16[128,2048]{1,0:T(8,128)(2,1)S(1)}, u32[]{:S(2)}, u32[]{:S(2)}) collective-permute-start(bf16[128,2048]{1,0:T(8,128)(2,1)} %param.8), channel_id=1, source_target_pairs={{0,2},{4,0},{8,4},{12,8},{14,12},{10,14},{6,10},{2,6},{1,3},{5,1},... | collective-permute-start | bytes 1572872 | tf_op jit(solution)/shard_map/ppermute | solution.py:114
  42.5 68.5 %collective-permute-start.9 = (bf16[384,2048]{1,0:T(8,128)(2,1)}, bf16[384,2048]{1,0:T(8,128)(2,1)S(1)}, u32[]{:S(2)}, u32[]{:S(2)}) collective-permute-start(bf16[384,2048]{1,0:T(8,128)(2,1)} %bitcast.73), channel_id=1, source_target_pairs={{0,1},{1,0},{2,3},{3,2},{4,5},{5,4},{6,7},{7,6},{8,9},{9,8},{10,11... | collective-permute-start | bytes 4718600 | tf_op jit(solution)/shard_map/ppermute | solution.py:117
  42.5 18.0 %collective-permute-start.16 = (bf16[128,2048]{1,0:T(8,128)(2,1)S(1)}, bf16[128,2048]{1,0:T(8,128)(2,1)S(1)}, u32[]{:S(2)}, u32[]{:S(2)}) collective-permute-start(bf16[128,2048]{1,0:T(8,128)(2,1)S(1)} %collective-permute-done.10), channel_id=1, source_target_pairs={{0,4},{4,8},{8,12},{12,14},{14,10},{10,6},{6,2},{2,0},{1,5},{5,9},... | collective-permute-start | bytes 1572872 | tf_op jit(solution)/shard_map/ppermute | solution.py:114
  42.6 29.2 %collective-permute-start.14 = (bf16[128,2048]{1,0:T(8,128)(2,1)S(1)}, bf16[128,2048]{1,0:T(8,128)(2,1)S(1)}, u32[]{:S(2)}, u32[]{:S(2)}) collective-permute-start(bf16[128,2048]{1,0:T(8,128)(2,1)S(1)} %collective-permute-done.7), channel_id=1, source_target_pairs={{0,4},{4,8},{8,12},{12,14},{14,10},{10,6},{6,2},{2,0},{1,5},{5,9},... | collective-permute-start | bytes 1572872 | tf_op jit(solution)/shard_map/ppermute | solution.py:114
  48.4 15.4 %collective-permute-start.17 = (bf16[128,2048]{1,0:T(8,128)(2,1)S(1)}, bf16[128,2048]{1,0:T(8,128)(2,1)S(1)}, u32[]{:S(2)}, u32[]{:S(2)}) collective-permute-start(bf16[128,2048]{1,0:T(8,128)(2,1)S(1)} %collective-permute-done.11), channel_id=1, source_target_pairs={{0,2},{4,0},{8,4},{12,8},{14,12},{10,14},{6,10},{2,6},{1,3},{5,1},... | collective-permute-start | bytes 1572872 | tf_op jit(solution)/shard_map/ppermute | solution.py:114
  48.5 25.8 %collective-permute-start.15 = (bf16[128,2048]{1,0:T(8,128)(2,1)S(1)}, bf16[128,2048]{1,0:T(8,128)(2,1)S(1)}, u32[]{:S(2)}, u32[]{:S(2)}) collective-permute-start(bf16[128,2048]{1,0:T(8,128)(2,1)S(1)} %collective-permute-done.8), channel_id=1, source_target_pairs={{0,2},{4,0},{8,4},{12,8},{14,12},{10,14},{6,10},{2,6},{1,3},{5,1},... | collective-permute-start | bytes 1572872 | tf_op jit(solution)/shard_map/ppermute | solution.py:114
  60.5 49.5 %collective-permute-start.13 = (bf16[2048,384]{1,0:T(8,128)(2,1)S(1)}, bf16[2048,384]{1,0:T(8,128)(2,1)S(1)}, u32[]{:S(2)}, u32[]{:S(2)}) collective-permute-start(bf16[2048,384]{1,0:T(8,128)(2,1)S(1)} %bitcast.87), channel_id=1, source_target_pairs={{0,1},{1,0},{2,3},{3,2},{4,5},{5,4},{6,7},{7,6},{8,9},{9,8},{10,11... | collective-permute-start | bytes 4718600 | tf_op jit(solution)/shard_map/ppermute | solution.py:117
  63.9 32.1 %collective-permute-start.20 = (bf16[128,2048]{1,0:T(8,128)(2,1)S(1)}, bf16[128,2048]{1,0:T(8,128)(2,1)S(1)}, u32[]{:S(2)}, u32[]{:S(2)}) collective-permute-start(bf16[128,2048]{1,0:T(8,128)(2,1)S(1)} %collective-permute-done.16), channel_id=1, source_target_pairs={{0,4},{4,8},{8,12},{12,14},{14,10},{10,6},{6,2},{2,0},{1,5},{5,9},... | collective-permute-start | bytes 1572872 | tf_op jit(solution)/shard_map/ppermute | solution.py:114
  71.8 22.2 %collective-permute-start.18 = (bf16[128,2048]{1,0:T(8,128)(2,1)S(1)}, bf16[128,2048]{1,0:T(8,128)(2,1)S(1)}, u32[]{:S(2)}, u32[]{:S(2)}) collective-permute-start(bf16[128,2048]{1,0:T(8,128)(2,1)S(1)} %collective-permute-done.14), channel_id=1, source_target_pairs={{0,4},{4,8},{8,12},{12,14},{14,10},{10,6},{6,2},{2,0},{1,5},{5,9},... | collective-permute-start | bytes 1572872 | tf_op jit(solution)/shard_map/ppermute | solution.py:114
  74.3 21.5 %collective-permute-start.19 = (bf16[128,2048]{1,0:T(8,128)(2,1)S(1)}, bf16[128,2048]{1,0:T(8,128)(2,1)S(1)}, u32[]{:S(2)}, u32[]{:S(2)}) collective-permute-start(bf16[128,2048]{1,0:T(8,128)(2,1)S(1)} %collective-permute-done.15), channel_id=1, source_target_pairs={{0,2},{4,0},{8,4},{12,8},{14,12},{10,14},{6,10},{2,6},{1,3},{5,1},... | collective-permute-start | bytes 1572872 | tf_op jit(solution)/shard_map/ppermute | solution.py:114
  94.0 13.7 %collective-permute-start.21 = (bf16[128,2048]{1,0:T(8,128)(2,1)S(1)}, bf16[128,2048]{1,0:T(8,128)(2,1)S(1)}, u32[]{:S(2)}, u32[]{:S(2)}) collective-permute-start(bf16[128,2048]{1,0:T(8,128)(2,1)S(1)} %collective-permute-done.17), channel_id=1, source_target_pairs={{0,2},{4,0},{8,4},{12,8},{14,12},{10,14},{6,10},{2,6},{1,3},{5,1},... | collective-permute-start | bytes 1572872 | tf_op jit(solution)/shard_map/ppermute | solution.py:114
  95.8 16.6 %collective-permute-start.12 = (bf16[2048,384]{1,0:T(8,128)(2,1)S(1)}, bf16[2048,384]{1,0:T(8,128)(2,1)S(1)}, u32[]{:S(2)}, u32[]{:S(2)}) collective-permute-start(bf16[2048,384]{1,0:T(8,128)(2,1)S(1)} %bitcast.78), channel_id=1, source_target_pairs={{0,1},{1,0},{2,3},{3,2},{4,5},{5,4},{6,7},{7,6},{8,9},{9,8},{10,11... | collective-permute-start | bytes 4718600 | tf_op jit(solution)/shard_map/ppermute | solution.py:117
  96.0 38.3 %collective-permute-start.22 = (bf16[128,2048]{1,0:T(8,128)(2,1)S(1)}, bf16[128,2048]{1,0:T(8,128)(2,1)S(1)}, u32[]{:S(2)}, u32[]{:S(2)}) collective-permute-start(bf16[128,2048]{1,0:T(8,128)(2,1)S(1)} %collective-permute-done.18), channel_id=1, source_target_pairs={{0,4},{4,8},{8,12},{12,14},{14,10},{10,6},{6,2},{2,0},{1,5},{5,9},... | collective-permute-start | bytes 1572872 | tf_op jit(solution)/shard_map/ppermute | solution.py:114
  107.7 24.5 %collective-permute-start.23 = (bf16[128,2048]{1,0:T(8,128)(2,1)S(1)}, bf16[128,2048]{1,0:T(8,128)(2,1)S(1)}, u32[]{:S(2)}, u32[]{:S(2)}) collective-permute-start(bf16[128,2048]{1,0:T(8,128)(2,1)S(1)} %collective-permute-done.21), channel_id=1, source_target_pairs={{0,2},{4,0},{8,4},{12,8},{14,12},{10,14},{6,10},{2,6},{1,3},{5,1},... | collective-permute-start | bytes 1572872 | tf_op jit(solution)/shard_map/ppermute | solution.py:114
  130.1 28.4 %collective-permute-start.28 = (bf16[64,2048]{1,0:T(8,128)(2,1)S(1)}, bf16[64,2048]{1,0:T(8,128)(2,1)S(1)}, u32[]{:S(2)}, u32[]{:S(2)}) collective-permute-start(bf16[64,2048]{1,0:T(8,128)(2,1)S(1)} %get-tuple-element.49), channel_id=1, source_target_pairs={{0,2},{4,0},{8,4},{12,8},{14,12},{10,14},{6,10},{2,6},{1,3},{5,1},... | collective-permute-start | bytes 786440 | tf_op jit(solution)/shard_map/ppermute | solution.py:114
  131.8 27.4 %collective-permute-start.30 = (bf16[64,2048]{1,0:T(8,128)(2,1)S(1)}, bf16[64,2048]{1,0:T(8,128)(2,1)S(1)}, u32[]{:S(2)}, u32[]{:S(2)}) collective-permute-start(bf16[64,2048]{1,0:T(8,128)(2,1)S(1)} %get-tuple-element.48), channel_id=1, source_target_pairs={{0,4},{4,8},{8,12},{12,14},{14,10},{10,6},{6,2},{2,0},{1,5},{5,9},... | collective-permute-start | bytes 786440 | tf_op jit(solution)/shard_map/ppermute | solution.py:114
  137.8 54.0 %collective-permute-start.40 = (bf16[384,2048]{1,0:T(8,128)(2,1)S(1)}, bf16[384,2048]{1,0:T(8,128)(2,1)S(1)}, u32[]{:S(2)}, u32[]{:S(2)}) collective-permute-start(bf16[384,2048]{1,0:T(8,128)(2,1)S(1)} %convolution_convert_fusion), channel_id=1, source_target_pairs={{0,1},{1,0},{2,3},{3,2},{4,5},{5,4},{6,7},{7,6},{8,9},{9,8},{10,11... | collective-permute-start | bytes 4718600 | tf_op jit(solution)/shard_map/ppermute | solution.py:117
  140.1 8.8 %collective-permute-start.29 = (bf16[64,2048]{1,0:T(8,128)(2,1)S(1)}, bf16[64,2048]{1,0:T(8,128)(2,1)S(1)}, u32[]{:S(2)}, u32[]{:S(2)}) collective-permute-start(bf16[64,2048]{1,0:T(8,128)(2,1)S(1)} %get-tuple-element.46), channel_id=1, source_target_pairs={{0,4},{4,8},{8,12},{12,14},{14,10},{10,6},{6,2},{2,0},{1,5},{5,9},... | collective-permute-start | bytes 786440 | tf_op jit(solution)/shard_map/ppermute | solution.py:114
  144.0 50.8 %collective-permute-start.39 = (bf16[2048,384]{1,0:T(8,128)(2,1)S(1)}, bf16[2048,384]{1,0:T(8,128)(2,1)S(1)}, u32[]{:S(2)}, u32[]{:S(2)}) collective-permute-start(bf16[2048,384]{1,0:T(8,128)(2,1)S(1)} %convolution_convert_fusion.1), channel_id=1, source_target_pairs={{0,1},{1,0},{2,3},{3,2},{4,5},{5,4},{6,7},{7,6},{8,9},{9,8},{10,11... | collective-permute-start | bytes 4718600 | tf_op jit(solution)/shard_map/ppermute | solution.py:117
  148.8 8.1 %collective-permute-start.24 = (bf16[64,2048]{1,0:T(8,128)(2,1)S(1)}, bf16[64,2048]{1,0:T(8,128)(2,1)S(1)}, u32[]{:S(2)}, u32[]{:S(2)}) collective-permute-start(bf16[64,2048]{1,0:T(8,128)(2,1)S(1)} %get-tuple-element.47), channel_id=1, source_target_pairs={{0,2},{4,0},{8,4},{12,8},{14,12},{10,14},{6,10},{2,6},{1,3},{5,1},... | collective-permute-start | bytes 786440 | tf_op jit(solution)/shard_map/ppermute | solution.py:114
  158.5 9.2 %collective-permute-start.27 = (bf16[64,2048]{1,0:T(8,128)(2,1)S(1)}, bf16[64,2048]{1,0:T(8,128)(2,1)S(1)}, u32[]{:S(2)}, u32[]{:S(2)}) collective-permute-start(bf16[64,2048]{1,0:T(8,128)(2,1)S(1)} %add_convert_fusion.12), channel_id=1, source_target_pairs={{0,2},{4,0},{8,4},{12,8},{14,12},{10,14},{6,10},{2,6},{1,3},{5,1},... | collective-permute-start | bytes 786440 | tf_op jit(solution)/shard_map/ppermute | solution.py:114
  159.2 25.1 %collective-permute-start.37 = (bf16[64,2048]{1,0:T(8,128)(2,1)S(1)}, bf16[64,2048]{1,0:T(8,128)(2,1)S(1)}, u32[]{:S(2)}, u32[]{:S(2)}) collective-permute-start(bf16[64,2048]{1,0:T(8,128)(2,1)S(1)} %add_convert_fusion.10), channel_id=1, source_target_pairs={{0,2},{4,0},{8,4},{12,8},{14,12},{10,14},{6,10},{2,6},{1,3},{5,1},... | collective-permute-start | bytes 786440 | tf_op jit(solution)/shard_map/ppermute | solution.py:114
  163.9 23.5 %collective-permute-start.34 = (bf16[64,2048]{1,0:T(8,128)(2,1)S(1)}, bf16[64,2048]{1,0:T(8,128)(2,1)S(1)}, u32[]{:S(2)}, u32[]{:S(2)}) collective-permute-start(bf16[64,2048]{1,0:T(8,128)(2,1)S(1)} %add_convert_fusion.9), channel_id=1, source_target_pairs={{0,4},{4,8},{8,12},{12,14},{14,10},{10,6},{6,2},{2,0},{1,5},{5,9},... | collective-permute-start | bytes 786440 | tf_op jit(solution)/shard_map/ppermute | solution.py:114
  167.7 8.0 %collective-permute-start.35 = (bf16[64,2048]{1,0:T(8,128)(2,1)S(1)}, bf16[64,2048]{1,0:T(8,128)(2,1)S(1)}, u32[]{:S(2)}, u32[]{:S(2)}) collective-permute-start(bf16[64,2048]{1,0:T(8,128)(2,1)S(1)} %add_convert_fusion.7), channel_id=1, source_target_pairs={{0,4},{4,8},{8,12},{12,14},{14,10},{10,6},{6,2},{2,0},{1,5},{5,9},... | collective-permute-start | bytes 786440 | tf_op jit(solution)/shard_map/ppermute | solution.py:114
  187.5 10.8 %collective-permute-start.38 = (bf16[2048,384]{1,0:T(8,128)(2,1)S(1)}, bf16[2048,384]{1,0:T(8,128)(2,1)S(1)}, u32[]{:S(2)}, u32[]{:S(2)}) collective-permute-start(bf16[2048,384]{1,0:T(8,128)(2,1)S(1)} %convolution_convert_fusion.2), channel_id=1, source_target_pairs={{0,1},{1,0},{2,3},{3,2},{4,5},{5,4},{6,7},{7,6},{8,9},{9,8},{10,11... | collective-permute-start | bytes 4718600 | tf_op jit(solution)/shard_map/ppermute | solution.py:117
  (14 other events, 224.7 us)

commit v4 on v3

--- a/solution.py
+++ b/solution.py
@@ -138,8 +138,16 @@
     chosen = expert_ids[None, None, :, :] == expert[:, :, None, None]
     outgoing = jnp.sum(jnp.where(chosen, route_ratio[None, None], 0.0), axis=3)
 
+    blocks = [outgoing[d] for d in range(groups)]
+    for bit in range((groups - 1).bit_length()):
+        going = [d for d in range(groups) if d >> bit & 1]
+        packed = jnp.concatenate([blocks[d] for d in going], axis=0)
+        moved = shift(packed, 1 << bit)
+        for i, d in enumerate(going):
+            blocks[d] = moved[i * members : (i + 1) * members]
+
     def ratio_from(distance):
-        return shift(outgoing[-distance % groups], -distance)
+        return blocks[-distance % groups]
 
     gates, ups, downs = [w_gate[0]], [w_up[0]], [w_down[0]]
     for k in range(1, members):

time: 205 us -> 194 us (0.946)
  the two profiles are of different devices: /device:TPU:0 before, /device:TPU:15 now
where the time goes in v4:
time: 194 us; the launch traced here: 190 us
  waiting for transfers between devices  103 us (53%)
  starting transfers between devices  40.4 us (21%)
  matrix products  38.5 us (20%)
  other arithmetic  5.26 us (3%)
    ppermute x31, waiting for transfers between devices, shift(): return lax.ppermute(array, 'grp', at_distance(k))  103 us
    dot_general x26, matrix products, mm(): return lax.dot_general(a, b, dims, preferred_element_type=jnp.float32)  38.5 us
    ppermute x31, starting transfers between devices, shift(): return lax.ppermute(array, 'grp', at_distance(k))  25.4 us
    ppermute x6, starting transfers between devices, member_shift(): lax.ppermute(array, 'mem', [(m, (m + step) % members) for m in range(memb...  15 us
  transfers between devices with their start and end apart: 37, of which 13 were waited for; matrix products, arithmetic and copies ran while one was open for 20% of the time, Pallas kernels for 0%

profile of v4, /device:TPU:15, one launch (start us, length us, event | category | flops | bytes accessed | tf_op | source)
XLA Modules:
  0.0 190.3 jit_solution(14664716222364239092)
XLA Ops:
  4.3 1.2 collective-permute-start.4
  5.8 1.2 collective-permute-start.7
  7.0 1.3 collective-permute-start.1
  8.3 20.6 %collective-permute-done.1 = f32[8,128]{1,0:T(8,128)S(1)} collective-permute-done((f32[8,128]{1,0:T(8,128)S(1)}, f32[8,128]{1,0:T(8,128)S(1)}, u32[]{:S(2)}, u32[]{:S(2)}) %collective-permute-start.1) | collective-permute-done | bytes 4128 | tf_op jit(solution)/shard_map/ppermute | solution.py:114
  30.2 2.2 %collective-permute-done.2 = f32[8,128]{1,0:T(8,128)S(1)} collective-permute-done((f32[8,128]{1,0:T(8,128)S(1)}, f32[8,128]{1,0:T(8,128)S(1)}, u32[]{:S(2)}, u32[]{:S(2)}) %collective-permute-start.2) | collective-permute-done | bytes 4128 | tf_op jit(solution)/shard_map/ppermute | solution.py:114
  32.4 3.2 %collective-permute-start.5 = (bf16[384,2048]{1,0:T(8,128)(2,1)}, bf16[384,2048]{1,0:T(8,128)(2,1)S(1)}, u32[]{:S(2)}, u32[]{:S(2)}) collective-permute-start(bf16[384,2048]{1,0:T(8,128)(2,1)} %bitcast.73), channel_id=1, source_target_pairs={{0,1},{1,0},{2,3},{3,2},{4,5},{5,4},{6,7},{7,6},{8,9},{9,8},{10,11... | collective-permute-start | bytes 4718600 | tf_op jit(solution)/shard_map/ppermute | solution.py:117
  35.7 2.1 %collective-permute-start.12 = (bf16[128,2048]{1,0:T(8,128)(2,1)S(1)}, bf16[128,2048]{1,0:T(8,128)(2,1)S(1)}, u32[]{:S(2)}, u32[]{:S(2)}) collective-permute-start(bf16[128,2048]{1,0:T(8,128)(2,1)S(1)} %collective-permute-done.6), channel_id=1, source_target_pairs={{0,4},{4,8},{8,12},{12,14},{14,10},{10,6},{6,2},{2,0},{1,5},{5,9},... | collective-permute-start | bytes 1572872 | tf_op jit(solution)/shard_map/ppermute | solution.py:114
  38.1 1.3 collective-permute-start.13
  40.5 10.0 %collective-permute-done.12 = bf16[128,2048]{1,0:T(8,128)(2,1)S(1)} collective-permute-done((bf16[128,2048]{1,0:T(8,128)(2,1)S(1)}, bf16[128,2048]{1,0:T(8,128)(2,1)S(1)}, u32[]{:S(2)}, u32[]{:S(2)}) %collective-permute-start.12) | collective-permute-done | bytes 524320 | tf_op jit(solution)/shard_map/ppermute | solution.py:114
  51.5 1.3 collective-permute-start.16
  52.7 9.1 %collective-permute-done.10 = bf16[128,2048]{1,0:T(8,128)(2,1)S(1)} collective-permute-done((bf16[128,2048]{1,0:T(8,128)(2,1)S(1)}, bf16[128,2048]{1,0:T(8,128)(2,1)S(1)}, u32[]{:S(2)}, u32[]{:S(2)}) %collective-permute-start.10) | collective-permute-done | bytes 524320 | tf_op jit(solution)/shard_map/ppermute | solution.py:114
  63.9 20.4 %collective-permute-done.14 = bf16[128,2048]{1,0:T(8,128)(2,1)S(1)} collective-permute-done((bf16[128,2048]{1,0:T(8,128)(2,1)S(1)}, bf16[128,2048]{1,0:T(8,128)(2,1)S(1)}, u32[]{:S(2)}, u32[]{:S(2)}) %collective-permute-start.14) | collective-permute-done | bytes 524320 | tf_op jit(solution)/shard_map/ppermute | solution.py:114
  84.3 1.9 collective-permute-start.17
  87.3 9.9 %collective-permute-done.17 = bf16[128,2048]{1,0:T(8,128)(2,1)S(1)} collective-permute-done((bf16[128,2048]{1,0:T(8,128)(2,1)S(1)}, bf16[128,2048]{1,0:T(8,128)(2,1)S(1)}, u32[]{:S(2)}, u32[]{:S(2)}) %collective-permute-start.17) | collective-permute-done | bytes 524320 | tf_op jit(solution)/shard_map/ppermute | solution.py:114
  97.2 1.9 collective-permute-start.19
  101.9 1.2 fusion.19
  105.2 1.4 fusion.20
  108.6 1.4 fusion.21
  122.6 1.4 fusion.22
  124.2 1.8 convolution_convert_fusion
  126.0 3.8 %collective-permute-start.36 = (bf16[384,2048]{1,0:T(8,128)(2,1)S(1)}, bf16[384,2048]{1,0:T(8,128)(2,1)S(1)}, u32[]{:S(2)}, u32[]{:S(2)}) collective-permute-start(bf16[384,2048]{1,0:T(8,128)(2,1)S(1)} %convolution_convert_fusion), channel_id=1, source_target_pairs={{0,1},{1,0},{2,3},{3,2},{4,5},{5,4},{6,7},{7,6},{8,9},{9,8},{10,11... | collective-permute-start | bytes 4718600 | tf_op jit(solution)/shard_map/ppermute | solution.py:117
  132.7 2.4 %convolution_convert_fusion.1 = bf16[2048,384]{1,0:T(8,128)(2,1)S(1)} fusion(bf16[1024,2048]{1,0:T(8,128)(2,1)S(1)} %get-tuple-element.54, bf16[1024,768]{1,0:T(8,128)(2,1)S(1)} %pad_maximum_fusion.4), kind=kOutput, calls=%fused_computation.7 | convolution fusion | flops 1611399168 | bytes 6553600 | tf_op jit(solution)/shard_map/dot_general | solution.py:97
  135.5 4.4 %collective-permute-done.25 = bf16[64,2048]{1,0:T(8,128)(2,1)S(1)} collective-permute-done((bf16[64,2048]{1,0:T(8,128)(2,1)S(1)}, bf16[64,2048]{1,0:T(8,128)(2,1)S(1)}, u32[]{:S(2)}, u32[]{:S(2)}) %collective-permute-start.25) | collective-permute-done | bytes 262176 | tf_op jit(solution)/shard_map/ppermute | solution.py:114
  140.3 6.6 %collective-permute-done.20 = bf16[64,2048]{1,0:T(8,128)(2,1)S(1)} collective-permute-done((bf16[64,2048]{1,0:T(8,128)(2,1)S(1)}, bf16[64,2048]{1,0:T(8,128)(2,1)S(1)}, u32[]{:S(2)}, u32[]{:S(2)}) %collective-permute-start.20) | collective-permute-done | bytes 262176 | tf_op jit(solution)/shard_map/ppermute | solution.py:114
  149.0 4.0 %collective-permute-done.28 = bf16[64,2048]{1,0:T(8,128)(2,1)S(1)} collective-permute-done((bf16[64,2048]{1,0:T(8,128)(2,1)S(1)}, bf16[64,2048]{1,0:T(8,128)(2,1)S(1)}, u32[]{:S(2)}, u32[]{:S(2)}) %collective-permute-start.28) | collective-permute-done | bytes 262176 | tf_op jit(solution)/shard_map/ppermute | solution.py:114
  153.9 10.1 %collective-permute-done.31 = bf16[64,2048]{1,0:T(8,128)(2,1)S(1)} collective-permute-done((bf16[64,2048]{1,0:T(8,128)(2,1)S(1)}, bf16[64,2048]{1,0:T(8,128)(2,1)S(1)}, u32[]{:S(2)}, u32[]{:S(2)}) %collective-permute-start.31) | collective-permute-done | bytes 262176 | tf_op jit(solution)/shard_map/ppermute | solution.py:114
  164.3 4.9 %collective-permute-done.27 = bf16[64,2048]{1,0:T(8,128)(2,1)S(1)} collective-permute-done((bf16[64,2048]{1,0:T(8,128)(2,1)S(1)}, bf16[64,2048]{1,0:T(8,128)(2,1)S(1)}, u32[]{:S(2)}, u32[]{:S(2)}) %collective-permute-start.27) | collective-permute-done | bytes 262176 | tf_op jit(solution)/shard_map/ppermute | solution.py:114
  170.8 2.4 %convolution_convert_fusion.2 = bf16[2048,384]{1,0:T(8,128)(2,1)S(1)} fusion(bf16[1024,2048]{1,0:T(8,128)(2,1)S(1)} %get-tuple-element.54, bf16[1024,768]{1,0:T(8,128)(2,1)S(1)} %pad_maximum_fusion.3), kind=kOutput, calls=%fused_computation.8 | convolution fusion | flops 1611399168 | bytes 6553600 | tf_op jit(solution)/shard_map/dot_general | solution.py:97
  173.2 6.0 %collective-permute-start.34 = (bf16[2048,384]{1,0:T(8,128)(2,1)S(1)}, bf16[2048,384]{1,0:T(8,128)(2,1)S(1)}, u32[]{:S(2)}, u32[]{:S(2)}) collective-permute-start(bf16[2048,384]{1,0:T(8,128)(2,1)S(1)} %convolution_convert_fusion.2), channel_id=1, source_target_pairs={{0,1},{1,0},{2,3},{3,2},{4,5},{5,4},{6,7},{7,6},{8,9},{9,8},{10,11... | collective-permute-start | bytes 4718600 | tf_op jit(solution)/shard_map/ppermute | solution.py:117
  180.3 3.0 %fusion.6 = bf16[1,384,2048]{2,1,0:T(8,128)(2,1)} fusion(bf16[1024,2048]{1,0:T(8,128)(2,1)S(1)} %constant_dynamic-update-slice_fusion.16, bf16[384,2048]{1,0:T(8,128)(2,1)S(1)} %collective-permute-done.36, bf16[1024,768]{1,0:T(8,128)(2,1)S(1)} %pad_maximum_fusion.5), kind=kOutput, calls=%fused_computation.19 | convolution fusion | flops 1612972032 | bytes 8126464 | tf_op jit(solution)/shard_map/dot_general | solution.py:97
  183.2 3.5 %fusion.5 = bf16[1,2048,384]{2,1,0:T(8,128)(2,1)} fusion(bf16[1024,2048]{1,0:T(8,128)(2,1)S(1)} %get-tuple-element.54, bf16[2048,384]{1,0:T(8,128)(2,1)S(1)} %collective-permute-done.35, bf16[1024,768]{1,0:T(8,128)(2,1)S(1)} %pad_maximum_fusion.4), kind=kOutput, calls=%fused_computation.18 | convolution fusion | flops 1612972032 | bytes 8126464 | tf_op jit(solution)/shard_map/dot_general | solution.py:97
  186.8 3.5 %fusion.4 = bf16[1,2048,384]{2,1,0:T(8,128)(2,1)} fusion(bf16[1024,2048]{1,0:T(8,128)(2,1)S(1)} %get-tuple-element.54, bf16[2048,384]{1,0:T(8,128)(2,1)S(1)} %collective-permute-done.34, bf16[1024,768]{1,0:T(8,128)(2,1)S(1)} %pad_maximum_fusion.3), kind=kOutput, calls=%fused_computation.17 | convolution fusion | flops 1612972032 | bytes 8126464 | tf_op jit(solution)/shard_map/dot_general | solution.py:97
  (137 shorter events, 39.7 us)
Async XLA Ops:
  4.1 33.7 %collective-permute-start.3 = (bf16[128,2048]{1,0:T(8,128)(2,1)}, bf16[128,2048]{1,0:T(8,128)(2,1)S(1)}, u32[]{:S(2)}, u32[]{:S(2)}) collective-permute-start(bf16[128,2048]{1,0:T(8,128)(2,1)} %param.9), channel_id=1, source_target_pairs={{0,4},{4,8},{8,12},{12,14},{14,10},{10,6},{6,2},{2,0},{1,5},{5,9},... | collective-permute-start | bytes 1572872 | tf_op jit(solution)/shard_map/ppermute | solution.py:114
  4.3 35.1 %collective-permute-start.4 = (bf16[128,2048]{1,0:T(8,128)(2,1)}, bf16[128,2048]{1,0:T(8,128)(2,1)S(1)}, u32[]{:S(2)}, u32[]{:S(2)}) collective-permute-start(bf16[128,2048]{1,0:T(8,128)(2,1)} %param.9), channel_id=1, source_target_pairs={{0,2},{4,0},{8,4},{12,8},{14,12},{10,14},{6,10},{2,6},{1,3},{5,1},... | collective-permute-start | bytes 1572872 | tf_op jit(solution)/shard_map/ppermute | solution.py:114
  5.5 30.1 %collective-permute-start.6 = (bf16[128,2048]{1,0:T(8,128)(2,1)}, bf16[128,2048]{1,0:T(8,128)(2,1)S(1)}, u32[]{:S(2)}, u32[]{:S(2)}) collective-permute-start(bf16[128,2048]{1,0:T(8,128)(2,1)} %param.8), channel_id=1, source_target_pairs={{0,4},{4,8},{8,12},{12,14},{14,10},{10,6},{6,2},{2,0},{1,5},{5,9},... | collective-permute-start | bytes 1572872 | tf_op jit(solution)/shard_map/ppermute | solution.py:114
  5.8 32.3 %collective-permute-start.7 = (bf16[128,2048]{1,0:T(8,128)(2,1)}, bf16[128,2048]{1,0:T(8,128)(2,1)S(1)}, u32[]{:S(2)}, u32[]{:S(2)}) collective-permute-start(bf16[128,2048]{1,0:T(8,128)(2,1)} %param.8), channel_id=1, source_target_pairs={{0,2},{4,0},{8,4},{12,8},{14,12},{10,14},{6,10},{2,6},{1,3},{5,1},... | collective-permute-start | bytes 1572872 | tf_op jit(solution)/shard_map/ppermute | solution.py:114
  7.0 21.9 %collective-permute-start.1 = (f32[8,128]{1,0:T(8,128)S(1)}, f32[8,128]{1,0:T(8,128)S(1)}, u32[]{:S(2)}, u32[]{:S(2)}) collective-permute-start(f32[8,128]{1,0:T(8,128)S(1)} %pad_maximum_fusion.8), channel_id=1, source_target_pairs={{0,8},{4,12},{8,14},{12,10},{14,6},{10,2},{6,0},{2,4},{1,9},{5,13}... | collective-permute-start | bytes 12296 | tf_op jit(solution)/shard_map/ppermute | solution.py:114
  32.4 68.0 %collective-permute-start.5 = (bf16[384,2048]{1,0:T(8,128)(2,1)}, bf16[384,2048]{1,0:T(8,128)(2,1)S(1)}, u32[]{:S(2)}, u32[]{:S(2)}) collective-permute-start(bf16[384,2048]{1,0:T(8,128)(2,1)} %bitcast.73), channel_id=1, source_target_pairs={{0,1},{1,0},{2,3},{3,2},{4,5},{5,4},{6,7},{7,6},{8,9},{9,8},{10,11... | collective-permute-start | bytes 4718600 | tf_op jit(solution)/shard_map/ppermute | solution.py:117
  35.7 14.9 %collective-permute-start.12 = (bf16[128,2048]{1,0:T(8,128)(2,1)S(1)}, bf16[128,2048]{1,0:T(8,128)(2,1)S(1)}, u32[]{:S(2)}, u32[]{:S(2)}) collective-permute-start(bf16[128,2048]{1,0:T(8,128)(2,1)S(1)} %collective-permute-done.6), channel_id=1, source_target_pairs={{0,4},{4,8},{8,12},{12,14},{14,10},{10,6},{6,2},{2,0},{1,5},{5,9},... | collective-permute-start | bytes 1572872 | tf_op jit(solution)/shard_map/ppermute | solution.py:114
  37.7 24.1 %collective-permute-start.10 = (bf16[128,2048]{1,0:T(8,128)(2,1)S(1)}, bf16[128,2048]{1,0:T(8,128)(2,1)S(1)}, u32[]{:S(2)}, u32[]{:S(2)}) collective-permute-start(bf16[128,2048]{1,0:T(8,128)(2,1)S(1)} %collective-permute-done.3), channel_id=1, source_target_pairs={{0,4},{4,8},{8,12},{12,14},{14,10},{10,6},{6,2},{2,0},{1,5},{5,9},... | collective-permute-start | bytes 1572872 | tf_op jit(solution)/shard_map/ppermute | solution.py:114
  38.1 13.3 %collective-permute-start.13 = (bf16[128,2048]{1,0:T(8,128)(2,1)S(1)}, bf16[128,2048]{1,0:T(8,128)(2,1)S(1)}, u32[]{:S(2)}, u32[]{:S(2)}) collective-permute-start(bf16[128,2048]{1,0:T(8,128)(2,1)S(1)} %collective-permute-done.7), channel_id=1, source_target_pairs={{0,2},{4,0},{8,4},{12,8},{14,12},{10,14},{6,10},{2,6},{1,3},{5,1},... | collective-permute-start | bytes 1572872 | tf_op jit(solution)/shard_map/ppermute | solution.py:114
  39.4 23.1 %collective-permute-start.11 = (bf16[128,2048]{1,0:T(8,128)(2,1)S(1)}, bf16[128,2048]{1,0:T(8,128)(2,1)S(1)}, u32[]{:S(2)}, u32[]{:S(2)}) collective-permute-start(bf16[128,2048]{1,0:T(8,128)(2,1)S(1)} %collective-permute-done.4), channel_id=1, source_target_pairs={{0,2},{4,0},{8,4},{12,8},{14,12},{10,14},{6,10},{2,6},{1,3},{5,1},... | collective-permute-start | bytes 1572872 | tf_op jit(solution)/shard_map/ppermute | solution.py:114
  50.6 48.8 %collective-permute-start.9 = (bf16[2048,384]{1,0:T(8,128)(2,1)S(1)}, bf16[2048,384]{1,0:T(8,128)(2,1)S(1)}, u32[]{:S(2)}, u32[]{:S(2)}) collective-permute-start(bf16[2048,384]{1,0:T(8,128)(2,1)S(1)} %bitcast.87), channel_id=1, source_target_pairs={{0,1},{1,0},{2,3},{3,2},{4,5},{5,4},{6,7},{7,6},{8,9},{9,8},{10,11... | collective-permute-start | bytes 4718600 | tf_op jit(solution)/shard_map/ppermute | solution.py:117
  51.5 35.8 %collective-permute-start.16 = (bf16[128,2048]{1,0:T(8,128)(2,1)S(1)}, bf16[128,2048]{1,0:T(8,128)(2,1)S(1)}, u32[]{:S(2)}, u32[]{:S(2)}) collective-permute-start(bf16[128,2048]{1,0:T(8,128)(2,1)S(1)} %collective-permute-done.12), channel_id=1, source_target_pairs={{0,4},{4,8},{8,12},{12,14},{14,10},{10,6},{6,2},{2,0},{1,5},{5,9},... | collective-permute-start | bytes 1572872 | tf_op jit(solution)/shard_map/ppermute | solution.py:114
  61.8 22.5 %collective-permute-start.14 = (bf16[128,2048]{1,0:T(8,128)(2,1)S(1)}, bf16[128,2048]{1,0:T(8,128)(2,1)S(1)}, u32[]{:S(2)}, u32[]{:S(2)}) collective-permute-start(bf16[128,2048]{1,0:T(8,128)(2,1)S(1)} %collective-permute-done.10), channel_id=1, source_target_pairs={{0,4},{4,8},{8,12},{12,14},{14,10},{10,6},{6,2},{2,0},{1,5},{5,9},... | collective-permute-start | bytes 1572872 | tf_op jit(solution)/shard_map/ppermute | solution.py:114
  62.4 23.7 %collective-permute-start.15 = (bf16[128,2048]{1,0:T(8,128)(2,1)S(1)}, bf16[128,2048]{1,0:T(8,128)(2,1)S(1)}, u32[]{:S(2)}, u32[]{:S(2)}) collective-permute-start(bf16[128,2048]{1,0:T(8,128)(2,1)S(1)} %collective-permute-done.11), channel_id=1, source_target_pairs={{0,2},{4,0},{8,4},{12,8},{14,12},{10,14},{6,10},{2,6},{1,3},{5,1},... | collective-permute-start | bytes 1572872 | tf_op jit(solution)/shard_map/ppermute | solution.py:114
  84.3 12.9 %collective-permute-start.17 = (bf16[128,2048]{1,0:T(8,128)(2,1)S(1)}, bf16[128,2048]{1,0:T(8,128)(2,1)S(1)}, u32[]{:S(2)}, u32[]{:S(2)}) collective-permute-start(bf16[128,2048]{1,0:T(8,128)(2,1)S(1)} %collective-permute-done.13), channel_id=1, source_target_pairs={{0,2},{4,0},{8,4},{12,8},{14,12},{10,14},{6,10},{2,6},{1,3},{5,1},... | collective-permute-start | bytes 1572872 | tf_op jit(solution)/shard_map/ppermute | solution.py:114
  86.2 15.7 %collective-permute-start.8 = (bf16[2048,384]{1,0:T(8,128)(2,1)S(1)}, bf16[2048,384]{1,0:T(8,128)(2,1)S(1)}, u32[]{:S(2)}, u32[]{:S(2)}) collective-permute-start(bf16[2048,384]{1,0:T(8,128)(2,1)S(1)} %bitcast.78), channel_id=1, source_target_pairs={{0,1},{1,0},{2,3},{3,2},{4,5},{5,4},{6,7},{7,6},{8,9},{9,8},{10,11... | collective-permute-start | bytes 4718600 | tf_op jit(solution)/shard_map/ppermute | solution.py:117
  87.2 35.4 %collective-permute-start.18 = (bf16[128,2048]{1,0:T(8,128)(2,1)S(1)}, bf16[128,2048]{1,0:T(8,128)(2,1)S(1)}, u32[]{:S(2)}, u32[]{:S(2)}) collective-permute-start(bf16[128,2048]{1,0:T(8,128)(2,1)S(1)} %collective-permute-done.14), channel_id=1, source_target_pairs={{0,4},{4,8},{8,12},{12,14},{14,10},{10,6},{6,2},{2,0},{1,5},{5,9},... | collective-permute-start | bytes 1572872 | tf_op jit(solution)/shard_map/ppermute | solution.py:114
  97.2 23.3 %collective-permute-start.19 = (bf16[128,2048]{1,0:T(8,128)(2,1)S(1)}, bf16[128,2048]{1,0:T(8,128)(2,1)S(1)}, u32[]{:S(2)}, u32[]{:S(2)}) collective-permute-start(bf16[128,2048]{1,0:T(8,128)(2,1)S(1)} %collective-permute-done.17), channel_id=1, source_target_pairs={{0,2},{4,0},{8,4},{12,8},{14,12},{10,14},{6,10},{2,6},{1,3},{5,1},... | collective-permute-start | bytes 1572872 | tf_op jit(solution)/shard_map/ppermute | solution.py:114
  112.3 6.2 %collective-permute-start.21 = (bf16[64,2048]{1,0:T(8,128)(2,1)S(1)}, bf16[64,2048]{1,0:T(8,128)(2,1)S(1)}, u32[]{:S(2)}, u32[]{:S(2)}) collective-permute-start(bf16[64,2048]{1,0:T(8,128)(2,1)S(1)} %get-tuple-element.51), channel_id=1, source_target_pairs={{0,2},{4,0},{8,4},{12,8},{14,12},{10,14},{6,10},{2,6},{1,3},{5,1},... | collective-permute-start | bytes 786440 | tf_op jit(solution)/shard_map/ppermute | solution.py:114
  118.9 28.6 %collective-permute-start.24 = (bf16[64,2048]{1,0:T(8,128)(2,1)S(1)}, bf16[64,2048]{1,0:T(8,128)(2,1)S(1)}, u32[]{:S(2)}, u32[]{:S(2)}) collective-permute-start(bf16[64,2048]{1,0:T(8,128)(2,1)S(1)} %get-tuple-element.49), channel_id=1, source_target_pairs={{0,2},{4,0},{8,4},{12,8},{14,12},{10,14},{6,10},{2,6},{1,3},{5,1},... | collective-permute-start | bytes 786440 | tf_op jit(solution)/shard_map/ppermute | solution.py:114
  119.3 29.3 %collective-permute-start.26 = (bf16[64,2048]{1,0:T(8,128)(2,1)S(1)}, bf16[64,2048]{1,0:T(8,128)(2,1)S(1)}, u32[]{:S(2)}, u32[]{:S(2)}) collective-permute-start(bf16[64,2048]{1,0:T(8,128)(2,1)S(1)} %get-tuple-element.48), channel_id=1, source_target_pairs={{0,4},{4,8},{8,12},{12,14},{14,10},{10,6},{6,2},{2,0},{1,5},{5,9},... | collective-permute-start | bytes 786440 | tf_op jit(solution)/shard_map/ppermute | solution.py:114
  126.0 54.2 %collective-permute-start.36 = (bf16[384,2048]{1,0:T(8,128)(2,1)S(1)}, bf16[384,2048]{1,0:T(8,128)(2,1)S(1)}, u32[]{:S(2)}, u32[]{:S(2)}) collective-permute-start(bf16[384,2048]{1,0:T(8,128)(2,1)S(1)} %convolution_convert_fusion), channel_id=1, source_target_pairs={{0,1},{1,0},{2,3},{3,2},{4,5},{5,4},{6,7},{7,6},{8,9},{9,8},{10,11... | collective-permute-start | bytes 4718600 | tf_op jit(solution)/shard_map/ppermute | solution.py:117
  132.1 7.9 %collective-permute-start.25 = (bf16[64,2048]{1,0:T(8,128)(2,1)S(1)}, bf16[64,2048]{1,0:T(8,128)(2,1)S(1)}, u32[]{:S(2)}, u32[]{:S(2)}) collective-permute-start(bf16[64,2048]{1,0:T(8,128)(2,1)S(1)} %get-tuple-element.46), channel_id=1, source_target_pairs={{0,4},{4,8},{8,12},{12,14},{14,10},{10,6},{6,2},{2,0},{1,5},{5,9},... | collective-permute-start | bytes 786440 | tf_op jit(solution)/shard_map/ppermute | solution.py:114
  135.0 48.2 %collective-permute-start.35 = (bf16[2048,384]{1,0:T(8,128)(2,1)S(1)}, bf16[2048,384]{1,0:T(8,128)(2,1)S(1)}, u32[]{:S(2)}, u32[]{:S(2)}) collective-permute-start(bf16[2048,384]{1,0:T(8,128)(2,1)S(1)} %convolution_convert_fusion.1), channel_id=1, source_target_pairs={{0,1},{1,0},{2,3},{3,2},{4,5},{5,4},{6,7},{7,6},{8,9},{9,8},{10,11... | collective-permute-start | bytes 4718600 | tf_op jit(solution)/shard_map/ppermute | solution.py:117
  139.9 7.0 %collective-permute-start.20 = (bf16[64,2048]{1,0:T(8,128)(2,1)S(1)}, bf16[64,2048]{1,0:T(8,128)(2,1)S(1)}, u32[]{:S(2)}, u32[]{:S(2)}) collective-permute-start(bf16[64,2048]{1,0:T(8,128)(2,1)S(1)} %get-tuple-element.47), channel_id=1, source_target_pairs={{0,2},{4,0},{8,4},{12,8},{14,12},{10,14},{6,10},{2,6},{1,3},{5,1},... | collective-permute-start | bytes 786440 | tf_op jit(solution)/shard_map/ppermute | solution.py:114
  147.6 6.1 %collective-permute-start.23 = (bf16[64,2048]{1,0:T(8,128)(2,1)S(1)}, bf16[64,2048]{1,0:T(8,128)(2,1)S(1)}, u32[]{:S(2)}, u32[]{:S(2)}) collective-permute-start(bf16[64,2048]{1,0:T(8,128)(2,1)S(1)} %add_convert_fusion.12), channel_id=1, source_target_pairs={{0,2},{4,0},{8,4},{12,8},{14,12},{10,14},{6,10},{2,6},{1,3},{5,1},... | collective-permute-start | bytes 786440 | tf_op jit(solution)/shard_map/ppermute | solution.py:114
  148.6 21.2 %collective-permute-start.33 = (bf16[64,2048]{1,0:T(8,128)(2,1)S(1)}, bf16[64,2048]{1,0:T(8,128)(2,1)S(1)}, u32[]{:S(2)}, u32[]{:S(2)}) collective-permute-start(bf16[64,2048]{1,0:T(8,128)(2,1)S(1)} %add_convert_fusion.10), channel_id=1, source_target_pairs={{0,2},{4,0},{8,4},{12,8},{14,12},{10,14},{6,10},{2,6},{1,3},{5,1},... | collective-permute-start | bytes 786440 | tf_op jit(solution)/shard_map/ppermute | solution.py:114
  153.1 20.1 %collective-permute-start.30 = (bf16[64,2048]{1,0:T(8,128)(2,1)S(1)}, bf16[64,2048]{1,0:T(8,128)(2,1)S(1)}, u32[]{:S(2)}, u32[]{:S(2)}) collective-permute-start(bf16[64,2048]{1,0:T(8,128)(2,1)S(1)} %add_convert_fusion.9), channel_id=1, source_target_pairs={{0,4},{4,8},{8,12},{12,14},{14,10},{10,6},{6,2},{2,0},{1,5},{5,9},... | collective-permute-start | bytes 786440 | tf_op jit(solution)/shard_map/ppermute | solution.py:114
  153.7 10.2 %collective-permute-start.31 = (bf16[64,2048]{1,0:T(8,128)(2,1)S(1)}, bf16[64,2048]{1,0:T(8,128)(2,1)S(1)}, u32[]{:S(2)}, u32[]{:S(2)}) collective-permute-start(bf16[64,2048]{1,0:T(8,128)(2,1)S(1)} %add_convert_fusion.7), channel_id=1, source_target_pairs={{0,4},{4,8},{8,12},{12,14},{14,10},{10,6},{6,2},{2,0},{1,5},{5,9},... | collective-permute-start | bytes 786440 | tf_op jit(solution)/shard_map/ppermute | solution.py:114
  169.2 10.0 %collective-permute-start.32 = (bf16[64,2048]{1,0:T(8,128)(2,1)S(1)}, bf16[64,2048]{1,0:T(8,128)(2,1)S(1)}, u32[]{:S(2)}, u32[]{:S(2)}) collective-permute-start(bf16[64,2048]{1,0:T(8,128)(2,1)S(1)} %add_convert_fusion.4), channel_id=1, source_target_pairs={{0,4},{4,8},{8,12},{12,14},{14,10},{10,6},{6,2},{2,0},{1,5},{5,9},... | collective-permute-start | bytes 786440 | tf_op jit(solution)/shard_map/ppermute | solution.py:114
  169.8 9.3 %collective-permute-start.29 = (bf16[64,2048]{1,0:T(8,128)(2,1)S(1)}, bf16[64,2048]{1,0:T(8,128)(2,1)S(1)}, u32[]{:S(2)}, u32[]{:S(2)}) collective-permute-start(bf16[64,2048]{1,0:T(8,128)(2,1)S(1)} %add_convert_fusion.6), channel_id=1, source_target_pairs={{0,2},{4,0},{8,4},{12,8},{14,12},{10,14},{6,10},{2,6},{1,3},{5,1},... | collective-permute-start | bytes 786440 | tf_op jit(solution)/shard_map/ppermute | solution.py:114
  173.2 13.6 %collective-permute-start.34 = (bf16[2048,384]{1,0:T(8,128)(2,1)S(1)}, bf16[2048,384]{1,0:T(8,128)(2,1)S(1)}, u32[]{:S(2)}, u32[]{:S(2)}) collective-permute-start(bf16[2048,384]{1,0:T(8,128)(2,1)S(1)} %convolution_convert_fusion.2), channel_id=1, source_target_pairs={{0,1},{1,0},{2,3},{3,2},{4,5},{5,4},{6,7},{7,6},{8,9},{9,8},{10,11... | collective-permute-start | bytes 4718600 | tf_op jit(solution)/shard_map/ppermute | solution.py:117
  (10 other events, 180.8 us)

commit v5 on v4

--- a/solution.py
+++ b/solution.py
@@ -116,13 +116,19 @@
     def member_shift(array, step):
         return lax.ppermute(array, "mem", [(m, (m + step) % members) for m in range(members)])
 
+    half = tok_rows // 2
+    low, high = slice(0, half), slice(half, tok_rows)
+    rg, lx = output_grad, layer_input
+    rx = {high: layer_input[high], low: layer_input[low]}
+    lg = {low: output_grad[low], high: output_grad[high]}
     from_left, from_right = [], []
-    rx, rg, lx, lg = layer_input, output_grad, layer_input, output_grad
-    for _ in range(1, full_steps + 1):
+    for k in range(1, full_steps + 1):
         rg, lx = shift(rg, 1), shift(lx, -1)
-        rx, lg = shift(rx, 1), shift(lg, -1)
-        from_left.append((rx, rg))
-        from_right.append((lx, lg))
+        rx = {high: shift(rx[high], 1), low: shift(rx[low], 1)}
+        lg = {low: shift(lg[low], -1), high: shift(lg[high], -1)}
+        from_left.append((rx, {low: rg[low], high: rg[high]}))
+        from_right.append(({low: lx[low], high: lx[high]}, lg, lx))
+        from_left[-1] += (rg,)
     far = (shift(lx, -1), shift(rg, 1)) if has_far else None
 
     quotas = route_ints.astype(jnp.float32)
@@ -173,32 +179,45 @@
         part = mm(gg, gate_w, NT) + mm(ug, up_w, NT)
         return part, gg, ug, hidden
 
-    kept, part_left, part_right = [], [], []
-
-    def step_piece(steps, ratios):
-        x = jnp.concatenate([x for x, _ in steps], axis=0)
-        og = jnp.concatenate([og for _, og in steps], axis=0)
+    kept = []
+
+    def step_piece(xs, ogs, ratios, apart=False):
+        x, og = jnp.concatenate(xs, axis=0), jnp.concatenate(ogs, axis=0)
+        if apart:
+            x, og = lax.optimization_barrier((x, og))
         ratio = jnp.concatenate(ratios, axis=1).T
         if kept:
             ratio = lax.optimization_barrier((ratio, kept[-1][2]))[0]
         part, *rest = piece(x, og, ratio)
         kept.append((x, og, *rest))
-        part = part.astype(jnp.bfloat16)
-        return part[:tok_rows], part[tok_rows:]
-
-    for k in range(1, full_steps + 1):
-        ratio = [ratio_from(-k), ratio_from(k)]
-        parts = step_piece((from_left[k - 1], from_right[k - 1]), ratio)
-        part_left.append(parts[0])
-        part_right.append(parts[1])
-    half = tok_rows // 2
-    steps, ratio = [(layer_input, output_grad)], [outgoing[0]]
-    if has_far:
-        steps.append(far)
-        ratio.append(ratio_from(groups // 2))
-    own_part, far_part = step_piece(steps, ratio)
-
-    low, high = slice(0, half), slice(half, tok_rows)
+        return part.astype(jnp.bfloat16)
+
+    parts = {}
+    for k in range(1, full_steps):
+        lefts, rights = from_left[k - 1], from_right[k - 1]
+        xs = [lefts[0][low], lefts[0][high], rights[2]]
+        ogs = [lefts[2], rights[1][low], rights[1][high]]
+        part = step_piece(xs, ogs, [ratio_from(-k), ratio_from(k)])
+        parts[k] = [
+            {rows: part[at + rows.start : at + rows.stop] for rows in (low, high)}
+            for at in (0, tok_rows)
+        ]
+    own_and_far = [(layer_input, output_grad)] + [far] * has_far
+    ratio = [outgoing[0]] + [ratio_from(groups // 2)] * has_far
+    part = step_piece([x for x, _ in own_and_far], [og for _, og in own_and_far], ratio)
+    own_part, far_part = part[:tok_rows], part[tok_rows:]
+    if full_steps:
+        k = full_steps
+        lefts, rights = from_left[k - 1], from_right[k - 1]
+        parts[k] = [{}, {}]
+        for one, two in ((high, low), (low, high)):
+            part = step_piece(
+                [lefts[0][one], rights[0][two]],
+                [lefts[1][one], rights[1][two]],
+                [ratio_from(-k)[:, one], ratio_from(k)[:, two]],
+                apart=True,
+            )
+            parts[k][0][one], parts[k][1][two] = part[:half], part[half:]
 
     def join(moved, part):
         return (moved.astype(jnp.float32) + part.astype(jnp.float32)).astype(jnp.bfloat16)
@@ -207,27 +226,24 @@
         return shift(pair[0], -1), shift(pair[1], 1)
 
     def parts_at(k, rows):
-        return part_left[k - 1][rows[0]], part_right[k - 1][rows[1]]
+        return parts[k][0][rows[0]], parts[k][1][rows[1]]
 
     long_rows, short_rows = (low, high), (high, low)
-    long_way = short_way = None
-    if full_steps:
-        short_way = send(parts_at(full_steps, short_rows))
+    long_way = short_way = before = None
+
+    def gated(pair):
+        return pair if before is None else lax.optimization_barrier((pair, before))[0]
+
     if has_far:
         long_way = send((far_part[low], far_part[high]))
-    before = None
-
-    def gated(parts):
-        return parts if before is None else lax.optimization_barrier((parts, before))[0]
-
     for k in reversed(range(1, full_steps + 1)):
-        if k > 1:
-            sums = tuple(map(join, short_way, gated(parts_at(k - 1, short_rows))))
-            short_way, before = send(sums), sums
+        sums = parts_at(k, short_rows)
+        if short_way is not None:
+            sums = before = tuple(map(join, short_way, gated(sums)))
+        short_way = send(sums)
         sums = parts_at(k, long_rows)
         if long_way is not None:
-            sums = tuple(map(join, long_way, gated(sums)))
-            before = sums
+            sums = before = tuple(map(join, long_way, gated(sums)))
         long_way = send(sums)
     back_low = [long_way and long_way[0], short_way and short_way[1]]
     back_high = [long_way and long_way[1], short_way and short_way[0]]
@@ -245,19 +261,19 @@
         jnp.concatenate([k[i] for k in kept], axis=0) for i in range(5)
     )
 
-    def member_sum(product):
-        total = None
-        for k in reversed(range(members)):
-            columns = slice(k * width, (k + 1) * width)
-            block = product(columns)
-            if k:
-                block = member_shift(block.astype(jnp.bfloat16), k).astype(jnp.float32)
-            total = block if total is None else total + block
+    def member_sum(product, axis):
+        both = lax.optimization_barrier(product.astype(jnp.bfloat16))
+        blocks = jnp.split(both, members, axis=axis)
+        moved = [member_shift(blocks[k], k) for k in range(1, members)]
+        total = sum(block.astype(jnp.float32) for block in [blocks[0], *moved])
         return total.astype(jnp.bfloat16)[None]
 
-    gate_g = member_sum(lambda c: mm(x_all, gg_all[:, c], TN))
-    up_g = member_sum(lambda c: mm(x_all, ug_all[:, c], TN))
-    down_g = member_sum(lambda c: mm(hidden_all[:, c], og_all, TN))
+    gate_p = mm(x_all, gg_all, TN)
+    up_p = mm(x_all, ug_all, TN)
+    down_p = mm(hidden_all, og_all, TN)
+    gate_g = member_sum(gate_p, 1)
+    up_g = member_sum(up_p, 1)
+    down_g = member_sum(down_p, 0)
     return (input_grad, gate_g, up_g, down_g)
 
 

time: 194 us -> 193 us (level)
  waiting for transfers between devices: 103 us -> 87.2 us
  starting transfers between devices: 40.4 us -> 47.7 us
  other arithmetic: 5.26 us -> 9.93 us
  local copies, waits for them, and re-layouts: 1.86 us -> 5.52 us
    ppermute x31 -> x37, waiting for transfers between devices: 103 us -> 87.2 us  [shift(): return lax.ppermute(array, 'grp', at_distance(k))]
    ppermute x6, starting transfers between devices: 15 us -> 21 us  [member_shift(): lax.ppermute(array, 'mem', [(m, (m + step) % members) for m in range(memb...]
    broadcast_in_dim x0 -> x3, other arithmetic: none -> 4.82 us  [member_sum(): return total.astype(jnp.bfloat16)[None]]
    slice x3 -> x9, local copies, waits for them, and re-layouts: 0.19 us -> 2.7 us  [the longest x1 1.18 us: ring_plan(): lg = {low: output_grad[low], high: output_grad[high]}]
    ppermute x31 -> x37, starting transfers between devices: 25.4 us -> 26.7 us  [shift(): return lax.ppermute(array, 'grp', at_distance(k))]
    dot_general x26 -> x28, matrix products: 38.5 us -> 38.4 us  [mm(): return lax.dot_general(a, b, dims, preferred_element_type=jnp.float32)]
  transfers between devices with their start and end apart: 37 -> 43, of which waited for: 13 -> 18; matrix products, arithmetic and copies ran while one was open for 20% -> 25% of each run, Pallas kernels for 0% -> 0%
where the time goes in v5:
time: 193 us; the launch traced here: 190 us
  waiting for transfers between devices  87.2 us (45%)
  starting transfers between devices  47.7 us (25%)
  matrix products  38.4 us (20%)
  other arithmetic  9.93 us (5%)
  local copies, waits for them, and re-layouts  5.52 us (3%)
    ppermute x37, waiting for transfers between devices, shift(): return lax.ppermute(array, 'grp', at_distance(k))  87.2 us
    dot_general x28, matrix products, mm(): return lax.dot_general(a, b, dims, preferred_element_type=jnp.float32)  38.4 us
    ppermute x37, starting transfers between devices, shift(): return lax.ppermute(array, 'grp', at_distance(k))  26.7 us
    ppermute x6, starting transfers between devices, member_shift(): lax.ppermute(array, 'mem', [(m, (m + step) % members) for m in range(memb...  21 us
    broadcast_in_dim x3, other arithmetic, member_sum(): return total.astype(jnp.bfloat16)[None]  4.82 us
  transfers between devices with their start and end apart: 43, of which 18 were waited for; matrix products, arithmetic and copies ran while one was open for 25% of the time, Pallas kernels for 0%

profile of v5, /device:TPU:15, one launch (start us, length us, event | category | flops | bytes accessed | tf_op | source)
XLA Modules:
  0.0 190.2 jit_solution(2484523705092884779)
XLA Ops:
  9.3 4.5 %collective-permute-done = f32[8,128]{1,0:T(8,128)S(1)} collective-permute-done((f32[8,128]{1,0:T(8,128)S(1)}, f32[8,128]{1,0:T(8,128)S(1)}, u32[]{:S(2)}, u32[]{:S(2)}) %collective-permute-start) | collective-permute-done | bytes 4128 | tf_op jit(solution)/shard_map/ppermute | solution.py:114
  14.0 6.2 %collective-permute-done.1 = f32[8,128]{1,0:T(8,128)S(1)} collective-permute-done((f32[8,128]{1,0:T(8,128)S(1)}, f32[8,128]{1,0:T(8,128)S(1)}, u32[]{:S(2)}, u32[]{:S(2)}) %collective-permute-start.1) | collective-permute-done | bytes 4128 | tf_op jit(solution)/shard_map/ppermute | solution.py:114
  20.5 3.2 %collective-permute-done.2 = f32[8,128]{1,0:T(8,128)S(1)} collective-permute-done((f32[8,128]{1,0:T(8,128)S(1)}, f32[8,128]{1,0:T(8,128)S(1)}, u32[]{:S(2)}, u32[]{:S(2)}) %collective-permute-start.2) | collective-permute-done | bytes 4128 | tf_op jit(solution)/shard_map/ppermute | solution.py:114
  23.7 2.0 %collective-permute-start.8 = (bf16[64,2048]{1,0:T(8,128)(2,1)S(1)}, bf16[64,2048]{1,0:T(8,128)(2,1)S(1)}, u32[]{:S(2)}, u32[]{:S(2)}) collective-permute-start(bf16[64,2048]{1,0:T(8,128)(2,1)S(1)} %get-tuple-element.99), channel_id=1, source_target_pairs={{0,4},{4,8},{8,12},{12,14},{14,10},{10,6},{6,2},{2,0},{1,5},{5,9},... | collective-permute-start | bytes 786440 | tf_op jit(solution)/shard_map/ppermute | solution.py:114
  26.3 3.4 %collective-permute-done.8 = bf16[64,2048]{1,0:T(8,128)(2,1)S(1)} collective-permute-done((bf16[64,2048]{1,0:T(8,128)(2,1)S(1)}, bf16[64,2048]{1,0:T(8,128)(2,1)S(1)}, u32[]{:S(2)}, u32[]{:S(2)}) %collective-permute-start.8) | collective-permute-done | bytes 262176 | tf_op jit(solution)/shard_map/ppermute | solution.py:114
  29.7 4.0 %collective-permute-start.6 = (bf16[384,2048]{1,0:T(8,128)(2,1)}, bf16[384,2048]{1,0:T(8,128)(2,1)S(1)}, u32[]{:S(2)}, u32[]{:S(2)}) collective-permute-start(bf16[384,2048]{1,0:T(8,128)(2,1)} %bitcast.85), channel_id=1, source_target_pairs={{0,1},{1,0},{2,3},{3,2},{4,5},{5,4},{6,7},{7,6},{8,9},{9,8},{10,11... | collective-permute-start | bytes 4718600 | tf_op jit(solution)/shard_map/ppermute | solution.py:117
  33.7 1.4 collective-permute-start.15
  35.5 6.7 %collective-permute-done.15 = bf16[64,2048]{1,0:T(8,128)(2,1)S(1)} collective-permute-done((bf16[64,2048]{1,0:T(8,128)(2,1)S(1)}, bf16[64,2048]{1,0:T(8,128)(2,1)S(1)}, u32[]{:S(2)}, u32[]{:S(2)}) %collective-permute-start.15) | collective-permute-done | bytes 262176 | tf_op jit(solution)/shard_map/ppermute | solution.py:114
  43.0 4.8 %collective-permute-done.16 = bf16[64,2048]{1,0:T(8,128)(2,1)S(1)} collective-permute-done((bf16[64,2048]{1,0:T(8,128)(2,1)S(1)}, bf16[64,2048]{1,0:T(8,128)(2,1)S(1)}, u32[]{:S(2)}, u32[]{:S(2)}) %collective-permute-start.16) | collective-permute-done | bytes 262176 | tf_op jit(solution)/shard_map/ppermute | solution.py:114
  50.7 10.0 %collective-permute-done.12 = bf16[128,2048]{1,0:T(8,128)(2,1)S(1)} collective-permute-done((bf16[128,2048]{1,0:T(8,128)(2,1)S(1)}, bf16[128,2048]{1,0:T(8,128)(2,1)S(1)}, u32[]{:S(2)}, u32[]{:S(2)}) %collective-permute-start.12) | collective-permute-done | bytes 524320 | tf_op jit(solution)/shard_map/ppermute | solution.py:114
  60.7 1.4 collective-permute-start.11
  62.2 4.5 %collective-permute-done.13 = bf16[64,2048]{1,0:T(8,128)(2,1)S(1)} collective-permute-done((bf16[64,2048]{1,0:T(8,128)(2,1)S(1)}, bf16[64,2048]{1,0:T(8,128)(2,1)S(1)}, u32[]{:S(2)}, u32[]{:S(2)}) %collective-permute-start.13) | collective-permute-done | bytes 262176 | tf_op jit(solution)/shard_map/ppermute | solution.py:114
  68.7 3.8 %collective-permute-done.14 = bf16[64,2048]{1,0:T(8,128)(2,1)S(1)} collective-permute-done((bf16[64,2048]{1,0:T(8,128)(2,1)S(1)}, bf16[64,2048]{1,0:T(8,128)(2,1)S(1)}, u32[]{:S(2)}, u32[]{:S(2)}) %collective-permute-start.14) | collective-permute-done | bytes 262176 | tf_op jit(solution)/shard_map/ppermute | solution.py:114
  73.0 10.9 %collective-permute-done.20 = bf16[128,2048]{1,0:T(8,128)(2,1)S(1)} collective-permute-done((bf16[128,2048]{1,0:T(8,128)(2,1)S(1)}, bf16[128,2048]{1,0:T(8,128)(2,1)S(1)}, u32[]{:S(2)}, u32[]{:S(2)}) %collective-permute-start.20) | collective-permute-done | bytes 524320 | tf_op jit(solution)/shard_map/ppermute | solution.py:114
  85.4 3.8 %collective-permute-done.23 = bf16[64,2048]{1,0:T(8,128)(2,1)S(1)} collective-permute-done((bf16[64,2048]{1,0:T(8,128)(2,1)S(1)}, bf16[64,2048]{1,0:T(8,128)(2,1)S(1)}, u32[]{:S(2)}, u32[]{:S(2)}) %collective-permute-start.23) | collective-permute-done | bytes 262176 | tf_op jit(solution)/shard_map/ppermute | solution.py:114
  89.4 1.5 collective-permute-start.26
  90.9 4.2 %collective-permute-done.25 = bf16[64,2048]{1,0:T(8,128)(2,1)S(1)} collective-permute-done((bf16[64,2048]{1,0:T(8,128)(2,1)S(1)}, bf16[64,2048]{1,0:T(8,128)(2,1)S(1)}, u32[]{:S(2)}, u32[]{:S(2)}) %collective-permute-start.25) | collective-permute-done | bytes 262176 | tf_op jit(solution)/shard_map/ppermute | solution.py:114
  112.1 1.6 constant_dynamic-update-slice_fusion.20
  118.8 1.4 constant_dynamic-update-slice_fusion.19
  126.0 1.4 constant_dynamic-update-slice_fusion.18
  127.4 3.7 %convolution_convert_fusion.2 = bf16[2048,768]{1,0:T(8,128)(2,1)S(1)} fusion(bf16[1024,2048]{1,0:T(8,128)(2,1)S(1)} %constant_dynamic-update-slice_fusion.8, bf16[1024,768]{1,0:T(8,128)(2,1)S(1)} %get-tuple-element.46), kind=kOutput, calls=%fused_computation.2 | convolution fusion | flops 3222798336 | bytes 8912896 | tf_op jit(solution)/shard_map/dot_general | solution.py:97
  131.3 9.1 %collective-permute-start.40 = (bf16[2048,384]{1,0:T(8,128)(2,1)S(1)}, bf16[2048,384]{1,0:T(8,128)(2,1)S(1)}, u32[]{:S(2)}, u32[]{:S(2)}) collective-permute-start(bf16[2048,384]{1,0:T(8,128)(2,1)S(1)} %split.25), channel_id=1, source_target_pairs={{0,1},{1,0},{2,3},{3,2},{4,5},{5,4},{6,7},{7,6},{8,9},{9,8},{10,11... | collective-permute-start | bytes 4718600 | tf_op jit(solution)/shard_map/ppermute | solution.py:117
  140.4 3.7 %convolution_convert_fusion.1 = bf16[2048,768]{1,0:T(8,128)(2,1)S(1)} fusion(bf16[1024,2048]{1,0:T(8,128)(2,1)S(1)} %constant_dynamic-update-slice_fusion.8, bf16[1024,768]{1,0:T(8,128)(2,1)S(1)} %copy-done.8), kind=kOutput, calls=%fused_computation.1 | convolution fusion | flops 3222798336 | bytes 8912896 | tf_op jit(solution)/shard_map/dot_general | solution.py:97
  149.8 6.2 %collective-permute-done.27 = bf16[64,2048]{1,0:T(8,128)(2,1)S(1)} collective-permute-done((bf16[64,2048]{1,0:T(8,128)(2,1)S(1)}, bf16[64,2048]{1,0:T(8,128)(2,1)S(1)}, u32[]{:S(2)}, u32[]{:S(2)}) %collective-permute-start.27) | collective-permute-done | bytes 262176 | tf_op jit(solution)/shard_map/ppermute | solution.py:114
  157.7 4.6 %collective-permute-done.34 = bf16[64,2048]{1,0:T(8,128)(2,1)S(1)} collective-permute-done((bf16[64,2048]{1,0:T(8,128)(2,1)S(1)}, bf16[64,2048]{1,0:T(8,128)(2,1)S(1)}, u32[]{:S(2)}, u32[]{:S(2)}) %collective-permute-start.34) | collective-permute-done | bytes 262176 | tf_op jit(solution)/shard_map/ppermute | solution.py:114
  164.1 4.5 %collective-permute-done.31 = bf16[64,2048]{1,0:T(8,128)(2,1)S(1)} collective-permute-done((bf16[64,2048]{1,0:T(8,128)(2,1)S(1)}, bf16[64,2048]{1,0:T(8,128)(2,1)S(1)}, u32[]{:S(2)}, u32[]{:S(2)}) %collective-permute-start.31) | collective-permute-done | bytes 262176 | tf_op jit(solution)/shard_map/ppermute | solution.py:114
  168.6 5.4 %collective-permute-done.37 = bf16[64,2048]{1,0:T(8,128)(2,1)S(1)} collective-permute-done((bf16[64,2048]{1,0:T(8,128)(2,1)S(1)}, bf16[64,2048]{1,0:T(8,128)(2,1)S(1)}, u32[]{:S(2)}, u32[]{:S(2)}) %collective-permute-start.37) | collective-permute-done | bytes 262176 | tf_op jit(solution)/shard_map/ppermute | solution.py:114
  175.9 3.7 %convolution_convert_fusion = bf16[768,2048]{1,0:T(8,128)(2,1)S(1)} fusion(bf16[1024,768]{1,0:T(8,128)(2,1)S(1)} %get-tuple-element.77, bf16[1024,2048]{1,0:T(8,128)(2,1)S(1)} %constant_dynamic-update-slice_fusion.28), kind=kOutput, calls=%fused_computation | convolution fusion | flops 3222798336 | bytes 8912896 | tf_op jit(solution)/shard_map/dot_general | solution.py:97
  179.7 4.6 %collective-permute-start.42 = (bf16[384,2048]{1,0:T(8,128)(2,1)S(1)}, bf16[384,2048]{1,0:T(8,128)(2,1)S(1)}, u32[]{:S(2)}, u32[]{:S(2)}) collective-permute-start(bf16[384,2048]{1,0:T(8,128)(2,1)S(1)} %split.29), channel_id=1, source_target_pairs={{0,1},{1,0},{2,3},{3,2},{4,5},{5,4},{6,7},{7,6},{8,9},{9,8},{10,11... | collective-permute-start | bytes 4718600 | tf_op jit(solution)/shard_map/ppermute | solution.py:117
  185.4 1.5 fusion.5
  186.9 1.5 fusion.6
  188.5 1.7 fusion.7
  (177 shorter events, 57.9 us)
Async XLA Ops:
  0.6 34.6 %collective-permute-start.3 = (bf16[128,2048]{1,0:T(8,128)(2,1)}, bf16[128,2048]{1,0:T(8,128)(2,1)S(1)}, u32[]{:S(2)}, u32[]{:S(2)}) collective-permute-start(bf16[128,2048]{1,0:T(8,128)(2,1)} %param.9), channel_id=1, source_target_pairs={{0,4},{4,8},{8,12},{12,14},{14,10},{10,6},{6,2},{2,0},{1,5},{5,9},... | collective-permute-start | bytes 1572872 | tf_op jit(solution)/shard_map/ppermute | solution.py:114
  2.0 47.4 %collective-permute-start.5 = (bf16[64,2048]{1,0:T(8,128)(2,1)S(1)}, bf16[64,2048]{1,0:T(8,128)(2,1)S(1)}, u32[]{:S(2)}, u32[]{:S(2)}) collective-permute-start(bf16[64,2048]{1,0:T(8,128)(2,1)S(1)} %get-tuple-element.102), channel_id=1, source_target_pairs={{0,2},{4,0},{8,4},{12,8},{14,12},{10,14},{6,10},{2,6},{1,3},{5,1},... | collective-permute-start | bytes 786440 | tf_op jit(solution)/shard_map/ppermute | solution.py:114
  6.7 27.0 %collective-permute-start.9 = (bf16[128,2048]{1,0:T(8,128)(2,1)}, bf16[128,2048]{1,0:T(8,128)(2,1)S(1)}, u32[]{:S(2)}, u32[]{:S(2)}) collective-permute-start(bf16[128,2048]{1,0:T(8,128)(2,1)} %param.8), channel_id=1, source_target_pairs={{0,2},{4,0},{8,4},{12,8},{14,12},{10,14},{6,10},{2,6},{1,3},{5,1},... | collective-permute-start | bytes 1572872 | tf_op jit(solution)/shard_map/ppermute | solution.py:114
  9.1 16.8 %collective-permute-start.7 = (bf16[64,2048]{1,0:T(8,128)(2,1)S(1)}, bf16[64,2048]{1,0:T(8,128)(2,1)S(1)}, u32[]{:S(2)}, u32[]{:S(2)}) collective-permute-start(bf16[64,2048]{1,0:T(8,128)(2,1)S(1)} %get-tuple-element.100), channel_id=1, source_target_pairs={{0,4},{4,8},{8,12},{12,14},{14,10},{10,6},{6,2},{2,0},{1,5},{5,9},... | collective-permute-start | bytes 786440 | tf_op jit(solution)/shard_map/ppermute | solution.py:114
  25.9 22.8 %collective-permute-start.4 = (bf16[64,2048]{1,0:T(8,128)(2,1)S(1)}, bf16[64,2048]{1,0:T(8,128)(2,1)S(1)}, u32[]{:S(2)}, u32[]{:S(2)}) collective-permute-start(bf16[64,2048]{1,0:T(8,128)(2,1)S(1)} %get-tuple-element.101), channel_id=1, source_target_pairs={{0,2},{4,0},{8,4},{12,8},{14,12},{10,14},{6,10},{2,6},{1,3},{5,1},... | collective-permute-start | bytes 786440 | tf_op jit(solution)/shard_map/ppermute | solution.py:114
  29.7 68.6 %collective-permute-start.6 = (bf16[384,2048]{1,0:T(8,128)(2,1)}, bf16[384,2048]{1,0:T(8,128)(2,1)S(1)}, u32[]{:S(2)}, u32[]{:S(2)}) collective-permute-start(bf16[384,2048]{1,0:T(8,128)(2,1)} %bitcast.85), channel_id=1, source_target_pairs={{0,1},{1,0},{2,3},{3,2},{4,5},{5,4},{6,7},{7,6},{8,9},{9,8},{10,11... | collective-permute-start | bytes 4718600 | tf_op jit(solution)/shard_map/ppermute | solution.py:117
  33.7 8.5 %collective-permute-start.15 = (bf16[64,2048]{1,0:T(8,128)(2,1)S(1)}, bf16[64,2048]{1,0:T(8,128)(2,1)S(1)}, u32[]{:S(2)}, u32[]{:S(2)}) collective-permute-start(bf16[64,2048]{1,0:T(8,128)(2,1)S(1)} %collective-permute-done.7), channel_id=1, source_target_pairs={{0,4},{4,8},{8,12},{12,14},{14,10},{10,6},{6,2},{2,0},{1,5},{5,9},... | collective-permute-start | bytes 786440 | tf_op jit(solution)/shard_map/ppermute | solution.py:114
  35.3 12.6 %collective-permute-start.16 = (bf16[64,2048]{1,0:T(8,128)(2,1)S(1)}, bf16[64,2048]{1,0:T(8,128)(2,1)S(1)}, u32[]{:S(2)}, u32[]{:S(2)}) collective-permute-start(bf16[64,2048]{1,0:T(8,128)(2,1)S(1)} %collective-permute-done.8), channel_id=1, source_target_pairs={{0,4},{4,8},{8,12},{12,14},{14,10},{10,6},{6,2},{2,0},{1,5},{5,9},... | collective-permute-start | bytes 786440 | tf_op jit(solution)/shard_map/ppermute | solution.py:114
  42.2 55.1 %collective-permute-start.10 = (bf16[2048,384]{1,0:T(8,128)(2,1)S(1)}, bf16[2048,384]{1,0:T(8,128)(2,1)S(1)}, u32[]{:S(2)}, u32[]{:S(2)}) collective-permute-start(bf16[2048,384]{1,0:T(8,128)(2,1)S(1)} %bitcast.91), channel_id=1, source_target_pairs={{0,1},{1,0},{2,3},{3,2},{4,5},{5,4},{6,7},{7,6},{8,9},{9,8},{10,11... | collective-permute-start | bytes 4718600 | tf_op jit(solution)/shard_map/ppermute | solution.py:117
  47.8 12.9 %collective-permute-start.12 = (bf16[128,2048]{1,0:T(8,128)(2,1)S(1)}, bf16[128,2048]{1,0:T(8,128)(2,1)S(1)}, u32[]{:S(2)}, u32[]{:S(2)}) collective-permute-start(bf16[128,2048]{1,0:T(8,128)(2,1)S(1)} %collective-permute-done.3), channel_id=1, source_target_pairs={{0,4},{4,8},{8,12},{12,14},{14,10},{10,6},{6,2},{2,0},{1,5},{5,9},... | collective-permute-start | bytes 1572872 | tf_op jit(solution)/shard_map/ppermute | solution.py:114
  48.7 19.0 %collective-permute-start.17 = (bf16[128,2048]{1,0:T(8,128)(2,1)S(1)}, bf16[128,2048]{1,0:T(8,128)(2,1)S(1)}, u32[]{:S(2)}, u32[]{:S(2)}) collective-permute-start(bf16[128,2048]{1,0:T(8,128)(2,1)S(1)} %collective-permute-done.9), channel_id=1, source_target_pairs={{0,2},{4,0},{8,4},{12,8},{14,12},{10,14},{6,10},{2,6},{1,3},{5,1},... | collective-permute-start | bytes 1572872 | tf_op jit(solution)/shard_map/ppermute | solution.py:114
  49.5 17.2 %collective-permute-start.13 = (bf16[64,2048]{1,0:T(8,128)(2,1)S(1)}, bf16[64,2048]{1,0:T(8,128)(2,1)S(1)}, u32[]{:S(2)}, u32[]{:S(2)}) collective-permute-start(bf16[64,2048]{1,0:T(8,128)(2,1)S(1)} %collective-permute-done.4), channel_id=1, source_target_pairs={{0,2},{4,0},{8,4},{12,8},{14,12},{10,14},{6,10},{2,6},{1,3},{5,1},... | collective-permute-start | bytes 786440 | tf_op jit(solution)/shard_map/ppermute | solution.py:114
  60.7 39.0 %collective-permute-start.11 = (bf16[2048,384]{1,0:T(8,128)(2,1)S(1)}, bf16[2048,384]{1,0:T(8,128)(2,1)S(1)}, u32[]{:S(2)}, u32[]{:S(2)}) collective-permute-start(bf16[2048,384]{1,0:T(8,128)(2,1)S(1)} %bitcast.102), channel_id=1, source_target_pairs={{0,1},{1,0},{2,3},{3,2},{4,5},{5,4},{6,7},{7,6},{8,9},{9,8},{10,11... | collective-permute-start | bytes 4718600 | tf_op jit(solution)/shard_map/ppermute | solution.py:117
  67.7 16.1 %collective-permute-start.20 = (bf16[128,2048]{1,0:T(8,128)(2,1)S(1)}, bf16[128,2048]{1,0:T(8,128)(2,1)S(1)}, u32[]{:S(2)}, u32[]{:S(2)}) collective-permute-start(bf16[128,2048]{1,0:T(8,128)(2,1)S(1)} %collective-permute-done.17), channel_id=1, source_target_pairs={{0,2},{4,0},{8,4},{12,8},{14,12},{10,14},{6,10},{2,6},{1,3},{5,1},... | collective-permute-start | bytes 1572872 | tf_op jit(solution)/shard_map/ppermute | solution.py:114
  72.6 11.5 %collective-permute-start.18 = (bf16[128,2048]{1,0:T(8,128)(2,1)S(1)}, bf16[128,2048]{1,0:T(8,128)(2,1)S(1)}, u32[]{:S(2)}, u32[]{:S(2)}) collective-permute-start(bf16[128,2048]{1,0:T(8,128)(2,1)S(1)} %collective-permute-done.12), channel_id=1, source_target_pairs={{0,4},{4,8},{8,12},{12,14},{14,10},{10,6},{6,2},{2,0},{1,5},{5,9},... | collective-permute-start | bytes 1572872 | tf_op jit(solution)/shard_map/ppermute | solution.py:114
  95.8 14.2 %collective-permute-start.21 = (bf16[128,2048]{1,0:T(8,128)(2,1)S(1)}, bf16[128,2048]{1,0:T(8,128)(2,1)S(1)}, u32[]{:S(2)}, u32[]{:S(2)}) collective-permute-start(bf16[128,2048]{1,0:T(8,128)(2,1)S(1)} %collective-permute-done.20), channel_id=1, source_target_pairs={{0,2},{4,0},{8,4},{12,8},{14,12},{10,14},{6,10},{2,6},{1,3},{5,1},... | collective-permute-start | bytes 1572872 | tf_op jit(solution)/shard_map/ppermute | solution.py:114
  97.1 15.0 %collective-permute-start.19 = (bf16[128,2048]{1,0:T(8,128)(2,1)S(1)}, bf16[128,2048]{1,0:T(8,128)(2,1)S(1)}, u32[]{:S(2)}, u32[]{:S(2)}) collective-permute-start(bf16[128,2048]{1,0:T(8,128)(2,1)S(1)} %collective-permute-done.18), channel_id=1, source_target_pairs={{0,4},{4,8},{8,12},{12,14},{14,10},{10,6},{6,2},{2,0},{1,5},{5,9},... | collective-permute-start | bytes 1572872 | tf_op jit(solution)/shard_map/ppermute | solution.py:114
  116.4 30.3 %collective-permute-start.29 = (bf16[64,2048]{1,0:T(8,128)(2,1)S(1)}, bf16[64,2048]{1,0:T(8,128)(2,1)S(1)}, u32[]{:S(2)}, u32[]{:S(2)}) collective-permute-start(bf16[64,2048]{1,0:T(8,128)(2,1)S(1)} %get-tuple-element.71), channel_id=1, source_target_pairs={{0,4},{4,8},{8,12},{12,14},{14,10},{10,6},{6,2},{2,0},{1,5},{5,9},... | collective-permute-start | bytes 786440 | tf_op jit(solution)/shard_map/ppermute | solution.py:114
  120.2 27.7 %collective-permute-start.22 = (bf16[64,2048]{1,0:T(8,128)(2,1)S(1)}, bf16[64,2048]{1,0:T(8,128)(2,1)S(1)}, u32[]{:S(2)}, u32[]{:S(2)}) collective-permute-start(bf16[64,2048]{1,0:T(8,128)(2,1)S(1)} %get-tuple-element.72), channel_id=1, source_target_pairs={{0,2},{4,0},{8,4},{12,8},{14,12},{10,14},{6,10},{2,6},{1,3},{5,1},... | collective-permute-start | bytes 786440 | tf_op jit(solution)/shard_map/ppermute | solution.py:114
  123.1 26.6 %collective-permute-start.28 = (bf16[64,2048]{1,0:T(8,128)(2,1)S(1)}, bf16[64,2048]{1,0:T(8,128)(2,1)S(1)}, u32[]{:S(2)}, u32[]{:S(2)}) collective-permute-start(bf16[64,2048]{1,0:T(8,128)(2,1)S(1)} %get-tuple-element.92), channel_id=1, source_target_pairs={{0,2},{4,0},{8,4},{12,8},{14,12},{10,14},{6,10},{2,6},{1,3},{5,1},... | collective-permute-start | bytes 786440 | tf_op jit(solution)/shard_map/ppermute | solution.py:114
  124.4 24.7 %collective-permute-start.30 = (bf16[64,2048]{1,0:T(8,128)(2,1)S(1)}, bf16[64,2048]{1,0:T(8,128)(2,1)S(1)}, u32[]{:S(2)}, u32[]{:S(2)}) collective-permute-start(bf16[64,2048]{1,0:T(8,128)(2,1)S(1)} %get-tuple-element.91), channel_id=1, source_target_pairs={{0,4},{4,8},{8,12},{12,14},{14,10},{10,6},{6,2},{2,0},{1,5},{5,9},... | collective-permute-start | bytes 786440 | tf_op jit(solution)/shard_map/ppermute | solution.py:114
  131.3 54.1 %collective-permute-start.40 = (bf16[2048,384]{1,0:T(8,128)(2,1)S(1)}, bf16[2048,384]{1,0:T(8,128)(2,1)S(1)}, u32[]{:S(2)}, u32[]{:S(2)}) collective-permute-start(bf16[2048,384]{1,0:T(8,128)(2,1)S(1)} %split.25), channel_id=1, source_target_pairs={{0,1},{1,0},{2,3},{3,2},{4,5},{5,4},{6,7},{7,6},{8,9},{9,8},{10,11... | collective-permute-start | bytes 4718600 | tf_op jit(solution)/shard_map/ppermute | solution.py:117
  146.7 40.2 %collective-permute-start.41 = (bf16[2048,384]{1,0:T(8,128)(2,1)S(1)}, bf16[2048,384]{1,0:T(8,128)(2,1)S(1)}, u32[]{:S(2)}, u32[]{:S(2)}) collective-permute-start(bf16[2048,384]{1,0:T(8,128)(2,1)S(1)} %split.27), channel_id=1, source_target_pairs={{0,1},{1,0},{2,3},{3,2},{4,5},{5,4},{6,7},{7,6},{8,9},{9,8},{10,11... | collective-permute-start | bytes 4718600 | tf_op jit(solution)/shard_map/ppermute | solution.py:117
  148.1 7.9 %collective-permute-start.27 = (bf16[64,2048]{1,0:T(8,128)(2,1)S(1)}, bf16[64,2048]{1,0:T(8,128)(2,1)S(1)}, u32[]{:S(2)}, u32[]{:S(2)}) collective-permute-start(bf16[64,2048]{1,0:T(8,128)(2,1)S(1)} %get-tuple-element.94), channel_id=1, source_target_pairs={{0,2},{4,0},{8,4},{12,8},{14,12},{10,14},{6,10},{2,6},{1,3},{5,1},... | collective-permute-start | bytes 786440 | tf_op jit(solution)/shard_map/ppermute | solution.py:114
  149.1 7.9 %collective-permute-start.33 = (bf16[64,2048]{1,0:T(8,128)(2,1)S(1)}, bf16[64,2048]{1,0:T(8,128)(2,1)S(1)}, u32[]{:S(2)}, u32[]{:S(2)}) collective-permute-start(bf16[64,2048]{1,0:T(8,128)(2,1)S(1)} %get-tuple-element.93), channel_id=1, source_target_pairs={{0,4},{4,8},{8,12},{12,14},{14,10},{10,6},{6,2},{2,0},{1,5},{5,9},... | collective-permute-start | bytes 786440 | tf_op jit(solution)/shard_map/ppermute | solution.py:114
  149.7 12.7 %collective-permute-start.34 = (bf16[64,2048]{1,0:T(8,128)(2,1)S(1)}, bf16[64,2048]{1,0:T(8,128)(2,1)S(1)}, u32[]{:S(2)}, u32[]{:S(2)}) collective-permute-start(bf16[64,2048]{1,0:T(8,128)(2,1)S(1)} %add_convert_fusion.11), channel_id=1, source_target_pairs={{0,4},{4,8},{8,12},{12,14},{14,10},{10,6},{6,2},{2,0},{1,5},{5,9},... | collective-permute-start | bytes 786440 | tf_op jit(solution)/shard_map/ppermute | solution.py:114
  157.1 11.5 %collective-permute-start.31 = (bf16[64,2048]{1,0:T(8,128)(2,1)S(1)}, bf16[64,2048]{1,0:T(8,128)(2,1)S(1)}, u32[]{:S(2)}, u32[]{:S(2)}) collective-permute-start(bf16[64,2048]{1,0:T(8,128)(2,1)S(1)} %add_convert_fusion.10), channel_id=1, source_target_pairs={{0,2},{4,0},{8,4},{12,8},{14,12},{10,14},{6,10},{2,6},{1,3},{5,1},... | collective-permute-start | bytes 786440 | tf_op jit(solution)/shard_map/ppermute | solution.py:114
  162.4 12.8 %collective-permute-start.36 = (bf16[64,2048]{1,0:T(8,128)(2,1)S(1)}, bf16[64,2048]{1,0:T(8,128)(2,1)S(1)}, u32[]{:S(2)}, u32[]{:S(2)}) collective-permute-start(bf16[64,2048]{1,0:T(8,128)(2,1)S(1)} %add_convert_fusion.7), channel_id=1, source_target_pairs={{0,4},{4,8},{8,12},{12,14},{14,10},{10,6},{6,2},{2,0},{1,5},{5,9},... | collective-permute-start | bytes 786440 | tf_op jit(solution)/shard_map/ppermute | solution.py:114
  163.0 16.7 %collective-permute-start.39 = (bf16[64,2048]{1,0:T(8,128)(2,1)S(1)}, bf16[64,2048]{1,0:T(8,128)(2,1)S(1)}, u32[]{:S(2)}, u32[]{:S(2)}) collective-permute-start(bf16[64,2048]{1,0:T(8,128)(2,1)S(1)} %add_convert_fusion.8), channel_id=1, source_target_pairs={{0,2},{4,0},{8,4},{12,8},{14,12},{10,14},{6,10},{2,6},{1,3},{5,1},... | collective-permute-start | bytes 786440 | tf_op jit(solution)/shard_map/ppermute | solution.py:114
  174.1 10.2 %collective-permute-start.35 = (bf16[64,2048]{1,0:T(8,128)(2,1)S(1)}, bf16[64,2048]{1,0:T(8,128)(2,1)S(1)}, u32[]{:S(2)}, u32[]{:S(2)}) collective-permute-start(bf16[64,2048]{1,0:T(8,128)(2,1)S(1)} %add_convert_fusion.6), channel_id=1, source_target_pairs={{0,2},{4,0},{8,4},{12,8},{14,12},{10,14},{6,10},{2,6},{1,3},{5,1},... | collective-permute-start | bytes 786440 | tf_op jit(solution)/shard_map/ppermute | solution.py:114
  175.2 9.1 %collective-permute-start.38 = (bf16[64,2048]{1,0:T(8,128)(2,1)S(1)}, bf16[64,2048]{1,0:T(8,128)(2,1)S(1)}, u32[]{:S(2)}, u32[]{:S(2)}) collective-permute-start(bf16[64,2048]{1,0:T(8,128)(2,1)S(1)} %add_convert_fusion.4), channel_id=1, source_target_pairs={{0,4},{4,8},{8,12},{12,14},{14,10},{10,6},{6,2},{2,0},{1,5},{5,9},... | collective-permute-start | bytes 786440 | tf_op jit(solution)/shard_map/ppermute | solution.py:114
  179.7 8.7 %collective-permute-start.42 = (bf16[384,2048]{1,0:T(8,128)(2,1)S(1)}, bf16[384,2048]{1,0:T(8,128)(2,1)S(1)}, u32[]{:S(2)}, u32[]{:S(2)}) collective-permute-start(bf16[384,2048]{1,0:T(8,128)(2,1)S(1)} %split.29), channel_id=1, source_target_pairs={{0,1},{1,0},{2,3},{3,2},{4,5},{5,4},{6,7},{7,6},{8,9},{9,8},{10,11... | collective-permute-start | bytes 4718600 | tf_op jit(solution)/shard_map/ppermute | solution.py:117
  (20 other events, 209.5 us)

commit v6 on v5

--- a/solution.py
+++ b/solution.py
@@ -100,7 +100,7 @@
 def ring_plan(layer_input, output_grad, expert_ids, route_ints, w_gate, w_up, w_down):
     groups = lax.axis_size("grp")
     members = lax.axis_size("mem")
-    tok_rows, _ = layer_input.shape
+    tok_rows, model_width = layer_input.shape
     width = w_gate.shape[2]
     span = members * width
     order = ring_order(groups)
@@ -197,25 +197,28 @@
         lefts, rights = from_left[k - 1], from_right[k - 1]
         xs = [lefts[0][low], lefts[0][high], rights[2]]
         ogs = [lefts[2], rights[1][low], rights[1][high]]
-        part = step_piece(xs, ogs, [ratio_from(-k), ratio_from(k)])
+        ratio = [ratio_from(-k), ratio_from(k)]
+        if k == 1:
+            xs, ogs, ratio = xs + [layer_input], ogs + [output_grad], ratio + [outgoing[0]]
+        part = step_piece(xs, ogs, ratio)
         parts[k] = [
             {rows: part[at + rows.start : at + rows.stop] for rows in (low, high)}
             for at in (0, tok_rows)
         ]
-    own_and_far = [(layer_input, output_grad)] + [far] * has_far
-    ratio = [outgoing[0]] + [ratio_from(groups // 2)] * has_far
-    part = step_piece([x for x, _ in own_and_far], [og for _, og in own_and_far], ratio)
-    own_part, far_part = part[:tok_rows], part[tok_rows:]
+        if k == 1:
+            own_part = part[2 * tok_rows :]
+    if full_steps < 2:
+        own_part = step_piece([layer_input], [output_grad], [outgoing[0]])
+    if has_far:
+        far_part = step_piece([far[0]], [far[1]], [ratio_from(groups // 2)])
     if full_steps:
         k = full_steps
         lefts, rights = from_left[k - 1], from_right[k - 1]
         parts[k] = [{}, {}]
         for one, two in ((high, low), (low, high)):
+            ratio = [ratio_from(-k)[:, one], ratio_from(k)[:, two]]
             part = step_piece(
-                [lefts[0][one], rights[0][two]],
-                [lefts[1][one], rights[1][two]],
-                [ratio_from(-k)[:, one], ratio_from(k)[:, two]],
-                apart=True,
+                [lefts[0][one], rights[0][two]], [lefts[1][one], rights[1][two]], ratio, apart=True
             )
             parts[k][0][one], parts[k][1][two] = part[:half], part[half:]
 
@@ -255,7 +258,9 @@
                 total = total + piece_back.astype(jnp.float32)
         return total.astype(jnp.bfloat16)
 
-    input_grad = jnp.concatenate([closing(low, back_low), closing(high, back_high)], axis=0)
+    input_grad = jnp.zeros((tok_rows, model_width), jnp.bfloat16)
+    input_grad = lax.dynamic_update_slice(input_grad, closing(low, back_low), (0, 0))
+    input_grad = lax.dynamic_update_slice(input_grad, closing(high, back_high), (half, 0))
 
     x_all, og_all, gg_all, ug_all, hidden_all = (
         jnp.concatenate([k[i] for k in kept], axis=0) for i in range(5)

time: 193 us -> 191 us (0.990)
  waiting for transfers between devices: 87.2 us -> 79.4 us
  matrix products: 38.4 us -> 42.7 us
    ppermute x37, waiting for transfers between devices: 87.2 us -> 79.4 us  [shift(): return lax.ppermute(array, 'grp', at_distance(k))]
    dot_general x28, matrix products: 38.4 us -> 42.7 us  [mm(): return lax.dot_general(a, b, dims, preferred_element_type=jnp.float32)]
    ppermute x37, starting transfers between devices: 26.7 us -> 29.9 us  [shift(): return lax.ppermute(array, 'grp', at_distance(k))]
    ppermute x6, starting transfers between devices: 21 us -> 18.1 us  [member_shift(): lax.ppermute(array, 'mem', [(m, (m + step) % members) for m in range(memb...]
  transfers between devices with their start and end apart: 43 -> 43, of which waited for: 18 -> 18; matrix products, arithmetic and copies ran while one was open for 25% -> 27% of each run, Pallas kernels for 0% -> 0%
where the time goes in v6:
time: 191 us; the launch traced here: 187 us
  waiting for transfers between devices  79.4 us (42%)
  starting transfers between devices  48 us (25%)
  matrix products  42.7 us (22%)
  other arithmetic  9.93 us (5%)
  local copies, waits for them, and re-layouts  5.79 us (3%)
    ppermute x37, waiting for transfers between devices, shift(): return lax.ppermute(array, 'grp', at_distance(k))  79.4 us
    dot_general x28, matrix products, mm(): return lax.dot_general(a, b, dims, preferred_element_type=jnp.float32)  42.7 us
    ppermute x37, starting transfers between devices, shift(): return lax.ppermute(array, 'grp', at_distance(k))  29.9 us
    ppermute x6, starting transfers between devices, member_shift(): lax.ppermute(array, 'mem', [(m, (m + step) % members) for m in range(memb...  18.1 us
    broadcast_in_dim x3, other arithmetic, member_sum(): return total.astype(jnp.bfloat16)[None]  4.82 us
  transfers between devices with their start and end apart: 43, of which 18 were waited for; matrix products, arithmetic and copies ran while one was open for 27% of the time, Pallas kernels for 0%

profile of v6, /device:TPU:15, one launch (start us, length us, event | category | flops | bytes accessed | tf_op | source)
XLA Modules:
  0.0 187.3 jit_solution(13612898092245400119)
XLA Ops:
  9.3 4.5 %collective-permute-done = f32[8,128]{1,0:T(8,128)S(1)} collective-permute-done((f32[8,128]{1,0:T(8,128)S(1)}, f32[8,128]{1,0:T(8,128)S(1)}, u32[]{:S(2)}, u32[]{:S(2)}) %collective-permute-start) | collective-permute-done | bytes 4128 | tf_op jit(solution)/shard_map/ppermute | solution.py:114
  14.0 6.2 %collective-permute-done.1 = f32[8,128]{1,0:T(8,128)S(1)} collective-permute-done((f32[8,128]{1,0:T(8,128)S(1)}, f32[8,128]{1,0:T(8,128)S(1)}, u32[]{:S(2)}, u32[]{:S(2)}) %collective-permute-start.1) | collective-permute-done | bytes 4128 | tf_op jit(solution)/shard_map/ppermute | solution.py:114
  20.5 3.2 %collective-permute-done.2 = f32[8,128]{1,0:T(8,128)S(1)} collective-permute-done((f32[8,128]{1,0:T(8,128)S(1)}, f32[8,128]{1,0:T(8,128)S(1)}, u32[]{:S(2)}, u32[]{:S(2)}) %collective-permute-start.2) | collective-permute-done | bytes 4128 | tf_op jit(solution)/shard_map/ppermute | solution.py:114
  23.7 2.0 %collective-permute-start.8 = (bf16[64,2048]{1,0:T(8,128)(2,1)S(1)}, bf16[64,2048]{1,0:T(8,128)(2,1)S(1)}, u32[]{:S(2)}, u32[]{:S(2)}) collective-permute-start(bf16[64,2048]{1,0:T(8,128)(2,1)S(1)} %get-tuple-element.99), channel_id=1, source_target_pairs={{0,4},{4,8},{8,12},{12,14},{14,10},{10,6},{6,2},{2,0},{1,5},{5,9},... | collective-permute-start | bytes 786440 | tf_op jit(solution)/shard_map/ppermute | solution.py:114
  26.3 3.4 %collective-permute-done.8 = bf16[64,2048]{1,0:T(8,128)(2,1)S(1)} collective-permute-done((bf16[64,2048]{1,0:T(8,128)(2,1)S(1)}, bf16[64,2048]{1,0:T(8,128)(2,1)S(1)}, u32[]{:S(2)}, u32[]{:S(2)}) %collective-permute-start.8) | collective-permute-done | bytes 262176 | tf_op jit(solution)/shard_map/ppermute | solution.py:114
  29.7 4.0 %collective-permute-start.6 = (bf16[384,2048]{1,0:T(8,128)(2,1)}, bf16[384,2048]{1,0:T(8,128)(2,1)S(1)}, u32[]{:S(2)}, u32[]{:S(2)}) collective-permute-start(bf16[384,2048]{1,0:T(8,128)(2,1)} %bitcast.88), channel_id=1, source_target_pairs={{0,1},{1,0},{2,3},{3,2},{4,5},{5,4},{6,7},{7,6},{8,9},{9,8},{10,11... | collective-permute-start | bytes 4718600 | tf_op jit(solution)/shard_map/ppermute | solution.py:117
  36.5 5.4 %collective-permute-done.15 = bf16[64,2048]{1,0:T(8,128)(2,1)S(1)} collective-permute-done((bf16[64,2048]{1,0:T(8,128)(2,1)S(1)}, bf16[64,2048]{1,0:T(8,128)(2,1)S(1)}, u32[]{:S(2)}, u32[]{:S(2)}) %collective-permute-start.15) | collective-permute-done | bytes 262176 | tf_op jit(solution)/shard_map/ppermute | solution.py:114
  43.1 4.4 %collective-permute-done.16 = bf16[64,2048]{1,0:T(8,128)(2,1)S(1)} collective-permute-done((bf16[64,2048]{1,0:T(8,128)(2,1)S(1)}, bf16[64,2048]{1,0:T(8,128)(2,1)S(1)}, u32[]{:S(2)}, u32[]{:S(2)}) %collective-permute-start.16) | collective-permute-done | bytes 262176 | tf_op jit(solution)/shard_map/ppermute | solution.py:114
  48.7 10.0 %collective-permute-done.12 = bf16[128,2048]{1,0:T(8,128)(2,1)S(1)} collective-permute-done((bf16[128,2048]{1,0:T(8,128)(2,1)S(1)}, bf16[128,2048]{1,0:T(8,128)(2,1)S(1)}, u32[]{:S(2)}, u32[]{:S(2)}) %collective-permute-start.12) | collective-permute-done | bytes 524320 | tf_op jit(solution)/shard_map/ppermute | solution.py:114
  59.9 1.5 collective-permute-start.14
  62.6 3.2 %collective-permute-done.14 = bf16[64,2048]{1,0:T(8,128)(2,1)S(1)} collective-permute-done((bf16[64,2048]{1,0:T(8,128)(2,1)S(1)}, bf16[64,2048]{1,0:T(8,128)(2,1)S(1)}, u32[]{:S(2)}, u32[]{:S(2)}) %collective-permute-start.14) | collective-permute-done | bytes 262176 | tf_op jit(solution)/shard_map/ppermute | solution.py:114
  67.2 9.9 %collective-permute-done.20 = bf16[128,2048]{1,0:T(8,128)(2,1)S(1)} collective-permute-done((bf16[128,2048]{1,0:T(8,128)(2,1)S(1)}, bf16[128,2048]{1,0:T(8,128)(2,1)S(1)}, u32[]{:S(2)}, u32[]{:S(2)}) %collective-permute-start.20) | collective-permute-done | bytes 524320 | tf_op jit(solution)/shard_map/ppermute | solution.py:114
  79.0 3.6 %collective-permute-done.23 = bf16[64,2048]{1,0:T(8,128)(2,1)S(1)} collective-permute-done((bf16[64,2048]{1,0:T(8,128)(2,1)S(1)}, bf16[64,2048]{1,0:T(8,128)(2,1)S(1)}, u32[]{:S(2)}, u32[]{:S(2)}) %collective-permute-start.23) | collective-permute-done | bytes 262176 | tf_op jit(solution)/shard_map/ppermute | solution.py:114
  84.2 4.1 %collective-permute-done.25 = bf16[64,2048]{1,0:T(8,128)(2,1)S(1)} collective-permute-done((bf16[64,2048]{1,0:T(8,128)(2,1)S(1)}, bf16[64,2048]{1,0:T(8,128)(2,1)S(1)}, u32[]{:S(2)}, u32[]{:S(2)}) %collective-permute-start.25) | collective-permute-done | bytes 262176 | tf_op jit(solution)/shard_map/ppermute | solution.py:114
  88.4 1.7 collective-permute-done.26
  94.5 2.9 %constant_dynamic-update-slice_fusion.21 = (bf16[1024,768]{1,0:T(8,128)(2,1)}, bf16[384,768]{1,0:T(8,128)(2,1)S(1)}, bf16[1024,768]{1,0:T(8,128)(2,1)S(1)}, bf16[1024,768]{1,0:T(8,128)(2,1)}, bf16[384,768]{1,0:T(8,128)(2,1)S(1)}) fusion(f32[384,768]{1,0:T(8,128)S(1)} %select_multiply_fusion.1, f32[384,768]{1,0:T(8,128)S(1)} %fusion.57, ...), kind=kOutput, calls=%fused_computation.115 | convolution fusion | flops 1219264512 | bytes 10030848 | tf_op jit(solution)/shard_map/dot_general | solution.py:97
  98.8 1.5 add_convert_fusion.3
  102.8 2.1 %constant_dynamic-update-slice_fusion.20 = (bf16[1024,768]{1,0:T(8,128)(2,1)S(1)}, bf16[256,768]{1,0:T(8,128)(2,1)S(1)}, bf16[1024,768]{1,0:T(8,128)(2,1)S(1)}, bf16[1024,768]{1,0:T(8,128)(2,1)}, bf16[256,768]{1,0:T(8,128)(2,1)S(1)}) fusion(bf16[1024,768]{1,0:T(8,128)(2,1)S(1)} %copy-done.7, f32[256,768]{1,0:T(8,128)S(1)} %fusion.47, ...), kind=kOutput, calls=%fused_computation.114 | convolution fusion | flops 818282496 | bytes 7736320 | tf_op jit(solution)/shard_map/dot_general | solution.py:97
  116.9 1.5 constant_dynamic-update-slice_fusion.18
  124.9 1.5 constant_dynamic-update-slice_fusion.17
  126.3 3.7 %convolution_convert_fusion.2 = bf16[2048,768]{1,0:T(8,128)(2,1)S(1)} fusion(bf16[1024,2048]{1,0:T(8,128)(2,1)S(1)} %constant_dynamic-update-slice_fusion.7, bf16[1024,768]{1,0:T(8,128)(2,1)S(1)} %get-tuple-element.48), kind=kOutput, calls=%fused_computation.2 | convolution fusion | flops 3222798336 | bytes 8912896 | tf_op jit(solution)/shard_map/dot_general | solution.py:97
  130.3 7.3 %collective-permute-start.40 = (bf16[2048,384]{1,0:T(8,128)(2,1)S(1)}, bf16[2048,384]{1,0:T(8,128)(2,1)S(1)}, u32[]{:S(2)}, u32[]{:S(2)}) collective-permute-start(bf16[2048,384]{1,0:T(8,128)(2,1)S(1)} %split.25), channel_id=1, source_target_pairs={{0,1},{1,0},{2,3},{3,2},{4,5},{5,4},{6,7},{7,6},{8,9},{9,8},{10,11... | collective-permute-start | bytes 4718600 | tf_op jit(solution)/shard_map/ppermute | solution.py:117
  137.5 3.7 %convolution_convert_fusion.1 = bf16[2048,768]{1,0:T(8,128)(2,1)S(1)} fusion(bf16[1024,2048]{1,0:T(8,128)(2,1)S(1)} %constant_dynamic-update-slice_fusion.7, bf16[1024,768]{1,0:T(8,128)(2,1)S(1)} %copy-done.8), kind=kOutput, calls=%fused_computation.1 | convolution fusion | flops 3222798336 | bytes 8912896 | tf_op jit(solution)/shard_map/dot_general | solution.py:97
  147.3 5.8 %collective-permute-done.27 = bf16[64,2048]{1,0:T(8,128)(2,1)S(1)} collective-permute-done((bf16[64,2048]{1,0:T(8,128)(2,1)S(1)}, bf16[64,2048]{1,0:T(8,128)(2,1)S(1)}, u32[]{:S(2)}, u32[]{:S(2)}) %collective-permute-start.27) | collective-permute-done | bytes 262176 | tf_op jit(solution)/shard_map/ppermute | solution.py:114
  155.4 4.0 %collective-permute-done.34 = bf16[64,2048]{1,0:T(8,128)(2,1)S(1)} collective-permute-done((bf16[64,2048]{1,0:T(8,128)(2,1)S(1)}, bf16[64,2048]{1,0:T(8,128)(2,1)S(1)}, u32[]{:S(2)}, u32[]{:S(2)}) %collective-permute-start.34) | collective-permute-done | bytes 262176 | tf_op jit(solution)/shard_map/ppermute | solution.py:114
  161.3 4.4 %collective-permute-done.31 = bf16[64,2048]{1,0:T(8,128)(2,1)S(1)} collective-permute-done((bf16[64,2048]{1,0:T(8,128)(2,1)S(1)}, bf16[64,2048]{1,0:T(8,128)(2,1)S(1)}, u32[]{:S(2)}, u32[]{:S(2)}) %collective-permute-start.31) | collective-permute-done | bytes 262176 | tf_op jit(solution)/shard_map/ppermute | solution.py:114
  166.1 5.1 %collective-permute-done.37 = bf16[64,2048]{1,0:T(8,128)(2,1)S(1)} collective-permute-done((bf16[64,2048]{1,0:T(8,128)(2,1)S(1)}, bf16[64,2048]{1,0:T(8,128)(2,1)S(1)}, u32[]{:S(2)}, u32[]{:S(2)}) %collective-permute-start.37) | collective-permute-done | bytes 262176 | tf_op jit(solution)/shard_map/ppermute | solution.py:114
  173.1 3.7 %convolution_convert_fusion = bf16[768,2048]{1,0:T(8,128)(2,1)S(1)} fusion(bf16[1024,768]{1,0:T(8,128)(2,1)S(1)} %get-tuple-element.74, bf16[1024,2048]{1,0:T(8,128)(2,1)S(1)} %constant_dynamic-update-slice_fusion.27), kind=kOutput, calls=%fused_computation | convolution fusion | flops 3222798336 | bytes 8912896 | tf_op jit(solution)/shard_map/dot_general | solution.py:97
  176.9 4.6 %collective-permute-start.42 = (bf16[384,2048]{1,0:T(8,128)(2,1)S(1)}, bf16[384,2048]{1,0:T(8,128)(2,1)S(1)}, u32[]{:S(2)}, u32[]{:S(2)}) collective-permute-start(bf16[384,2048]{1,0:T(8,128)(2,1)S(1)} %split.29), channel_id=1, source_target_pairs={{0,1},{1,0},{2,3},{3,2},{4,5},{5,4},{6,7},{7,6},{8,9},{9,8},{10,11... | collective-permute-start | bytes 4718600 | tf_op jit(solution)/shard_map/ppermute | solution.py:117
  182.5 1.5 fusion.4
  184.0 1.5 fusion.5
  185.6 1.7 fusion.6
  (176 shorter events, 62.4 us)
Async XLA Ops:
  0.6 33.1 %collective-permute-start.3 = (bf16[128,2048]{1,0:T(8,128)(2,1)}, bf16[128,2048]{1,0:T(8,128)(2,1)S(1)}, u32[]{:S(2)}, u32[]{:S(2)}) collective-permute-start(bf16[128,2048]{1,0:T(8,128)(2,1)} %param.9), channel_id=1, source_target_pairs={{0,4},{4,8},{8,12},{12,14},{14,10},{10,6},{6,2},{2,0},{1,5},{5,9},... | collective-permute-start | bytes 1572872 | tf_op jit(solution)/shard_map/ppermute | solution.py:114
  2.1 33.7 %collective-permute-start.5 = (bf16[64,2048]{1,0:T(8,128)(2,1)S(1)}, bf16[64,2048]{1,0:T(8,128)(2,1)S(1)}, u32[]{:S(2)}, u32[]{:S(2)}) collective-permute-start(bf16[64,2048]{1,0:T(8,128)(2,1)S(1)} %get-tuple-element.102), channel_id=1, source_target_pairs={{0,2},{4,0},{8,4},{12,8},{14,12},{10,14},{6,10},{2,6},{1,3},{5,1},... | collective-permute-start | bytes 786440 | tf_op jit(solution)/shard_map/ppermute | solution.py:114
  6.7 27.2 %collective-permute-start.9 = (bf16[128,2048]{1,0:T(8,128)(2,1)}, bf16[128,2048]{1,0:T(8,128)(2,1)S(1)}, u32[]{:S(2)}, u32[]{:S(2)}) collective-permute-start(bf16[128,2048]{1,0:T(8,128)(2,1)} %param.8), channel_id=1, source_target_pairs={{0,2},{4,0},{8,4},{12,8},{14,12},{10,14},{6,10},{2,6},{1,3},{5,1},... | collective-permute-start | bytes 1572872 | tf_op jit(solution)/shard_map/ppermute | solution.py:114
  9.1 16.8 %collective-permute-start.7 = (bf16[64,2048]{1,0:T(8,128)(2,1)S(1)}, bf16[64,2048]{1,0:T(8,128)(2,1)S(1)}, u32[]{:S(2)}, u32[]{:S(2)}) collective-permute-start(bf16[64,2048]{1,0:T(8,128)(2,1)S(1)} %get-tuple-element.100), channel_id=1, source_target_pairs={{0,4},{4,8},{8,12},{12,14},{14,10},{10,6},{6,2},{2,0},{1,5},{5,9},... | collective-permute-start | bytes 786440 | tf_op jit(solution)/shard_map/ppermute | solution.py:114
  25.9 9.5 %collective-permute-start.4 = (bf16[64,2048]{1,0:T(8,128)(2,1)S(1)}, bf16[64,2048]{1,0:T(8,128)(2,1)S(1)}, u32[]{:S(2)}, u32[]{:S(2)}) collective-permute-start(bf16[64,2048]{1,0:T(8,128)(2,1)S(1)} %get-tuple-element.101), channel_id=1, source_target_pairs={{0,2},{4,0},{8,4},{12,8},{14,12},{10,14},{6,10},{2,6},{1,3},{5,1},... | collective-permute-start | bytes 786440 | tf_op jit(solution)/shard_map/ppermute | solution.py:114
  29.7 63.4 %collective-permute-start.6 = (bf16[384,2048]{1,0:T(8,128)(2,1)}, bf16[384,2048]{1,0:T(8,128)(2,1)S(1)}, u32[]{:S(2)}, u32[]{:S(2)}) collective-permute-start(bf16[384,2048]{1,0:T(8,128)(2,1)} %bitcast.88), channel_id=1, source_target_pairs={{0,1},{1,0},{2,3},{3,2},{4,5},{5,4},{6,7},{7,6},{8,9},{9,8},{10,11... | collective-permute-start | bytes 4718600 | tf_op jit(solution)/shard_map/ppermute | solution.py:117
  33.8 57.9 %collective-permute-start.10 = (bf16[2048,384]{1,0:T(8,128)(2,1)S(1)}, bf16[2048,384]{1,0:T(8,128)(2,1)S(1)}, u32[]{:S(2)}, u32[]{:S(2)}) collective-permute-start(bf16[2048,384]{1,0:T(8,128)(2,1)S(1)} %bitcast.94), channel_id=1, source_target_pairs={{0,1},{1,0},{2,3},{3,2},{4,5},{5,4},{6,7},{7,6},{8,9},{9,8},{10,11... | collective-permute-start | bytes 4718600 | tf_op jit(solution)/shard_map/ppermute | solution.py:117
  33.9 8.0 %collective-permute-start.15 = (bf16[64,2048]{1,0:T(8,128)(2,1)S(1)}, bf16[64,2048]{1,0:T(8,128)(2,1)S(1)}, u32[]{:S(2)}, u32[]{:S(2)}) collective-permute-start(bf16[64,2048]{1,0:T(8,128)(2,1)S(1)} %collective-permute-done.7), channel_id=1, source_target_pairs={{0,4},{4,8},{8,12},{12,14},{14,10},{10,6},{6,2},{2,0},{1,5},{5,9},... | collective-permute-start | bytes 786440 | tf_op jit(solution)/shard_map/ppermute | solution.py:114
  35.4 12.1 %collective-permute-start.16 = (bf16[64,2048]{1,0:T(8,128)(2,1)S(1)}, bf16[64,2048]{1,0:T(8,128)(2,1)S(1)}, u32[]{:S(2)}, u32[]{:S(2)}) collective-permute-start(bf16[64,2048]{1,0:T(8,128)(2,1)S(1)} %collective-permute-done.8), channel_id=1, source_target_pairs={{0,4},{4,8},{8,12},{12,14},{14,10},{10,6},{6,2},{2,0},{1,5},{5,9},... | collective-permute-start | bytes 786440 | tf_op jit(solution)/shard_map/ppermute | solution.py:114
  35.8 22.9 %collective-permute-start.12 = (bf16[128,2048]{1,0:T(8,128)(2,1)S(1)}, bf16[128,2048]{1,0:T(8,128)(2,1)S(1)}, u32[]{:S(2)}, u32[]{:S(2)}) collective-permute-start(bf16[128,2048]{1,0:T(8,128)(2,1)S(1)} %collective-permute-done.3), channel_id=1, source_target_pairs={{0,4},{4,8},{8,12},{12,14},{14,10},{10,6},{6,2},{2,0},{1,5},{5,9},... | collective-permute-start | bytes 1572872 | tf_op jit(solution)/shard_map/ppermute | solution.py:114
  41.9 19.5 %collective-permute-start.17 = (bf16[128,2048]{1,0:T(8,128)(2,1)S(1)}, bf16[128,2048]{1,0:T(8,128)(2,1)S(1)}, u32[]{:S(2)}, u32[]{:S(2)}) collective-permute-start(bf16[128,2048]{1,0:T(8,128)(2,1)S(1)} %collective-permute-done.9), channel_id=1, source_target_pairs={{0,2},{4,0},{8,4},{12,8},{14,12},{10,14},{6,10},{2,6},{1,3},{5,1},... | collective-permute-start | bytes 1572872 | tf_op jit(solution)/shard_map/ppermute | solution.py:114
  47.5 12.4 %collective-permute-start.13 = (bf16[64,2048]{1,0:T(8,128)(2,1)S(1)}, bf16[64,2048]{1,0:T(8,128)(2,1)S(1)}, u32[]{:S(2)}, u32[]{:S(2)}) collective-permute-start(bf16[64,2048]{1,0:T(8,128)(2,1)S(1)} %collective-permute-done.4), channel_id=1, source_target_pairs={{0,2},{4,0},{8,4},{12,8},{14,12},{10,14},{6,10},{2,6},{1,3},{5,1},... | collective-permute-start | bytes 786440 | tf_op jit(solution)/shard_map/ppermute | solution.py:114
  58.7 35.8 %collective-permute-start.11 = (bf16[2048,384]{1,0:T(8,128)(2,1)S(1)}, bf16[2048,384]{1,0:T(8,128)(2,1)S(1)}, u32[]{:S(2)}, u32[]{:S(2)}) collective-permute-start(bf16[2048,384]{1,0:T(8,128)(2,1)S(1)} %bitcast.105), channel_id=1, source_target_pairs={{0,1},{1,0},{2,3},{3,2},{4,5},{5,4},{6,7},{7,6},{8,9},{9,8},{10,11... | collective-permute-start | bytes 4718600 | tf_op jit(solution)/shard_map/ppermute | solution.py:117
  61.4 15.7 %collective-permute-start.20 = (bf16[128,2048]{1,0:T(8,128)(2,1)S(1)}, bf16[128,2048]{1,0:T(8,128)(2,1)S(1)}, u32[]{:S(2)}, u32[]{:S(2)}) collective-permute-start(bf16[128,2048]{1,0:T(8,128)(2,1)S(1)} %collective-permute-done.17), channel_id=1, source_target_pairs={{0,2},{4,0},{8,4},{12,8},{14,12},{10,14},{6,10},{2,6},{1,3},{5,1},... | collective-permute-start | bytes 1572872 | tf_op jit(solution)/shard_map/ppermute | solution.py:114
  65.9 12.6 %collective-permute-start.18 = (bf16[128,2048]{1,0:T(8,128)(2,1)S(1)}, bf16[128,2048]{1,0:T(8,128)(2,1)S(1)}, u32[]{:S(2)}, u32[]{:S(2)}) collective-permute-start(bf16[128,2048]{1,0:T(8,128)(2,1)S(1)} %collective-permute-done.12), channel_id=1, source_target_pairs={{0,4},{4,8},{8,12},{12,14},{14,10},{10,6},{6,2},{2,0},{1,5},{5,9},... | collective-permute-start | bytes 1572872 | tf_op jit(solution)/shard_map/ppermute | solution.py:114
  90.1 20.0 %collective-permute-start.19 = (bf16[128,2048]{1,0:T(8,128)(2,1)S(1)}, bf16[128,2048]{1,0:T(8,128)(2,1)S(1)}, u32[]{:S(2)}, u32[]{:S(2)}) collective-permute-start(bf16[128,2048]{1,0:T(8,128)(2,1)S(1)} %collective-permute-done.18), channel_id=1, source_target_pairs={{0,4},{4,8},{8,12},{12,14},{14,10},{10,6},{6,2},{2,0},{1,5},{5,9},... | collective-permute-start | bytes 1572872 | tf_op jit(solution)/shard_map/ppermute | solution.py:114
  90.2 19.3 %collective-permute-start.21 = (bf16[128,2048]{1,0:T(8,128)(2,1)S(1)}, bf16[128,2048]{1,0:T(8,128)(2,1)S(1)}, u32[]{:S(2)}, u32[]{:S(2)}) collective-permute-start(bf16[128,2048]{1,0:T(8,128)(2,1)S(1)} %collective-permute-done.20), channel_id=1, source_target_pairs={{0,2},{4,0},{8,4},{12,8},{14,12},{10,14},{6,10},{2,6},{1,3},{5,1},... | collective-permute-start | bytes 1572872 | tf_op jit(solution)/shard_map/ppermute | solution.py:114
  115.4 28.4 %collective-permute-start.29 = (bf16[64,2048]{1,0:T(8,128)(2,1)S(1)}, bf16[64,2048]{1,0:T(8,128)(2,1)S(1)}, u32[]{:S(2)}, u32[]{:S(2)}) collective-permute-start(bf16[64,2048]{1,0:T(8,128)(2,1)S(1)} %get-tuple-element.93), channel_id=1, source_target_pairs={{0,4},{4,8},{8,12},{12,14},{14,10},{10,6},{6,2},{2,0},{1,5},{5,9},... | collective-permute-start | bytes 786440 | tf_op jit(solution)/shard_map/ppermute | solution.py:114
  118.3 26.7 %collective-permute-start.22 = (bf16[64,2048]{1,0:T(8,128)(2,1)S(1)}, bf16[64,2048]{1,0:T(8,128)(2,1)S(1)}, u32[]{:S(2)}, u32[]{:S(2)}) collective-permute-start(bf16[64,2048]{1,0:T(8,128)(2,1)S(1)} %get-tuple-element.94), channel_id=1, source_target_pairs={{0,2},{4,0},{8,4},{12,8},{14,12},{10,14},{6,10},{2,6},{1,3},{5,1},... | collective-permute-start | bytes 786440 | tf_op jit(solution)/shard_map/ppermute | solution.py:114
  121.9 24.9 %collective-permute-start.28 = (bf16[64,2048]{1,0:T(8,128)(2,1)S(1)}, bf16[64,2048]{1,0:T(8,128)(2,1)S(1)}, u32[]{:S(2)}, u32[]{:S(2)}) collective-permute-start(bf16[64,2048]{1,0:T(8,128)(2,1)S(1)} %get-tuple-element.90), channel_id=1, source_target_pairs={{0,2},{4,0},{8,4},{12,8},{14,12},{10,14},{6,10},{2,6},{1,3},{5,1},... | collective-permute-start | bytes 786440 | tf_op jit(solution)/shard_map/ppermute | solution.py:114
  122.3 24.0 %collective-permute-start.30 = (bf16[64,2048]{1,0:T(8,128)(2,1)S(1)}, bf16[64,2048]{1,0:T(8,128)(2,1)S(1)}, u32[]{:S(2)}, u32[]{:S(2)}) collective-permute-start(bf16[64,2048]{1,0:T(8,128)(2,1)S(1)} %get-tuple-element.89), channel_id=1, source_target_pairs={{0,4},{4,8},{8,12},{12,14},{14,10},{10,6},{6,2},{2,0},{1,5},{5,9},... | collective-permute-start | bytes 786440 | tf_op jit(solution)/shard_map/ppermute | solution.py:114
  130.3 52.2 %collective-permute-start.40 = (bf16[2048,384]{1,0:T(8,128)(2,1)S(1)}, bf16[2048,384]{1,0:T(8,128)(2,1)S(1)}, u32[]{:S(2)}, u32[]{:S(2)}) collective-permute-start(bf16[2048,384]{1,0:T(8,128)(2,1)S(1)} %split.25), channel_id=1, source_target_pairs={{0,1},{1,0},{2,3},{3,2},{4,5},{5,4},{6,7},{7,6},{8,9},{9,8},{10,11... | collective-permute-start | bytes 4718600 | tf_op jit(solution)/shard_map/ppermute | solution.py:117
  143.8 40.2 %collective-permute-start.41 = (bf16[2048,384]{1,0:T(8,128)(2,1)S(1)}, bf16[2048,384]{1,0:T(8,128)(2,1)S(1)}, u32[]{:S(2)}, u32[]{:S(2)}) collective-permute-start(bf16[2048,384]{1,0:T(8,128)(2,1)S(1)} %split.27), channel_id=1, source_target_pairs={{0,1},{1,0},{2,3},{3,2},{4,5},{5,4},{6,7},{7,6},{8,9},{9,8},{10,11... | collective-permute-start | bytes 4718600 | tf_op jit(solution)/shard_map/ppermute | solution.py:117
  145.2 7.9 %collective-permute-start.27 = (bf16[64,2048]{1,0:T(8,128)(2,1)S(1)}, bf16[64,2048]{1,0:T(8,128)(2,1)S(1)}, u32[]{:S(2)}, u32[]{:S(2)}) collective-permute-start(bf16[64,2048]{1,0:T(8,128)(2,1)S(1)} %get-tuple-element.92), channel_id=1, source_target_pairs={{0,2},{4,0},{8,4},{12,8},{14,12},{10,14},{6,10},{2,6},{1,3},{5,1},... | collective-permute-start | bytes 786440 | tf_op jit(solution)/shard_map/ppermute | solution.py:114
  146.3 7.9 %collective-permute-start.33 = (bf16[64,2048]{1,0:T(8,128)(2,1)S(1)}, bf16[64,2048]{1,0:T(8,128)(2,1)S(1)}, u32[]{:S(2)}, u32[]{:S(2)}) collective-permute-start(bf16[64,2048]{1,0:T(8,128)(2,1)S(1)} %get-tuple-element.91), channel_id=1, source_target_pairs={{0,4},{4,8},{8,12},{12,14},{14,10},{10,6},{6,2},{2,0},{1,5},{5,9},... | collective-permute-start | bytes 786440 | tf_op jit(solution)/shard_map/ppermute | solution.py:114
  146.8 12.7 %collective-permute-start.34 = (bf16[64,2048]{1,0:T(8,128)(2,1)S(1)}, bf16[64,2048]{1,0:T(8,128)(2,1)S(1)}, u32[]{:S(2)}, u32[]{:S(2)}) collective-permute-start(bf16[64,2048]{1,0:T(8,128)(2,1)S(1)} %add_convert_fusion.12), channel_id=1, source_target_pairs={{0,4},{4,8},{8,12},{12,14},{14,10},{10,6},{6,2},{2,0},{1,5},{5,9},... | collective-permute-start | bytes 786440 | tf_op jit(solution)/shard_map/ppermute | solution.py:114
  154.2 11.5 %collective-permute-start.31 = (bf16[64,2048]{1,0:T(8,128)(2,1)S(1)}, bf16[64,2048]{1,0:T(8,128)(2,1)S(1)}, u32[]{:S(2)}, u32[]{:S(2)}) collective-permute-start(bf16[64,2048]{1,0:T(8,128)(2,1)S(1)} %add_convert_fusion.11), channel_id=1, source_target_pairs={{0,2},{4,0},{8,4},{12,8},{14,12},{10,14},{6,10},{2,6},{1,3},{5,1},... | collective-permute-start | bytes 786440 | tf_op jit(solution)/shard_map/ppermute | solution.py:114
  159.6 12.8 %collective-permute-start.36 = (bf16[64,2048]{1,0:T(8,128)(2,1)S(1)}, bf16[64,2048]{1,0:T(8,128)(2,1)S(1)}, u32[]{:S(2)}, u32[]{:S(2)}) collective-permute-start(bf16[64,2048]{1,0:T(8,128)(2,1)S(1)} %add_convert_fusion.8), channel_id=1, source_target_pairs={{0,4},{4,8},{8,12},{12,14},{14,10},{10,6},{6,2},{2,0},{1,5},{5,9},... | collective-permute-start | bytes 786440 | tf_op jit(solution)/shard_map/ppermute | solution.py:114
  160.1 16.7 %collective-permute-start.39 = (bf16[64,2048]{1,0:T(8,128)(2,1)S(1)}, bf16[64,2048]{1,0:T(8,128)(2,1)S(1)}, u32[]{:S(2)}, u32[]{:S(2)}) collective-permute-start(bf16[64,2048]{1,0:T(8,128)(2,1)S(1)} %add_convert_fusion.9), channel_id=1, source_target_pairs={{0,2},{4,0},{8,4},{12,8},{14,12},{10,14},{6,10},{2,6},{1,3},{5,1},... | collective-permute-start | bytes 786440 | tf_op jit(solution)/shard_map/ppermute | solution.py:114
  171.2 10.2 %collective-permute-start.35 = (bf16[64,2048]{1,0:T(8,128)(2,1)S(1)}, bf16[64,2048]{1,0:T(8,128)(2,1)S(1)}, u32[]{:S(2)}, u32[]{:S(2)}) collective-permute-start(bf16[64,2048]{1,0:T(8,128)(2,1)S(1)} %add_convert_fusion.7), channel_id=1, source_target_pairs={{0,2},{4,0},{8,4},{12,8},{14,12},{10,14},{6,10},{2,6},{1,3},{5,1},... | collective-permute-start | bytes 786440 | tf_op jit(solution)/shard_map/ppermute | solution.py:114
  172.3 9.1 %collective-permute-start.38 = (bf16[64,2048]{1,0:T(8,128)(2,1)S(1)}, bf16[64,2048]{1,0:T(8,128)(2,1)S(1)}, u32[]{:S(2)}, u32[]{:S(2)}) collective-permute-start(bf16[64,2048]{1,0:T(8,128)(2,1)S(1)} %add_convert_fusion.5), channel_id=1, source_target_pairs={{0,4},{4,8},{8,12},{12,14},{14,10},{10,6},{6,2},{2,0},{1,5},{5,9},... | collective-permute-start | bytes 786440 | tf_op jit(solution)/shard_map/ppermute | solution.py:114
  176.9 8.7 %collective-permute-start.42 = (bf16[384,2048]{1,0:T(8,128)(2,1)S(1)}, bf16[384,2048]{1,0:T(8,128)(2,1)S(1)}, u32[]{:S(2)}, u32[]{:S(2)}) collective-permute-start(bf16[384,2048]{1,0:T(8,128)(2,1)S(1)} %split.29), channel_id=1, source_target_pairs={{0,1},{1,0},{2,3},{3,2},{4,5},{5,4},{6,7},{7,6},{8,9},{9,8},{10,11... | collective-permute-start | bytes 4718600 | tf_op jit(solution)/shard_map/ppermute | solution.py:117
  (20 other events, 177.8 us)

commit v7 on v6

--- a/solution.py
+++ b/solution.py
@@ -144,16 +144,20 @@
     chosen = expert_ids[None, None, :, :] == expert[:, :, None, None]
     outgoing = jnp.sum(jnp.where(chosen, route_ratio[None, None], 0.0), axis=3)
 
-    blocks = [outgoing[d] for d in range(groups)]
-    for bit in range((groups - 1).bit_length()):
-        going = [d for d in range(groups) if d >> bit & 1]
-        packed = jnp.concatenate([blocks[d] for d in going], axis=0)
-        moved = shift(packed, 1 << bit)
-        for i, d in enumerate(going):
-            blocks[d] = moved[i * members : (i + 1) * members]
+    distances = [d for k in range(1, full_steps + 1) for d in (k, -k)] + [groups // 2] * has_far
+    blocks = {d: outgoing[d % groups] for d in distances}
+    for bit in range((groups // 2).bit_length()):
+        for sign in (1, -1):
+            going = [d for d in distances if d * sign > 0 and abs(d) >> bit & 1]
+            if not going:
+                continue
+            packed = jnp.concatenate([blocks[d] for d in going], axis=0)
+            moved = shift(packed, sign << bit)
+            for i, d in enumerate(going):
+                blocks[d] = moved[i * members : (i + 1) * members]
 
     def ratio_from(distance):
-        return blocks[-distance % groups]
+        return blocks[-distance]
 
     gates, ups, downs = [w_gate[0]], [w_up[0]], [w_down[0]]
     for k in range(1, members):
@@ -209,18 +213,24 @@
             own_part = part[2 * tok_rows :]
     if full_steps < 2:
         own_part = step_piece([layer_input], [output_grad], [outgoing[0]])
-    if has_far:
-        far_part = step_piece([far[0]], [far[1]], [ratio_from(groups // 2)])
+
+    def far_piece():
+        return step_piece([far[0]], [far[1]], [blocks[groups // 2]]) if has_far else None
+
     if full_steps:
         k = full_steps
         lefts, rights = from_left[k - 1], from_right[k - 1]
         parts[k] = [{}, {}]
-        for one, two in ((high, low), (low, high)):
+        for name, one, two in (("a", high, low), ("b", low, high)):
+            if name == "b":
+                far_part = far_piece()
             ratio = [ratio_from(-k)[:, one], ratio_from(k)[:, two]]
             part = step_piece(
                 [lefts[0][one], rights[0][two]], [lefts[1][one], rights[1][two]], ratio, apart=True
             )
             parts[k][0][one], parts[k][1][two] = part[:half], part[half:]
+    else:
+        far_part = far_piece()
 
     def join(moved, part):
         return (moved.astype(jnp.float32) + part.astype(jnp.float32)).astype(jnp.bfloat16)

time: 191 us -> 191 us (level)
  the two profiles are of different devices: /device:TPU:15 before, /device:TPU:0 now
where the time goes in v7:
time: 191 us; the launch traced here: 190 us
  waiting for transfers between devices  85.8 us (45%)
  starting transfers between devices  47 us (25%)
  matrix products  41.7 us (22%)
  other arithmetic  9.96 us (5%)
  local copies, waits for them, and re-layouts  4.35 us (2%)
    ppermute x39, waiting for transfers between devices, shift(): return lax.ppermute(array, 'grp', at_distance(k))  85.7 us
    ppermute x39, starting transfers between devices, shift(): return lax.ppermute(array, 'grp', at_distance(k))  45.8 us
    dot_general x28, matrix products, mm(): return lax.dot_general(a, b, dims, preferred_element_type=jnp.float32)  41.7 us
    broadcast_in_dim x3, other arithmetic, member_sum(): return total.astype(jnp.bfloat16)[None]  4.82 us
  transfers between devices with their start and end apart: 45, of which 20 were waited for; matrix products, arithmetic and copies ran while one was open for 28% of the time, Pallas kernels for 0%

profile of v7, /device:TPU:0, one launch (start us, length us, event | category | flops | bytes accessed | tf_op | source)
XLA Modules:
  0.0 190.3 jit_solution(1652626534579513853)
XLA Ops:
  0.6 3.1 %collective-permute-start.2 = (bf16[128,2048]{1,0:T(8,128)(2,1)}, bf16[128,2048]{1,0:T(8,128)(2,1)S(1)}, u32[]{:S(2)}, u32[]{:S(2)}) collective-permute-start(bf16[128,2048]{1,0:T(8,128)(2,1)} %param.9), channel_id=1, source_target_pairs={{0,4},{4,8},{8,12},{12,14},{14,10},{10,6},{6,2},{2,0},{1,5},{5,9},... | collective-permute-start | bytes 1572872 | tf_op jit(solution)/shard_map/ppermute | solution.py:114
  8.1 1.9 %collective-permute-start.1 = (f32[4,128]{1,0:T(4,128)S(1)}, f32[4,128]{1,0:T(4,128)S(1)}, u32[]{:S(2)}, u32[]{:S(2)}) collective-permute-start(f32[4,128]{1,0:T(4,128)S(1)} %pad_maximum_fusion.9), channel_id=1, source_target_pairs={{0,2},{4,0},{8,4},{12,8},{14,12},{10,14},{6,10},{2,6},{1,3},{5,1},... | collective-permute-start | bytes 6152 | tf_op jit(solution)/shard_map/ppermute | solution.py:114
  16.8 3.1 %collective-permute-start.13 = (f32[4,128]{1,0:T(4,128)S(1)}, f32[4,128]{1,0:T(4,128)S(1)}, u32[]{:S(2)}, u32[]{:S(2)}) collective-permute-start(f32[4,128]{1,0:T(4,128)S(1)} %pad_maximum_fusion.11), channel_id=1, source_target_pairs={{0,6},{4,2},{8,0},{12,4},{14,8},{10,12},{6,14},{2,10},{1,7},{5,3},... | collective-permute-start | bytes 6152 | tf_op jit(solution)/shard_map/ppermute | solution.py:114
  19.9 5.1 %collective-permute-done.13 = f32[4,128]{1,0:T(4,128)S(1)} collective-permute-done((f32[4,128]{1,0:T(4,128)S(1)}, f32[4,128]{1,0:T(4,128)S(1)}, u32[]{:S(2)}, u32[]{:S(2)}) %collective-permute-start.13) | collective-permute-done | bytes 2080 | tf_op jit(solution)/shard_map/ppermute | solution.py:114
  25.4 4.1 %collective-permute-done.12 = f32[4,128]{1,0:T(4,128)S(1)} collective-permute-done((f32[4,128]{1,0:T(4,128)S(1)}, f32[4,128]{1,0:T(4,128)S(1)}, u32[]{:S(2)}, u32[]{:S(2)}) %collective-permute-start.12) | collective-permute-done | bytes 2080 | tf_op jit(solution)/shard_map/ppermute | solution.py:114
  31.8 4.0 %collective-permute-done.7 = bf16[64,2048]{1,0:T(8,128)(2,1)S(1)} collective-permute-done((bf16[64,2048]{1,0:T(8,128)(2,1)S(1)}, bf16[64,2048]{1,0:T(8,128)(2,1)S(1)}, u32[]{:S(2)}, u32[]{:S(2)}) %collective-permute-start.7) | collective-permute-done | bytes 262176 | tf_op jit(solution)/shard_map/ppermute | solution.py:114
  38.6 2.5 %collective-permute-start.14 = (bf16[128,2048]{1,0:T(8,128)(2,1)S(1)}, bf16[128,2048]{1,0:T(8,128)(2,1)S(1)}, u32[]{:S(2)}, u32[]{:S(2)}) collective-permute-start(bf16[128,2048]{1,0:T(8,128)(2,1)S(1)} %collective-permute-done.2), channel_id=1, source_target_pairs={{0,4},{4,8},{8,12},{12,14},{14,10},{10,6},{6,2},{2,0},{1,5},{5,9},... | collective-permute-start | bytes 1572872 | tf_op jit(solution)/shard_map/ppermute | solution.py:114
  41.2 4.6 %collective-permute-done.17 = bf16[64,2048]{1,0:T(8,128)(2,1)S(1)} collective-permute-done((bf16[64,2048]{1,0:T(8,128)(2,1)S(1)}, bf16[64,2048]{1,0:T(8,128)(2,1)S(1)}, u32[]{:S(2)}, u32[]{:S(2)}) %collective-permute-start.17) | collective-permute-done | bytes 262176 | tf_op jit(solution)/shard_map/ppermute | solution.py:114
  46.3 5.1 %collective-permute-done.18 = bf16[64,2048]{1,0:T(8,128)(2,1)S(1)} collective-permute-done((bf16[64,2048]{1,0:T(8,128)(2,1)S(1)}, bf16[64,2048]{1,0:T(8,128)(2,1)S(1)}, u32[]{:S(2)}, u32[]{:S(2)}) %collective-permute-start.18) | collective-permute-done | bytes 262176 | tf_op jit(solution)/shard_map/ppermute | solution.py:114
  51.9 9.8 %collective-permute-done.14 = bf16[128,2048]{1,0:T(8,128)(2,1)S(1)} collective-permute-done((bf16[128,2048]{1,0:T(8,128)(2,1)S(1)}, bf16[128,2048]{1,0:T(8,128)(2,1)S(1)}, u32[]{:S(2)}, u32[]{:S(2)}) %collective-permute-start.14) | collective-permute-done | bytes 524320 | tf_op jit(solution)/shard_map/ppermute | solution.py:114
  65.1 7.6 %collective-permute-done.16 = bf16[64,2048]{1,0:T(8,128)(2,1)S(1)} collective-permute-done((bf16[64,2048]{1,0:T(8,128)(2,1)S(1)}, bf16[64,2048]{1,0:T(8,128)(2,1)S(1)}, u32[]{:S(2)}, u32[]{:S(2)}) %collective-permute-start.16) | collective-permute-done | bytes 262176 | tf_op jit(solution)/shard_map/ppermute | solution.py:114
  74.2 7.6 %collective-permute-done.21 = bf16[128,2048]{1,0:T(8,128)(2,1)S(1)} collective-permute-done((bf16[128,2048]{1,0:T(8,128)(2,1)S(1)}, bf16[128,2048]{1,0:T(8,128)(2,1)S(1)}, u32[]{:S(2)}, u32[]{:S(2)}) %collective-permute-start.21) | collective-permute-done | bytes 524320 | tf_op jit(solution)/shard_map/ppermute | solution.py:114
  84.0 4.7 %collective-permute-done.20 = bf16[64,2048]{1,0:T(8,128)(2,1)S(1)} collective-permute-done((bf16[64,2048]{1,0:T(8,128)(2,1)S(1)}, bf16[64,2048]{1,0:T(8,128)(2,1)S(1)}, u32[]{:S(2)}, u32[]{:S(2)}) %collective-permute-start.20) | collective-permute-done | bytes 262176 | tf_op jit(solution)/shard_map/ppermute | solution.py:114
  90.9 4.2 %collective-permute-done.27 = bf16[64,2048]{1,0:T(8,128)(2,1)S(1)} collective-permute-done((bf16[64,2048]{1,0:T(8,128)(2,1)S(1)}, bf16[64,2048]{1,0:T(8,128)(2,1)S(1)}, u32[]{:S(2)}, u32[]{:S(2)}) %collective-permute-start.27) | collective-permute-done | bytes 262176 | tf_op jit(solution)/shard_map/ppermute | solution.py:114
  95.1 3.0 %collective-permute-start.11 = (f32[2,128]{1,0:T(2,128)S(1)}, f32[2,128]{1,0:T(2,128)S(1)}, u32[]{:S(2)}, u32[]{:S(2)}) collective-permute-start(f32[2,128]{1,0:T(2,128)S(1)} %get-tuple-element.111), channel_id=1, source_target_pairs={{0,14},{4,10},{8,6},{12,2},{14,0},{10,4},{6,8},{2,12},{1,15},{5,11... | collective-permute-start | bytes 3080 | tf_op jit(solution)/shard_map/ppermute | solution.py:114
  98.3 2.6 %collective-permute-start.25 = (bf16[128,2048]{1,0:T(8,128)(2,1)S(1)}, bf16[128,2048]{1,0:T(8,128)(2,1)S(1)}, u32[]{:S(2)}, u32[]{:S(2)}) collective-permute-start(bf16[128,2048]{1,0:T(8,128)(2,1)S(1)} %collective-permute-done.21), channel_id=1, source_target_pairs={{0,2},{4,0},{8,4},{12,8},{14,12},{10,14},{6,10},{2,6},{1,3},{5,1},... | collective-permute-start | bytes 1572872 | tf_op jit(solution)/shard_map/ppermute | solution.py:114
  103.8 2.6 %constant_dynamic-update-slice_fusion.21 = (bf16[1024,768]{1,0:T(8,128)(2,1)S(1)}, bf16[384,768]{1,0:T(8,128)(2,1)S(1)}, bf16[1024,768]{1,0:T(8,128)(2,1)S(1)}, bf16[1024,768]{1,0:T(8,128)(2,1)}, bf16[384,768]{1,0:T(8,128)(2,1)S(1)}) fusion(f32[384,768]{1,0:T(8,128)S(1)} %select_multiply_fusion.1, f32[384,768]{1,0:T(8,128)S(1)} %fusion.57, ...), kind=kOutput, calls=%fused_computation.115 | convolution fusion | flops 1219264512 | bytes 10030848 | tf_op jit(solution)/shard_map/dot_general | solution.py:97
  111.3 2.1 %constant_dynamic-update-slice_fusion.20 = (bf16[1024,768]{1,0:T(8,128)(2,1)S(1)}, bf16[256,768]{1,0:T(8,128)(2,1)S(1)}, bf16[1024,768]{1,0:T(8,128)(2,1)S(1)}, bf16[1024,768]{1,0:T(8,128)(2,1)}, bf16[256,768]{1,0:T(8,128)(2,1)S(1)}) fusion(bf16[1024,768]{1,0:T(8,128)(2,1)S(1)} %get-tuple-element.56, f32[256,768]{1,0:T(8,128)S(1)} %fusion.47, ...), kind=kOutput, calls=%fused_computation.114 | convolution fusion | flops 818282496 | bytes 7736320 | tf_op jit(solution)/shard_map/dot_general | solution.py:97
  121.4 2.1 %collective-permute-start.30 = (bf16[64,2048]{1,0:T(8,128)(2,1)S(1)}, bf16[64,2048]{1,0:T(8,128)(2,1)S(1)}, u32[]{:S(2)}, u32[]{:S(2)}) collective-permute-start(bf16[64,2048]{1,0:T(8,128)(2,1)S(1)} %get-tuple-element.90), channel_id=1, source_target_pairs={{0,2},{4,0},{8,4},{12,8},{14,12},{10,14},{6,10},{2,6},{1,3},{5,1},... | collective-permute-start | bytes 786440 | tf_op jit(solution)/shard_map/ppermute | solution.py:114
  129.9 2.1 %collective-permute-start.26 = (bf16[64,2048]{1,0:T(8,128)(2,1)S(1)}, bf16[64,2048]{1,0:T(8,128)(2,1)S(1)}, u32[]{:S(2)}, u32[]{:S(2)}) collective-permute-start(bf16[64,2048]{1,0:T(8,128)(2,1)S(1)} %get-tuple-element.94), channel_id=1, source_target_pairs={{0,2},{4,0},{8,4},{12,8},{14,12},{10,14},{6,10},{2,6},{1,3},{5,1},... | collective-permute-start | bytes 786440 | tf_op jit(solution)/shard_map/ppermute | solution.py:114
  134.3 3.8 %convolution_convert_fusion.2 = bf16[2048,768]{1,0:T(8,128)(2,1)S(1)} fusion(bf16[1024,2048]{1,0:T(8,128)(2,1)S(1)} %get-tuple-element.135, bf16[1024,768]{1,0:T(8,128)(2,1)S(1)} %get-tuple-element.48), kind=kOutput, calls=%fused_computation.2 | convolution fusion | flops 3222798336 | bytes 8912896 | tf_op jit(solution)/shard_map/dot_general | solution.py:97
  138.3 3.8 %convolution_convert_fusion.1 = bf16[2048,768]{1,0:T(8,128)(2,1)S(1)} fusion(bf16[1024,2048]{1,0:T(8,128)(2,1)S(1)} %get-tuple-element.135, bf16[1024,768]{1,0:T(8,128)(2,1)S(1)} %get-tuple-element.75), kind=kOutput, calls=%fused_computation.1 | convolution fusion | flops 3222798336 | bytes 8912896 | tf_op jit(solution)/shard_map/dot_general | solution.py:97
  145.2 2.0 %collective-permute-start.29 = (bf16[64,2048]{1,0:T(8,128)(2,1)S(1)}, bf16[64,2048]{1,0:T(8,128)(2,1)S(1)}, u32[]{:S(2)}, u32[]{:S(2)}) collective-permute-start(bf16[64,2048]{1,0:T(8,128)(2,1)S(1)} %get-tuple-element.92), channel_id=1, source_target_pairs={{0,2},{4,0},{8,4},{12,8},{14,12},{10,14},{6,10},{2,6},{1,3},{5,1},... | collective-permute-start | bytes 786440 | tf_op jit(solution)/shard_map/ppermute | solution.py:114
  147.5 6.0 %collective-permute-done.29 = bf16[64,2048]{1,0:T(8,128)(2,1)S(1)} collective-permute-done((bf16[64,2048]{1,0:T(8,128)(2,1)S(1)}, bf16[64,2048]{1,0:T(8,128)(2,1)S(1)}, u32[]{:S(2)}, u32[]{:S(2)}) %collective-permute-start.29) | collective-permute-done | bytes 262176 | tf_op jit(solution)/shard_map/ppermute | solution.py:114
  153.6 2.0 %collective-permute-start.34 = (bf16[64,2048]{1,0:T(8,128)(2,1)S(1)}, bf16[64,2048]{1,0:T(8,128)(2,1)S(1)}, u32[]{:S(2)}, u32[]{:S(2)}) collective-permute-start(bf16[64,2048]{1,0:T(8,128)(2,1)S(1)} %add_convert_fusion.13), channel_id=1, source_target_pairs={{0,2},{4,0},{8,4},{12,8},{14,12},{10,14},{6,10},{2,6},{1,3},{5,1},... | collective-permute-start | bytes 786440 | tf_op jit(solution)/shard_map/ppermute | solution.py:114
  156.6 4.3 %collective-permute-done.36 = bf16[64,2048]{1,0:T(8,128)(2,1)S(1)} collective-permute-done((bf16[64,2048]{1,0:T(8,128)(2,1)S(1)}, bf16[64,2048]{1,0:T(8,128)(2,1)S(1)}, u32[]{:S(2)}, u32[]{:S(2)}) %collective-permute-start.36) | collective-permute-done | bytes 262176 | tf_op jit(solution)/shard_map/ppermute | solution.py:114
  162.8 2.0 %collective-permute-start.41 = (bf16[64,2048]{1,0:T(8,128)(2,1)S(1)}, bf16[64,2048]{1,0:T(8,128)(2,1)S(1)}, u32[]{:S(2)}, u32[]{:S(2)}) collective-permute-start(bf16[64,2048]{1,0:T(8,128)(2,1)S(1)} %add_convert_fusion.9), channel_id=1, source_target_pairs={{0,2},{4,0},{8,4},{12,8},{14,12},{10,14},{6,10},{2,6},{1,3},{5,1},... | collective-permute-start | bytes 786440 | tf_op jit(solution)/shard_map/ppermute | solution.py:114
  164.8 3.5 %collective-permute-done.33 = bf16[64,2048]{1,0:T(8,128)(2,1)S(1)} collective-permute-done((bf16[64,2048]{1,0:T(8,128)(2,1)S(1)}, bf16[64,2048]{1,0:T(8,128)(2,1)S(1)}, u32[]{:S(2)}, u32[]{:S(2)}) %collective-permute-start.33) | collective-permute-done | bytes 262176 | tf_op jit(solution)/shard_map/ppermute | solution.py:114
  168.4 6.3 %collective-permute-done.39 = bf16[64,2048]{1,0:T(8,128)(2,1)S(1)} collective-permute-done((bf16[64,2048]{1,0:T(8,128)(2,1)S(1)}, bf16[64,2048]{1,0:T(8,128)(2,1)S(1)}, u32[]{:S(2)}, u32[]{:S(2)}) %collective-permute-start.39) | collective-permute-done | bytes 262176 | tf_op jit(solution)/shard_map/ppermute | solution.py:114
  174.7 2.9 %collective-permute-start.37 = (bf16[64,2048]{1,0:T(8,128)(2,1)S(1)}, bf16[64,2048]{1,0:T(8,128)(2,1)S(1)}, u32[]{:S(2)}, u32[]{:S(2)}) collective-permute-start(bf16[64,2048]{1,0:T(8,128)(2,1)S(1)} %add_convert_fusion.7), channel_id=1, source_target_pairs={{0,2},{4,0},{8,4},{12,8},{14,12},{10,14},{6,10},{2,6},{1,3},{5,1},... | collective-permute-start | bytes 786440 | tf_op jit(solution)/shard_map/ppermute | solution.py:114
  178.0 3.7 %convolution_convert_fusion = bf16[768,2048]{1,0:T(8,128)(2,1)S(1)} fusion(bf16[1024,768]{1,0:T(8,128)(2,1)S(1)} %get-tuple-element.74, bf16[1024,2048]{1,0:T(8,128)(2,1)S(1)} %get-tuple-element.136), kind=kOutput, calls=%fused_computation | convolution fusion | flops 3222798336 | bytes 8912896 | tf_op jit(solution)/shard_map/dot_general | solution.py:97
  181.9 2.4 %collective-permute-done.40 = bf16[64,2048]{1,0:T(8,128)(2,1)S(1)} collective-permute-done((bf16[64,2048]{1,0:T(8,128)(2,1)S(1)}, bf16[64,2048]{1,0:T(8,128)(2,1)S(1)}, u32[]{:S(2)}, u32[]{:S(2)}) %collective-permute-start.40) | collective-permute-done | bytes 262176 | tf_op jit(solution)/shard_map/ppermute | solution.py:114
  (175 shorter events, 64.2 us)
Async XLA Ops:
  0.6 35.3 %collective-permute-start.2 = (bf16[128,2048]{1,0:T(8,128)(2,1)}, bf16[128,2048]{1,0:T(8,128)(2,1)S(1)}, u32[]{:S(2)}, u32[]{:S(2)}) collective-permute-start(bf16[128,2048]{1,0:T(8,128)(2,1)} %param.9), channel_id=1, source_target_pairs={{0,4},{4,8},{8,12},{12,14},{14,10},{10,6},{6,2},{2,0},{1,5},{5,9},... | collective-permute-start | bytes 1572872 | tf_op jit(solution)/shard_map/ppermute | solution.py:114
  4.8 33.7 %collective-permute-start.4 = (bf16[64,2048]{1,0:T(8,128)(2,1)S(1)}, bf16[64,2048]{1,0:T(8,128)(2,1)S(1)}, u32[]{:S(2)}, u32[]{:S(2)}) collective-permute-start(bf16[64,2048]{1,0:T(8,128)(2,1)S(1)} %get-tuple-element.102), channel_id=1, source_target_pairs={{0,2},{4,0},{8,4},{12,8},{14,12},{10,14},{6,10},{2,6},{1,3},{5,1},... | collective-permute-start | bytes 786440 | tf_op jit(solution)/shard_map/ppermute | solution.py:114
  10.2 26.4 %collective-permute-start.8 = (bf16[128,2048]{1,0:T(8,128)(2,1)}, bf16[128,2048]{1,0:T(8,128)(2,1)S(1)}, u32[]{:S(2)}, u32[]{:S(2)}) collective-permute-start(bf16[128,2048]{1,0:T(8,128)(2,1)} %param.8), channel_id=1, source_target_pairs={{0,2},{4,0},{8,4},{12,8},{14,12},{10,14},{6,10},{2,6},{1,3},{5,1},... | collective-permute-start | bytes 1572872 | tf_op jit(solution)/shard_map/ppermute | solution.py:114
  13.4 17.9 %collective-permute-start.6 = (bf16[64,2048]{1,0:T(8,128)(2,1)S(1)}, bf16[64,2048]{1,0:T(8,128)(2,1)S(1)}, u32[]{:S(2)}, u32[]{:S(2)}) collective-permute-start(bf16[64,2048]{1,0:T(8,128)(2,1)S(1)} %get-tuple-element.100), channel_id=1, source_target_pairs={{0,4},{4,8},{8,12},{12,14},{14,10},{10,6},{6,2},{2,0},{1,5},{5,9},... | collective-permute-start | bytes 786440 | tf_op jit(solution)/shard_map/ppermute | solution.py:114
  16.8 8.2 %collective-permute-start.13 = (f32[4,128]{1,0:T(4,128)S(1)}, f32[4,128]{1,0:T(4,128)S(1)}, u32[]{:S(2)}, u32[]{:S(2)}) collective-permute-start(f32[4,128]{1,0:T(4,128)S(1)} %pad_maximum_fusion.11), channel_id=1, source_target_pairs={{0,6},{4,2},{8,0},{12,4},{14,8},{10,12},{6,14},{2,10},{1,7},{5,3},... | collective-permute-start | bytes 6152 | tf_op jit(solution)/shard_map/ppermute | solution.py:114
  35.9 66.4 %collective-permute-start.5 = (bf16[384,2048]{1,0:T(8,128)(2,1)}, bf16[384,2048]{1,0:T(8,128)(2,1)S(1)}, u32[]{:S(2)}, u32[]{:S(2)}) collective-permute-start(bf16[384,2048]{1,0:T(8,128)(2,1)} %bitcast.88), channel_id=1, source_target_pairs={{0,1},{1,0},{2,3},{3,2},{4,5},{5,4},{6,7},{7,6},{8,9},{9,8},{10,11... | collective-permute-start | bytes 4718600 | tf_op jit(solution)/shard_map/ppermute | solution.py:117
  36.0 62.3 %collective-permute-start.9 = (bf16[2048,384]{1,0:T(8,128)(2,1)S(1)}, bf16[2048,384]{1,0:T(8,128)(2,1)S(1)}, u32[]{:S(2)}, u32[]{:S(2)}) collective-permute-start(bf16[2048,384]{1,0:T(8,128)(2,1)S(1)} %bitcast.94), channel_id=1, source_target_pairs={{0,1},{1,0},{2,3},{3,2},{4,5},{5,4},{6,7},{7,6},{8,9},{9,8},{10,11... | collective-permute-start | bytes 4718600 | tf_op jit(solution)/shard_map/ppermute | solution.py:117
  36.6 9.2 %collective-permute-start.17 = (bf16[64,2048]{1,0:T(8,128)(2,1)S(1)}, bf16[64,2048]{1,0:T(8,128)(2,1)S(1)}, u32[]{:S(2)}, u32[]{:S(2)}) collective-permute-start(bf16[64,2048]{1,0:T(8,128)(2,1)S(1)} %collective-permute-done.6), channel_id=1, source_target_pairs={{0,4},{4,8},{8,12},{12,14},{14,10},{10,6},{6,2},{2,0},{1,5},{5,9},... | collective-permute-start | bytes 786440 | tf_op jit(solution)/shard_map/ppermute | solution.py:114
  38.3 13.1 %collective-permute-start.18 = (bf16[64,2048]{1,0:T(8,128)(2,1)S(1)}, bf16[64,2048]{1,0:T(8,128)(2,1)S(1)}, u32[]{:S(2)}, u32[]{:S(2)}) collective-permute-start(bf16[64,2048]{1,0:T(8,128)(2,1)S(1)} %collective-permute-done.7), channel_id=1, source_target_pairs={{0,4},{4,8},{8,12},{12,14},{14,10},{10,6},{6,2},{2,0},{1,5},{5,9},... | collective-permute-start | bytes 786440 | tf_op jit(solution)/shard_map/ppermute | solution.py:114
  38.6 23.2 %collective-permute-start.14 = (bf16[128,2048]{1,0:T(8,128)(2,1)S(1)}, bf16[128,2048]{1,0:T(8,128)(2,1)S(1)}, u32[]{:S(2)}, u32[]{:S(2)}) collective-permute-start(bf16[128,2048]{1,0:T(8,128)(2,1)S(1)} %collective-permute-done.2), channel_id=1, source_target_pairs={{0,4},{4,8},{8,12},{12,14},{14,10},{10,6},{6,2},{2,0},{1,5},{5,9},... | collective-permute-start | bytes 1572872 | tf_op jit(solution)/shard_map/ppermute | solution.py:114
  45.8 18.1 %collective-permute-start.19 = (bf16[128,2048]{1,0:T(8,128)(2,1)S(1)}, bf16[128,2048]{1,0:T(8,128)(2,1)S(1)}, u32[]{:S(2)}, u32[]{:S(2)}) collective-permute-start(bf16[128,2048]{1,0:T(8,128)(2,1)S(1)} %collective-permute-done.8), channel_id=1, source_target_pairs={{0,2},{4,0},{8,4},{12,8},{14,12},{10,14},{6,10},{2,6},{1,3},{5,1},... | collective-permute-start | bytes 1572872 | tf_op jit(solution)/shard_map/ppermute | solution.py:114
  51.4 12.0 %collective-permute-start.15 = (bf16[64,2048]{1,0:T(8,128)(2,1)S(1)}, bf16[64,2048]{1,0:T(8,128)(2,1)S(1)}, u32[]{:S(2)}, u32[]{:S(2)}) collective-permute-start(bf16[64,2048]{1,0:T(8,128)(2,1)S(1)} %collective-permute-done.3), channel_id=1, source_target_pairs={{0,2},{4,0},{8,4},{12,8},{14,12},{10,14},{6,10},{2,6},{1,3},{5,1},... | collective-permute-start | bytes 786440 | tf_op jit(solution)/shard_map/ppermute | solution.py:114
  61.7 42.0 %collective-permute-start.10 = (bf16[2048,384]{1,0:T(8,128)(2,1)S(1)}, bf16[2048,384]{1,0:T(8,128)(2,1)S(1)}, u32[]{:S(2)}, u32[]{:S(2)}) collective-permute-start(bf16[2048,384]{1,0:T(8,128)(2,1)S(1)} %bitcast.105), channel_id=1, source_target_pairs={{0,1},{1,0},{2,3},{3,2},{4,5},{5,4},{6,7},{7,6},{8,9},{9,8},{10,11... | collective-permute-start | bytes 4718600 | tf_op jit(solution)/shard_map/ppermute | solution.py:117
  63.5 9.2 %collective-permute-start.16 = (bf16[64,2048]{1,0:T(8,128)(2,1)S(1)}, bf16[64,2048]{1,0:T(8,128)(2,1)S(1)}, u32[]{:S(2)}, u32[]{:S(2)}) collective-permute-start(bf16[64,2048]{1,0:T(8,128)(2,1)S(1)} %collective-permute-done.4), channel_id=1, source_target_pairs={{0,2},{4,0},{8,4},{12,8},{14,12},{10,14},{6,10},{2,6},{1,3},{5,1},... | collective-permute-start | bytes 786440 | tf_op jit(solution)/shard_map/ppermute | solution.py:114
  63.9 17.9 %collective-permute-start.21 = (bf16[128,2048]{1,0:T(8,128)(2,1)S(1)}, bf16[128,2048]{1,0:T(8,128)(2,1)S(1)}, u32[]{:S(2)}, u32[]{:S(2)}) collective-permute-start(bf16[128,2048]{1,0:T(8,128)(2,1)S(1)} %collective-permute-done.19), channel_id=1, source_target_pairs={{0,2},{4,0},{8,4},{12,8},{14,12},{10,14},{6,10},{2,6},{1,3},{5,1},... | collective-permute-start | bytes 1572872 | tf_op jit(solution)/shard_map/ppermute | solution.py:114
  72.6 10.7 %collective-permute-start.22 = (bf16[128,2048]{1,0:T(8,128)(2,1)S(1)}, bf16[128,2048]{1,0:T(8,128)(2,1)S(1)}, u32[]{:S(2)}, u32[]{:S(2)}) collective-permute-start(bf16[128,2048]{1,0:T(8,128)(2,1)S(1)} %collective-permute-done.14), channel_id=1, source_target_pairs={{0,4},{4,8},{8,12},{12,14},{14,10},{10,6},{6,2},{2,0},{1,5},{5,9},... | collective-permute-start | bytes 1572872 | tf_op jit(solution)/shard_map/ppermute | solution.py:114
  95.1 29.1 %collective-permute-start.11 = (f32[2,128]{1,0:T(2,128)S(1)}, f32[2,128]{1,0:T(2,128)S(1)}, u32[]{:S(2)}, u32[]{:S(2)}) collective-permute-start(f32[2,128]{1,0:T(2,128)S(1)} %get-tuple-element.111), channel_id=1, source_target_pairs={{0,14},{4,10},{8,6},{12,2},{14,0},{10,4},{6,8},{2,12},{1,15},{5,11... | collective-permute-start | bytes 3080 | tf_op jit(solution)/shard_map/ppermute | solution.py:114
  98.1 26.7 %collective-permute-start.24 = (bf16[128,2048]{1,0:T(8,128)(2,1)S(1)}, bf16[128,2048]{1,0:T(8,128)(2,1)S(1)}, u32[]{:S(2)}, u32[]{:S(2)}) collective-permute-start(bf16[128,2048]{1,0:T(8,128)(2,1)S(1)} %collective-permute-done.22), channel_id=1, source_target_pairs={{0,4},{4,8},{8,12},{12,14},{14,10},{10,6},{6,2},{2,0},{1,5},{5,9},... | collective-permute-start | bytes 1572872 | tf_op jit(solution)/shard_map/ppermute | solution.py:114
  98.3 25.9 %collective-permute-start.25 = (bf16[128,2048]{1,0:T(8,128)(2,1)S(1)}, bf16[128,2048]{1,0:T(8,128)(2,1)S(1)}, u32[]{:S(2)}, u32[]{:S(2)}) collective-permute-start(bf16[128,2048]{1,0:T(8,128)(2,1)S(1)} %collective-permute-done.21), channel_id=1, source_target_pairs={{0,2},{4,0},{8,4},{12,8},{14,12},{10,14},{6,10},{2,6},{1,3},{5,1},... | collective-permute-start | bytes 1572872 | tf_op jit(solution)/shard_map/ppermute | solution.py:114
  121.4 26.0 %collective-permute-start.30 = (bf16[64,2048]{1,0:T(8,128)(2,1)S(1)}, bf16[64,2048]{1,0:T(8,128)(2,1)S(1)}, u32[]{:S(2)}, u32[]{:S(2)}) collective-permute-start(bf16[64,2048]{1,0:T(8,128)(2,1)S(1)} %get-tuple-element.90), channel_id=1, source_target_pairs={{0,2},{4,0},{8,4},{12,8},{14,12},{10,14},{6,10},{2,6},{1,3},{5,1},... | collective-permute-start | bytes 786440 | tf_op jit(solution)/shard_map/ppermute | solution.py:114
  123.5 23.8 %collective-permute-start.32 = (bf16[64,2048]{1,0:T(8,128)(2,1)S(1)}, bf16[64,2048]{1,0:T(8,128)(2,1)S(1)}, u32[]{:S(2)}, u32[]{:S(2)}) collective-permute-start(bf16[64,2048]{1,0:T(8,128)(2,1)S(1)} %get-tuple-element.89), channel_id=1, source_target_pairs={{0,4},{4,8},{8,12},{12,14},{14,10},{10,6},{6,2},{2,0},{1,5},{5,9},... | collective-permute-start | bytes 786440 | tf_op jit(solution)/shard_map/ppermute | solution.py:114
  129.8 14.8 %collective-permute-start.31 = (bf16[64,2048]{1,0:T(8,128)(2,1)S(1)}, bf16[64,2048]{1,0:T(8,128)(2,1)S(1)}, u32[]{:S(2)}, u32[]{:S(2)}) collective-permute-start(bf16[64,2048]{1,0:T(8,128)(2,1)S(1)} %get-tuple-element.93), channel_id=1, source_target_pairs={{0,4},{4,8},{8,12},{12,14},{14,10},{10,6},{6,2},{2,0},{1,5},{5,9},... | collective-permute-start | bytes 786440 | tf_op jit(solution)/shard_map/ppermute | solution.py:114
  129.9 15.3 %collective-permute-start.26 = (bf16[64,2048]{1,0:T(8,128)(2,1)S(1)}, bf16[64,2048]{1,0:T(8,128)(2,1)S(1)}, u32[]{:S(2)}, u32[]{:S(2)}) collective-permute-start(bf16[64,2048]{1,0:T(8,128)(2,1)S(1)} %get-tuple-element.94), channel_id=1, source_target_pairs={{0,2},{4,0},{8,4},{12,8},{14,12},{10,14},{6,10},{2,6},{1,3},{5,1},... | collective-permute-start | bytes 786440 | tf_op jit(solution)/shard_map/ppermute | solution.py:114
  138.2 47.2 %collective-permute-start.42 = (bf16[2048,384]{1,0:T(8,128)(2,1)S(1)}, bf16[2048,384]{1,0:T(8,128)(2,1)S(1)}, u32[]{:S(2)}, u32[]{:S(2)}) collective-permute-start(bf16[2048,384]{1,0:T(8,128)(2,1)S(1)} %split.25), channel_id=1, source_target_pairs={{0,1},{1,0},{2,3},{3,2},{4,5},{5,4},{6,7},{7,6},{8,9},{9,8},{10,11... | collective-permute-start | bytes 4718600 | tf_op jit(solution)/shard_map/ppermute | solution.py:117
  144.6 42.4 %collective-permute-start.43 = (bf16[2048,384]{1,0:T(8,128)(2,1)S(1)}, bf16[2048,384]{1,0:T(8,128)(2,1)S(1)}, u32[]{:S(2)}, u32[]{:S(2)}) collective-permute-start(bf16[2048,384]{1,0:T(8,128)(2,1)S(1)} %split.27), channel_id=1, source_target_pairs={{0,1},{1,0},{2,3},{3,2},{4,5},{5,4},{6,7},{7,6},{8,9},{9,8},{10,11... | collective-permute-start | bytes 4718600 | tf_op jit(solution)/shard_map/ppermute | solution.py:117
  145.2 8.3 %collective-permute-start.29 = (bf16[64,2048]{1,0:T(8,128)(2,1)S(1)}, bf16[64,2048]{1,0:T(8,128)(2,1)S(1)}, u32[]{:S(2)}, u32[]{:S(2)}) collective-permute-start(bf16[64,2048]{1,0:T(8,128)(2,1)S(1)} %get-tuple-element.92), channel_id=1, source_target_pairs={{0,2},{4,0},{8,4},{12,8},{14,12},{10,14},{6,10},{2,6},{1,3},{5,1},... | collective-permute-start | bytes 786440 | tf_op jit(solution)/shard_map/ppermute | solution.py:114
  147.3 9.2 %collective-permute-start.35 = (bf16[64,2048]{1,0:T(8,128)(2,1)S(1)}, bf16[64,2048]{1,0:T(8,128)(2,1)S(1)}, u32[]{:S(2)}, u32[]{:S(2)}) collective-permute-start(bf16[64,2048]{1,0:T(8,128)(2,1)S(1)} %get-tuple-element.91), channel_id=1, source_target_pairs={{0,4},{4,8},{8,12},{12,14},{14,10},{10,6},{6,2},{2,0},{1,5},{5,9},... | collective-permute-start | bytes 786440 | tf_op jit(solution)/shard_map/ppermute | solution.py:114
  147.4 13.5 %collective-permute-start.36 = (bf16[64,2048]{1,0:T(8,128)(2,1)S(1)}, bf16[64,2048]{1,0:T(8,128)(2,1)S(1)}, u32[]{:S(2)}, u32[]{:S(2)}) collective-permute-start(bf16[64,2048]{1,0:T(8,128)(2,1)S(1)} %add_convert_fusion.12), channel_id=1, source_target_pairs={{0,4},{4,8},{8,12},{12,14},{14,10},{10,6},{6,2},{2,0},{1,5},{5,9},... | collective-permute-start | bytes 786440 | tf_op jit(solution)/shard_map/ppermute | solution.py:114
  153.6 9.2 %collective-permute-start.34 = (bf16[64,2048]{1,0:T(8,128)(2,1)S(1)}, bf16[64,2048]{1,0:T(8,128)(2,1)S(1)}, u32[]{:S(2)}, u32[]{:S(2)}) collective-permute-start(bf16[64,2048]{1,0:T(8,128)(2,1)S(1)} %add_convert_fusion.13), channel_id=1, source_target_pairs={{0,2},{4,0},{8,4},{12,8},{14,12},{10,14},{6,10},{2,6},{1,3},{5,1},... | collective-permute-start | bytes 786440 | tf_op jit(solution)/shard_map/ppermute | solution.py:114
  156.5 11.9 %collective-permute-start.33 = (bf16[64,2048]{1,0:T(8,128)(2,1)S(1)}, bf16[64,2048]{1,0:T(8,128)(2,1)S(1)}, u32[]{:S(2)}, u32[]{:S(2)}) collective-permute-start(bf16[64,2048]{1,0:T(8,128)(2,1)S(1)} %add_convert_fusion.11), channel_id=1, source_target_pairs={{0,2},{4,0},{8,4},{12,8},{14,12},{10,14},{6,10},{2,6},{1,3},{5,1},... | collective-permute-start | bytes 786440 | tf_op jit(solution)/shard_map/ppermute | solution.py:114
  160.9 16.7 %collective-permute-start.38 = (bf16[64,2048]{1,0:T(8,128)(2,1)S(1)}, bf16[64,2048]{1,0:T(8,128)(2,1)S(1)}, u32[]{:S(2)}, u32[]{:S(2)}) collective-permute-start(bf16[64,2048]{1,0:T(8,128)(2,1)S(1)} %add_convert_fusion.8), channel_id=1, source_target_pairs={{0,4},{4,8},{8,12},{12,14},{14,10},{10,6},{6,2},{2,0},{1,5},{5,9},... | collective-permute-start | bytes 786440 | tf_op jit(solution)/shard_map/ppermute | solution.py:114
  162.8 19.0 %collective-permute-start.41 = (bf16[64,2048]{1,0:T(8,128)(2,1)S(1)}, bf16[64,2048]{1,0:T(8,128)(2,1)S(1)}, u32[]{:S(2)}, u32[]{:S(2)}) collective-permute-start(bf16[64,2048]{1,0:T(8,128)(2,1)S(1)} %add_convert_fusion.9), channel_id=1, source_target_pairs={{0,2},{4,0},{8,4},{12,8},{14,12},{10,14},{6,10},{2,6},{1,3},{5,1},... | collective-permute-start | bytes 786440 | tf_op jit(solution)/shard_map/ppermute | solution.py:114
  (19 other events, 189.5 us)

commit v8 on v7

--- a/solution.py
+++ b/solution.py
@@ -217,20 +217,17 @@
     def far_piece():
         return step_piece([far[0]], [far[1]], [blocks[groups // 2]]) if has_far else None
 
+    far_part = far_piece()
     if full_steps:
         k = full_steps
         lefts, rights = from_left[k - 1], from_right[k - 1]
         parts[k] = [{}, {}]
-        for name, one, two in (("a", high, low), ("b", low, high)):
-            if name == "b":
-                far_part = far_piece()
+        for one, two in ((high, low), (low, high)):
             ratio = [ratio_from(-k)[:, one], ratio_from(k)[:, two]]
             part = step_piece(
                 [lefts[0][one], rights[0][two]], [lefts[1][one], rights[1][two]], ratio, apart=True
             )
             parts[k][0][one], parts[k][1][two] = part[:half], part[half:]
-    else:
-        far_part = far_piece()
 
     def join(moved, part):
         return (moved.astype(jnp.float32) + part.astype(jnp.float32)).astype(jnp.bfloat16)

time: 191 us -> 188 us (0.984)
  matrix products: 41.7 us -> 39.6 us
    dot_general x28, matrix products: 41.7 us -> 39.6 us  [mm(): return lax.dot_general(a, b, dims, preferred_element_type=jnp.float32)]
  transfers between devices with their start and end apart: 45 -> 45, of which waited for: 20 -> 20; matrix products, arithmetic and copies ran while one was open for 28% -> 25% of each run, Pallas kernels for 0% -> 0%
where the time goes in v8:
time: 188 us
  waiting for transfers between devices  86.1 us (46%)
  starting transfers between devices  46.5 us (25%)
  matrix products  39.6 us (21%)
  other arithmetic  9.96 us (5%)
  local copies, waits for them, and re-layouts  4.51 us (2%)
    ppermute x39, waiting for transfers between devices, shift(): return lax.ppermute(array, 'grp', at_distance(k))  86.1 us
    ppermute x39, starting transfers between devices, shift(): return lax.ppermute(array, 'grp', at_distance(k))  45.2 us
    dot_general x28, matrix products, mm(): return lax.dot_general(a, b, dims, preferred_element_type=jnp.float32)  39.6 us
    broadcast_in_dim x3, other arithmetic, member_sum(): return total.astype(jnp.bfloat16)[None]  4.82 us
  transfers between devices with their start and end apart: 45, of which 20 were waited for; matrix products, arithmetic and copies ran while one was open for 25% of the time, Pallas kernels for 0%

profile of v8, /device:TPU:0, one launch (start us, length us, event | category | flops | bytes accessed | tf_op | source)
XLA Modules:
  0.0 188.1 jit_solution(14934472688012821854)
XLA Ops:
  0.6 3.1 %collective-permute-start.2 = (bf16[128,2048]{1,0:T(8,128)(2,1)}, bf16[128,2048]{1,0:T(8,128)(2,1)S(1)}, u32[]{:S(2)}, u32[]{:S(2)}) collective-permute-start(bf16[128,2048]{1,0:T(8,128)(2,1)} %param.9), channel_id=1, source_target_pairs={{0,4},{4,8},{8,12},{12,14},{14,10},{10,6},{6,2},{2,0},{1,5},{5,9},... | collective-permute-start | bytes 1572872 | tf_op jit(solution)/shard_map/ppermute | solution.py:114
  8.1 1.9 %collective-permute-start.1 = (f32[4,128]{1,0:T(4,128)S(1)}, f32[4,128]{1,0:T(4,128)S(1)}, u32[]{:S(2)}, u32[]{:S(2)}) collective-permute-start(f32[4,128]{1,0:T(4,128)S(1)} %pad_maximum_fusion.9), channel_id=1, source_target_pairs={{0,2},{4,0},{8,4},{12,8},{14,12},{10,14},{6,10},{2,6},{1,3},{5,1},... | collective-permute-start | bytes 6152 | tf_op jit(solution)/shard_map/ppermute | solution.py:114
  10.2 1.9 collective-permute-start.8
  14.9 1.8 collective-permute-done
  16.8 3.1 %collective-permute-start.13 = (f32[4,128]{1,0:T(4,128)S(1)}, f32[4,128]{1,0:T(4,128)S(1)}, u32[]{:S(2)}, u32[]{:S(2)}) collective-permute-start(f32[4,128]{1,0:T(4,128)S(1)} %pad_maximum_fusion.11), channel_id=1, source_target_pairs={{0,6},{4,2},{8,0},{12,4},{14,8},{10,12},{6,14},{2,10},{1,7},{5,3},... | collective-permute-start | bytes 6152 | tf_op jit(solution)/shard_map/ppermute | solution.py:114
  19.9 5.1 %collective-permute-done.13 = f32[4,128]{1,0:T(4,128)S(1)} collective-permute-done((f32[4,128]{1,0:T(4,128)S(1)}, f32[4,128]{1,0:T(4,128)S(1)}, u32[]{:S(2)}, u32[]{:S(2)}) %collective-permute-start.13) | collective-permute-done | bytes 2080 | tf_op jit(solution)/shard_map/ppermute | solution.py:114
  25.4 4.1 %collective-permute-done.12 = f32[4,128]{1,0:T(4,128)S(1)} collective-permute-done((f32[4,128]{1,0:T(4,128)S(1)}, f32[4,128]{1,0:T(4,128)S(1)}, u32[]{:S(2)}, u32[]{:S(2)}) %collective-permute-start.12) | collective-permute-done | bytes 2080 | tf_op jit(solution)/shard_map/ppermute | solution.py:114
  31.8 4.0 %collective-permute-done.7 = bf16[64,2048]{1,0:T(8,128)(2,1)S(1)} collective-permute-done((bf16[64,2048]{1,0:T(8,128)(2,1)S(1)}, bf16[64,2048]{1,0:T(8,128)(2,1)S(1)}, u32[]{:S(2)}, u32[]{:S(2)}) %collective-permute-start.7) | collective-permute-done | bytes 262176 | tf_op jit(solution)/shard_map/ppermute | solution.py:114
  38.6 2.5 %collective-permute-start.14 = (bf16[128,2048]{1,0:T(8,128)(2,1)S(1)}, bf16[128,2048]{1,0:T(8,128)(2,1)S(1)}, u32[]{:S(2)}, u32[]{:S(2)}) collective-permute-start(bf16[128,2048]{1,0:T(8,128)(2,1)S(1)} %collective-permute-done.2), channel_id=1, source_target_pairs={{0,4},{4,8},{8,12},{12,14},{14,10},{10,6},{6,2},{2,0},{1,5},{5,9},... | collective-permute-start | bytes 1572872 | tf_op jit(solution)/shard_map/ppermute | solution.py:114
  41.2 4.6 %collective-permute-done.17 = bf16[64,2048]{1,0:T(8,128)(2,1)S(1)} collective-permute-done((bf16[64,2048]{1,0:T(8,128)(2,1)S(1)}, bf16[64,2048]{1,0:T(8,128)(2,1)S(1)}, u32[]{:S(2)}, u32[]{:S(2)}) %collective-permute-start.17) | collective-permute-done | bytes 262176 | tf_op jit(solution)/shard_map/ppermute | solution.py:114
  46.3 5.1 %collective-permute-done.18 = bf16[64,2048]{1,0:T(8,128)(2,1)S(1)} collective-permute-done((bf16[64,2048]{1,0:T(8,128)(2,1)S(1)}, bf16[64,2048]{1,0:T(8,128)(2,1)S(1)}, u32[]{:S(2)}, u32[]{:S(2)}) %collective-permute-start.18) | collective-permute-done | bytes 262176 | tf_op jit(solution)/shard_map/ppermute | solution.py:114
  51.9 9.8 %collective-permute-done.14 = bf16[128,2048]{1,0:T(8,128)(2,1)S(1)} collective-permute-done((bf16[128,2048]{1,0:T(8,128)(2,1)S(1)}, bf16[128,2048]{1,0:T(8,128)(2,1)S(1)}, u32[]{:S(2)}, u32[]{:S(2)}) %collective-permute-start.14) | collective-permute-done | bytes 524320 | tf_op jit(solution)/shard_map/ppermute | solution.py:114
  65.1 7.6 %collective-permute-done.16 = bf16[64,2048]{1,0:T(8,128)(2,1)S(1)} collective-permute-done((bf16[64,2048]{1,0:T(8,128)(2,1)S(1)}, bf16[64,2048]{1,0:T(8,128)(2,1)S(1)}, u32[]{:S(2)}, u32[]{:S(2)}) %collective-permute-start.16) | collective-permute-done | bytes 262176 | tf_op jit(solution)/shard_map/ppermute | solution.py:114
  74.2 7.6 %collective-permute-done.22 = bf16[128,2048]{1,0:T(8,128)(2,1)S(1)} collective-permute-done((bf16[128,2048]{1,0:T(8,128)(2,1)S(1)}, bf16[128,2048]{1,0:T(8,128)(2,1)S(1)}, u32[]{:S(2)}, u32[]{:S(2)}) %collective-permute-start.22) | collective-permute-done | bytes 524320 | tf_op jit(solution)/shard_map/ppermute | solution.py:114
  84.0 4.7 %collective-permute-done.25 = bf16[64,2048]{1,0:T(8,128)(2,1)S(1)} collective-permute-done((bf16[64,2048]{1,0:T(8,128)(2,1)S(1)}, bf16[64,2048]{1,0:T(8,128)(2,1)S(1)}, u32[]{:S(2)}, u32[]{:S(2)}) %collective-permute-start.25) | collective-permute-done | bytes 262176 | tf_op jit(solution)/shard_map/ppermute | solution.py:114
  90.9 4.2 %collective-permute-done.27 = bf16[64,2048]{1,0:T(8,128)(2,1)S(1)} collective-permute-done((bf16[64,2048]{1,0:T(8,128)(2,1)S(1)}, bf16[64,2048]{1,0:T(8,128)(2,1)S(1)}, u32[]{:S(2)}, u32[]{:S(2)}) %collective-permute-start.27) | collective-permute-done | bytes 262176 | tf_op jit(solution)/shard_map/ppermute | solution.py:114
  95.1 3.0 %collective-permute-start.11 = (f32[2,128]{1,0:T(2,128)S(1)}, f32[2,128]{1,0:T(2,128)S(1)}, u32[]{:S(2)}, u32[]{:S(2)}) collective-permute-start(f32[2,128]{1,0:T(2,128)S(1)} %get-tuple-element.111), channel_id=1, source_target_pairs={{0,14},{4,10},{8,6},{12,2},{14,0},{10,4},{6,8},{2,12},{1,15},{5,11... | collective-permute-start | bytes 3080 | tf_op jit(solution)/shard_map/ppermute | solution.py:114
  98.2 2.6 %collective-permute-start.23 = (bf16[128,2048]{1,0:T(8,128)(2,1)S(1)}, bf16[128,2048]{1,0:T(8,128)(2,1)S(1)}, u32[]{:S(2)}, u32[]{:S(2)}) collective-permute-start(bf16[128,2048]{1,0:T(8,128)(2,1)S(1)} %collective-permute-done.22), channel_id=1, source_target_pairs={{0,2},{4,0},{8,4},{12,8},{14,12},{10,14},{6,10},{2,6},{1,3},{5,1},... | collective-permute-start | bytes 1572872 | tf_op jit(solution)/shard_map/ppermute | solution.py:114
  103.7 2.6 %constant_dynamic-update-slice_fusion.21 = (bf16[1024,768]{1,0:T(8,128)(2,1)S(1)}, bf16[384,768]{1,0:T(8,128)(2,1)S(1)}, bf16[1024,768]{1,0:T(8,128)(2,1)S(1)}, bf16[1024,768]{1,0:T(8,128)(2,1)}, bf16[384,768]{1,0:T(8,128)(2,1)S(1)}) fusion(f32[384,768]{1,0:T(8,128)S(1)} %select_multiply_fusion.1, f32[384,768]{1,0:T(8,128)S(1)} %fusion.57, ...), kind=kOutput, calls=%fused_computation.115 | convolution fusion | flops 1219264512 | bytes 10030848 | tf_op jit(solution)/shard_map/dot_general | solution.py:97
  123.6 2.1 %collective-permute-start.24 = (bf16[64,2048]{1,0:T(8,128)(2,1)S(1)}, bf16[64,2048]{1,0:T(8,128)(2,1)S(1)}, u32[]{:S(2)}, u32[]{:S(2)}) collective-permute-start(bf16[64,2048]{1,0:T(8,128)(2,1)S(1)} %get-tuple-element.94), channel_id=1, source_target_pairs={{0,2},{4,0},{8,4},{12,8},{14,12},{10,14},{6,10},{2,6},{1,3},{5,1},... | collective-permute-start | bytes 786440 | tf_op jit(solution)/shard_map/ppermute | solution.py:114
  128.0 1.8 collective-permute-start.30
  132.3 3.8 %convolution_convert_fusion.2 = bf16[2048,768]{1,0:T(8,128)(2,1)S(1)} fusion(bf16[1024,2048]{1,0:T(8,128)(2,1)S(1)} %constant_dynamic-update-slice_fusion.7, bf16[1024,768]{1,0:T(8,128)(2,1)S(1)} %get-tuple-element.48), kind=kOutput, calls=%fused_computation.2 | convolution fusion | flops 3222798336 | bytes 8912896 | tf_op jit(solution)/shard_map/dot_general | solution.py:97
  136.3 3.8 %convolution_convert_fusion.1 = bf16[2048,768]{1,0:T(8,128)(2,1)S(1)} fusion(bf16[1024,2048]{1,0:T(8,128)(2,1)S(1)} %constant_dynamic-update-slice_fusion.7, bf16[1024,768]{1,0:T(8,128)(2,1)S(1)} %get-tuple-element.75), kind=kOutput, calls=%fused_computation.1 | convolution fusion | flops 3222798336 | bytes 8912896 | tf_op jit(solution)/shard_map/dot_general | solution.py:97
  143.3 1.8 collective-permute-start.29
  145.6 6.0 %collective-permute-done.29 = bf16[64,2048]{1,0:T(8,128)(2,1)S(1)} collective-permute-done((bf16[64,2048]{1,0:T(8,128)(2,1)S(1)}, bf16[64,2048]{1,0:T(8,128)(2,1)S(1)}, u32[]{:S(2)}, u32[]{:S(2)}) %collective-permute-start.29) | collective-permute-done | bytes 262176 | tf_op jit(solution)/shard_map/ppermute | solution.py:114
  154.5 4.3 %collective-permute-done.36 = bf16[64,2048]{1,0:T(8,128)(2,1)S(1)} collective-permute-done((bf16[64,2048]{1,0:T(8,128)(2,1)S(1)}, bf16[64,2048]{1,0:T(8,128)(2,1)S(1)}, u32[]{:S(2)}, u32[]{:S(2)}) %collective-permute-start.36) | collective-permute-done | bytes 262176 | tf_op jit(solution)/shard_map/ppermute | solution.py:114
  160.9 1.8 collective-permute-start.41
  162.7 3.7 %collective-permute-done.33 = bf16[64,2048]{1,0:T(8,128)(2,1)S(1)} collective-permute-done((bf16[64,2048]{1,0:T(8,128)(2,1)S(1)}, bf16[64,2048]{1,0:T(8,128)(2,1)S(1)}, u32[]{:S(2)}, u32[]{:S(2)}) %collective-permute-start.33) | collective-permute-done | bytes 262176 | tf_op jit(solution)/shard_map/ppermute | solution.py:114
  166.5 6.3 %collective-permute-done.39 = bf16[64,2048]{1,0:T(8,128)(2,1)S(1)} collective-permute-done((bf16[64,2048]{1,0:T(8,128)(2,1)S(1)}, bf16[64,2048]{1,0:T(8,128)(2,1)S(1)}, u32[]{:S(2)}, u32[]{:S(2)}) %collective-permute-start.39) | collective-permute-done | bytes 262176 | tf_op jit(solution)/shard_map/ppermute | solution.py:114
  172.8 2.6 %collective-permute-start.37 = (bf16[64,2048]{1,0:T(8,128)(2,1)S(1)}, bf16[64,2048]{1,0:T(8,128)(2,1)S(1)}, u32[]{:S(2)}, u32[]{:S(2)}) collective-permute-start(bf16[64,2048]{1,0:T(8,128)(2,1)S(1)} %add_convert_fusion.7), channel_id=1, source_target_pairs={{0,2},{4,0},{8,4},{12,8},{14,12},{10,14},{6,10},{2,6},{1,3},{5,1},... | collective-permute-start | bytes 786440 | tf_op jit(solution)/shard_map/ppermute | solution.py:114
  175.8 3.7 %convolution_convert_fusion = bf16[768,2048]{1,0:T(8,128)(2,1)S(1)} fusion(bf16[1024,768]{1,0:T(8,128)(2,1)S(1)} %get-tuple-element.74, bf16[1024,2048]{1,0:T(8,128)(2,1)S(1)} %constant_dynamic-update-slice_fusion.27), kind=kOutput, calls=%fused_computation | convolution fusion | flops 3222798336 | bytes 8912896 | tf_op jit(solution)/shard_map/dot_general | solution.py:97
  179.7 2.4 %collective-permute-done.40 = bf16[64,2048]{1,0:T(8,128)(2,1)S(1)} collective-permute-done((bf16[64,2048]{1,0:T(8,128)(2,1)S(1)}, bf16[64,2048]{1,0:T(8,128)(2,1)S(1)}, u32[]{:S(2)}, u32[]{:S(2)}) %collective-permute-start.40) | collective-permute-done | bytes 262176 | tf_op jit(solution)/shard_map/ppermute | solution.py:114
  (175 shorter events, 63.1 us)
Async XLA Ops:
  0.6 35.3 %collective-permute-start.2 = (bf16[128,2048]{1,0:T(8,128)(2,1)}, bf16[128,2048]{1,0:T(8,128)(2,1)S(1)}, u32[]{:S(2)}, u32[]{:S(2)}) collective-permute-start(bf16[128,2048]{1,0:T(8,128)(2,1)} %param.9), channel_id=1, source_target_pairs={{0,4},{4,8},{8,12},{12,14},{14,10},{10,6},{6,2},{2,0},{1,5},{5,9},... | collective-permute-start | bytes 1572872 | tf_op jit(solution)/shard_map/ppermute | solution.py:114
  4.8 33.7 %collective-permute-start.4 = (bf16[64,2048]{1,0:T(8,128)(2,1)S(1)}, bf16[64,2048]{1,0:T(8,128)(2,1)S(1)}, u32[]{:S(2)}, u32[]{:S(2)}) collective-permute-start(bf16[64,2048]{1,0:T(8,128)(2,1)S(1)} %get-tuple-element.102), channel_id=1, source_target_pairs={{0,2},{4,0},{8,4},{12,8},{14,12},{10,14},{6,10},{2,6},{1,3},{5,1},... | collective-permute-start | bytes 786440 | tf_op jit(solution)/shard_map/ppermute | solution.py:114
  10.2 26.4 %collective-permute-start.8 = (bf16[128,2048]{1,0:T(8,128)(2,1)}, bf16[128,2048]{1,0:T(8,128)(2,1)S(1)}, u32[]{:S(2)}, u32[]{:S(2)}) collective-permute-start(bf16[128,2048]{1,0:T(8,128)(2,1)} %param.8), channel_id=1, source_target_pairs={{0,2},{4,0},{8,4},{12,8},{14,12},{10,14},{6,10},{2,6},{1,3},{5,1},... | collective-permute-start | bytes 1572872 | tf_op jit(solution)/shard_map/ppermute | solution.py:114
  13.4 17.9 %collective-permute-start.6 = (bf16[64,2048]{1,0:T(8,128)(2,1)S(1)}, bf16[64,2048]{1,0:T(8,128)(2,1)S(1)}, u32[]{:S(2)}, u32[]{:S(2)}) collective-permute-start(bf16[64,2048]{1,0:T(8,128)(2,1)S(1)} %get-tuple-element.100), channel_id=1, source_target_pairs={{0,4},{4,8},{8,12},{12,14},{14,10},{10,6},{6,2},{2,0},{1,5},{5,9},... | collective-permute-start | bytes 786440 | tf_op jit(solution)/shard_map/ppermute | solution.py:114
  16.8 8.2 %collective-permute-start.13 = (f32[4,128]{1,0:T(4,128)S(1)}, f32[4,128]{1,0:T(4,128)S(1)}, u32[]{:S(2)}, u32[]{:S(2)}) collective-permute-start(f32[4,128]{1,0:T(4,128)S(1)} %pad_maximum_fusion.11), channel_id=1, source_target_pairs={{0,6},{4,2},{8,0},{12,4},{14,8},{10,12},{6,14},{2,10},{1,7},{5,3},... | collective-permute-start | bytes 6152 | tf_op jit(solution)/shard_map/ppermute | solution.py:114
  35.9 66.3 %collective-permute-start.5 = (bf16[384,2048]{1,0:T(8,128)(2,1)}, bf16[384,2048]{1,0:T(8,128)(2,1)S(1)}, u32[]{:S(2)}, u32[]{:S(2)}) collective-permute-start(bf16[384,2048]{1,0:T(8,128)(2,1)} %bitcast.88), channel_id=1, source_target_pairs={{0,1},{1,0},{2,3},{3,2},{4,5},{5,4},{6,7},{7,6},{8,9},{9,8},{10,11... | collective-permute-start | bytes 4718600 | tf_op jit(solution)/shard_map/ppermute | solution.py:117
  36.0 62.2 %collective-permute-start.9 = (bf16[2048,384]{1,0:T(8,128)(2,1)S(1)}, bf16[2048,384]{1,0:T(8,128)(2,1)S(1)}, u32[]{:S(2)}, u32[]{:S(2)}) collective-permute-start(bf16[2048,384]{1,0:T(8,128)(2,1)S(1)} %bitcast.94), channel_id=1, source_target_pairs={{0,1},{1,0},{2,3},{3,2},{4,5},{5,4},{6,7},{7,6},{8,9},{9,8},{10,11... | collective-permute-start | bytes 4718600 | tf_op jit(solution)/shard_map/ppermute | solution.py:117
  36.6 9.2 %collective-permute-start.17 = (bf16[64,2048]{1,0:T(8,128)(2,1)S(1)}, bf16[64,2048]{1,0:T(8,128)(2,1)S(1)}, u32[]{:S(2)}, u32[]{:S(2)}) collective-permute-start(bf16[64,2048]{1,0:T(8,128)(2,1)S(1)} %collective-permute-done.6), channel_id=1, source_target_pairs={{0,4},{4,8},{8,12},{12,14},{14,10},{10,6},{6,2},{2,0},{1,5},{5,9},... | collective-permute-start | bytes 786440 | tf_op jit(solution)/shard_map/ppermute | solution.py:114
  38.3 13.1 %collective-permute-start.18 = (bf16[64,2048]{1,0:T(8,128)(2,1)S(1)}, bf16[64,2048]{1,0:T(8,128)(2,1)S(1)}, u32[]{:S(2)}, u32[]{:S(2)}) collective-permute-start(bf16[64,2048]{1,0:T(8,128)(2,1)S(1)} %collective-permute-done.7), channel_id=1, source_target_pairs={{0,4},{4,8},{8,12},{12,14},{14,10},{10,6},{6,2},{2,0},{1,5},{5,9},... | collective-permute-start | bytes 786440 | tf_op jit(solution)/shard_map/ppermute | solution.py:114
  38.6 23.2 %collective-permute-start.14 = (bf16[128,2048]{1,0:T(8,128)(2,1)S(1)}, bf16[128,2048]{1,0:T(8,128)(2,1)S(1)}, u32[]{:S(2)}, u32[]{:S(2)}) collective-permute-start(bf16[128,2048]{1,0:T(8,128)(2,1)S(1)} %collective-permute-done.2), channel_id=1, source_target_pairs={{0,4},{4,8},{8,12},{12,14},{14,10},{10,6},{6,2},{2,0},{1,5},{5,9},... | collective-permute-start | bytes 1572872 | tf_op jit(solution)/shard_map/ppermute | solution.py:114
  45.8 18.1 %collective-permute-start.19 = (bf16[128,2048]{1,0:T(8,128)(2,1)S(1)}, bf16[128,2048]{1,0:T(8,128)(2,1)S(1)}, u32[]{:S(2)}, u32[]{:S(2)}) collective-permute-start(bf16[128,2048]{1,0:T(8,128)(2,1)S(1)} %collective-permute-done.8), channel_id=1, source_target_pairs={{0,2},{4,0},{8,4},{12,8},{14,12},{10,14},{6,10},{2,6},{1,3},{5,1},... | collective-permute-start | bytes 1572872 | tf_op jit(solution)/shard_map/ppermute | solution.py:114
  51.4 12.0 %collective-permute-start.15 = (bf16[64,2048]{1,0:T(8,128)(2,1)S(1)}, bf16[64,2048]{1,0:T(8,128)(2,1)S(1)}, u32[]{:S(2)}, u32[]{:S(2)}) collective-permute-start(bf16[64,2048]{1,0:T(8,128)(2,1)S(1)} %collective-permute-done.3), channel_id=1, source_target_pairs={{0,2},{4,0},{8,4},{12,8},{14,12},{10,14},{6,10},{2,6},{1,3},{5,1},... | collective-permute-start | bytes 786440 | tf_op jit(solution)/shard_map/ppermute | solution.py:114
  61.7 41.9 %collective-permute-start.10 = (bf16[2048,384]{1,0:T(8,128)(2,1)S(1)}, bf16[2048,384]{1,0:T(8,128)(2,1)S(1)}, u32[]{:S(2)}, u32[]{:S(2)}) collective-permute-start(bf16[2048,384]{1,0:T(8,128)(2,1)S(1)} %bitcast.105), channel_id=1, source_target_pairs={{0,1},{1,0},{2,3},{3,2},{4,5},{5,4},{6,7},{7,6},{8,9},{9,8},{10,11... | collective-permute-start | bytes 4718600 | tf_op jit(solution)/shard_map/ppermute | solution.py:117
  63.5 9.2 %collective-permute-start.16 = (bf16[64,2048]{1,0:T(8,128)(2,1)S(1)}, bf16[64,2048]{1,0:T(8,128)(2,1)S(1)}, u32[]{:S(2)}, u32[]{:S(2)}) collective-permute-start(bf16[64,2048]{1,0:T(8,128)(2,1)S(1)} %collective-permute-done.4), channel_id=1, source_target_pairs={{0,2},{4,0},{8,4},{12,8},{14,12},{10,14},{6,10},{2,6},{1,3},{5,1},... | collective-permute-start | bytes 786440 | tf_op jit(solution)/shard_map/ppermute | solution.py:114
  63.9 17.9 %collective-permute-start.22 = (bf16[128,2048]{1,0:T(8,128)(2,1)S(1)}, bf16[128,2048]{1,0:T(8,128)(2,1)S(1)}, u32[]{:S(2)}, u32[]{:S(2)}) collective-permute-start(bf16[128,2048]{1,0:T(8,128)(2,1)S(1)} %collective-permute-done.19), channel_id=1, source_target_pairs={{0,2},{4,0},{8,4},{12,8},{14,12},{10,14},{6,10},{2,6},{1,3},{5,1},... | collective-permute-start | bytes 1572872 | tf_op jit(solution)/shard_map/ppermute | solution.py:114
  72.6 10.7 %collective-permute-start.20 = (bf16[128,2048]{1,0:T(8,128)(2,1)S(1)}, bf16[128,2048]{1,0:T(8,128)(2,1)S(1)}, u32[]{:S(2)}, u32[]{:S(2)}) collective-permute-start(bf16[128,2048]{1,0:T(8,128)(2,1)S(1)} %collective-permute-done.14), channel_id=1, source_target_pairs={{0,4},{4,8},{8,12},{12,14},{14,10},{10,6},{6,2},{2,0},{1,5},{5,9},... | collective-permute-start | bytes 1572872 | tf_op jit(solution)/shard_map/ppermute | solution.py:114
  95.1 21.3 %collective-permute-start.11 = (f32[2,128]{1,0:T(2,128)S(1)}, f32[2,128]{1,0:T(2,128)S(1)}, u32[]{:S(2)}, u32[]{:S(2)}) collective-permute-start(f32[2,128]{1,0:T(2,128)S(1)} %get-tuple-element.111), channel_id=1, source_target_pairs={{0,14},{4,10},{8,6},{12,2},{14,0},{10,4},{6,8},{2,12},{1,15},{5,11... | collective-permute-start | bytes 3080 | tf_op jit(solution)/shard_map/ppermute | solution.py:114
  98.1 18.9 %collective-permute-start.21 = (bf16[128,2048]{1,0:T(8,128)(2,1)S(1)}, bf16[128,2048]{1,0:T(8,128)(2,1)S(1)}, u32[]{:S(2)}, u32[]{:S(2)}) collective-permute-start(bf16[128,2048]{1,0:T(8,128)(2,1)S(1)} %collective-permute-done.20), channel_id=1, source_target_pairs={{0,4},{4,8},{8,12},{12,14},{14,10},{10,6},{6,2},{2,0},{1,5},{5,9},... | collective-permute-start | bytes 1572872 | tf_op jit(solution)/shard_map/ppermute | solution.py:114
  98.2 18.2 %collective-permute-start.23 = (bf16[128,2048]{1,0:T(8,128)(2,1)S(1)}, bf16[128,2048]{1,0:T(8,128)(2,1)S(1)}, u32[]{:S(2)}, u32[]{:S(2)}) collective-permute-start(bf16[128,2048]{1,0:T(8,128)(2,1)S(1)} %collective-permute-done.22), channel_id=1, source_target_pairs={{0,2},{4,0},{8,4},{12,8},{14,12},{10,14},{6,10},{2,6},{1,3},{5,1},... | collective-permute-start | bytes 1572872 | tf_op jit(solution)/shard_map/ppermute | solution.py:114
  121.6 21.1 %collective-permute-start.31 = (bf16[64,2048]{1,0:T(8,128)(2,1)S(1)}, bf16[64,2048]{1,0:T(8,128)(2,1)S(1)}, u32[]{:S(2)}, u32[]{:S(2)}) collective-permute-start(bf16[64,2048]{1,0:T(8,128)(2,1)S(1)} %get-tuple-element.93), channel_id=1, source_target_pairs={{0,4},{4,8},{8,12},{12,14},{14,10},{10,6},{6,2},{2,0},{1,5},{5,9},... | collective-permute-start | bytes 786440 | tf_op jit(solution)/shard_map/ppermute | solution.py:114
  123.6 19.6 %collective-permute-start.24 = (bf16[64,2048]{1,0:T(8,128)(2,1)S(1)}, bf16[64,2048]{1,0:T(8,128)(2,1)S(1)}, u32[]{:S(2)}, u32[]{:S(2)}) collective-permute-start(bf16[64,2048]{1,0:T(8,128)(2,1)S(1)} %get-tuple-element.94), channel_id=1, source_target_pairs={{0,2},{4,0},{8,4},{12,8},{14,12},{10,14},{6,10},{2,6},{1,3},{5,1},... | collective-permute-start | bytes 786440 | tf_op jit(solution)/shard_map/ppermute | solution.py:114
  128.0 17.4 %collective-permute-start.30 = (bf16[64,2048]{1,0:T(8,128)(2,1)S(1)}, bf16[64,2048]{1,0:T(8,128)(2,1)S(1)}, u32[]{:S(2)}, u32[]{:S(2)}) collective-permute-start(bf16[64,2048]{1,0:T(8,128)(2,1)S(1)} %get-tuple-element.90), channel_id=1, source_target_pairs={{0,2},{4,0},{8,4},{12,8},{14,12},{10,14},{6,10},{2,6},{1,3},{5,1},... | collective-permute-start | bytes 786440 | tf_op jit(solution)/shard_map/ppermute | solution.py:114
  129.9 15.3 %collective-permute-start.32 = (bf16[64,2048]{1,0:T(8,128)(2,1)S(1)}, bf16[64,2048]{1,0:T(8,128)(2,1)S(1)}, u32[]{:S(2)}, u32[]{:S(2)}) collective-permute-start(bf16[64,2048]{1,0:T(8,128)(2,1)S(1)} %get-tuple-element.89), channel_id=1, source_target_pairs={{0,4},{4,8},{8,12},{12,14},{14,10},{10,6},{6,2},{2,0},{1,5},{5,9},... | collective-permute-start | bytes 786440 | tf_op jit(solution)/shard_map/ppermute | solution.py:114
  136.3 47.0 %collective-permute-start.42 = (bf16[2048,384]{1,0:T(8,128)(2,1)S(1)}, bf16[2048,384]{1,0:T(8,128)(2,1)S(1)}, u32[]{:S(2)}, u32[]{:S(2)}) collective-permute-start(bf16[2048,384]{1,0:T(8,128)(2,1)S(1)} %split.25), channel_id=1, source_target_pairs={{0,1},{1,0},{2,3},{3,2},{4,5},{5,4},{6,7},{7,6},{8,9},{9,8},{10,11... | collective-permute-start | bytes 4718600 | tf_op jit(solution)/shard_map/ppermute | solution.py:117
  142.6 42.2 %collective-permute-start.43 = (bf16[2048,384]{1,0:T(8,128)(2,1)S(1)}, bf16[2048,384]{1,0:T(8,128)(2,1)S(1)}, u32[]{:S(2)}, u32[]{:S(2)}) collective-permute-start(bf16[2048,384]{1,0:T(8,128)(2,1)S(1)} %split.27), channel_id=1, source_target_pairs={{0,1},{1,0},{2,3},{3,2},{4,5},{5,4},{6,7},{7,6},{8,9},{9,8},{10,11... | collective-permute-start | bytes 4718600 | tf_op jit(solution)/shard_map/ppermute | solution.py:117
  143.3 8.3 %collective-permute-start.29 = (bf16[64,2048]{1,0:T(8,128)(2,1)S(1)}, bf16[64,2048]{1,0:T(8,128)(2,1)S(1)}, u32[]{:S(2)}, u32[]{:S(2)}) collective-permute-start(bf16[64,2048]{1,0:T(8,128)(2,1)S(1)} %get-tuple-element.92), channel_id=1, source_target_pairs={{0,2},{4,0},{8,4},{12,8},{14,12},{10,14},{6,10},{2,6},{1,3},{5,1},... | collective-permute-start | bytes 786440 | tf_op jit(solution)/shard_map/ppermute | solution.py:114
  145.1 9.2 %collective-permute-start.35 = (bf16[64,2048]{1,0:T(8,128)(2,1)S(1)}, bf16[64,2048]{1,0:T(8,128)(2,1)S(1)}, u32[]{:S(2)}, u32[]{:S(2)}) collective-permute-start(bf16[64,2048]{1,0:T(8,128)(2,1)S(1)} %get-tuple-element.91), channel_id=1, source_target_pairs={{0,4},{4,8},{8,12},{12,14},{14,10},{10,6},{6,2},{2,0},{1,5},{5,9},... | collective-permute-start | bytes 786440 | tf_op jit(solution)/shard_map/ppermute | solution.py:114
  145.5 13.2 %collective-permute-start.36 = (bf16[64,2048]{1,0:T(8,128)(2,1)S(1)}, bf16[64,2048]{1,0:T(8,128)(2,1)S(1)}, u32[]{:S(2)}, u32[]{:S(2)}) collective-permute-start(bf16[64,2048]{1,0:T(8,128)(2,1)S(1)} %add_convert_fusion.12), channel_id=1, source_target_pairs={{0,4},{4,8},{8,12},{12,14},{14,10},{10,6},{6,2},{2,0},{1,5},{5,9},... | collective-permute-start | bytes 786440 | tf_op jit(solution)/shard_map/ppermute | solution.py:114
  151.6 9.2 %collective-permute-start.34 = (bf16[64,2048]{1,0:T(8,128)(2,1)S(1)}, bf16[64,2048]{1,0:T(8,128)(2,1)S(1)}, u32[]{:S(2)}, u32[]{:S(2)}) collective-permute-start(bf16[64,2048]{1,0:T(8,128)(2,1)S(1)} %add_convert_fusion.13), channel_id=1, source_target_pairs={{0,2},{4,0},{8,4},{12,8},{14,12},{10,14},{6,10},{2,6},{1,3},{5,1},... | collective-permute-start | bytes 786440 | tf_op jit(solution)/shard_map/ppermute | solution.py:114
  154.3 12.1 %collective-permute-start.33 = (bf16[64,2048]{1,0:T(8,128)(2,1)S(1)}, bf16[64,2048]{1,0:T(8,128)(2,1)S(1)}, u32[]{:S(2)}, u32[]{:S(2)}) collective-permute-start(bf16[64,2048]{1,0:T(8,128)(2,1)S(1)} %add_convert_fusion.11), channel_id=1, source_target_pairs={{0,2},{4,0},{8,4},{12,8},{14,12},{10,14},{6,10},{2,6},{1,3},{5,1},... | collective-permute-start | bytes 786440 | tf_op jit(solution)/shard_map/ppermute | solution.py:114
  158.8 16.7 %collective-permute-start.38 = (bf16[64,2048]{1,0:T(8,128)(2,1)S(1)}, bf16[64,2048]{1,0:T(8,128)(2,1)S(1)}, u32[]{:S(2)}, u32[]{:S(2)}) collective-permute-start(bf16[64,2048]{1,0:T(8,128)(2,1)S(1)} %add_convert_fusion.8), channel_id=1, source_target_pairs={{0,4},{4,8},{8,12},{12,14},{14,10},{10,6},{6,2},{2,0},{1,5},{5,9},... | collective-permute-start | bytes 786440 | tf_op jit(solution)/shard_map/ppermute | solution.py:114
  160.9 18.8 %collective-permute-start.41 = (bf16[64,2048]{1,0:T(8,128)(2,1)S(1)}, bf16[64,2048]{1,0:T(8,128)(2,1)S(1)}, u32[]{:S(2)}, u32[]{:S(2)}) collective-permute-start(bf16[64,2048]{1,0:T(8,128)(2,1)S(1)} %add_convert_fusion.9), channel_id=1, source_target_pairs={{0,2},{4,0},{8,4},{12,8},{14,12},{10,14},{6,10},{2,6},{1,3},{5,1},... | collective-permute-start | bytes 786440 | tf_op jit(solution)/shard_map/ppermute | solution.py:114
  (19 other events, 189.2 us)

commit v9 on v8

--- a/solution.py
+++ b/solution.py
@@ -197,7 +197,8 @@
         return part.astype(jnp.bfloat16)
 
     parts = {}
-    for k in range(1, full_steps):
+
+    def whole_step(k):
         lefts, rights = from_left[k - 1], from_right[k - 1]
         xs = [lefts[0][low], lefts[0][high], rights[2]]
         ogs = [lefts[2], rights[1][low], rights[1][high]]
@@ -209,8 +210,11 @@
             {rows: part[at + rows.start : at + rows.stop] for rows in (low, high)}
             for at in (0, tok_rows)
         ]
-        if k == 1:
-            own_part = part[2 * tok_rows :]
+        return part[2 * tok_rows :]
+
+    own_part = None
+    for k in range(1, full_steps - 1):
+        own_part = whole_step(k) if k == 1 else (whole_step(k), own_part)[1]
     if full_steps < 2:
         own_part = step_piece([layer_input], [output_grad], [outgoing[0]])
 
@@ -218,6 +222,9 @@
         return step_piece([far[0]], [far[1]], [blocks[groups // 2]]) if has_far else None
 
     far_part = far_piece()
+    if full_steps > 1:
+        rest = whole_step(full_steps - 1)
+        own_part = rest if own_part is None else own_part
     if full_steps:
         k = full_steps
         lefts, rights = from_left[k - 1], from_right[k - 1]

time: 188 us -> 184 us (0.979)
  waiting for transfers between devices: 86.1 us -> 77.9 us
  matrix products: 39.6 us -> 42.3 us
    ppermute x39, waiting for transfers between devices: 86.1 us -> 77.9 us  [shift(): return lax.ppermute(array, 'grp', at_distance(k))]
    dot_general x28, matrix products: 39.6 us -> 42.3 us  [mm(): return lax.dot_general(a, b, dims, preferred_element_type=jnp.float32)]
  transfers between devices with their start and end apart: 45 -> 45, of which waited for: 20 -> 22; matrix products, arithmetic and copies ran while one was open for 25% -> 23% of each run, Pallas kernels for 0% -> 0%
where the time goes in v9:
time: 184 us
  waiting for transfers between devices  77.9 us (42%)
  starting transfers between devices  47.1 us (26%)
  matrix products  42.3 us (23%)
  other arithmetic  9.94 us (5%)
  local copies, waits for them, and re-layouts  5.28 us (3%)
    ppermute x39, waiting for transfers between devices, shift(): return lax.ppermute(array, 'grp', at_distance(k))  77.9 us
    ppermute x39, starting transfers between devices, shift(): return lax.ppermute(array, 'grp', at_distance(k))  46.7 us
    dot_general x28, matrix products, mm(): return lax.dot_general(a, b, dims, preferred_element_type=jnp.float32)  42.3 us
    broadcast_in_dim x3, other arithmetic, member_sum(): return total.astype(jnp.bfloat16)[None]  4.82 us
  transfers between devices with their start and end apart: 45, of which 22 were waited for; matrix products, arithmetic and copies ran while one was open for 23% of the time, Pallas kernels for 0%

profile of v9, /device:TPU:0, one launch (start us, length us, event | category | flops | bytes accessed | tf_op | source)
XLA Modules:
  0.0 184.0 jit_solution(4069406605710474211)
XLA Ops:
  0.6 3.1 %collective-permute-start.2 = (bf16[128,2048]{1,0:T(8,128)(2,1)}, bf16[128,2048]{1,0:T(8,128)(2,1)S(1)}, u32[]{:S(2)}, u32[]{:S(2)}) collective-permute-start(bf16[128,2048]{1,0:T(8,128)(2,1)} %param.9), channel_id=1, source_target_pairs={{0,4},{4,8},{8,12},{12,14},{14,10},{10,6},{6,2},{2,0},{1,5},{5,9},... | collective-permute-start | bytes 1572872 | tf_op jit(solution)/shard_map/ppermute | solution.py:114
  8.0 2.0 %collective-permute-start.1 = (f32[4,128]{1,0:T(4,128)S(1)}, f32[4,128]{1,0:T(4,128)S(1)}, u32[]{:S(2)}, u32[]{:S(2)}) collective-permute-start(f32[4,128]{1,0:T(4,128)S(1)} %pad_maximum_fusion.9), channel_id=1, source_target_pairs={{0,2},{4,0},{8,4},{12,8},{14,12},{10,14},{6,10},{2,6},{1,3},{5,1},... | collective-permute-start | bytes 6152 | tf_op jit(solution)/shard_map/ppermute | solution.py:114
  10.1 1.9 %collective-permute-start.8 = (bf16[128,2048]{1,0:T(8,128)(2,1)}, bf16[128,2048]{1,0:T(8,128)(2,1)S(1)}, u32[]{:S(2)}, u32[]{:S(2)}) collective-permute-start(bf16[128,2048]{1,0:T(8,128)(2,1)} %param.8), channel_id=1, source_target_pairs={{0,2},{4,0},{8,4},{12,8},{14,12},{10,14},{6,10},{2,6},{1,3},{5,1},... | collective-permute-start | bytes 1572872 | tf_op jit(solution)/shard_map/ppermute | solution.py:114
  14.8 1.9 %collective-permute-done = f32[4,128]{1,0:T(4,128)S(1)} collective-permute-done((f32[4,128]{1,0:T(4,128)S(1)}, f32[4,128]{1,0:T(4,128)S(1)}, u32[]{:S(2)}, u32[]{:S(2)}) %collective-permute-start) | collective-permute-done | bytes 2080 | tf_op jit(solution)/shard_map/ppermute | solution.py:114
  16.8 3.1 %collective-permute-start.20 = (f32[4,128]{1,0:T(4,128)S(1)}, f32[4,128]{1,0:T(4,128)S(1)}, u32[]{:S(2)}, u32[]{:S(2)}) collective-permute-start(f32[4,128]{1,0:T(4,128)S(1)} %pad_maximum_fusion.11), channel_id=1, source_target_pairs={{0,6},{4,2},{8,0},{12,4},{14,8},{10,12},{6,14},{2,10},{1,7},{5,3},... | collective-permute-start | bytes 6152 | tf_op jit(solution)/shard_map/ppermute | solution.py:114
  19.9 5.1 %collective-permute-done.20 = f32[4,128]{1,0:T(4,128)S(1)} collective-permute-done((f32[4,128]{1,0:T(4,128)S(1)}, f32[4,128]{1,0:T(4,128)S(1)}, u32[]{:S(2)}, u32[]{:S(2)}) %collective-permute-start.20) | collective-permute-done | bytes 2080 | tf_op jit(solution)/shard_map/ppermute | solution.py:114
  25.4 4.1 %collective-permute-done.19 = f32[4,128]{1,0:T(4,128)S(1)} collective-permute-done((f32[4,128]{1,0:T(4,128)S(1)}, f32[4,128]{1,0:T(4,128)S(1)}, u32[]{:S(2)}, u32[]{:S(2)}) %collective-permute-start.19) | collective-permute-done | bytes 2080 | tf_op jit(solution)/shard_map/ppermute | solution.py:114
  31.8 4.0 %collective-permute-done.7 = bf16[64,2048]{1,0:T(8,128)(2,1)S(1)} collective-permute-done((bf16[64,2048]{1,0:T(8,128)(2,1)S(1)}, bf16[64,2048]{1,0:T(8,128)(2,1)S(1)}, u32[]{:S(2)}, u32[]{:S(2)}) %collective-permute-start.7) | collective-permute-done | bytes 262176 | tf_op jit(solution)/shard_map/ppermute | solution.py:114
  36.6 1.6 collective-permute-start.23
  38.3 1.6 collective-permute-start.12
  40.5 9.8 %collective-permute-done.15 = bf16[128,2048]{1,0:T(8,128)(2,1)S(1)} collective-permute-done((bf16[128,2048]{1,0:T(8,128)(2,1)S(1)}, bf16[128,2048]{1,0:T(8,128)(2,1)S(1)}, u32[]{:S(2)}, u32[]{:S(2)}) %collective-permute-start.15) | collective-permute-done | bytes 524320 | tf_op jit(solution)/shard_map/ppermute | solution.py:114
  50.9 6.1 %collective-permute-done.12 = bf16[128,2048]{1,0:T(8,128)(2,1)S(1)} collective-permute-done((bf16[128,2048]{1,0:T(8,128)(2,1)S(1)}, bf16[128,2048]{1,0:T(8,128)(2,1)S(1)}, u32[]{:S(2)}, u32[]{:S(2)}) %collective-permute-start.12) | collective-permute-done | bytes 524320 | tf_op jit(solution)/shard_map/ppermute | solution.py:114
  58.7 5.1 %collective-permute-done.16 = bf16[128,2048]{1,0:T(8,128)(2,1)S(1)} collective-permute-done((bf16[128,2048]{1,0:T(8,128)(2,1)S(1)}, bf16[128,2048]{1,0:T(8,128)(2,1)S(1)}, u32[]{:S(2)}, u32[]{:S(2)}) %collective-permute-start.16) | collective-permute-done | bytes 524320 | tf_op jit(solution)/shard_map/ppermute | solution.py:114
  65.2 7.7 %collective-permute-done.21 = bf16[64,2048]{1,0:T(8,128)(2,1)S(1)} collective-permute-done((bf16[64,2048]{1,0:T(8,128)(2,1)S(1)}, bf16[64,2048]{1,0:T(8,128)(2,1)S(1)}, u32[]{:S(2)}, u32[]{:S(2)}) %collective-permute-start.21) | collective-permute-done | bytes 262176 | tf_op jit(solution)/shard_map/ppermute | solution.py:114
  75.0 5.0 %collective-permute-done.25 = bf16[64,2048]{1,0:T(8,128)(2,1)S(1)} collective-permute-done((bf16[64,2048]{1,0:T(8,128)(2,1)S(1)}, bf16[64,2048]{1,0:T(8,128)(2,1)S(1)}, u32[]{:S(2)}, u32[]{:S(2)}) %collective-permute-start.25) | collective-permute-done | bytes 262176 | tf_op jit(solution)/shard_map/ppermute | solution.py:114
  82.5 3.8 %collective-permute-done.27 = bf16[64,2048]{1,0:T(8,128)(2,1)S(1)} collective-permute-done((bf16[64,2048]{1,0:T(8,128)(2,1)S(1)}, bf16[64,2048]{1,0:T(8,128)(2,1)S(1)}, u32[]{:S(2)}, u32[]{:S(2)}) %collective-permute-start.27) | collective-permute-done | bytes 262176 | tf_op jit(solution)/shard_map/ppermute | solution.py:114
  86.4 2.7 %collective-permute-start.11 = (f32[2,128]{1,0:T(2,128)S(1)}, f32[2,128]{1,0:T(2,128)S(1)}, u32[]{:S(2)}, u32[]{:S(2)}) collective-permute-start(f32[2,128]{1,0:T(2,128)S(1)} %get-tuple-element.113), channel_id=1, source_target_pairs={{0,14},{4,10},{8,6},{12,2},{14,0},{10,4},{6,8},{2,12},{1,15},{5,11... | collective-permute-start | bytes 3080 | tf_op jit(solution)/shard_map/ppermute | solution.py:114
  95.3 2.7 %constant_dynamic-update-slice_fusion.21 = (bf16[1024,768]{1,0:T(8,128)(2,1)S(1)}, bf16[384,768]{1,0:T(8,128)(2,1)S(1)}, bf16[1024,768]{1,0:T(8,128)(2,1)S(1)}, bf16[1024,768]{1,0:T(8,128)(2,1)}, bf16[384,768]{1,0:T(8,128)(2,1)S(1)}) fusion(f32[384,768]{1,0:T(8,128)S(1)} %select_multiply_fusion.1, f32[384,768]{1,0:T(8,128)S(1)} %fusion.57, ...), kind=kOutput, calls=%fused_computation.115 | convolution fusion | flops 1219264512 | bytes 10030848 | tf_op jit(solution)/shard_map/dot_general | solution.py:97
  102.2 1.9 %collective-permute-done.17 = bf16[128,2048]{1,0:T(8,128)(2,1)S(1)} collective-permute-done((bf16[128,2048]{1,0:T(8,128)(2,1)S(1)}, bf16[128,2048]{1,0:T(8,128)(2,1)S(1)}, u32[]{:S(2)}, u32[]{:S(2)}) %collective-permute-start.17) | collective-permute-done | bytes 524320 | tf_op jit(solution)/shard_map/ppermute | solution.py:114
  109.5 2.1 %constant_dynamic-update-slice_fusion.19 = (bf16[1024,768]{1,0:T(8,128)(2,1)S(1)}, bf16[256,768]{1,0:T(8,128)(2,1)S(1)}, bf16[1024,768]{1,0:T(8,128)(2,1)S(1)}, bf16[1024,768]{1,0:T(8,128)(2,1)}, bf16[256,768]{1,0:T(8,128)(2,1)S(1)}) fusion(bf16[1024,768]{1,0:T(8,128)(2,1)S(1)} %get-tuple-element.54, f32[256,768]{1,0:T(8,128)S(1)} %fusion.47, ...), kind=kOutput, calls=%fused_computation.113 | convolution fusion | flops 818282496 | bytes 7736320 | tf_op jit(solution)/shard_map/dot_general | solution.py:97
  116.4 1.8 collective-permute-start.31
  128.6 3.7 %convolution_convert_fusion.2 = bf16[2048,768]{1,0:T(8,128)(2,1)S(1)} fusion(bf16[1024,2048]{1,0:T(8,128)(2,1)S(1)} %get-tuple-element.135, bf16[1024,768]{1,0:T(8,128)(2,1)S(1)} %get-tuple-element.48), kind=kOutput, calls=%fused_computation.2 | convolution fusion | flops 3222798336 | bytes 8912896 | tf_op jit(solution)/shard_map/dot_general | solution.py:97
  133.7 3.7 %convolution_convert_fusion.1 = bf16[2048,768]{1,0:T(8,128)(2,1)S(1)} fusion(bf16[1024,2048]{1,0:T(8,128)(2,1)S(1)} %get-tuple-element.135, bf16[1024,768]{1,0:T(8,128)(2,1)S(1)} %copy-done.5), kind=kOutput, calls=%fused_computation.1 | convolution fusion | flops 3222798336 | bytes 8912896 | tf_op jit(solution)/shard_map/dot_general | solution.py:97
  142.3 1.8 collective-permute-start.36
  144.2 4.7 %collective-permute-done.29 = bf16[64,2048]{1,0:T(8,128)(2,1)S(1)} collective-permute-done((bf16[64,2048]{1,0:T(8,128)(2,1)S(1)}, bf16[64,2048]{1,0:T(8,128)(2,1)S(1)}, u32[]{:S(2)}, u32[]{:S(2)}) %collective-permute-start.29) | collective-permute-done | bytes 262176 | tf_op jit(solution)/shard_map/ppermute | solution.py:114
  151.3 4.2 %collective-permute-done.36 = bf16[64,2048]{1,0:T(8,128)(2,1)S(1)} collective-permute-done((bf16[64,2048]{1,0:T(8,128)(2,1)S(1)}, bf16[64,2048]{1,0:T(8,128)(2,1)S(1)}, u32[]{:S(2)}, u32[]{:S(2)}) %collective-permute-start.36) | collective-permute-done | bytes 262176 | tf_op jit(solution)/shard_map/ppermute | solution.py:114
  156.5 1.6 collective-permute-done.34
  159.4 4.3 %collective-permute-done.33 = bf16[64,2048]{1,0:T(8,128)(2,1)S(1)} collective-permute-done((bf16[64,2048]{1,0:T(8,128)(2,1)S(1)}, bf16[64,2048]{1,0:T(8,128)(2,1)S(1)}, u32[]{:S(2)}, u32[]{:S(2)}) %collective-permute-start.33) | collective-permute-done | bytes 262176 | tf_op jit(solution)/shard_map/ppermute | solution.py:114
  163.7 1.7 collective-permute-start.39
  165.5 4.6 %collective-permute-done.39 = bf16[64,2048]{1,0:T(8,128)(2,1)S(1)} collective-permute-done((bf16[64,2048]{1,0:T(8,128)(2,1)S(1)}, bf16[64,2048]{1,0:T(8,128)(2,1)S(1)}, u32[]{:S(2)}, u32[]{:S(2)}) %collective-permute-start.39) | collective-permute-done | bytes 262176 | tf_op jit(solution)/shard_map/ppermute | solution.py:114
  172.6 3.7 %convolution_convert_fusion = bf16[768,2048]{1,0:T(8,128)(2,1)S(1)} fusion(bf16[1024,768]{1,0:T(8,128)(2,1)S(1)} %get-tuple-element.74, bf16[1024,2048]{1,0:T(8,128)(2,1)S(1)} %get-tuple-element.136), kind=kOutput, calls=%fused_computation | convolution fusion | flops 3222798336 | bytes 8912896 | tf_op jit(solution)/shard_map/dot_general | solution.py:97
  182.3 1.7 fusion.6
  (175 shorter events, 69.5 us)
Async XLA Ops:
  0.6 35.9 %collective-permute-start.2 = (bf16[128,2048]{1,0:T(8,128)(2,1)}, bf16[128,2048]{1,0:T(8,128)(2,1)S(1)}, u32[]{:S(2)}, u32[]{:S(2)}) collective-permute-start(bf16[128,2048]{1,0:T(8,128)(2,1)} %param.9), channel_id=1, source_target_pairs={{0,4},{4,8},{8,12},{12,14},{14,10},{10,6},{6,2},{2,0},{1,5},{5,9},... | collective-permute-start | bytes 1572872 | tf_op jit(solution)/shard_map/ppermute | solution.py:114
  4.8 35.1 %collective-permute-start.4 = (bf16[64,2048]{1,0:T(8,128)(2,1)S(1)}, bf16[64,2048]{1,0:T(8,128)(2,1)S(1)}, u32[]{:S(2)}, u32[]{:S(2)}) collective-permute-start(bf16[64,2048]{1,0:T(8,128)(2,1)S(1)} %get-tuple-element.102), channel_id=1, source_target_pairs={{0,2},{4,0},{8,4},{12,8},{14,12},{10,14},{6,10},{2,6},{1,3},{5,1},... | collective-permute-start | bytes 786440 | tf_op jit(solution)/shard_map/ppermute | solution.py:114
  10.1 25.8 %collective-permute-start.8 = (bf16[128,2048]{1,0:T(8,128)(2,1)}, bf16[128,2048]{1,0:T(8,128)(2,1)S(1)}, u32[]{:S(2)}, u32[]{:S(2)}) collective-permute-start(bf16[128,2048]{1,0:T(8,128)(2,1)} %param.8), channel_id=1, source_target_pairs={{0,2},{4,0},{8,4},{12,8},{14,12},{10,14},{6,10},{2,6},{1,3},{5,1},... | collective-permute-start | bytes 1572872 | tf_op jit(solution)/shard_map/ppermute | solution.py:114
  13.4 17.9 %collective-permute-start.6 = (bf16[64,2048]{1,0:T(8,128)(2,1)S(1)}, bf16[64,2048]{1,0:T(8,128)(2,1)S(1)}, u32[]{:S(2)}, u32[]{:S(2)}) collective-permute-start(bf16[64,2048]{1,0:T(8,128)(2,1)S(1)} %get-tuple-element.100), channel_id=1, source_target_pairs={{0,4},{4,8},{8,12},{12,14},{14,10},{10,6},{6,2},{2,0},{1,5},{5,9},... | collective-permute-start | bytes 786440 | tf_op jit(solution)/shard_map/ppermute | solution.py:114
  35.9 55.6 %collective-permute-start.9 = (bf16[2048,384]{1,0:T(8,128)(2,1)}, bf16[2048,384]{1,0:T(8,128)(2,1)S(1)}, u32[]{:S(2)}, u32[]{:S(2)}) collective-permute-start(bf16[2048,384]{1,0:T(8,128)(2,1)} %bitcast.94), channel_id=1, source_target_pairs={{0,1},{1,0},{2,3},{3,2},{4,5},{5,4},{6,7},{7,6},{8,9},{9,8},{10,11... | collective-permute-start | bytes 4718600 | tf_op jit(solution)/shard_map/ppermute | solution.py:117
  35.9 14.4 %collective-permute-start.15 = (bf16[128,2048]{1,0:T(8,128)(2,1)S(1)}, bf16[128,2048]{1,0:T(8,128)(2,1)S(1)}, u32[]{:S(2)}, u32[]{:S(2)}) collective-permute-start(bf16[128,2048]{1,0:T(8,128)(2,1)S(1)} %collective-permute-done.8), channel_id=1, source_target_pairs={{0,2},{4,0},{8,4},{12,8},{14,12},{10,14},{6,10},{2,6},{1,3},{5,1},... | collective-permute-start | bytes 1572872 | tf_op jit(solution)/shard_map/ppermute | solution.py:114
  36.6 27.7 %collective-permute-start.23 = (bf16[64,2048]{1,0:T(8,128)(2,1)S(1)}, bf16[64,2048]{1,0:T(8,128)(2,1)S(1)}, u32[]{:S(2)}, u32[]{:S(2)}) collective-permute-start(bf16[64,2048]{1,0:T(8,128)(2,1)S(1)} %collective-permute-done.6), channel_id=1, source_target_pairs={{0,4},{4,8},{8,12},{12,14},{14,10},{10,6},{6,2},{2,0},{1,5},{5,9},... | collective-permute-start | bytes 786440 | tf_op jit(solution)/shard_map/ppermute | solution.py:114
  38.3 18.8 %collective-permute-start.12 = (bf16[128,2048]{1,0:T(8,128)(2,1)S(1)}, bf16[128,2048]{1,0:T(8,128)(2,1)S(1)}, u32[]{:S(2)}, u32[]{:S(2)}) collective-permute-start(bf16[128,2048]{1,0:T(8,128)(2,1)S(1)} %collective-permute-done.2), channel_id=1, source_target_pairs={{0,4},{4,8},{8,12},{12,14},{14,10},{10,6},{6,2},{2,0},{1,5},{5,9},... | collective-permute-start | bytes 1572872 | tf_op jit(solution)/shard_map/ppermute | solution.py:114
  39.9 24.5 %collective-permute-start.24 = (bf16[64,2048]{1,0:T(8,128)(2,1)S(1)}, bf16[64,2048]{1,0:T(8,128)(2,1)S(1)}, u32[]{:S(2)}, u32[]{:S(2)}) collective-permute-start(bf16[64,2048]{1,0:T(8,128)(2,1)S(1)} %collective-permute-done.7), channel_id=1, source_target_pairs={{0,4},{4,8},{8,12},{12,14},{14,10},{10,6},{6,2},{2,0},{1,5},{5,9},... | collective-permute-start | bytes 786440 | tf_op jit(solution)/shard_map/ppermute | solution.py:114
  50.3 13.5 %collective-permute-start.16 = (bf16[128,2048]{1,0:T(8,128)(2,1)S(1)}, bf16[128,2048]{1,0:T(8,128)(2,1)S(1)}, u32[]{:S(2)}, u32[]{:S(2)}) collective-permute-start(bf16[128,2048]{1,0:T(8,128)(2,1)S(1)} %collective-permute-done.15), channel_id=1, source_target_pairs={{0,2},{4,0},{8,4},{12,8},{14,12},{10,14},{6,10},{2,6},{1,3},{5,1},... | collective-permute-start | bytes 1572872 | tf_op jit(solution)/shard_map/ppermute | solution.py:114
  57.0 17.5 %collective-permute-start.13 = (bf16[128,2048]{1,0:T(8,128)(2,1)S(1)}, bf16[128,2048]{1,0:T(8,128)(2,1)S(1)}, u32[]{:S(2)}, u32[]{:S(2)}) collective-permute-start(bf16[128,2048]{1,0:T(8,128)(2,1)S(1)} %collective-permute-done.12), channel_id=1, source_target_pairs={{0,4},{4,8},{8,12},{12,14},{14,10},{10,6},{6,2},{2,0},{1,5},{5,9},... | collective-permute-start | bytes 1572872 | tf_op jit(solution)/shard_map/ppermute | solution.py:114
  63.8 9.2 %collective-permute-start.21 = (bf16[64,2048]{1,0:T(8,128)(2,1)S(1)}, bf16[64,2048]{1,0:T(8,128)(2,1)S(1)}, u32[]{:S(2)}, u32[]{:S(2)}) collective-permute-start(bf16[64,2048]{1,0:T(8,128)(2,1)S(1)} %collective-permute-done.3), channel_id=1, source_target_pairs={{0,2},{4,0},{8,4},{12,8},{14,12},{10,14},{6,10},{2,6},{1,3},{5,1},... | collective-permute-start | bytes 786440 | tf_op jit(solution)/shard_map/ppermute | solution.py:114
  64.3 29.6 %collective-permute-start.5 = (bf16[384,2048]{1,0:T(8,128)(2,1)S(1)}, bf16[384,2048]{1,0:T(8,128)(2,1)S(1)}, u32[]{:S(2)}, u32[]{:S(2)}) collective-permute-start(bf16[384,2048]{1,0:T(8,128)(2,1)S(1)} %bitcast.88), channel_id=1, source_target_pairs={{0,1},{1,0},{2,3},{3,2},{4,5},{5,4},{6,7},{7,6},{8,9},{9,8},{10,11... | collective-permute-start | bytes 4718600 | tf_op jit(solution)/shard_map/ppermute | solution.py:117
  64.4 17.1 %collective-permute-start.22 = (bf16[64,2048]{1,0:T(8,128)(2,1)S(1)}, bf16[64,2048]{1,0:T(8,128)(2,1)S(1)}, u32[]{:S(2)}, u32[]{:S(2)}) collective-permute-start(bf16[64,2048]{1,0:T(8,128)(2,1)S(1)} %collective-permute-done.4), channel_id=1, source_target_pairs={{0,2},{4,0},{8,4},{12,8},{14,12},{10,14},{6,10},{2,6},{1,3},{5,1},... | collective-permute-start | bytes 786440 | tf_op jit(solution)/shard_map/ppermute | solution.py:114
  81.6 13.7 %collective-permute-start.10 = (bf16[2048,384]{1,0:T(8,128)(2,1)S(1)}, bf16[2048,384]{1,0:T(8,128)(2,1)S(1)}, u32[]{:S(2)}, u32[]{:S(2)}) collective-permute-start(bf16[2048,384]{1,0:T(8,128)(2,1)S(1)} %bitcast.105), channel_id=1, source_target_pairs={{0,1},{1,0},{2,3},{3,2},{4,5},{5,4},{6,7},{7,6},{8,9},{9,8},{10,11... | collective-permute-start | bytes 4718600 | tf_op jit(solution)/shard_map/ppermute | solution.py:117
  82.0 8.3 %collective-permute-start.28 = (bf16[64,2048]{1,0:T(8,128)(2,1)S(1)}, bf16[64,2048]{1,0:T(8,128)(2,1)S(1)}, u32[]{:S(2)}, u32[]{:S(2)}) collective-permute-start(bf16[64,2048]{1,0:T(8,128)(2,1)S(1)} %collective-permute-done.22), channel_id=1, source_target_pairs={{0,2},{4,0},{8,4},{12,8},{14,12},{10,14},{6,10},{2,6},{1,3},{5,1},... | collective-permute-start | bytes 786440 | tf_op jit(solution)/shard_map/ppermute | solution.py:114
  86.4 15.8 %collective-permute-start.11 = (f32[2,128]{1,0:T(2,128)S(1)}, f32[2,128]{1,0:T(2,128)S(1)}, u32[]{:S(2)}, u32[]{:S(2)}) collective-permute-start(f32[2,128]{1,0:T(2,128)S(1)} %get-tuple-element.113), channel_id=1, source_target_pairs={{0,14},{4,10},{8,6},{12,2},{14,0},{10,4},{6,8},{2,12},{1,15},{5,11... | collective-permute-start | bytes 3080 | tf_op jit(solution)/shard_map/ppermute | solution.py:114
  90.4 14.3 %collective-permute-start.14 = (bf16[128,2048]{1,0:T(8,128)(2,1)S(1)}, bf16[128,2048]{1,0:T(8,128)(2,1)S(1)}, u32[]{:S(2)}, u32[]{:S(2)}) collective-permute-start(bf16[128,2048]{1,0:T(8,128)(2,1)S(1)} %collective-permute-done.13), channel_id=1, source_target_pairs={{0,4},{4,8},{8,12},{12,14},{14,10},{10,6},{6,2},{2,0},{1,5},{5,9},... | collective-permute-start | bytes 1572872 | tf_op jit(solution)/shard_map/ppermute | solution.py:114
  91.5 12.6 %collective-permute-start.17 = (bf16[128,2048]{1,0:T(8,128)(2,1)S(1)}, bf16[128,2048]{1,0:T(8,128)(2,1)S(1)}, u32[]{:S(2)}, u32[]{:S(2)}) collective-permute-start(bf16[128,2048]{1,0:T(8,128)(2,1)S(1)} %collective-permute-done.16), channel_id=1, source_target_pairs={{0,2},{4,0},{8,4},{12,8},{14,12},{10,14},{6,10},{2,6},{1,3},{5,1},... | collective-permute-start | bytes 1572872 | tf_op jit(solution)/shard_map/ppermute | solution.py:114
  116.4 23.5 %collective-permute-start.31 = (bf16[64,2048]{1,0:T(8,128)(2,1)S(1)}, bf16[64,2048]{1,0:T(8,128)(2,1)S(1)}, u32[]{:S(2)}, u32[]{:S(2)}) collective-permute-start(bf16[64,2048]{1,0:T(8,128)(2,1)S(1)} %get-tuple-element.93), channel_id=1, source_target_pairs={{0,4},{4,8},{8,12},{12,14},{14,10},{10,6},{6,2},{2,0},{1,5},{5,9},... | collective-permute-start | bytes 786440 | tf_op jit(solution)/shard_map/ppermute | solution.py:114
  120.9 19.2 %collective-permute-start.18 = (bf16[64,2048]{1,0:T(8,128)(2,1)S(1)}, bf16[64,2048]{1,0:T(8,128)(2,1)S(1)}, u32[]{:S(2)}, u32[]{:S(2)}) collective-permute-start(bf16[64,2048]{1,0:T(8,128)(2,1)S(1)} %get-tuple-element.94), channel_id=1, source_target_pairs={{0,2},{4,0},{8,4},{12,8},{14,12},{10,14},{6,10},{2,6},{1,3},{5,1},... | collective-permute-start | bytes 786440 | tf_op jit(solution)/shard_map/ppermute | solution.py:114
  123.5 18.8 %collective-permute-start.30 = (bf16[64,2048]{1,0:T(8,128)(2,1)S(1)}, bf16[64,2048]{1,0:T(8,128)(2,1)S(1)}, u32[]{:S(2)}, u32[]{:S(2)}) collective-permute-start(bf16[64,2048]{1,0:T(8,128)(2,1)S(1)} %get-tuple-element.90), channel_id=1, source_target_pairs={{0,2},{4,0},{8,4},{12,8},{14,12},{10,14},{6,10},{2,6},{1,3},{5,1},... | collective-permute-start | bytes 786440 | tf_op jit(solution)/shard_map/ppermute | solution.py:114
  124.7 16.7 %collective-permute-start.32 = (bf16[64,2048]{1,0:T(8,128)(2,1)S(1)}, bf16[64,2048]{1,0:T(8,128)(2,1)S(1)}, u32[]{:S(2)}, u32[]{:S(2)}) collective-permute-start(bf16[64,2048]{1,0:T(8,128)(2,1)S(1)} %get-tuple-element.89), channel_id=1, source_target_pairs={{0,4},{4,8},{8,12},{12,14},{14,10},{10,6},{6,2},{2,0},{1,5},{5,9},... | collective-permute-start | bytes 786440 | tf_op jit(solution)/shard_map/ppermute | solution.py:114
  132.5 46.7 %collective-permute-start.42 = (bf16[2048,384]{1,0:T(8,128)(2,1)S(1)}, bf16[2048,384]{1,0:T(8,128)(2,1)S(1)}, u32[]{:S(2)}, u32[]{:S(2)}) collective-permute-start(bf16[2048,384]{1,0:T(8,128)(2,1)S(1)} %split.25), channel_id=1, source_target_pairs={{0,1},{1,0},{2,3},{3,2},{4,5},{5,4},{6,7},{7,6},{8,9},{9,8},{10,11... | collective-permute-start | bytes 4718600 | tf_op jit(solution)/shard_map/ppermute | solution.py:117
  139.9 40.8 %collective-permute-start.43 = (bf16[2048,384]{1,0:T(8,128)(2,1)S(1)}, bf16[2048,384]{1,0:T(8,128)(2,1)S(1)}, u32[]{:S(2)}, u32[]{:S(2)}) collective-permute-start(bf16[2048,384]{1,0:T(8,128)(2,1)S(1)} %split.27), channel_id=1, source_target_pairs={{0,1},{1,0},{2,3},{3,2},{4,5},{5,4},{6,7},{7,6},{8,9},{9,8},{10,11... | collective-permute-start | bytes 4718600 | tf_op jit(solution)/shard_map/ppermute | solution.py:117
  140.2 8.8 %collective-permute-start.29 = (bf16[64,2048]{1,0:T(8,128)(2,1)S(1)}, bf16[64,2048]{1,0:T(8,128)(2,1)S(1)}, u32[]{:S(2)}, u32[]{:S(2)}) collective-permute-start(bf16[64,2048]{1,0:T(8,128)(2,1)S(1)} %get-tuple-element.92), channel_id=1, source_target_pairs={{0,2},{4,0},{8,4},{12,8},{14,12},{10,14},{6,10},{2,6},{1,3},{5,1},... | collective-permute-start | bytes 786440 | tf_op jit(solution)/shard_map/ppermute | solution.py:114
  141.4 9.2 %collective-permute-start.35 = (bf16[64,2048]{1,0:T(8,128)(2,1)S(1)}, bf16[64,2048]{1,0:T(8,128)(2,1)S(1)}, u32[]{:S(2)}, u32[]{:S(2)}) collective-permute-start(bf16[64,2048]{1,0:T(8,128)(2,1)S(1)} %get-tuple-element.91), channel_id=1, source_target_pairs={{0,4},{4,8},{8,12},{12,14},{14,10},{10,6},{6,2},{2,0},{1,5},{5,9},... | collective-permute-start | bytes 786440 | tf_op jit(solution)/shard_map/ppermute | solution.py:114
  142.3 13.1 %collective-permute-start.36 = (bf16[64,2048]{1,0:T(8,128)(2,1)S(1)}, bf16[64,2048]{1,0:T(8,128)(2,1)S(1)}, u32[]{:S(2)}, u32[]{:S(2)}) collective-permute-start(bf16[64,2048]{1,0:T(8,128)(2,1)S(1)} %add_convert_fusion.12), channel_id=1, source_target_pairs={{0,4},{4,8},{8,12},{12,14},{14,10},{10,6},{6,2},{2,0},{1,5},{5,9},... | collective-permute-start | bytes 786440 | tf_op jit(solution)/shard_map/ppermute | solution.py:114
  148.9 9.2 %collective-permute-start.34 = (bf16[64,2048]{1,0:T(8,128)(2,1)S(1)}, bf16[64,2048]{1,0:T(8,128)(2,1)S(1)}, u32[]{:S(2)}, u32[]{:S(2)}) collective-permute-start(bf16[64,2048]{1,0:T(8,128)(2,1)S(1)} %add_convert_fusion.13), channel_id=1, source_target_pairs={{0,2},{4,0},{8,4},{12,8},{14,12},{10,14},{6,10},{2,6},{1,3},{5,1},... | collective-permute-start | bytes 786440 | tf_op jit(solution)/shard_map/ppermute | solution.py:114
  150.6 13.2 %collective-permute-start.33 = (bf16[64,2048]{1,0:T(8,128)(2,1)S(1)}, bf16[64,2048]{1,0:T(8,128)(2,1)S(1)}, u32[]{:S(2)}, u32[]{:S(2)}) collective-permute-start(bf16[64,2048]{1,0:T(8,128)(2,1)S(1)} %add_convert_fusion.11), channel_id=1, source_target_pairs={{0,2},{4,0},{8,4},{12,8},{14,12},{10,14},{6,10},{2,6},{1,3},{5,1},... | collective-permute-start | bytes 786440 | tf_op jit(solution)/shard_map/ppermute | solution.py:114
  155.5 15.9 %collective-permute-start.38 = (bf16[64,2048]{1,0:T(8,128)(2,1)S(1)}, bf16[64,2048]{1,0:T(8,128)(2,1)S(1)}, u32[]{:S(2)}, u32[]{:S(2)}) collective-permute-start(bf16[64,2048]{1,0:T(8,128)(2,1)S(1)} %add_convert_fusion.8), channel_id=1, source_target_pairs={{0,4},{4,8},{8,12},{12,14},{14,10},{10,6},{6,2},{2,0},{1,5},{5,9},... | collective-permute-start | bytes 786440 | tf_op jit(solution)/shard_map/ppermute | solution.py:114
  158.2 18.2 %collective-permute-start.41 = (bf16[64,2048]{1,0:T(8,128)(2,1)S(1)}, bf16[64,2048]{1,0:T(8,128)(2,1)S(1)}, u32[]{:S(2)}, u32[]{:S(2)}) collective-permute-start(bf16[64,2048]{1,0:T(8,128)(2,1)S(1)} %add_convert_fusion.9), channel_id=1, source_target_pairs={{0,2},{4,0},{8,4},{12,8},{14,12},{10,14},{6,10},{2,6},{1,3},{5,1},... | collective-permute-start | bytes 786440 | tf_op jit(solution)/shard_map/ppermute | solution.py:114
  (19 other events, 256.8 us)

commit v10 on v8

--- a/solution.py
+++ b/solution.py
@@ -1,6 +1,7 @@
 import jax
 import jax.numpy as jnp
 from jax import lax
+from jax.experimental.layout import Layout, with_layout_constraint
 from jax.sharding import PartitionSpec as P
 
 
@@ -166,7 +167,9 @@
         downs.append(member_shift(w_down[0], members - k))
     gate_w = jnp.concatenate(gates, axis=1)
     up_w = jnp.concatenate(ups, axis=1)
-    down_w = jnp.concatenate(downs, axis=0)
+    down_t = with_layout_constraint(
+        jnp.concatenate(downs, axis=0).T, Layout(major_to_minor=(0, 1))
+    )
     column = jnp.arange(span, dtype=jnp.int32)[None, :] // width
 
     def piece(x, og, ratio):
@@ -177,7 +180,7 @@
         s = jax.nn.sigmoid(gate)
         act = gate * s
         hidden = (act * up * r).astype(jnp.bfloat16)
-        hg = r * mm(og, down_w, NT)
+        hg = r * mm(og, down_t)
         ug = (hg * act).astype(jnp.bfloat16)
         gg = (hg * up * s * (1.0 + gate * (1.0 - s))).astype(jnp.bfloat16)
         part = mm(gg, gate_w, NT) + mm(ug, up_w, NT)

time: 188 us -> 196 us (1.043)
  the two profiles are of different devices: /device:TPU:0 before, /device:TPU:15 now
where the time goes in v10:
time: 196 us; the launch traced here: 193 us
  waiting for transfers between devices  88.9 us (45%)
  starting transfers between devices  51.9 us (26%)
  matrix products  37 us (19%)
  other arithmetic  10.1 us (5%)
  local copies, waits for them, and re-layouts  3.94 us (2%)
    ppermute x39, waiting for transfers between devices, shift(): return lax.ppermute(array, 'grp', at_distance(k))  88.9 us
    dot_general x28, matrix products, mm(): return lax.dot_general(a, b, dims, preferred_element_type=jnp.float32)  37 us
    ppermute x39, starting transfers between devices, shift(): return lax.ppermute(array, 'grp', at_distance(k))  31 us
    ppermute x6, starting transfers between devices, member_shift(): lax.ppermute(array, 'mem', [(m, (m + step) % members) for m in range(memb...  20.9 us
    broadcast_in_dim x3, other arithmetic, member_sum(): return total.astype(jnp.bfloat16)[None]  4.89 us
  transfers between devices with their start and end apart: 45, of which 22 were waited for; matrix products, arithmetic and copies ran while one was open for 20% of the time, Pallas kernels for 0%

profile of v10, /device:TPU:15, one launch (start us, length us, event | category | flops | bytes accessed | tf_op | source)
XLA Modules:
  0.0 193.2 jit_solution(17980913044035996954)
XLA Ops:
  5.4 1.9 copy.15
  11.7 16.6 %collective-permute-done.12 = f32[4,128]{1,0:T(4,128)S(1)} collective-permute-done((f32[4,128]{1,0:T(4,128)S(1)}, f32[4,128]{1,0:T(4,128)S(1)}, u32[]{:S(2)}, u32[]{:S(2)}) %collective-permute-start.12) | collective-permute-done | bytes 2080 | tf_op jit(solution)/shard_map/ppermute | solution.py:115
  29.7 2.0 %collective-permute-done.13 = f32[4,128]{1,0:T(4,128)S(1)} collective-permute-done((f32[4,128]{1,0:T(4,128)S(1)}, f32[4,128]{1,0:T(4,128)S(1)}, u32[]{:S(2)}, u32[]{:S(2)}) %collective-permute-start.13) | collective-permute-done | bytes 2080 | tf_op jit(solution)/shard_map/ppermute | solution.py:115
  33.4 3.5 %collective-permute-done.7 = bf16[64,2048]{1,0:T(8,128)(2,1)S(1)} collective-permute-done((bf16[64,2048]{1,0:T(8,128)(2,1)S(1)}, bf16[64,2048]{1,0:T(8,128)(2,1)S(1)}, u32[]{:S(2)}, u32[]{:S(2)}) %collective-permute-start.7) | collective-permute-done | bytes 262176 | tf_op jit(solution)/shard_map/ppermute | solution.py:115
  37.6 3.3 %collective-permute-start.9 = (bf16[2048,384]{1,0:T(8,128)(2,1)S(1)}, bf16[2048,384]{1,0:T(8,128)(2,1)S(1)}, u32[]{:S(2)}, u32[]{:S(2)}) collective-permute-start(bf16[2048,384]{1,0:T(8,128)(2,1)S(1)} %bitcast.103), channel_id=1, source_target_pairs={{0,1},{1,0},{2,3},{3,2},{4,5},{5,4},{6,7},{7,6},{8,9},{9,8},{10,11... | collective-permute-start | bytes 4718600 | tf_op jit(solution)/shard_map/ppermute | solution.py:118
  41.0 1.5 collective-permute-start.17
  43.7 5.3 %collective-permute-done.17 = bf16[64,2048]{1,0:T(8,128)(2,1)S(1)} collective-permute-done((bf16[64,2048]{1,0:T(8,128)(2,1)S(1)}, bf16[64,2048]{1,0:T(8,128)(2,1)S(1)}, u32[]{:S(2)}, u32[]{:S(2)}) %collective-permute-start.17) | collective-permute-done | bytes 262176 | tf_op jit(solution)/shard_map/ppermute | solution.py:115
  50.4 4.2 %collective-permute-done.18 = bf16[64,2048]{1,0:T(8,128)(2,1)S(1)} collective-permute-done((bf16[64,2048]{1,0:T(8,128)(2,1)S(1)}, bf16[64,2048]{1,0:T(8,128)(2,1)S(1)}, u32[]{:S(2)}, u32[]{:S(2)}) %collective-permute-start.18) | collective-permute-done | bytes 262176 | tf_op jit(solution)/shard_map/ppermute | solution.py:115
  56.0 9.8 %collective-permute-done.14 = bf16[128,2048]{1,0:T(8,128)(2,1)S(1)} collective-permute-done((bf16[128,2048]{1,0:T(8,128)(2,1)S(1)}, bf16[128,2048]{1,0:T(8,128)(2,1)S(1)}, u32[]{:S(2)}, u32[]{:S(2)}) %collective-permute-start.14) | collective-permute-done | bytes 524320 | tf_op jit(solution)/shard_map/ppermute | solution.py:115
  67.5 1.5 collective-permute-start.10
  69.0 3.9 %collective-permute-done.16 = bf16[64,2048]{1,0:T(8,128)(2,1)S(1)} collective-permute-done((bf16[64,2048]{1,0:T(8,128)(2,1)S(1)}, bf16[64,2048]{1,0:T(8,128)(2,1)S(1)}, u32[]{:S(2)}, u32[]{:S(2)}) %collective-permute-start.16) | collective-permute-done | bytes 262176 | tf_op jit(solution)/shard_map/ppermute | solution.py:115
  74.2 5.4 %collective-permute-done.20 = bf16[128,2048]{1,0:T(8,128)(2,1)S(1)} collective-permute-done((bf16[128,2048]{1,0:T(8,128)(2,1)S(1)}, bf16[128,2048]{1,0:T(8,128)(2,1)S(1)}, u32[]{:S(2)}, u32[]{:S(2)}) %collective-permute-start.20) | collective-permute-done | bytes 524320 | tf_op jit(solution)/shard_map/ppermute | solution.py:115
  80.0 4.7 %collective-permute-done.22 = bf16[128,2048]{1,0:T(8,128)(2,1)S(1)} collective-permute-done((bf16[128,2048]{1,0:T(8,128)(2,1)S(1)}, bf16[128,2048]{1,0:T(8,128)(2,1)S(1)}, u32[]{:S(2)}, u32[]{:S(2)}) %collective-permute-start.22) | collective-permute-done | bytes 524320 | tf_op jit(solution)/shard_map/ppermute | solution.py:115
  85.9 4.4 %collective-permute-done.26 = bf16[64,2048]{1,0:T(8,128)(2,1)S(1)} collective-permute-done((bf16[64,2048]{1,0:T(8,128)(2,1)S(1)}, bf16[64,2048]{1,0:T(8,128)(2,1)S(1)}, u32[]{:S(2)}, u32[]{:S(2)}) %collective-permute-start.26) | collective-permute-done | bytes 262176 | tf_op jit(solution)/shard_map/ppermute | solution.py:115
  91.9 3.9 %collective-permute-done.28 = bf16[64,2048]{1,0:T(8,128)(2,1)S(1)} collective-permute-done((bf16[64,2048]{1,0:T(8,128)(2,1)S(1)}, bf16[64,2048]{1,0:T(8,128)(2,1)S(1)}, u32[]{:S(2)}, u32[]{:S(2)}) %collective-permute-start.28) | collective-permute-done | bytes 262176 | tf_op jit(solution)/shard_map/ppermute | solution.py:115
  95.9 2.3 %collective-permute-done.27 = bf16[64,2048]{1,0:T(8,128)(2,1)S(1)} collective-permute-done((bf16[64,2048]{1,0:T(8,128)(2,1)S(1)}, bf16[64,2048]{1,0:T(8,128)(2,1)S(1)}, u32[]{:S(2)}, u32[]{:S(2)}) %collective-permute-start.27) | collective-permute-done | bytes 262176 | tf_op jit(solution)/shard_map/ppermute | solution.py:115
  102.7 1.8 constant_dynamic-update-slice_fusion.21
  111.4 1.5 add_convert_fusion.3
  119.5 3.7 %convolution_convert_fusion = bf16[768,2048]{1,0:T(8,128)(2,1)S(1)} fusion(bf16[1024,768]{1,0:T(8,128)(2,1)S(1)} %get-tuple-element.74, bf16[1024,2048]{1,0:T(8,128)(2,1)S(1)} %constant_dynamic-update-slice_fusion.27), kind=kOutput, calls=%fused_computation | convolution fusion | flops 3222798336 | bytes 8912896 | tf_op jit(solution)/shard_map/dot_general | solution.py:98
  123.4 9.2 %collective-permute-start.44 = (bf16[384,2048]{1,0:T(8,128)(2,1)S(1)}, bf16[384,2048]{1,0:T(8,128)(2,1)S(1)}, u32[]{:S(2)}, u32[]{:S(2)}) collective-permute-start(bf16[384,2048]{1,0:T(8,128)(2,1)S(1)} %split.29), channel_id=1, source_target_pairs={{0,1},{1,0},{2,3},{3,2},{4,5},{5,4},{6,7},{7,6},{8,9},{9,8},{10,11... | collective-permute-start | bytes 4718600 | tf_op jit(solution)/shard_map/ppermute | solution.py:118
  132.6 3.8 %convolution_convert_fusion.1 = bf16[2048,768]{1,0:T(8,128)(2,1)S(1)} fusion(bf16[1024,2048]{1,0:T(8,128)(2,1)S(1)} %constant_dynamic-update-slice_fusion.7, bf16[1024,768]{1,0:T(8,128)(2,1)S(1)} %get-tuple-element.75), kind=kOutput, calls=%fused_computation.1 | convolution fusion | flops 3222798336 | bytes 8912896 | tf_op jit(solution)/shard_map/dot_general | solution.py:98
  146.5 3.3 %collective-permute-done.24 = bf16[64,2048]{1,0:T(8,128)(2,1)S(1)} collective-permute-done((bf16[64,2048]{1,0:T(8,128)(2,1)S(1)}, bf16[64,2048]{1,0:T(8,128)(2,1)S(1)}, u32[]{:S(2)}, u32[]{:S(2)}) %collective-permute-start.24) | collective-permute-done | bytes 262176 | tf_op jit(solution)/shard_map/ppermute | solution.py:115
  150.1 2.0 %collective-permute-done.31 = bf16[64,2048]{1,0:T(8,128)(2,1)S(1)} collective-permute-done((bf16[64,2048]{1,0:T(8,128)(2,1)S(1)}, bf16[64,2048]{1,0:T(8,128)(2,1)S(1)}, u32[]{:S(2)}, u32[]{:S(2)}) %collective-permute-start.31) | collective-permute-done | bytes 262176 | tf_op jit(solution)/shard_map/ppermute | solution.py:115
  153.6 2.5 %collective-permute-done.30 = bf16[64,2048]{1,0:T(8,128)(2,1)S(1)} collective-permute-done((bf16[64,2048]{1,0:T(8,128)(2,1)S(1)}, bf16[64,2048]{1,0:T(8,128)(2,1)S(1)}, u32[]{:S(2)}, u32[]{:S(2)}) %collective-permute-start.30) | collective-permute-done | bytes 262176 | tf_op jit(solution)/shard_map/ppermute | solution.py:115
  156.4 1.4 collective-permute-start.34
  161.8 5.3 %collective-permute-done.34 = bf16[64,2048]{1,0:T(8,128)(2,1)S(1)} collective-permute-done((bf16[64,2048]{1,0:T(8,128)(2,1)S(1)}, bf16[64,2048]{1,0:T(8,128)(2,1)S(1)}, u32[]{:S(2)}, u32[]{:S(2)}) %collective-permute-start.34) | collective-permute-done | bytes 262176 | tf_op jit(solution)/shard_map/ppermute | solution.py:115
  173.0 4.5 %collective-permute-done.41 = bf16[64,2048]{1,0:T(8,128)(2,1)S(1)} collective-permute-done((bf16[64,2048]{1,0:T(8,128)(2,1)S(1)}, bf16[64,2048]{1,0:T(8,128)(2,1)S(1)}, u32[]{:S(2)}, u32[]{:S(2)}) %collective-permute-start.41) | collective-permute-done | bytes 262176 | tf_op jit(solution)/shard_map/ppermute | solution.py:115
  177.8 3.7 %convolution_convert_fusion.2 = bf16[2048,768]{1,0:T(8,128)(2,1)S(1)} fusion(bf16[1024,2048]{1,0:T(8,128)(2,1)S(1)} %constant_dynamic-update-slice_fusion.7, bf16[1024,768]{1,0:T(8,128)(2,1)S(1)} %get-tuple-element.48), kind=kOutput, calls=%fused_computation.2 | convolution fusion | flops 3222798336 | bytes 8912896 | tf_op jit(solution)/shard_map/dot_general | solution.py:98
  181.7 5.6 %collective-permute-start.42 = (bf16[2048,384]{1,0:T(8,128)(2,1)S(1)}, bf16[2048,384]{1,0:T(8,128)(2,1)S(1)}, u32[]{:S(2)}, u32[]{:S(2)}) collective-permute-start(bf16[2048,384]{1,0:T(8,128)(2,1)S(1)} %split.25), channel_id=1, source_target_pairs={{0,1},{1,0},{2,3},{3,2},{4,5},{5,4},{6,7},{7,6},{8,9},{9,8},{10,11... | collective-permute-start | bytes 4718600 | tf_op jit(solution)/shard_map/ppermute | solution.py:118
  188.3 1.7 fusion.6
  190.1 1.5 fusion.5
  191.6 1.6 fusion.4
  (172 shorter events, 64.5 us)
Async XLA Ops:
  7.2 94.0 %collective-permute-start.5 = (bf16[384,2048]{0,1:T(8,128)(2,1)S(1)}, bf16[384,2048]{0,1:T(8,128)(2,1)S(1)}, u32[]{:S(2)}, u32[]{:S(2)}) collective-permute-start(bf16[384,2048]{0,1:T(8,128)(2,1)S(1)} %bitcast.94), channel_id=1, source_target_pairs={{0,1},{1,0},{2,3},{3,2},{4,5},{5,4},{6,7},{7,6},{8,9},{9,8},{10,11... | collective-permute-start | bytes 4718600 | tf_op jit(solution)/shard_map/ppermute | solution.py:118
  8.6 29.0 %collective-permute-start.2 = (bf16[128,2048]{1,0:T(8,128)(2,1)S(1)}, bf16[128,2048]{1,0:T(8,128)(2,1)S(1)}, u32[]{:S(2)}, u32[]{:S(2)}) collective-permute-start(bf16[128,2048]{1,0:T(8,128)(2,1)S(1)} %copy-done.1), channel_id=1, source_target_pairs={{0,4},{4,8},{8,12},{12,14},{14,10},{10,6},{6,2},{2,0},{1,5},{5,9},... | collective-permute-start | bytes 1572872 | tf_op jit(solution)/shard_map/ppermute | solution.py:115
  8.7 32.2 %collective-permute-start.8 = (bf16[128,2048]{1,0:T(8,128)(2,1)S(1)}, bf16[128,2048]{1,0:T(8,128)(2,1)S(1)}, u32[]{:S(2)}, u32[]{:S(2)}) collective-permute-start(bf16[128,2048]{1,0:T(8,128)(2,1)S(1)} %copy-done), channel_id=1, source_target_pairs={{0,2},{4,0},{8,4},{12,8},{14,12},{10,14},{6,10},{2,6},{1,3},{5,1},... | collective-permute-start | bytes 1572872 | tf_op jit(solution)/shard_map/ppermute | solution.py:115
  10.1 21.9 %collective-permute-start.6 = (bf16[64,2048]{1,0:T(8,128)(2,1)S(1)}, bf16[64,2048]{1,0:T(8,128)(2,1)S(1)}, u32[]{:S(2)}, u32[]{:S(2)}) collective-permute-start(bf16[64,2048]{1,0:T(8,128)(2,1)S(1)} %get-tuple-element.100), channel_id=1, source_target_pairs={{0,4},{4,8},{8,12},{12,14},{14,10},{10,6},{6,2},{2,0},{1,5},{5,9},... | collective-permute-start | bytes 786440 | tf_op jit(solution)/shard_map/ppermute | solution.py:115
  10.4 17.9 %collective-permute-start.12 = (f32[4,128]{1,0:T(4,128)S(1)}, f32[4,128]{1,0:T(4,128)S(1)}, u32[]{:S(2)}, u32[]{:S(2)}) collective-permute-start(f32[4,128]{1,0:T(4,128)S(1)} %pad_maximum_fusion.9), channel_id=1, source_target_pairs={{0,8},{4,12},{8,14},{12,10},{14,6},{10,2},{6,0},{2,4},{1,9},{5,13}... | collective-permute-start | bytes 6152 | tf_op jit(solution)/shard_map/ppermute | solution.py:115
  32.1 10.5 %collective-permute-start.3 = (bf16[64,2048]{1,0:T(8,128)(2,1)S(1)}, bf16[64,2048]{1,0:T(8,128)(2,1)S(1)}, u32[]{:S(2)}, u32[]{:S(2)}) collective-permute-start(bf16[64,2048]{1,0:T(8,128)(2,1)S(1)} %get-tuple-element.101), channel_id=1, source_target_pairs={{0,2},{4,0},{8,4},{12,8},{14,12},{10,14},{6,10},{2,6},{1,3},{5,1},... | collective-permute-start | bytes 786440 | tf_op jit(solution)/shard_map/ppermute | solution.py:115
  37.6 62.0 %collective-permute-start.9 = (bf16[2048,384]{1,0:T(8,128)(2,1)S(1)}, bf16[2048,384]{1,0:T(8,128)(2,1)S(1)}, u32[]{:S(2)}, u32[]{:S(2)}) collective-permute-start(bf16[2048,384]{1,0:T(8,128)(2,1)S(1)} %bitcast.103), channel_id=1, source_target_pairs={{0,1},{1,0},{2,3},{3,2},{4,5},{5,4},{6,7},{7,6},{8,9},{9,8},{10,11... | collective-permute-start | bytes 4718600 | tf_op jit(solution)/shard_map/ppermute | solution.py:118
  41.0 8.0 %collective-permute-start.17 = (bf16[64,2048]{1,0:T(8,128)(2,1)S(1)}, bf16[64,2048]{1,0:T(8,128)(2,1)S(1)}, u32[]{:S(2)}, u32[]{:S(2)}) collective-permute-start(bf16[64,2048]{1,0:T(8,128)(2,1)S(1)} %collective-permute-done.6), channel_id=1, source_target_pairs={{0,4},{4,8},{8,12},{12,14},{14,10},{10,6},{6,2},{2,0},{1,5},{5,9},... | collective-permute-start | bytes 786440 | tf_op jit(solution)/shard_map/ppermute | solution.py:115
  42.6 12.0 %collective-permute-start.18 = (bf16[64,2048]{1,0:T(8,128)(2,1)S(1)}, bf16[64,2048]{1,0:T(8,128)(2,1)S(1)}, u32[]{:S(2)}, u32[]{:S(2)}) collective-permute-start(bf16[64,2048]{1,0:T(8,128)(2,1)S(1)} %collective-permute-done.7), channel_id=1, source_target_pairs={{0,4},{4,8},{8,12},{12,14},{14,10},{10,6},{6,2},{2,0},{1,5},{5,9},... | collective-permute-start | bytes 786440 | tf_op jit(solution)/shard_map/ppermute | solution.py:115
  43.6 22.2 %collective-permute-start.14 = (bf16[128,2048]{1,0:T(8,128)(2,1)S(1)}, bf16[128,2048]{1,0:T(8,128)(2,1)S(1)}, u32[]{:S(2)}, u32[]{:S(2)}) collective-permute-start(bf16[128,2048]{1,0:T(8,128)(2,1)S(1)} %collective-permute-done.2), channel_id=1, source_target_pairs={{0,4},{4,8},{8,12},{12,14},{14,10},{10,6},{6,2},{2,0},{1,5},{5,9},... | collective-permute-start | bytes 1572872 | tf_op jit(solution)/shard_map/ppermute | solution.py:115
  49.0 18.3 %collective-permute-start.15 = (bf16[64,2048]{1,0:T(8,128)(2,1)S(1)}, bf16[64,2048]{1,0:T(8,128)(2,1)S(1)}, u32[]{:S(2)}, u32[]{:S(2)}) collective-permute-start(bf16[64,2048]{1,0:T(8,128)(2,1)S(1)} %collective-permute-done.3), channel_id=1, source_target_pairs={{0,2},{4,0},{8,4},{12,8},{14,12},{10,14},{6,10},{2,6},{1,3},{5,1},... | collective-permute-start | bytes 786440 | tf_op jit(solution)/shard_map/ppermute | solution.py:115
  54.6 12.8 %collective-permute-start.19 = (bf16[128,2048]{1,0:T(8,128)(2,1)S(1)}, bf16[128,2048]{1,0:T(8,128)(2,1)S(1)}, u32[]{:S(2)}, u32[]{:S(2)}) collective-permute-start(bf16[128,2048]{1,0:T(8,128)(2,1)S(1)} %collective-permute-done.8), channel_id=1, source_target_pairs={{0,2},{4,0},{8,4},{12,8},{14,12},{10,14},{6,10},{2,6},{1,3},{5,1},... | collective-permute-start | bytes 1572872 | tf_op jit(solution)/shard_map/ppermute | solution.py:115
  67.3 12.4 %collective-permute-start.20 = (bf16[128,2048]{1,0:T(8,128)(2,1)S(1)}, bf16[128,2048]{1,0:T(8,128)(2,1)S(1)}, u32[]{:S(2)}, u32[]{:S(2)}) collective-permute-start(bf16[128,2048]{1,0:T(8,128)(2,1)S(1)} %collective-permute-done.14), channel_id=1, source_target_pairs={{0,4},{4,8},{8,12},{12,14},{14,10},{10,6},{6,2},{2,0},{1,5},{5,9},... | collective-permute-start | bytes 1572872 | tf_op jit(solution)/shard_map/ppermute | solution.py:115
  67.5 35.2 %collective-permute-start.10 = (bf16[2048,384]{1,0:T(8,128)(2,1)S(1)}, bf16[2048,384]{1,0:T(8,128)(2,1)S(1)}, u32[]{:S(2)}, u32[]{:S(2)}) collective-permute-start(bf16[2048,384]{1,0:T(8,128)(2,1)S(1)} %bitcast.114), channel_id=1, source_target_pairs={{0,1},{1,0},{2,3},{3,2},{4,5},{5,4},{6,7},{7,6},{8,9},{9,8},{10,11... | collective-permute-start | bytes 4718600 | tf_op jit(solution)/shard_map/ppermute | solution.py:118
  72.9 11.8 %collective-permute-start.22 = (bf16[128,2048]{1,0:T(8,128)(2,1)S(1)}, bf16[128,2048]{1,0:T(8,128)(2,1)S(1)}, u32[]{:S(2)}, u32[]{:S(2)}) collective-permute-start(bf16[128,2048]{1,0:T(8,128)(2,1)S(1)} %collective-permute-done.19), channel_id=1, source_target_pairs={{0,2},{4,0},{8,4},{12,8},{14,12},{10,14},{6,10},{2,6},{1,3},{5,1},... | collective-permute-start | bytes 1572872 | tf_op jit(solution)/shard_map/ppermute | solution.py:115
  79.7 10.7 %collective-permute-start.26 = (bf16[64,2048]{1,0:T(8,128)(2,1)S(1)}, bf16[64,2048]{1,0:T(8,128)(2,1)S(1)}, u32[]{:S(2)}, u32[]{:S(2)}) collective-permute-start(bf16[64,2048]{1,0:T(8,128)(2,1)S(1)} %collective-permute-done.15), channel_id=1, source_target_pairs={{0,2},{4,0},{8,4},{12,8},{14,12},{10,14},{6,10},{2,6},{1,3},{5,1},... | collective-permute-start | bytes 786440 | tf_op jit(solution)/shard_map/ppermute | solution.py:115
  95.8 18.4 %collective-permute-start.11 = (f32[2,128]{1,0:T(2,128)S(1)}, f32[2,128]{1,0:T(2,128)S(1)}, u32[]{:S(2)}, u32[]{:S(2)}) collective-permute-start(f32[2,128]{1,0:T(2,128)S(1)} %get-tuple-element.111), channel_id=1, source_target_pairs={{0,14},{4,10},{8,6},{12,2},{14,0},{10,4},{6,8},{2,12},{1,15},{5,11... | collective-permute-start | bytes 3080 | tf_op jit(solution)/shard_map/ppermute | solution.py:115
  98.2 16.6 %collective-permute-start.21 = (bf16[128,2048]{1,0:T(8,128)(2,1)S(1)}, bf16[128,2048]{1,0:T(8,128)(2,1)S(1)}, u32[]{:S(2)}, u32[]{:S(2)}) collective-permute-start(bf16[128,2048]{1,0:T(8,128)(2,1)S(1)} %collective-permute-done.20), channel_id=1, source_target_pairs={{0,4},{4,8},{8,12},{12,14},{14,10},{10,6},{6,2},{2,0},{1,5},{5,9},... | collective-permute-start | bytes 1572872 | tf_op jit(solution)/shard_map/ppermute | solution.py:115
  99.5 14.7 %collective-permute-start.23 = (bf16[128,2048]{1,0:T(8,128)(2,1)S(1)}, bf16[128,2048]{1,0:T(8,128)(2,1)S(1)}, u32[]{:S(2)}, u32[]{:S(2)}) collective-permute-start(bf16[128,2048]{1,0:T(8,128)(2,1)S(1)} %collective-permute-done.22), channel_id=1, source_target_pairs={{0,2},{4,0},{8,4},{12,8},{14,12},{10,14},{6,10},{2,6},{1,3},{5,1},... | collective-permute-start | bytes 1572872 | tf_op jit(solution)/shard_map/ppermute | solution.py:115
  123.4 65.0 %collective-permute-start.44 = (bf16[384,2048]{1,0:T(8,128)(2,1)S(1)}, bf16[384,2048]{1,0:T(8,128)(2,1)S(1)}, u32[]{:S(2)}, u32[]{:S(2)}) collective-permute-start(bf16[384,2048]{1,0:T(8,128)(2,1)S(1)} %split.29), channel_id=1, source_target_pairs={{0,1},{1,0},{2,3},{3,2},{4,5},{5,4},{6,7},{7,6},{8,9},{9,8},{10,11... | collective-permute-start | bytes 4718600 | tf_op jit(solution)/shard_map/ppermute | solution.py:118
  136.5 53.6 %collective-permute-start.43 = (bf16[2048,384]{1,0:T(8,128)(2,1)S(1)}, bf16[2048,384]{1,0:T(8,128)(2,1)S(1)}, u32[]{:S(2)}, u32[]{:S(2)}) collective-permute-start(bf16[2048,384]{1,0:T(8,128)(2,1)S(1)} %split.27), channel_id=1, source_target_pairs={{0,1},{1,0},{2,3},{3,2},{4,5},{5,4},{6,7},{7,6},{8,9},{9,8},{10,11... | collective-permute-start | bytes 4718600 | tf_op jit(solution)/shard_map/ppermute | solution.py:118
  139.0 17.4 %collective-permute-start.32 = (bf16[64,2048]{1,0:T(8,128)(2,1)S(1)}, bf16[64,2048]{1,0:T(8,128)(2,1)S(1)}, u32[]{:S(2)}, u32[]{:S(2)}) collective-permute-start(bf16[64,2048]{1,0:T(8,128)(2,1)S(1)} %get-tuple-element.89), channel_id=1, source_target_pairs={{0,4},{4,8},{8,12},{12,14},{14,10},{10,6},{6,2},{2,0},{1,5},{5,9},... | collective-permute-start | bytes 786440 | tf_op jit(solution)/shard_map/ppermute | solution.py:115
  142.7 7.1 %collective-permute-start.24 = (bf16[64,2048]{1,0:T(8,128)(2,1)S(1)}, bf16[64,2048]{1,0:T(8,128)(2,1)S(1)}, u32[]{:S(2)}, u32[]{:S(2)}) collective-permute-start(bf16[64,2048]{1,0:T(8,128)(2,1)S(1)} %get-tuple-element.94), channel_id=1, source_target_pairs={{0,2},{4,0},{8,4},{12,8},{14,12},{10,14},{6,10},{2,6},{1,3},{5,1},... | collective-permute-start | bytes 786440 | tf_op jit(solution)/shard_map/ppermute | solution.py:115
  142.9 9.2 %collective-permute-start.31 = (bf16[64,2048]{1,0:T(8,128)(2,1)S(1)}, bf16[64,2048]{1,0:T(8,128)(2,1)S(1)}, u32[]{:S(2)}, u32[]{:S(2)}) collective-permute-start(bf16[64,2048]{1,0:T(8,128)(2,1)S(1)} %get-tuple-element.93), channel_id=1, source_target_pairs={{0,4},{4,8},{8,12},{12,14},{14,10},{10,6},{6,2},{2,0},{1,5},{5,9},... | collective-permute-start | bytes 786440 | tf_op jit(solution)/shard_map/ppermute | solution.py:115
  156.4 10.7 %collective-permute-start.34 = (bf16[64,2048]{1,0:T(8,128)(2,1)S(1)}, bf16[64,2048]{1,0:T(8,128)(2,1)S(1)}, u32[]{:S(2)}, u32[]{:S(2)}) collective-permute-start(bf16[64,2048]{1,0:T(8,128)(2,1)S(1)} %add_convert_fusion.13), channel_id=1, source_target_pairs={{0,2},{4,0},{8,4},{12,8},{14,12},{10,14},{6,10},{2,6},{1,3},{5,1},... | collective-permute-start | bytes 786440 | tf_op jit(solution)/shard_map/ppermute | solution.py:115
  158.8 8.6 %collective-permute-start.36 = (bf16[64,2048]{1,0:T(8,128)(2,1)S(1)}, bf16[64,2048]{1,0:T(8,128)(2,1)S(1)}, u32[]{:S(2)}, u32[]{:S(2)}) collective-permute-start(bf16[64,2048]{1,0:T(8,128)(2,1)S(1)} %add_convert_fusion.12), channel_id=1, source_target_pairs={{0,4},{4,8},{8,12},{12,14},{14,10},{10,6},{6,2},{2,0},{1,5},{5,9},... | collective-permute-start | bytes 786440 | tf_op jit(solution)/shard_map/ppermute | solution.py:115
  161.3 8.7 %collective-permute-start.39 = (bf16[64,2048]{1,0:T(8,128)(2,1)S(1)}, bf16[64,2048]{1,0:T(8,128)(2,1)S(1)}, u32[]{:S(2)}, u32[]{:S(2)}) collective-permute-start(bf16[64,2048]{1,0:T(8,128)(2,1)S(1)} %add_convert_fusion.10), channel_id=1, source_target_pairs={{0,4},{4,8},{8,12},{12,14},{14,10},{10,6},{6,2},{2,0},{1,5},{5,9},... | collective-permute-start | bytes 786440 | tf_op jit(solution)/shard_map/ppermute | solution.py:115
  167.4 10.0 %collective-permute-start.41 = (bf16[64,2048]{1,0:T(8,128)(2,1)S(1)}, bf16[64,2048]{1,0:T(8,128)(2,1)S(1)}, u32[]{:S(2)}, u32[]{:S(2)}) collective-permute-start(bf16[64,2048]{1,0:T(8,128)(2,1)S(1)} %add_convert_fusion.9), channel_id=1, source_target_pairs={{0,2},{4,0},{8,4},{12,8},{14,12},{10,14},{6,10},{2,6},{1,3},{5,1},... | collective-permute-start | bytes 786440 | tf_op jit(solution)/shard_map/ppermute | solution.py:115
  170.0 11.7 %collective-permute-start.38 = (bf16[64,2048]{1,0:T(8,128)(2,1)S(1)}, bf16[64,2048]{1,0:T(8,128)(2,1)S(1)}, u32[]{:S(2)}, u32[]{:S(2)}) collective-permute-start(bf16[64,2048]{1,0:T(8,128)(2,1)S(1)} %add_convert_fusion.8), channel_id=1, source_target_pairs={{0,4},{4,8},{8,12},{12,14},{14,10},{10,6},{6,2},{2,0},{1,5},{5,9},... | collective-permute-start | bytes 786440 | tf_op jit(solution)/shard_map/ppermute | solution.py:115
  172.8 14.4 %collective-permute-start.40 = (bf16[64,2048]{1,0:T(8,128)(2,1)S(1)}, bf16[64,2048]{1,0:T(8,128)(2,1)S(1)}, u32[]{:S(2)}, u32[]{:S(2)}) collective-permute-start(bf16[64,2048]{1,0:T(8,128)(2,1)S(1)} %add_convert_fusion.5), channel_id=1, source_target_pairs={{0,4},{4,8},{8,12},{12,14},{14,10},{10,6},{6,2},{2,0},{1,5},{5,9},... | collective-permute-start | bytes 786440 | tf_op jit(solution)/shard_map/ppermute | solution.py:115
  177.5 9.8 %collective-permute-start.37 = (bf16[64,2048]{1,0:T(8,128)(2,1)S(1)}, bf16[64,2048]{1,0:T(8,128)(2,1)S(1)}, u32[]{:S(2)}, u32[]{:S(2)}) collective-permute-start(bf16[64,2048]{1,0:T(8,128)(2,1)S(1)} %add_convert_fusion.7), channel_id=1, source_target_pairs={{0,2},{4,0},{8,4},{12,8},{14,12},{10,14},{6,10},{2,6},{1,3},{5,1},... | collective-permute-start | bytes 786440 | tf_op jit(solution)/shard_map/ppermute | solution.py:115
  181.7 9.9 %collective-permute-start.42 = (bf16[2048,384]{1,0:T(8,128)(2,1)S(1)}, bf16[2048,384]{1,0:T(8,128)(2,1)S(1)}, u32[]{:S(2)}, u32[]{:S(2)}) collective-permute-start(bf16[2048,384]{1,0:T(8,128)(2,1)S(1)} %split.25), channel_id=1, source_target_pairs={{0,1},{1,0},{2,3},{3,2},{4,5},{5,4},{6,7},{7,6},{8,9},{9,8},{10,11... | collective-permute-start | bytes 4718600 | tf_op jit(solution)/shard_map/ppermute | solution.py:118
  (17 other events, 148.7 us)

commit v11 on v10

--- a/solution.py
+++ b/solution.py
@@ -101,7 +101,7 @@
 def ring_plan(layer_input, output_grad, expert_ids, route_ints, w_gate, w_up, w_down):
     groups = lax.axis_size("grp")
     members = lax.axis_size("mem")
-    tok_rows, model_width = layer_input.shape
+    tok_rows, _ = layer_input.shape
     width = w_gate.shape[2]
     span = members * width
     order = ring_order(groups)
@@ -258,19 +258,18 @@
         if long_way is not None:
             sums = before = tuple(map(join, long_way, gated(sums)))
         long_way = send(sums)
-    back_low = [long_way and long_way[0], short_way and short_way[1]]
-    back_high = [long_way and long_way[1], short_way and short_way[0]]
-
-    def closing(rows, returned):
-        total = own_part[rows].astype(jnp.float32)
-        for piece_back in returned:
-            if piece_back is not None:
-                total = total + piece_back.astype(jnp.float32)
-        return total.astype(jnp.bfloat16)
-
-    input_grad = jnp.zeros((tok_rows, model_width), jnp.bfloat16)
-    input_grad = lax.dynamic_update_slice(input_grad, closing(low, back_low), (0, 0))
-    input_grad = lax.dynamic_update_slice(input_grad, closing(high, back_high), (half, 0))
+
+    def spread(piece_back, rows):
+        edges = [(rows.start, tok_rows - rows.stop, 0), (0, 0, 0)]
+        return lax.pad(piece_back, jnp.zeros((), jnp.bfloat16), edges).astype(jnp.float32)
+
+    total = own_part.astype(jnp.float32)
+    if short_way is not None:
+        total = total + spread(short_way[0], high) + spread(short_way[1], low)
+        total = lax.optimization_barrier(total)
+    if long_way is not None:
+        total = total + spread(long_way[0], low) + spread(long_way[1], high)
+    input_grad = total.astype(jnp.bfloat16)
 
     x_all, og_all, gg_all, ug_all, hidden_all = (
         jnp.concatenate([k[i] for k in kept], axis=0) for i in range(5)

time: 196 us -> 212 us (1.082)
  the two profiles are of different devices: /device:TPU:15 before, /device:TPU:0 now
where the time goes in v11:
time: 212 us; the launch traced here: 211 us
  waiting for transfers between devices  107 us (50%)
  starting transfers between devices  49.8 us (23%)
  matrix products  36.9 us (17%)
  other arithmetic  10.1 us (5%)
  local copies, waits for them, and re-layouts  5.79 us (3%)
    ppermute x39, waiting for transfers between devices, shift(): return lax.ppermute(array, 'grp', at_distance(k))  107 us
    ppermute x39, starting transfers between devices, shift(): return lax.ppermute(array, 'grp', at_distance(k))  48.9 us
    dot_general x28, matrix products, mm(): return lax.dot_general(a, b, dims, preferred_element_type=jnp.float32)  36.9 us
    broadcast_in_dim x3, other arithmetic, member_sum(): return total.astype(jnp.bfloat16)[None]  4.9 us
    unnamed x34, local copies, waits for them, and re-layouts  4.6 us
  transfers between devices with their start and end apart: 45, of which 26 were waited for; matrix products, arithmetic and copies ran while one was open for 18% of the time, Pallas kernels for 0%

profile of v11, /device:TPU:0, one launch (start us, length us, event | category | flops | bytes accessed | tf_op | source)
XLA Modules:
  0.0 211.3 jit_solution(6256298898009504589)
XLA Ops:
  3.8 3.1 %collective-permute-start = (f32[4,128]{1,0:T(4,128)S(1)}, f32[4,128]{1,0:T(4,128)S(1)}, u32[]{:S(2)}, u32[]{:S(2)}) collective-permute-start(f32[4,128]{1,0:T(4,128)S(1)} %pad_maximum_fusion.6), channel_id=1, source_target_pairs={{0,4},{4,8},{8,12},{12,14},{14,10},{10,6},{6,2},{2,0},{1,5},{5,9},... | collective-permute-start | bytes 6152 | tf_op jit(solution)/shard_map/ppermute | solution.py:115
  8.9 2.1 collective-permute-start.2
  11.1 2.1 collective-permute-start.6
  13.3 2.6 %collective-permute-start.11 = (f32[4,128]{1,0:T(4,128)S(1)}, f32[4,128]{1,0:T(4,128)S(1)}, u32[]{:S(2)}, u32[]{:S(2)}) collective-permute-start(f32[4,128]{1,0:T(4,128)S(1)} %pad_maximum_fusion.8), channel_id=1, source_target_pairs={{0,8},{4,12},{8,14},{12,10},{14,6},{10,2},{6,0},{2,4},{1,9},{5,13}... | collective-permute-start | bytes 6152 | tf_op jit(solution)/shard_map/ppermute | solution.py:115
  15.9 14.4 %collective-permute-done.11 = f32[4,128]{1,0:T(4,128)S(1)} collective-permute-done((f32[4,128]{1,0:T(4,128)S(1)}, f32[4,128]{1,0:T(4,128)S(1)}, u32[]{:S(2)}, u32[]{:S(2)}) %collective-permute-start.11) | collective-permute-done | bytes 2080 | tf_op jit(solution)/shard_map/ppermute | solution.py:115
  30.3 2.6 %collective-permute-start.12 = (f32[4,128]{1,0:T(4,128)S(1)}, f32[4,128]{1,0:T(4,128)S(1)}, u32[]{:S(2)}, u32[]{:S(2)}) collective-permute-start(f32[4,128]{1,0:T(4,128)S(1)} %pad_maximum_fusion.9), channel_id=1, source_target_pairs={{0,6},{4,2},{8,0},{12,4},{14,8},{10,12},{6,14},{2,10},{1,7},{5,3},... | collective-permute-start | bytes 6152 | tf_op jit(solution)/shard_map/ppermute | solution.py:115
  37.1 4.1 %collective-permute-done.7 = bf16[64,2048]{1,0:T(8,128)(2,1)S(1)} collective-permute-done((bf16[64,2048]{1,0:T(8,128)(2,1)S(1)}, bf16[64,2048]{1,0:T(8,128)(2,1)S(1)}, u32[]{:S(2)}, u32[]{:S(2)}) %collective-permute-start.7) | collective-permute-done | bytes 262176 | tf_op jit(solution)/shard_map/ppermute | solution.py:115
  49.3 2.9 %collective-permute-done.17 = bf16[64,2048]{1,0:T(8,128)(2,1)S(1)} collective-permute-done((bf16[64,2048]{1,0:T(8,128)(2,1)S(1)}, bf16[64,2048]{1,0:T(8,128)(2,1)S(1)}, u32[]{:S(2)}, u32[]{:S(2)}) %collective-permute-start.17) | collective-permute-done | bytes 262176 | tf_op jit(solution)/shard_map/ppermute | solution.py:115
  53.8 4.0 %collective-permute-done.18 = bf16[64,2048]{1,0:T(8,128)(2,1)S(1)} collective-permute-done((bf16[64,2048]{1,0:T(8,128)(2,1)S(1)}, bf16[64,2048]{1,0:T(8,128)(2,1)S(1)}, u32[]{:S(2)}, u32[]{:S(2)}) %collective-permute-start.18) | collective-permute-done | bytes 262176 | tf_op jit(solution)/shard_map/ppermute | solution.py:115
  59.4 9.1 %collective-permute-done.14 = bf16[128,2048]{1,0:T(8,128)(2,1)S(1)} collective-permute-done((bf16[128,2048]{1,0:T(8,128)(2,1)S(1)}, bf16[128,2048]{1,0:T(8,128)(2,1)S(1)}, u32[]{:S(2)}, u32[]{:S(2)}) %collective-permute-start.14) | collective-permute-done | bytes 524320 | tf_op jit(solution)/shard_map/ppermute | solution.py:115
  70.9 5.5 %collective-permute-done.16 = bf16[64,2048]{1,0:T(8,128)(2,1)S(1)} collective-permute-done((bf16[64,2048]{1,0:T(8,128)(2,1)S(1)}, bf16[64,2048]{1,0:T(8,128)(2,1)S(1)}, u32[]{:S(2)}, u32[]{:S(2)}) %collective-permute-start.16) | collective-permute-done | bytes 262176 | tf_op jit(solution)/shard_map/ppermute | solution.py:115
  78.0 5.4 %collective-permute-done.20 = bf16[128,2048]{1,0:T(8,128)(2,1)S(1)} collective-permute-done((bf16[128,2048]{1,0:T(8,128)(2,1)S(1)}, bf16[128,2048]{1,0:T(8,128)(2,1)S(1)}, u32[]{:S(2)}, u32[]{:S(2)}) %collective-permute-start.20) | collective-permute-done | bytes 524320 | tf_op jit(solution)/shard_map/ppermute | solution.py:115
  83.9 7.3 %collective-permute-done.22 = bf16[128,2048]{1,0:T(8,128)(2,1)S(1)} collective-permute-done((bf16[128,2048]{1,0:T(8,128)(2,1)S(1)}, bf16[128,2048]{1,0:T(8,128)(2,1)S(1)}, u32[]{:S(2)}, u32[]{:S(2)}) %collective-permute-start.22) | collective-permute-done | bytes 524320 | tf_op jit(solution)/shard_map/ppermute | solution.py:115
  91.7 2.9 %collective-permute-done.25 = bf16[64,2048]{1,0:T(8,128)(2,1)S(1)} collective-permute-done((bf16[64,2048]{1,0:T(8,128)(2,1)S(1)}, bf16[64,2048]{1,0:T(8,128)(2,1)S(1)}, u32[]{:S(2)}, u32[]{:S(2)}) %collective-permute-start.25) | collective-permute-done | bytes 262176 | tf_op jit(solution)/shard_map/ppermute | solution.py:115
  96.3 2.3 %collective-permute-done.24 = bf16[64,2048]{1,0:T(8,128)(2,1)S(1)} collective-permute-done((bf16[64,2048]{1,0:T(8,128)(2,1)S(1)}, bf16[64,2048]{1,0:T(8,128)(2,1)S(1)}, u32[]{:S(2)}, u32[]{:S(2)}) %collective-permute-start.24) | collective-permute-done | bytes 262176 | tf_op jit(solution)/shard_map/ppermute | solution.py:115
  101.0 2.8 %collective-permute-start.13 = (f32[2,128]{1,0:T(2,128)S(1)}, f32[2,128]{1,0:T(2,128)S(1)}, u32[]{:S(2)}, u32[]{:S(2)}) collective-permute-start(f32[2,128]{1,0:T(2,128)S(1)} %get-tuple-element.109), channel_id=1, source_target_pairs={{0,14},{4,10},{8,6},{12,2},{14,0},{10,4},{6,8},{2,12},{1,15},{5,11... | collective-permute-start | bytes 3080 | tf_op jit(solution)/shard_map/ppermute | solution.py:115
  103.8 4.1 %collective-permute-done.28 = bf16[64,2048]{1,0:T(8,128)(2,1)S(1)} collective-permute-done((bf16[64,2048]{1,0:T(8,128)(2,1)S(1)}, bf16[64,2048]{1,0:T(8,128)(2,1)S(1)}, u32[]{:S(2)}, u32[]{:S(2)}) %collective-permute-start.28) | collective-permute-done | bytes 262176 | tf_op jit(solution)/shard_map/ppermute | solution.py:115
  108.0 2.7 %collective-permute-start.23 = (bf16[128,2048]{1,0:T(8,128)(2,1)S(1)}, bf16[128,2048]{1,0:T(8,128)(2,1)S(1)}, u32[]{:S(2)}, u32[]{:S(2)}) collective-permute-start(bf16[128,2048]{1,0:T(8,128)(2,1)S(1)} %collective-permute-done.22), channel_id=1, source_target_pairs={{0,2},{4,0},{8,4},{12,8},{14,12},{10,14},{6,10},{2,6},{1,3},{5,1},... | collective-permute-start | bytes 1572872 | tf_op jit(solution)/shard_map/ppermute | solution.py:115
  132.2 3.7 %convolution_convert_fusion = bf16[768,2048]{1,0:T(8,128)(2,1)S(1)} fusion(bf16[1024,768]{1,0:T(8,128)(2,1)S(1)} %get-tuple-element.72, bf16[1024,2048]{1,0:T(8,128)(2,1)S(1)} %constant_dynamic-update-slice_fusion.27), kind=kOutput, calls=%fused_computation | convolution fusion | flops 3222798336 | bytes 8912896 | tf_op jit(solution)/shard_map/dot_general | solution.py:98
  136.3 3.8 %convolution_convert_fusion.1 = bf16[2048,768]{1,0:T(8,128)(2,1)S(1)} fusion(bf16[1024,2048]{1,0:T(8,128)(2,1)S(1)} %constant_dynamic-update-slice_fusion.7, bf16[1024,768]{1,0:T(8,128)(2,1)S(1)} %get-tuple-element.73), kind=kOutput, calls=%fused_computation.1 | convolution fusion | flops 3222798336 | bytes 8912896 | tf_op jit(solution)/shard_map/dot_general | solution.py:98
  140.8 3.7 %convolution_convert_fusion.2 = bf16[2048,768]{1,0:T(8,128)(2,1)S(1)} fusion(bf16[1024,2048]{1,0:T(8,128)(2,1)S(1)} %constant_dynamic-update-slice_fusion.7, bf16[1024,768]{1,0:T(8,128)(2,1)S(1)} %get-tuple-element.48), kind=kOutput, calls=%fused_computation.2 | convolution fusion | flops 3222798336 | bytes 8912896 | tf_op jit(solution)/shard_map/dot_general | solution.py:98
  153.8 4.4 %collective-permute-done.27 = bf16[64,2048]{1,0:T(8,128)(2,1)S(1)} collective-permute-done((bf16[64,2048]{1,0:T(8,128)(2,1)S(1)}, bf16[64,2048]{1,0:T(8,128)(2,1)S(1)}, u32[]{:S(2)}, u32[]{:S(2)}) %collective-permute-start.27) | collective-permute-done | bytes 262176 | tf_op jit(solution)/shard_map/ppermute | solution.py:115
  160.4 5.6 %collective-permute-done.33 = bf16[64,2048]{1,0:T(8,128)(2,1)S(1)} collective-permute-done((bf16[64,2048]{1,0:T(8,128)(2,1)S(1)}, bf16[64,2048]{1,0:T(8,128)(2,1)S(1)}, u32[]{:S(2)}, u32[]{:S(2)}) %collective-permute-start.33) | collective-permute-done | bytes 262176 | tf_op jit(solution)/shard_map/ppermute | solution.py:115
  168.3 4.8 %collective-permute-done.34 = bf16[64,2048]{1,0:T(8,128)(2,1)S(1)} collective-permute-done((bf16[64,2048]{1,0:T(8,128)(2,1)S(1)}, bf16[64,2048]{1,0:T(8,128)(2,1)S(1)}, u32[]{:S(2)}, u32[]{:S(2)}) %collective-permute-start.34) | collective-permute-done | bytes 262176 | tf_op jit(solution)/shard_map/ppermute | solution.py:115
  175.2 4.3 %collective-permute-done.31 = bf16[64,2048]{1,0:T(8,128)(2,1)S(1)} collective-permute-done((bf16[64,2048]{1,0:T(8,128)(2,1)S(1)}, bf16[64,2048]{1,0:T(8,128)(2,1)S(1)}, u32[]{:S(2)}, u32[]{:S(2)}) %collective-permute-start.31) | collective-permute-done | bytes 262176 | tf_op jit(solution)/shard_map/ppermute | solution.py:115
  179.5 2.3 %collective-permute-start.38 = (bf16[64,2048]{1,0:T(8,128)(2,1)S(1)}, bf16[64,2048]{1,0:T(8,128)(2,1)S(1)}, u32[]{:S(2)}, u32[]{:S(2)}) collective-permute-start(bf16[64,2048]{1,0:T(8,128)(2,1)S(1)} %add_convert_fusion.10), channel_id=1, source_target_pairs={{0,2},{4,0},{8,4},{12,8},{14,12},{10,14},{6,10},{2,6},{1,3},{5,1},... | collective-permute-start | bytes 786440 | tf_op jit(solution)/shard_map/ppermute | solution.py:115
  182.0 5.5 %collective-permute-done.38 = bf16[64,2048]{1,0:T(8,128)(2,1)S(1)} collective-permute-done((bf16[64,2048]{1,0:T(8,128)(2,1)S(1)}, bf16[64,2048]{1,0:T(8,128)(2,1)S(1)}, u32[]{:S(2)}, u32[]{:S(2)}) %collective-permute-start.38) | collective-permute-done | bytes 262176 | tf_op jit(solution)/shard_map/ppermute | solution.py:115
  187.5 2.5 %collective-permute-start.35 = (bf16[64,2048]{1,0:T(8,128)(2,1)S(1)}, bf16[64,2048]{1,0:T(8,128)(2,1)S(1)}, u32[]{:S(2)}, u32[]{:S(2)}) collective-permute-start(bf16[64,2048]{1,0:T(8,128)(2,1)S(1)} %add_convert_fusion.8), channel_id=1, source_target_pairs={{0,2},{4,0},{8,4},{12,8},{14,12},{10,14},{6,10},{2,6},{1,3},{5,1},... | collective-permute-start | bytes 786440 | tf_op jit(solution)/shard_map/ppermute | solution.py:115
  190.2 6.3 %collective-permute-done.35 = bf16[64,2048]{1,0:T(8,128)(2,1)S(1)} collective-permute-done((bf16[64,2048]{1,0:T(8,128)(2,1)S(1)}, bf16[64,2048]{1,0:T(8,128)(2,1)S(1)}, u32[]{:S(2)}, u32[]{:S(2)}) %collective-permute-start.35) | collective-permute-done | bytes 262176 | tf_op jit(solution)/shard_map/ppermute | solution.py:115
  196.5 2.5 %collective-permute-start.39 = (bf16[64,2048]{1,0:T(8,128)(2,1)S(1)}, bf16[64,2048]{1,0:T(8,128)(2,1)S(1)}, u32[]{:S(2)}, u32[]{:S(2)}) collective-permute-start(bf16[64,2048]{1,0:T(8,128)(2,1)S(1)} %add_convert_fusion.6), channel_id=1, source_target_pairs={{0,2},{4,0},{8,4},{12,8},{14,12},{10,14},{6,10},{2,6},{1,3},{5,1},... | collective-permute-start | bytes 786440 | tf_op jit(solution)/shard_map/ppermute | solution.py:115
  199.2 3.6 %collective-permute-done.39 = bf16[64,2048]{1,0:T(8,128)(2,1)S(1)} collective-permute-done((bf16[64,2048]{1,0:T(8,128)(2,1)S(1)}, bf16[64,2048]{1,0:T(8,128)(2,1)S(1)}, u32[]{:S(2)}, u32[]{:S(2)}) %collective-permute-start.39) | collective-permute-done | bytes 262176 | tf_op jit(solution)/shard_map/ppermute | solution.py:115
  202.9 2.6 %collective-permute-done.41 = bf16[64,2048]{1,0:T(8,128)(2,1)S(1)} collective-permute-done((bf16[64,2048]{1,0:T(8,128)(2,1)S(1)}, bf16[64,2048]{1,0:T(8,128)(2,1)S(1)}, u32[]{:S(2)}, u32[]{:S(2)}) %collective-permute-start.41) | collective-permute-done | bytes 262176 | tf_op jit(solution)/shard_map/ppermute | solution.py:115
  (180 shorter events, 74.5 us)
Async XLA Ops:
  8.8 103.3 %collective-permute-start.5 = (bf16[384,2048]{0,1:T(8,128)(2,1)S(1)}, bf16[384,2048]{0,1:T(8,128)(2,1)S(1)}, u32[]{:S(2)}, u32[]{:S(2)}) collective-permute-start(bf16[384,2048]{0,1:T(8,128)(2,1)S(1)} %bitcast.94), channel_id=1, source_target_pairs={{0,1},{1,0},{2,3},{3,2},{4,5},{5,4},{6,7},{7,6},{8,9},{9,8},{10,11... | collective-permute-start | bytes 4718600 | tf_op jit(solution)/shard_map/ppermute | solution.py:118
  8.9 33.9 %collective-permute-start.2 = (bf16[128,2048]{1,0:T(8,128)(2,1)S(1)}, bf16[128,2048]{1,0:T(8,128)(2,1)S(1)}, u32[]{:S(2)}, u32[]{:S(2)}) collective-permute-start(bf16[128,2048]{1,0:T(8,128)(2,1)S(1)} %copy-done.1), channel_id=1, source_target_pairs={{0,4},{4,8},{8,12},{12,14},{14,10},{10,6},{6,2},{2,0},{1,5},{5,9},... | collective-permute-start | bytes 1572872 | tf_op jit(solution)/shard_map/ppermute | solution.py:115
  11.0 31.9 %collective-permute-start.8 = (bf16[128,2048]{1,0:T(8,128)(2,1)S(1)}, bf16[128,2048]{1,0:T(8,128)(2,1)S(1)}, u32[]{:S(2)}, u32[]{:S(2)}) collective-permute-start(bf16[128,2048]{1,0:T(8,128)(2,1)S(1)} %copy-done), channel_id=1, source_target_pairs={{0,2},{4,0},{8,4},{12,8},{14,12},{10,14},{6,10},{2,6},{1,3},{5,1},... | collective-permute-start | bytes 1572872 | tf_op jit(solution)/shard_map/ppermute | solution.py:115
  11.1 24.2 %collective-permute-start.6 = (bf16[64,2048]{1,0:T(8,128)(2,1)S(1)}, bf16[64,2048]{1,0:T(8,128)(2,1)S(1)}, u32[]{:S(2)}, u32[]{:S(2)}) collective-permute-start(bf16[64,2048]{1,0:T(8,128)(2,1)S(1)} %get-tuple-element.98), channel_id=1, source_target_pairs={{0,4},{4,8},{8,12},{12,14},{14,10},{10,6},{6,2},{2,0},{1,5},{5,9},... | collective-permute-start | bytes 786440 | tf_op jit(solution)/shard_map/ppermute | solution.py:115
  13.3 17.0 %collective-permute-start.11 = (f32[4,128]{1,0:T(4,128)S(1)}, f32[4,128]{1,0:T(4,128)S(1)}, u32[]{:S(2)}, u32[]{:S(2)}) collective-permute-start(f32[4,128]{1,0:T(4,128)S(1)} %pad_maximum_fusion.8), channel_id=1, source_target_pairs={{0,8},{4,12},{8,14},{12,10},{14,6},{10,2},{6,0},{2,4},{1,9},{5,13}... | collective-permute-start | bytes 6152 | tf_op jit(solution)/shard_map/ppermute | solution.py:115
  35.4 8.2 %collective-permute-start.3 = (bf16[64,2048]{1,0:T(8,128)(2,1)S(1)}, bf16[64,2048]{1,0:T(8,128)(2,1)S(1)}, u32[]{:S(2)}, u32[]{:S(2)}) collective-permute-start(bf16[64,2048]{1,0:T(8,128)(2,1)S(1)} %get-tuple-element.99), channel_id=1, source_target_pairs={{0,2},{4,0},{8,4},{12,8},{14,12},{10,14},{6,10},{2,6},{1,3},{5,1},... | collective-permute-start | bytes 786440 | tf_op jit(solution)/shard_map/ppermute | solution.py:115
  42.8 65.2 %collective-permute-start.9 = (bf16[2048,384]{1,0:T(8,128)(2,1)S(1)}, bf16[2048,384]{1,0:T(8,128)(2,1)S(1)}, u32[]{:S(2)}, u32[]{:S(2)}) collective-permute-start(bf16[2048,384]{1,0:T(8,128)(2,1)S(1)} %bitcast.103), channel_id=1, source_target_pairs={{0,1},{1,0},{2,3},{3,2},{4,5},{5,4},{6,7},{7,6},{8,9},{9,8},{10,11... | collective-permute-start | bytes 4718600 | tf_op jit(solution)/shard_map/ppermute | solution.py:118
  42.9 9.2 %collective-permute-start.17 = (bf16[64,2048]{1,0:T(8,128)(2,1)S(1)}, bf16[64,2048]{1,0:T(8,128)(2,1)S(1)}, u32[]{:S(2)}, u32[]{:S(2)}) collective-permute-start(bf16[64,2048]{1,0:T(8,128)(2,1)S(1)} %collective-permute-done.6), channel_id=1, source_target_pairs={{0,4},{4,8},{8,12},{12,14},{14,10},{10,6},{6,2},{2,0},{1,5},{5,9},... | collective-permute-start | bytes 786440 | tf_op jit(solution)/shard_map/ppermute | solution.py:115
  43.5 14.2 %collective-permute-start.18 = (bf16[64,2048]{1,0:T(8,128)(2,1)S(1)}, bf16[64,2048]{1,0:T(8,128)(2,1)S(1)}, u32[]{:S(2)}, u32[]{:S(2)}) collective-permute-start(bf16[64,2048]{1,0:T(8,128)(2,1)S(1)} %collective-permute-done.7), channel_id=1, source_target_pairs={{0,4},{4,8},{8,12},{12,14},{14,10},{10,6},{6,2},{2,0},{1,5},{5,9},... | collective-permute-start | bytes 786440 | tf_op jit(solution)/shard_map/ppermute | solution.py:115
  47.5 21.0 %collective-permute-start.14 = (bf16[128,2048]{1,0:T(8,128)(2,1)S(1)}, bf16[128,2048]{1,0:T(8,128)(2,1)S(1)}, u32[]{:S(2)}, u32[]{:S(2)}) collective-permute-start(bf16[128,2048]{1,0:T(8,128)(2,1)S(1)} %collective-permute-done.2), channel_id=1, source_target_pairs={{0,4},{4,8},{8,12},{12,14},{14,10},{10,6},{6,2},{2,0},{1,5},{5,9},... | collective-permute-start | bytes 1572872 | tf_op jit(solution)/shard_map/ppermute | solution.py:115
  52.2 18.0 %collective-permute-start.15 = (bf16[64,2048]{1,0:T(8,128)(2,1)S(1)}, bf16[64,2048]{1,0:T(8,128)(2,1)S(1)}, u32[]{:S(2)}, u32[]{:S(2)}) collective-permute-start(bf16[64,2048]{1,0:T(8,128)(2,1)S(1)} %collective-permute-done.3), channel_id=1, source_target_pairs={{0,2},{4,0},{8,4},{12,8},{14,12},{10,14},{6,10},{2,6},{1,3},{5,1},... | collective-permute-start | bytes 786440 | tf_op jit(solution)/shard_map/ppermute | solution.py:115
  57.8 13.0 %collective-permute-start.19 = (bf16[128,2048]{1,0:T(8,128)(2,1)S(1)}, bf16[128,2048]{1,0:T(8,128)(2,1)S(1)}, u32[]{:S(2)}, u32[]{:S(2)}) collective-permute-start(bf16[128,2048]{1,0:T(8,128)(2,1)S(1)} %collective-permute-done.8), channel_id=1, source_target_pairs={{0,2},{4,0},{8,4},{12,8},{14,12},{10,14},{6,10},{2,6},{1,3},{5,1},... | collective-permute-start | bytes 1572872 | tf_op jit(solution)/shard_map/ppermute | solution.py:115
  68.5 7.8 %collective-permute-start.16 = (bf16[64,2048]{1,0:T(8,128)(2,1)S(1)}, bf16[64,2048]{1,0:T(8,128)(2,1)S(1)}, u32[]{:S(2)}, u32[]{:S(2)}) collective-permute-start(bf16[64,2048]{1,0:T(8,128)(2,1)S(1)} %collective-permute-done.4), channel_id=1, source_target_pairs={{0,2},{4,0},{8,4},{12,8},{14,12},{10,14},{6,10},{2,6},{1,3},{5,1},... | collective-permute-start | bytes 786440 | tf_op jit(solution)/shard_map/ppermute | solution.py:115
  70.2 13.2 %collective-permute-start.20 = (bf16[128,2048]{1,0:T(8,128)(2,1)S(1)}, bf16[128,2048]{1,0:T(8,128)(2,1)S(1)}, u32[]{:S(2)}, u32[]{:S(2)}) collective-permute-start(bf16[128,2048]{1,0:T(8,128)(2,1)S(1)} %collective-permute-done.14), channel_id=1, source_target_pairs={{0,4},{4,8},{8,12},{12,14},{14,10},{10,6},{6,2},{2,0},{1,5},{5,9},... | collective-permute-start | bytes 1572872 | tf_op jit(solution)/shard_map/ppermute | solution.py:115
  70.8 42.8 %collective-permute-start.10 = (bf16[2048,384]{1,0:T(8,128)(2,1)S(1)}, bf16[2048,384]{1,0:T(8,128)(2,1)S(1)}, u32[]{:S(2)}, u32[]{:S(2)}) collective-permute-start(bf16[2048,384]{1,0:T(8,128)(2,1)S(1)} %bitcast.114), channel_id=1, source_target_pairs={{0,1},{1,0},{2,3},{3,2},{4,5},{5,4},{6,7},{7,6},{8,9},{9,8},{10,11... | collective-permute-start | bytes 4718600 | tf_op jit(solution)/shard_map/ppermute | solution.py:118
  76.4 14.8 %collective-permute-start.22 = (bf16[128,2048]{1,0:T(8,128)(2,1)S(1)}, bf16[128,2048]{1,0:T(8,128)(2,1)S(1)}, u32[]{:S(2)}, u32[]{:S(2)}) collective-permute-start(bf16[128,2048]{1,0:T(8,128)(2,1)S(1)} %collective-permute-done.19), channel_id=1, source_target_pairs={{0,2},{4,0},{8,4},{12,8},{14,12},{10,14},{6,10},{2,6},{1,3},{5,1},... | collective-permute-start | bytes 1572872 | tf_op jit(solution)/shard_map/ppermute | solution.py:115
  83.4 11.2 %collective-permute-start.25 = (bf16[64,2048]{1,0:T(8,128)(2,1)S(1)}, bf16[64,2048]{1,0:T(8,128)(2,1)S(1)}, u32[]{:S(2)}, u32[]{:S(2)}) collective-permute-start(bf16[64,2048]{1,0:T(8,128)(2,1)S(1)} %collective-permute-done.15), channel_id=1, source_target_pairs={{0,2},{4,0},{8,4},{12,8},{14,12},{10,14},{6,10},{2,6},{1,3},{5,1},... | collective-permute-start | bytes 786440 | tf_op jit(solution)/shard_map/ppermute | solution.py:115
  98.6 9.3 %collective-permute-start.28 = (bf16[64,2048]{1,0:T(8,128)(2,1)S(1)}, bf16[64,2048]{1,0:T(8,128)(2,1)S(1)}, u32[]{:S(2)}, u32[]{:S(2)}) collective-permute-start(bf16[64,2048]{1,0:T(8,128)(2,1)S(1)} %collective-permute-done.17), channel_id=1, source_target_pairs={{0,4},{4,8},{8,12},{12,14},{14,10},{10,6},{6,2},{2,0},{1,5},{5,9},... | collective-permute-start | bytes 786440 | tf_op jit(solution)/shard_map/ppermute | solution.py:115
  101.0 24.7 %collective-permute-start.13 = (f32[2,128]{1,0:T(2,128)S(1)}, f32[2,128]{1,0:T(2,128)S(1)}, u32[]{:S(2)}, u32[]{:S(2)}) collective-permute-start(f32[2,128]{1,0:T(2,128)S(1)} %get-tuple-element.109), channel_id=1, source_target_pairs={{0,14},{4,10},{8,6},{12,2},{14,0},{10,4},{6,8},{2,12},{1,15},{5,11... | collective-permute-start | bytes 3080 | tf_op jit(solution)/shard_map/ppermute | solution.py:115
  108.0 18.3 %collective-permute-start.21 = (bf16[128,2048]{1,0:T(8,128)(2,1)S(1)}, bf16[128,2048]{1,0:T(8,128)(2,1)S(1)}, u32[]{:S(2)}, u32[]{:S(2)}) collective-permute-start(bf16[128,2048]{1,0:T(8,128)(2,1)S(1)} %collective-permute-done.20), channel_id=1, source_target_pairs={{0,4},{4,8},{8,12},{12,14},{14,10},{10,6},{6,2},{2,0},{1,5},{5,9},... | collective-permute-start | bytes 1572872 | tf_op jit(solution)/shard_map/ppermute | solution.py:115
  108.0 17.7 %collective-permute-start.23 = (bf16[128,2048]{1,0:T(8,128)(2,1)S(1)}, bf16[128,2048]{1,0:T(8,128)(2,1)S(1)}, u32[]{:S(2)}, u32[]{:S(2)}) collective-permute-start(bf16[128,2048]{1,0:T(8,128)(2,1)S(1)} %collective-permute-done.22), channel_id=1, source_target_pairs={{0,2},{4,0},{8,4},{12,8},{14,12},{10,14},{6,10},{2,6},{1,3},{5,1},... | collective-permute-start | bytes 1572872 | tf_op jit(solution)/shard_map/ppermute | solution.py:115
  136.1 70.3 %collective-permute-start.44 = (bf16[384,2048]{1,0:T(8,128)(2,1)S(1)}, bf16[384,2048]{1,0:T(8,128)(2,1)S(1)}, u32[]{:S(2)}, u32[]{:S(2)}) collective-permute-start(bf16[384,2048]{1,0:T(8,128)(2,1)S(1)} %split.29), channel_id=1, source_target_pairs={{0,1},{1,0},{2,3},{3,2},{4,5},{5,4},{6,7},{7,6},{8,9},{9,8},{10,11... | collective-permute-start | bytes 4718600 | tf_op jit(solution)/shard_map/ppermute | solution.py:118
  140.2 68.0 %collective-permute-start.43 = (bf16[2048,384]{1,0:T(8,128)(2,1)S(1)}, bf16[2048,384]{1,0:T(8,128)(2,1)S(1)}, u32[]{:S(2)}, u32[]{:S(2)}) collective-permute-start(bf16[2048,384]{1,0:T(8,128)(2,1)S(1)} %split.27), channel_id=1, source_target_pairs={{0,1},{1,0},{2,3},{3,2},{4,5},{5,4},{6,7},{7,6},{8,9},{9,8},{10,11... | collective-permute-start | bytes 4718600 | tf_op jit(solution)/shard_map/ppermute | solution.py:118
  144.7 65.0 %collective-permute-start.42 = (bf16[2048,384]{1,0:T(8,128)(2,1)S(1)}, bf16[2048,384]{1,0:T(8,128)(2,1)S(1)}, u32[]{:S(2)}, u32[]{:S(2)}) collective-permute-start(bf16[2048,384]{1,0:T(8,128)(2,1)S(1)} %split.25), channel_id=1, source_target_pairs={{0,1},{1,0},{2,3},{3,2},{4,5},{5,4},{6,7},{7,6},{8,9},{9,8},{10,11... | collective-permute-start | bytes 4718600 | tf_op jit(solution)/shard_map/ppermute | solution.py:118
  149.5 8.7 %collective-permute-start.27 = (bf16[64,2048]{1,0:T(8,128)(2,1)S(1)}, bf16[64,2048]{1,0:T(8,128)(2,1)S(1)}, u32[]{:S(2)}, u32[]{:S(2)}) collective-permute-start(bf16[64,2048]{1,0:T(8,128)(2,1)S(1)} %get-tuple-element.92), channel_id=1, source_target_pairs={{0,2},{4,0},{8,4},{12,8},{14,12},{10,14},{6,10},{2,6},{1,3},{5,1},... | collective-permute-start | bytes 786440 | tf_op jit(solution)/shard_map/ppermute | solution.py:115
  151.3 8.4 %collective-permute-start.30 = (bf16[64,2048]{1,0:T(8,128)(2,1)S(1)}, bf16[64,2048]{1,0:T(8,128)(2,1)S(1)}, u32[]{:S(2)}, u32[]{:S(2)}) collective-permute-start(bf16[64,2048]{1,0:T(8,128)(2,1)S(1)} %get-tuple-element.91), channel_id=1, source_target_pairs={{0,4},{4,8},{8,12},{12,14},{14,10},{10,6},{6,2},{2,0},{1,5},{5,9},... | collective-permute-start | bytes 786440 | tf_op jit(solution)/shard_map/ppermute | solution.py:115
  158.2 7.8 %collective-permute-start.33 = (bf16[64,2048]{1,0:T(8,128)(2,1)S(1)}, bf16[64,2048]{1,0:T(8,128)(2,1)S(1)}, u32[]{:S(2)}, u32[]{:S(2)}) collective-permute-start(bf16[64,2048]{1,0:T(8,128)(2,1)S(1)} %get-tuple-element.87), channel_id=1, source_target_pairs={{0,4},{4,8},{8,12},{12,14},{14,10},{10,6},{6,2},{2,0},{1,5},{5,9},... | collective-permute-start | bytes 786440 | tf_op jit(solution)/shard_map/ppermute | solution.py:115
  167.2 7.6 %collective-permute-start.32 = (bf16[64,2048]{1,0:T(8,128)(2,1)S(1)}, bf16[64,2048]{1,0:T(8,128)(2,1)S(1)}, u32[]{:S(2)}, u32[]{:S(2)}) collective-permute-start(bf16[64,2048]{1,0:T(8,128)(2,1)S(1)} %get-tuple-element.90), channel_id=1, source_target_pairs={{0,2},{4,0},{8,4},{12,8},{14,12},{10,14},{6,10},{2,6},{1,3},{5,1},... | collective-permute-start | bytes 786440 | tf_op jit(solution)/shard_map/ppermute | solution.py:115
  179.5 8.0 %collective-permute-start.38 = (bf16[64,2048]{1,0:T(8,128)(2,1)S(1)}, bf16[64,2048]{1,0:T(8,128)(2,1)S(1)}, u32[]{:S(2)}, u32[]{:S(2)}) collective-permute-start(bf16[64,2048]{1,0:T(8,128)(2,1)S(1)} %add_convert_fusion.10), channel_id=1, source_target_pairs={{0,2},{4,0},{8,4},{12,8},{14,12},{10,14},{6,10},{2,6},{1,3},{5,1},... | collective-permute-start | bytes 786440 | tf_op jit(solution)/shard_map/ppermute | solution.py:115
  181.8 8.2 %collective-permute-start.40 = (bf16[64,2048]{1,0:T(8,128)(2,1)S(1)}, bf16[64,2048]{1,0:T(8,128)(2,1)S(1)}, u32[]{:S(2)}, u32[]{:S(2)}) collective-permute-start(bf16[64,2048]{1,0:T(8,128)(2,1)S(1)} %add_convert_fusion.9), channel_id=1, source_target_pairs={{0,4},{4,8},{8,12},{12,14},{14,10},{10,6},{6,2},{2,0},{1,5},{5,9},... | collective-permute-start | bytes 786440 | tf_op jit(solution)/shard_map/ppermute | solution.py:115
  187.5 9.0 %collective-permute-start.35 = (bf16[64,2048]{1,0:T(8,128)(2,1)S(1)}, bf16[64,2048]{1,0:T(8,128)(2,1)S(1)}, u32[]{:S(2)}, u32[]{:S(2)}) collective-permute-start(bf16[64,2048]{1,0:T(8,128)(2,1)S(1)} %add_convert_fusion.8), channel_id=1, source_target_pairs={{0,2},{4,0},{8,4},{12,8},{14,12},{10,14},{6,10},{2,6},{1,3},{5,1},... | collective-permute-start | bytes 786440 | tf_op jit(solution)/shard_map/ppermute | solution.py:115
  190.0 9.1 %collective-permute-start.37 = (bf16[64,2048]{1,0:T(8,128)(2,1)S(1)}, bf16[64,2048]{1,0:T(8,128)(2,1)S(1)}, u32[]{:S(2)}, u32[]{:S(2)}) collective-permute-start(bf16[64,2048]{1,0:T(8,128)(2,1)S(1)} %add_convert_fusion.7), channel_id=1, source_target_pairs={{0,4},{4,8},{8,12},{12,14},{14,10},{10,6},{6,2},{2,0},{1,5},{5,9},... | collective-permute-start | bytes 786440 | tf_op jit(solution)/shard_map/ppermute | solution.py:115
  (21 other events, 169.3 us)
